TPU v7x, 32 devices: a whole 2x2x4 slice. The times are simulated.
32 devices in a mesh: groups: 2 (over y), space: 16 (over z, x, core).
Axes of the slice: x: 2, y: 2, z: 4, core: 2. Of those that a mesh axis runs over, the one named last changes fastest.
Arguments:
- features: bfloat16 [64, 128, 2048], P(None, 'space', 'groups'), parts along dimension 2, may hold values from -6 to 6
- cotangent: bfloat16 [64, 128, 2048], P(None, 'space', 'groups'), parts along dimension 2, may hold values from -6 to 6
- kernels: bfloat16 [2, 2, 64, 576], replicated, may hold values from -0.25 to 0.25
Outputs:
- section_output: bfloat16 [64, 128, 2048], P(None, 'space', 'groups'), parts along dimension 2
- input_grad: bfloat16 [64, 128, 2048], P(None, 'space', 'groups'), parts along dimension 2
- kernel_grad: float32 [4, 2, 64, 576], P('groups'), parts along dimension 0
There are 2 independent parts, one for each index of `groups`. A program takes and returns all parts, laid end to end along the dimension named above; an argument that names none is the same for every part. Nothing has to cross between parts.
All inputs are finite; a program needn't handle non-finite values.
Results may differ from a plain program's by a relative error of at most 0.0085.
The roundings to bfloat16 on the way count: a program that leaves them out, or rounds other values in their place, can miss the bound.
Values may be sent and summed in bfloat16 or wider, within the bound.
No kernel may reach another device: no remote copies, remote signals or barrier semaphores. Data moves between devices by JAX's collectives and lax.ppermute only.
A program may use at most 128 MiB of HBM per device.

v0:
```python
import functools
import math

import jax
import jax.numpy as jnp
from jax import lax
from jax.experimental import pallas as pl
from jax.experimental.pallas import tpu as pltpu
from jax.sharding import PartitionSpec as P

CHAN = 64
STACK = 3 * CHAN
F32 = jnp.float32
BF16 = jnp.bfloat16
VMEM = pl.BlockSpec(memory_space=pltpu.VMEM)


def call(body, operands, outs, scratch, flops, name):
    nbytes = sum(v.size * v.dtype.itemsize for v in (*operands, *outs))
    held = sum(math.prod(v.shape) * jnp.dtype(v.dtype).itemsize for v in scratch)
    return pl.pallas_call(
        body,
        out_shape=outs,
        in_specs=[VMEM] * len(operands),
        out_specs=[VMEM] * len(outs),
        scratch_shapes=scratch,
        compiler_params=pltpu.CompilerParams(vmem_limit_bytes=nbytes + held + (6 << 20)),
        cost_estimate=pl.CostEstimate(flops=flops, bytes_accessed=nbytes, transcendentals=0),
        name=name,
    )(*operands)


def stacked(field):
    width = field.shape[1]
    lane = lax.broadcasted_iota(jnp.int32, field.shape, 1)
    zero = jnp.zeros_like(field)
    left = jnp.where(lane == 0, zero, pltpu.roll(field, 1, 1))
    right = jnp.where(lane == width - 1, zero, pltpu.roll(field, width - 1, 1))
    return jnp.concatenate([left, field, right], axis=0)


def put(ref, row, field):
    ref[row * STACK : (row + 1) * STACK, :] = stacked(field)


def middle(ref, row):
    return ref[row * STACK + CHAN : row * STACK + 2 * CHAN, :]


def one(ref, row):
    return ref[row * CHAN : (row + 1) * CHAN, :]


def stack_rows(pieces, target):
    at = 0
    for ref, count in pieces:
        for row in range(count):
            put(target, at, one(ref, row))
            at += 1


def two_rows(matrix_ref, target):
    target[...] = jnp.zeros_like(target)
    target[:CHAN, : 3 * STACK] = matrix_ref[...]
    target[CHAN:, STACK:] = matrix_ref[...]


def conv_rows(weight_ref, source, count, finish):
    for row in range(0, count, 2):
        total = jnp.dot(
            weight_ref[...],
            source[row * STACK : (row + 4) * STACK, :],
            preferred_element_type=F32,
        )
        finish(row, total[:CHAN])
        finish(row + 1, total[CHAN:])


def grad_rows(upper, upper_row, lower, lower_row, count):
    total = None
    for row in range(0, count, 2):
        left = upper[(row + upper_row) * STACK : (row + upper_row + 2) * STACK, :]
        right = lower[(row + lower_row) * CHAN : (row + lower_row + 4) * CHAN, :]
        term = lax.dot_general(
            left, right, (((1,), (1,)), ((), ())), preferred_element_type=F32
        )
        total = term if total is None else total + term
    return total[:STACK, :STACK] + total[STACK:, CHAN:]


def rows_first(tile_ref, wide, target):
    wide[...] = jnp.swapaxes(tile_ref[...].astype(F32), 0, 1)
    target[...] = wide[...].reshape(target.shape).astype(BF16)


def channels_first(wide, target):
    target[...] = jnp.swapaxes(wide[...], 0, 1).astype(BF16)


def entry_kernel(edge, tile_ref, rows_ref, top_ref, bottom_ref, wide):
    rows_first(tile_ref, wide, rows_ref)
    count = rows_ref.shape[0]
    top_ref[...] = rows_ref[: edge * CHAN, :]
    bottom_ref[...] = rows_ref[count - edge * CHAN :, :]


def forward_kernel(
    rows, height, x_ref, lo_ref, hi_ref, k00, k01, k10, hid0_ref, x1_ref, hid1_ref,
    x3, h3, y3, w00, w01, w10,
):
    first = lax.axis_index("space") * rows

    def inside(row, value):
        if 0 <= row < rows:
            return value
        keep = jnp.logical_and(first + row >= 0, first + row < height)
        return jnp.where(keep, value, 0.0)

    for matrix, target in ((k00, w00), (k01, w01), (k10, w10)):
        two_rows(matrix, target)
    stack_rows([(lo_ref, 4), (x_ref, rows), (hi_ref, 4)], x3)

    def hidden0(row, total):
        value = inside(row - 3, jnp.maximum(total, 0.0)).astype(BF16)
        put(h3, row, value)
        if 2 <= row < rows + 4:
            hid0_ref[(row - 2) * CHAN : (row - 1) * CHAN, :] = value

    conv_rows(w00, x3, rows + 6, hidden0)

    def next_x(row, total):
        value = inside(row - 2, middle(x3, row + 2).astype(F32) + total).astype(BF16)
        put(y3, row, value)
        if 1 <= row < rows + 3:
            x1_ref[(row - 1) * CHAN : row * CHAN, :] = value

    conv_rows(w01, h3, rows + 4, next_x)

    def hidden1(row, total):
        value = inside(row - 1, jnp.maximum(total, 0.0)).astype(BF16)
        hid1_ref[row * CHAN : (row + 1) * CHAN, :] = value

    conv_rows(w10, y3, rows + 2, hidden1)


def backward1_kernel(
    rows, g_ref, lo_ref, hi_ref, hid1_ref, f11, f10, g1_ref, top_ref, bottom_ref, dh1_ref,
    g3, d3, w11, w10,
):
    two_rows(f11, w11)
    two_rows(f10, w10)
    stack_rows([(lo_ref, 2), (g_ref, rows), (hi_ref, 2)], g3)

    def dhidden1(row, total):
        value = jnp.where(one(hid1_ref, row) > 0, total, 0.0).astype(BF16)
        put(d3, row, value)
        if 1 <= row < rows + 1:
            dh1_ref[(row - 1) * CHAN : row * CHAN, :] = value

    conv_rows(w11, g3, rows + 2, dhidden1)

    def next_g(row, total):
        value = (one(g_ref, row).astype(F32) + total).astype(BF16)
        g1_ref[row * CHAN : (row + 1) * CHAN, :] = value
        if row < 2:
            top_ref[row * CHAN : (row + 1) * CHAN, :] = value
        if row >= rows - 2:
            at = row - (rows - 2)
            bottom_ref[at * CHAN : (at + 1) * CHAN, :] = value

    conv_rows(w10, d3, rows, next_g)


def grads1_kernel(rows, g_ref, hid1_ref, dh1_ref, x1_ref, grad10, grad11, s3):
    stack_rows([(g_ref, rows)], s3)
    grad11[...] = grad_rows(s3, 0, hid1_ref, 0, rows)
    stack_rows([(dh1_ref, rows)], s3)
    grad10[...] = grad_rows(s3, 0, x1_ref, 0, rows)


def output_kernel(rows, hid1_ref, x1_ref, k11, out_ref, k3, w11, wide):
    two_rows(k11, w11)
    stack_rows([(hid1_ref, rows + 2)], k3)

    def last_x(row, total):
        wide[row] = one(x1_ref, row + 1).astype(F32) + total

    conv_rows(w11, k3, rows, last_x)
    channels_first(wide, out_ref)


def backward0_kernel(
    rows, scale, g1_ref, lo_ref, hi_ref, hid0_ref, x_ref, xlo_ref, xhi_ref, f01, grad10, grad11,
    dh0_ref, keep_ref, send_ref, g3, d3, xs, w01, both,
):
    two_rows(f01, w01)
    stack_rows([(lo_ref, 2), (g1_ref, rows), (hi_ref, 2)], g3)

    def dhidden0(row, total):
        value = jnp.where(one(hid0_ref, row) > 0, total, 0.0).astype(BF16)
        dh0_ref[row * CHAN : (row + 1) * CHAN, :] = value
        put(d3, row, value)

    conv_rows(w01, g3, rows + 2, dhidden0)
    xs[:CHAN, :] = one(xlo_ref, 3)
    xs[CHAN : (rows + 1) * CHAN, :] = x_ref[...]
    xs[(rows + 1) * CHAN :, :] = one(xhi_ref, 0)
    grad01 = grad_rows(g3, 2, hid0_ref, 0, rows)
    grad00 = grad_rows(d3, 1, xs, 0, rows)
    pairs = ((grad00, grad01), (grad10[...], grad11[...]))
    for section, pair in enumerate(pairs):
        for which, value in enumerate(pair):
            for a in range(3):
                for b in range(3):
                    block = value[(2 - b) * CHAN : (3 - b) * CHAN, a * CHAN : (a + 1) * CHAN]
                    at = which * 9 * CHAN + (3 * a + b) * CHAN
                    both[section, :, at : at + CHAN] = block * scale
    mine = lax.rem(lax.axis_index("space"), 2)
    keep_ref[...] = both[mine]
    send_ref[...] = both[1 - mine].astype(BF16)


def input_grad_kernel(rows, dh0_ref, g1_ref, f00, out_ref, d3, w00, wide):
    two_rows(f00, w00)
    stack_rows([(dh0_ref, rows + 2)], d3)

    def last_g(row, total):
        wide[row] = one(g1_ref, row).astype(F32) + total

    conv_rows(w00, d3, rows, last_g)
    channels_first(wide, out_ref)


def flipped(matrix):
    inner = matrix.reshape(CHAN, 3, 3, CHAN)[:, ::-1, ::-1, :]
    return inner.transpose(3, 1, 2, 0).reshape(CHAN, 9 * CHAN)


def exchange(value, mask, count):
    return lax.ppermute(value, "space", [(d, d ^ mask) for d in range(count)])


def local(features, cotangent, kernels):
    rows, width = features.shape[1], features.shape[2]
    count = lax.axis_size("space")
    height = rows * count
    scale = 1.0 / math.sqrt(height * width)
    place = lax.axis_index("space")
    down = [(i, i + 1) for i in range(count - 1)]
    up = [(i + 1, i) for i in range(count - 1)]

    def shape(n, dtype=BF16):
        return jax.ShapeDtypeStruct((n * CHAN, width), dtype)

    def vmem(n):
        return pltpu.VMEM((n * STACK, width), BF16)

    def ends(top, bottom):
        return lax.ppermute(bottom, "space", down), lax.ppermute(top, "space", up)

    weight = pltpu.VMEM((2 * CHAN, 4 * STACK), BF16)
    row_flops = 2 * CHAN * 9 * CHAN * width * 4
    grad = jax.ShapeDtypeStruct((STACK, STACK), F32)
    tile = jax.ShapeDtypeStruct((CHAN, rows, width), BF16)
    wide = pltpu.VMEM((rows, CHAN, width), F32)
    half = (CHAN, 18 * CHAN)

    x, x_top, x_bottom = call(
        functools.partial(entry_kernel, 4), (features,), (shape(rows), shape(4), shape(4)),
        [wide], 0, "x_rows",
    )
    xlo, xhi = ends(x_top, x_bottom)
    later, _ = lax.optimization_barrier((cotangent, x_top))
    g, g_top, g_bottom = call(
        functools.partial(entry_kernel, 2), (later,), (shape(rows), shape(2), shape(2)),
        [wide], 0, "g_rows",
    )
    glo, ghi = ends(g_top, g_bottom)
    k00, k01, k10, k11 = (kernels[s, j] for s in range(2) for j in range(2))
    f00, f01, f10, f11 = (flipped(kernels[s, j]) for s in range(2) for j in range(2))
    hid0, x1, hid1 = call(
        functools.partial(forward_kernel, rows, height), (x, xlo, xhi, k00, k01, k10),
        (shape(rows + 2),) * 3, [vmem(rows + 8), vmem(rows + 6), vmem(rows + 4)] + [weight] * 3,
        36 * row_flops, "forward",
    )
    g1, g1_top, g1_bottom, dh1 = call(
        functools.partial(backward1_kernel, rows), (g, glo, ghi, hid1, f11, f10),
        (shape(rows), shape(2), shape(2), shape(rows)),
        [vmem(rows + 4), vmem(rows + 2)] + [weight] * 2, 18 * row_flops, "backward1",
    )
    g1lo, g1hi = ends(g1_top, g1_bottom)
    grad10, grad11 = call(
        functools.partial(grads1_kernel, rows), (g, hid1, dh1, x1), (grad, grad), [vmem(rows)],
        16 * row_flops, "grads1",
    )
    dh0, part, send = call(
        functools.partial(backward0_kernel, rows, scale),
        (g1, g1lo, g1hi, hid0, x, xlo, xhi, f01, grad10, grad11),
        (shape(rows + 2), jax.ShapeDtypeStruct(half, F32), jax.ShapeDtypeStruct(half, BF16)),
        [vmem(rows + 4), vmem(rows + 2), pltpu.VMEM(((rows + 2) * CHAN, width), BF16), weight,
         pltpu.VMEM((2, *half), F32)],
        26 * row_flops, "backward0",
    )

    part = part + exchange(send, 1, count).astype(F32)
    low, high = part[: CHAN // 2], part[CHAN // 2 :]
    bit = (place & 2) != 0
    send = jnp.where(bit, low, high).astype(BF16)
    part = jnp.where(bit, high, low)
    arrived = exchange(send, 2, count)
    hid1_later, _ = lax.optimization_barrier((hid1, send))
    (section_output,) = call(
        functools.partial(output_kernel, rows), (hid1_later, x1, k11), (tile,),
        [vmem(rows + 2), weight, wide], 8 * row_flops, "output",
    )
    arrived, section_output = lax.optimization_barrier((arrived, section_output))
    part = part + arrived.astype(F32)
    step = 4
    input_grad = None
    while step < count:
        send = part.astype(BF16)
        masks = [step, 2 * step, 3 * step] if 2 * step < count else [step]
        arrived = [exchange(send, mask, count) for mask in masks]
        if input_grad is None:
            dh0_later, _ = lax.optimization_barrier((dh0, send))
            (input_grad,) = call(
                functools.partial(input_grad_kernel, rows), (dh0_later, g1, f00), (tile,),
                [vmem(rows + 2), weight, wide], 8 * row_flops, "input_grad",
            )
            arrived, input_grad = lax.optimization_barrier((arrived, input_grad))
        own = send.astype(F32)
        arrived = [value.astype(F32) for value in arrived]
        part = own + arrived[0]
        if len(masks) == 3:
            part = part + (arrived[1] + arrived[2])
        step *= len(masks) + 1
    done = part.astype(BF16)
    for mask in (2, 1):
        bit = (place & mask) != 0
        other = exchange(done, mask, count)
        done = jnp.where(
            bit, jnp.concatenate([other, done]), jnp.concatenate([done, other])
        )
    kernel_grad = done.astype(F32).reshape(2, CHAN, 2, 9 * CHAN).transpose(0, 2, 1, 3)
    return (section_output, input_grad, kernel_grad)


def solution(mesh):
    return jax.shard_map(
        local,
        mesh=mesh,
        in_specs=(P(None, "space", "groups"), P(None, "space", "groups"), P()),
        out_specs=(
            P(None, "space", "groups"),
            P(None, "space", "groups"),
            P("groups", None, None, None),
        ),
        check_vma=False,
    )
```

profile of v0, /device:TPU:0, one launch (start us, length us, event | category | flops | bytes accessed | tf_op | source)
XLA Modules:
  0.0 80.9 jit_solution(14062922009298139421)
XLA Ops:
  1.9 1.5 %x_rows.1 = (bf16[512,1024]{1,0:T(8,128)(2,1)S(1)}, bf16[256,1024]{1,0:T(8,128)(2,1)}, bf16[256,1024]{1,0:T(8,128)(2,1)}) custom-call(bf16[64,8,1024]{2,1,0:T(8,128)(2,1)S(1)} %copy-done), custom_call_target="tpu_custom_call" | custom-call | bytes 3145728 | tf_op jit(solution)/shard_map/x_rows/pallas_call | solution.py:21
  4.7 3.8 %collective-permute-start.2 = (bf16[256,1024]{1,0:T(8,128)(2,1)}, bf16[256,1024]{1,0:T(8,128)(2,1)}, u32[]{:S(2)}, u32[]{:S(2)}) collective-permute-start(bf16[256,1024]{1,0:T(8,128)(2,1)} %get-tuple-element.36), channel_id=1, source_target_pairs={{0,1},{1,2},{2,3},{3,4},{4,5},{5,6},{6,7},{7,8},{8,9},{9,10},{10,1... | collective-permute-start | bytes 1572872 | tf_op jit(solution)/shard_map/ppermute | solution.py:259
  8.5 1.4 %g_rows.1 = (bf16[512,1024]{1,0:T(8,128)(2,1)S(1)}, bf16[128,1024]{1,0:T(8,128)(2,1)}, bf16[128,1024]{1,0:T(8,128)(2,1)}) custom-call(bf16[64,8,1024]{2,1,0:T(8,128)(2,1)S(1)} %copy-done.1), custom_call_target="tpu_custom_call" | custom-call | bytes 2621440 | tf_op jit(solution)/shard_map/g_rows/pallas_call | solution.py:21
  9.9 3.7 %collective-permute-start = (bf16[128,1024]{1,0:T(8,128)(2,1)}, bf16[128,1024]{1,0:T(8,128)(2,1)S(1)}, u32[]{:S(2)}, u32[]{:S(2)}) collective-permute-start(bf16[128,1024]{1,0:T(8,128)(2,1)} %get-tuple-element.33), channel_id=1, source_target_pairs={{0,1},{1,2},{2,3},{3,4},{4,5},{5,6},{6,7},{7,8},{8,9},{9,10},{10,1... | collective-permute-start | bytes 786440 | tf_op jit(solution)/shard_map/ppermute | solution.py:259
  19.3 1.7 %copy.14 = bf16[64,3,3,64]{0,3,2,1:T(8,128)(2,1)} copy(bf16[64,3,3,64]{3,0,2,1:T(8,128)(2,1)} %reverse_bitcast_fusion.2) | data formatting | bytes 147456 | tf_op jit(solution)/shard_map/transpose | solution.py:236
  22.8 1.6 %reverse_bitcast_fusion.1 = bf16[64,3,3,64]{3,0,2,1:T(8,128)(2,1)} fusion(bf16[64,3,3,64]{0,3,2,1:T(8,128)(2,1)} %bitcast.32), kind=kLoop, calls=%fused_computation.9 | loop fusion | bytes 147456 | tf_op jit(solution)/shard_map/transpose | solution.py:236
  24.4 1.7 %copy.18 = bf16[64,3,3,64]{0,3,2,1:T(8,128)(2,1)} copy(bf16[64,3,3,64]{3,0,2,1:T(8,128)(2,1)} %reverse_bitcast_fusion.1) | data formatting | bytes 147456 | tf_op jit(solution)/shard_map/transpose | solution.py:236
  27.1 5.4 %forward.1 = (bf16[640,1024]{1,0:T(8,128)(2,1)S(1)}, bf16[640,1024]{1,0:T(8,128)(2,1)S(1)}, bf16[640,1024]{1,0:T(8,128)(2,1)S(1)}) custom-call(bf16[512,1024]{1,0:T(8,128)(2,1)S(1)} %get-tuple-element.35.x_ref, bf16[256,1024]{1,0:T(8,128)(2,1)} %collective-permute-done.2.lo_ref.xlo_ref, bf16[256,1024]{1,0:T(8,128)(2,1)S(1)} %collective-permute-done.3.hi_ref.xhi_ref, ...), custom_call_target="tpu_custom_call" | custom-call | flops 10871635968 | bytes 6250496 | tf_op jit(solution)/shard_map/forward/pallas_call | solution.py:21
  32.6 3.9 %backward1.1 = (bf16[512,1024]{1,0:T(8,128)(2,1)S(1)}, bf16[128,1024]{1,0:T(8,128)(2,1)S(1)}, bf16[128,1024]{1,0:T(8,128)(2,1)S(1)}, bf16[512,1024]{1,0:T(8,128)(2,1)S(1)}) custom-call(bf16[512,1024]{1,0:T(8,128)(2,1)S(1)} %get-tuple-element.32.g_ref, bf16[128,1024]{1,0:T(8,128)(2,1)S(1)} %collective-permute-done.lo_ref, ...), custom_call_target="tpu_custom_call" | custom-call | flops 5435817984 | bytes 5652480 | tf_op jit(solution)/shard_map/backward1/pallas_call | solution.py:21
  36.5 3.1 %collective-permute-start.4 = (bf16[128,1024]{1,0:T(8,128)(2,1)S(1)}, bf16[128,1024]{1,0:T(8,128)(2,1)S(1)}, u32[]{:S(2)}, u32[]{:S(2)}) collective-permute-start(bf16[128,1024]{1,0:T(8,128)(2,1)S(1)} %get-tuple-element.39), channel_id=1, source_target_pairs={{0,1},{1,2},{2,3},{3,4},{4,5},{5,6},{6,7},{7,8},{8,9},{9,10},{10,1... | collective-permute-start | bytes 786440 | tf_op jit(solution)/shard_map/ppermute | solution.py:259
  39.6 1.5 %collective-permute-start.5 = (bf16[128,1024]{1,0:T(8,128)(2,1)S(1)}, bf16[128,1024]{1,0:T(8,128)(2,1)S(1)}, u32[]{:S(2)}, u32[]{:S(2)}) collective-permute-start(bf16[128,1024]{1,0:T(8,128)(2,1)S(1)} %get-tuple-element.40), channel_id=1, source_target_pairs={{1,0},{2,1},{3,2},{4,3},{5,4},{6,5},{7,6},{8,7},{9,8},{10,9},{11,1... | collective-permute-start | bytes 786440 | tf_op jit(solution)/shard_map/ppermute | solution.py:259
  41.1 2.0 %grads1.1 = (f32[192,192]{1,0:T(8,128)S(1)}, f32[192,192]{1,0:T(8,128)S(1)}) custom-call(bf16[512,1024]{1,0:T(8,128)(2,1)S(1)} %get-tuple-element.32.g_ref, bf16[640,1024]{1,0:T(8,128)(2,1)S(1)} %get-tuple-element.48.hid1_ref, bf16[512,1024]{1,0:T(8,128)(2,1)S(1)} %get-tuple-element.42.dh1_ref, bf16[640,1024]{1,0:T(8,128)(2,1)S(1)} %get-tuple-element.43.x1_ref), custom_call_target="tpu_custom_call" | custom-call | flops 4831838208 | bytes 5013504 | tf_op jit(solution)/shard_map/grads1/pallas_call | solution.py:21
  43.1 1.3 %collective-permute-done.5.hi_ref = bf16[128,1024]{1,0:T(8,128)(2,1)S(1)} collective-permute-done((bf16[128,1024]{1,0:T(8,128)(2,1)S(1)}, bf16[128,1024]{1,0:T(8,128)(2,1)S(1)}, u32[]{:S(2)}, u32[]{:S(2)}) %collective-permute-start.5) | collective-permute-done | bytes 262176 | tf_op jit(solution)/shard_map/ppermute | solution.py:259
  44.5 4.7 %backward0.1 = (bf16[640,1024]{1,0:T(8,128)(2,1)S(1)}, f32[64,1152]{1,0:T(8,128)S(1)}, bf16[64,1152]{1,0:T(8,128)(2,1)S(1)}) custom-call(bf16[512,1024]{1,0:T(8,128)(2,1)S(1)} %get-tuple-element.38.g1_ref, bf16[128,1024]{1,0:T(8,128)(2,1)S(1)} %collective-permute-done.4.lo_ref, bf16[128,1024]{1,0:T(8,128)(2,1)S(1)} %collective-permute-done.5.hi_ref, ...), custom_call_target="tpu_custom_call" | custom-call | flops 7851737088 | bytes 7102464 | tf_op jit(solution)/shard_map/backward0/pallas_call | solution.py:21
  50.3 4.7 %collective-permute-start.6 = (bf16[64,1152]{1,0:T(8,128)(2,1)S(1)}, bf16[64,1152]{1,0:T(8,128)(2,1)S(1)}, u32[]{:S(2)}, u32[]{:S(2)}) collective-permute-start(bf16[64,1152]{1,0:T(8,128)(2,1)S(1)} %get-tuple-element.47), channel_id=1, source_target_pairs={{0,1},{1,0},{2,3},{3,2},{4,5},{5,4},{6,7},{7,6},{8,9},{9,8},{10,11... | collective-permute-start | bytes 442376 | tf_op jit(solution)/shard_map/ppermute | solution.py:240
  56.1 3.5 %collective-permute-start.7 = (bf16[32,1152]{1,0:T(8,128)(2,1)S(1)}, bf16[32,1152]{1,0:T(8,128)(2,1)S(1)}, u32[]{:S(2)}, u32[]{:S(2)}) collective-permute-start(bf16[32,1152]{1,0:T(8,128)(2,1)S(1)} %select_convert_fusion), channel_id=1, source_target_pairs={{0,2},{1,3},{2,0},{3,1},{4,6},{5,7},{6,4},{7,5},{8,10},{9,11},{10,... | collective-permute-start | bytes 221192 | tf_op jit(solution)/shard_map/ppermute | solution.py:240
  59.6 1.3 %copy-done.5 = bf16[640,1024]{1,0:T(8,128)(2,1)S(1)} copy-done((bf16[640,1024]{1,0:T(8,128)(2,1)S(1)}, bf16[640,1024]{1,0:T(8,128)(2,1)}, u32[]{:S(2)}) %copy-start.5) | copy-done | bytes 1310744
  60.9 2.6 %output.1 = bf16[64,8,1024]{2,1,0:T(8,128)(2,1)} custom-call(bf16[640,1024]{1,0:T(8,128)(2,1)S(1)} %copy-done.5, bf16[640,1024]{1,0:T(8,128)(2,1)S(1)} %copy-done.3, bf16[64,576]{1,0:T(8,128)(2,1)S(1)} %get-tuple-element.61.k11), custom_call_target="tpu_custom_call" | custom-call | flops 2415919104 | bytes 3743744 | tf_op jit(solution)/shard_map/output/pallas_call | solution.py:21
  63.5 1.9 %collective-permute-start.10 = (bf16[32,1152]{1,0:T(8,128)(2,1)S(1)}, bf16[32,1152]{1,0:T(8,128)(2,1)S(1)}, u32[]{:S(2)}, u32[]{:S(2)}) collective-permute-start(bf16[32,1152]{1,0:T(8,128)(2,1)S(1)} %add_convert_fusion.1), channel_id=1, source_target_pairs={{0,12},{1,13},{2,14},{3,15},{4,8},{5,9},{6,10},{7,11},{8,4},{9,5},... | collective-permute-start | bytes 221192 | tf_op jit(solution)/shard_map/ppermute | solution.py:240
  65.4 1.4 %collective-permute-start.8 = (bf16[32,1152]{1,0:T(8,128)(2,1)S(1)}, bf16[32,1152]{1,0:T(8,128)(2,1)S(1)}, u32[]{:S(2)}, u32[]{:S(2)}) collective-permute-start(bf16[32,1152]{1,0:T(8,128)(2,1)S(1)} %add_convert_fusion.1), channel_id=1, source_target_pairs={{0,4},{1,5},{2,6},{3,7},{4,0},{5,1},{6,2},{7,3},{8,12},{9,13},{10,... | collective-permute-start | bytes 221192 | tf_op jit(solution)/shard_map/ppermute | solution.py:240
  68.0 2.6 %input_grad.1 = bf16[64,8,1024]{2,1,0:T(8,128)(2,1)} custom-call(bf16[640,1024]{1,0:T(8,128)(2,1)S(1)} %copy-done.7, bf16[512,1024]{1,0:T(8,128)(2,1)S(1)} %copy-done.9, bf16[64,576]{1,0:T(8,128)(2,1)S(1)} %copy.22.f00), custom_call_target="tpu_custom_call" | custom-call | flops 2415919104 | bytes 3481600 | tf_op jit(solution)/shard_map/input_grad/pallas_call | solution.py:21
  70.8 2.8 %collective-permute-done.9 = bf16[32,1152]{1,0:T(8,128)(2,1)S(1)} collective-permute-done((bf16[32,1152]{1,0:T(8,128)(2,1)S(1)}, bf16[32,1152]{1,0:T(8,128)(2,1)S(1)}, u32[]{:S(2)}, u32[]{:S(2)}) %collective-permute-start.9) | collective-permute-done | bytes 73760 | tf_op jit(solution)/shard_map/ppermute | solution.py:240
  74.0 4.1 %collective-permute-done.11 = bf16[32,1152]{1,0:T(8,128)(2,1)S(1)} collective-permute-done((bf16[32,1152]{1,0:T(8,128)(2,1)S(1)}, bf16[32,1152]{1,0:T(8,128)(2,1)S(1)}, u32[]{:S(2)}, u32[]{:S(2)}) %collective-permute-start.11) | collective-permute-done | bytes 73760 | tf_op jit(solution)/shard_map/ppermute | solution.py:240
  78.2 1.4 %collective-permute-done.12 = bf16[64,1152]{1,0:T(8,128)(2,1)S(1)} collective-permute-done((bf16[64,1152]{1,0:T(8,128)(2,1)S(1)}, bf16[64,1152]{1,0:T(8,128)(2,1)S(1)}, u32[]{:S(2)}, u32[]{:S(2)}) %collective-permute-start.12) | collective-permute-done | bytes 147488 | tf_op jit(solution)/shard_map/ppermute | solution.py:240
  (61 shorter events, 16.6 us)
Async XLA Ops:
  1.9 6.7 %copy-start.1 = (bf16[64,8,1024]{2,1,0:T(8,128)(2,1)S(1)}, bf16[64,8,1024]{2,1,0:T(8,128)(2,1)}, u32[]{:S(2)}) copy-start(bf16[64,8,1024]{2,1,0:T(8,128)(2,1)} %tile_ref.2) | copy-start | bytes 3145732
  1.9 13.0 %copy-start.10 = (bf16[2,2,64,576]{3,2,1,0:T(8,128)(2,1)S(1)}, bf16[2,2,64,576]{3,2,1,0:T(8,128)(2,1)}, u32[]{:S(2)}) copy-start(bf16[2,2,64,576]{3,2,1,0:T(8,128)(2,1)} %param.5) | copy-start | bytes 884740
  3.4 23.7 %collective-permute-start.3 = (bf16[256,1024]{1,0:T(8,128)(2,1)}, bf16[256,1024]{1,0:T(8,128)(2,1)S(1)}, u32[]{:S(2)}, u32[]{:S(2)}) collective-permute-start(bf16[256,1024]{1,0:T(8,128)(2,1)} %get-tuple-element.30), channel_id=1, source_target_pairs={{1,0},{2,1},{3,2},{4,3},{5,4},{6,5},{7,6},{8,7},{9,8},{10,9},{11,1... | collective-permute-start | bytes 1572872 | tf_op jit(solution)/shard_map/ppermute | solution.py:259
  4.7 22.4 %collective-permute-start.2 = (bf16[256,1024]{1,0:T(8,128)(2,1)}, bf16[256,1024]{1,0:T(8,128)(2,1)}, u32[]{:S(2)}, u32[]{:S(2)}) collective-permute-start(bf16[256,1024]{1,0:T(8,128)(2,1)} %get-tuple-element.36), channel_id=1, source_target_pairs={{0,1},{1,2},{2,3},{3,4},{4,5},{5,6},{6,7},{7,8},{8,9},{9,10},{10,1... | collective-permute-start | bytes 1572872 | tf_op jit(solution)/shard_map/ppermute | solution.py:259
  9.9 22.7 %collective-permute-start = (bf16[128,1024]{1,0:T(8,128)(2,1)}, bf16[128,1024]{1,0:T(8,128)(2,1)S(1)}, u32[]{:S(2)}, u32[]{:S(2)}) collective-permute-start(bf16[128,1024]{1,0:T(8,128)(2,1)} %get-tuple-element.33), channel_id=1, source_target_pairs={{0,1},{1,2},{2,3},{3,4},{4,5},{5,6},{6,7},{7,8},{8,9},{9,10},{10,1... | collective-permute-start | bytes 786440 | tf_op jit(solution)/shard_map/ppermute | solution.py:259
  13.6 19.0 %collective-permute-start.1 = (bf16[128,1024]{1,0:T(8,128)(2,1)}, bf16[128,1024]{1,0:T(8,128)(2,1)}, u32[]{:S(2)}, u32[]{:S(2)}) collective-permute-start(bf16[128,1024]{1,0:T(8,128)(2,1)} %get-tuple-element.34), channel_id=1, source_target_pairs={{1,0},{2,1},{3,2},{4,3},{5,4},{6,5},{7,6},{8,7},{9,8},{10,9},{11,1... | collective-permute-start | bytes 786440 | tf_op jit(solution)/shard_map/ppermute | solution.py:259
  15.7 6.3 %copy-start.12 = (bf16[1,1,64,576]{3,2,1,0:T(8,128)(2,1)S(1)}, bf16[1,1,64,576]{3,2,1,0:T(8,128)(2,1)}, u32[]{:S(2)}) copy-start(bf16[1,1,64,576]{3,2,1,0:T(8,128)(2,1)} %get-tuple-element.62) | copy-start | bytes 221188
  32.5 8.5 %copy-start.2 = (bf16[640,1024]{1,0:T(8,128)(2,1)}, bf16[640,1024]{1,0:T(8,128)(2,1)S(1)}, u32[]{:S(2)}) copy-start(bf16[640,1024]{1,0:T(8,128)(2,1)S(1)} %get-tuple-element.43.x1_ref) | copy-start | bytes 3932164
  32.5 8.5 %copy-start.4 = (bf16[640,1024]{1,0:T(8,128)(2,1)}, bf16[640,1024]{1,0:T(8,128)(2,1)S(1)}, u32[]{:S(2)}) copy-start(bf16[640,1024]{1,0:T(8,128)(2,1)S(1)} %get-tuple-element.48.hid1_ref) | copy-start | bytes 3932164
  36.5 7.9 %copy-start.8 = (bf16[512,1024]{1,0:T(8,128)(2,1)}, bf16[512,1024]{1,0:T(8,128)(2,1)S(1)}, u32[]{:S(2)}) copy-start(bf16[512,1024]{1,0:T(8,128)(2,1)S(1)} %get-tuple-element.38.g1_ref) | copy-start | bytes 3145732
  36.5 6.6 %collective-permute-start.4 = (bf16[128,1024]{1,0:T(8,128)(2,1)S(1)}, bf16[128,1024]{1,0:T(8,128)(2,1)S(1)}, u32[]{:S(2)}, u32[]{:S(2)}) collective-permute-start(bf16[128,1024]{1,0:T(8,128)(2,1)S(1)} %get-tuple-element.39), channel_id=1, source_target_pairs={{0,1},{1,2},{2,3},{3,4},{4,5},{5,6},{6,7},{7,8},{8,9},{9,10},{10,1... | collective-permute-start | bytes 786440 | tf_op jit(solution)/shard_map/ppermute | solution.py:259
  39.6 4.9 %collective-permute-start.5 = (bf16[128,1024]{1,0:T(8,128)(2,1)S(1)}, bf16[128,1024]{1,0:T(8,128)(2,1)S(1)}, u32[]{:S(2)}, u32[]{:S(2)}) collective-permute-start(bf16[128,1024]{1,0:T(8,128)(2,1)S(1)} %get-tuple-element.40), channel_id=1, source_target_pairs={{1,0},{2,1},{3,2},{4,3},{5,4},{6,5},{7,6},{8,7},{9,8},{10,9},{11,1... | collective-permute-start | bytes 786440 | tf_op jit(solution)/shard_map/ppermute | solution.py:259
  44.5 10.6 %copy-start.11 = (bf16[1,1,64,576]{3,2,1,0:T(8,128)(2,1)S(1)}, bf16[1,1,64,576]{3,2,1,0:T(8,128)(2,1)}, u32[]{:S(2)}) copy-start(bf16[1,1,64,576]{3,2,1,0:T(8,128)(2,1)} %get-tuple-element.57) | copy-start | bytes 221188
  50.3 9.3 %copy-start.3 = (bf16[640,1024]{1,0:T(8,128)(2,1)S(1)}, bf16[640,1024]{1,0:T(8,128)(2,1)}, u32[]{:S(2)}) copy-start(bf16[640,1024]{1,0:T(8,128)(2,1)} %copy-done.2) | copy-start | bytes 3932164
  50.3 5.7 %collective-permute-start.6 = (bf16[64,1152]{1,0:T(8,128)(2,1)S(1)}, bf16[64,1152]{1,0:T(8,128)(2,1)S(1)}, u32[]{:S(2)}, u32[]{:S(2)}) collective-permute-start(bf16[64,1152]{1,0:T(8,128)(2,1)S(1)} %get-tuple-element.47), channel_id=1, source_target_pairs={{0,1},{1,0},{2,3},{3,2},{4,5},{5,4},{6,7},{7,6},{8,9},{9,8},{10,11... | collective-permute-start | bytes 442376 | tf_op jit(solution)/shard_map/ppermute | solution.py:240
  56.1 7.4 %collective-permute-start.7 = (bf16[32,1152]{1,0:T(8,128)(2,1)S(1)}, bf16[32,1152]{1,0:T(8,128)(2,1)S(1)}, u32[]{:S(2)}, u32[]{:S(2)}) collective-permute-start(bf16[32,1152]{1,0:T(8,128)(2,1)S(1)} %select_convert_fusion), channel_id=1, source_target_pairs={{0,2},{1,3},{2,0},{3,1},{4,6},{5,7},{6,4},{7,5},{8,10},{9,11},{10,... | collective-permute-start | bytes 221192 | tf_op jit(solution)/shard_map/ppermute | solution.py:240
  59.6 1.3 %copy-start.5 = (bf16[640,1024]{1,0:T(8,128)(2,1)S(1)}, bf16[640,1024]{1,0:T(8,128)(2,1)}, u32[]{:S(2)}) copy-start(bf16[640,1024]{1,0:T(8,128)(2,1)} %copy-done.4) | copy-start | bytes 3932164
  60.9 7.1 %copy-start.7 = (bf16[640,1024]{1,0:T(8,128)(2,1)S(1)}, bf16[640,1024]{1,0:T(8,128)(2,1)}, u32[]{:S(2)}) copy-start(bf16[640,1024]{1,0:T(8,128)(2,1)} %copy-done.6) | copy-start | bytes 3932164
  60.9 7.1 %copy-start.9 = (bf16[512,1024]{1,0:T(8,128)(2,1)S(1)}, bf16[512,1024]{1,0:T(8,128)(2,1)}, u32[]{:S(2)}) copy-start(bf16[512,1024]{1,0:T(8,128)(2,1)} %copy-done.8) | copy-start | bytes 3145732
  63.5 7.1 %collective-permute-start.10 = (bf16[32,1152]{1,0:T(8,128)(2,1)S(1)}, bf16[32,1152]{1,0:T(8,128)(2,1)S(1)}, u32[]{:S(2)}, u32[]{:S(2)}) collective-permute-start(bf16[32,1152]{1,0:T(8,128)(2,1)S(1)} %add_convert_fusion.1), channel_id=1, source_target_pairs={{0,12},{1,13},{2,14},{3,15},{4,8},{5,9},{6,10},{7,11},{8,4},{9,5},... | collective-permute-start | bytes 221192 | tf_op jit(solution)/shard_map/ppermute | solution.py:240
  65.4 5.4 %collective-permute-start.8 = (bf16[32,1152]{1,0:T(8,128)(2,1)S(1)}, bf16[32,1152]{1,0:T(8,128)(2,1)S(1)}, u32[]{:S(2)}, u32[]{:S(2)}) collective-permute-start(bf16[32,1152]{1,0:T(8,128)(2,1)S(1)} %add_convert_fusion.1), channel_id=1, source_target_pairs={{0,4},{1,5},{2,6},{3,7},{4,0},{5,1},{6,2},{7,3},{8,12},{9,13},{10,... | collective-permute-start | bytes 221192 | tf_op jit(solution)/shard_map/ppermute | solution.py:240
  66.7 6.8 %collective-permute-start.9 = (bf16[32,1152]{1,0:T(8,128)(2,1)S(1)}, bf16[32,1152]{1,0:T(8,128)(2,1)S(1)}, u32[]{:S(2)}, u32[]{:S(2)}) collective-permute-start(bf16[32,1152]{1,0:T(8,128)(2,1)S(1)} %add_convert_fusion.1), channel_id=1, source_target_pairs={{0,8},{1,9},{2,10},{3,11},{4,12},{5,13},{6,14},{7,15},{8,0},{9,1},... | collective-permute-start | bytes 221192 | tf_op jit(solution)/shard_map/ppermute | solution.py:240
  73.6 4.4 %collective-permute-start.11 = (bf16[32,1152]{1,0:T(8,128)(2,1)S(1)}, bf16[32,1152]{1,0:T(8,128)(2,1)S(1)}, u32[]{:S(2)}, u32[]{:S(2)}) collective-permute-start(bf16[32,1152]{1,0:T(8,128)(2,1)S(1)} %add_convert_fusion), channel_id=1, source_target_pairs={{0,2},{1,3},{2,0},{3,1},{4,6},{5,7},{6,4},{7,5},{8,10},{9,11},{10,... | collective-permute-start | bytes 221192 | tf_op jit(solution)/shard_map/ppermute | solution.py:240
  78.1 1.4 %collective-permute-start.12 = (bf16[64,1152]{1,0:T(8,128)(2,1)S(1)}, bf16[64,1152]{1,0:T(8,128)(2,1)S(1)}, u32[]{:S(2)}, u32[]{:S(2)}) collective-permute-start(bf16[64,1152]{1,0:T(8,128)(2,1)S(1)} %maximum_select_fusion.1), channel_id=1, source_target_pairs={{0,1},{1,0},{2,3},{3,2},{4,5},{5,4},{6,7},{7,6},{8,9},{9,8},{10,11... | collective-permute-start | bytes 442376 | tf_op jit(solution)/shard_map/ppermute | solution.py:240
  (2 other events, 2.3 us)
where the time goes:
time: 81.5 us; the launch traced here: 80.9 us
  starting transfers between devices  27.8 us (34%)
  Pallas kernels  24.2 us (30%)
  local copies, waits for them, and re-layouts  17.7 us (22%)
  waiting for transfers between devices  10.3 us (13%)
  between operations  0.91 us (1%)
    pallas_call x8, Pallas kernels, call(): pl.pallas_call(body, out_shape=outs, in_specs=[VMEM] * len(operands), out...  24.2 us
    ppermute x6, starting transfers between devices, ends(): return (lax.ppermute(bottom, 'space', down), lax.ppermute(top, 'space', up))  14.6 us
    ppermute x7, starting transfers between devices, exchange(): return lax.ppermute(value, 'space', [(d, d ^ mask) for d in range(count)])  13.1 us
    ppermute x7, waiting for transfers between devices, exchange(): return lax.ppermute(value, 'space', [(d, d ^ mask) for d in range(count)])  8.94 us
    transpose x8, local copies, waits for them, and re-layouts, flipped(): return inner.transpose(3, 1, 2, 0).reshape(CHAN, 9 * CHAN)  6.6 us
    unnamed x26, local copies, waits for them, and re-layouts  3.66 us
    reshape x4, local copies, waits for them, and re-layouts, flipped(): return inner.transpose(3, 1, 2, 0).reshape(CHAN, 9 * CHAN)  3.26 us
    slice x4, local copies, waits for them, and re-layouts, local(): k00, k01, k10, k11 = (kernels[s, j] for s in range(2) for j in range(2))  2.66 us
  transfers between devices with their start and end apart: 13, of which 6 were waited for; matrix products, arithmetic and copies ran while one was open for 16% of the time, Pallas kernels for 17%

commit v1 on v0

v1 whole, which is shorter than its diff:
```python
import functools
import math

import jax
import jax.numpy as jnp
from jax import lax
from jax.experimental import pallas as pl
from jax.experimental.pallas import tpu as pltpu
from jax.sharding import PartitionSpec as P

CHAN = 64
STACK = 3 * CHAN
F32 = jnp.float32
BF16 = jnp.bfloat16
VMEM = pl.BlockSpec(memory_space=pltpu.VMEM)
ANY = pl.BlockSpec(memory_space=pl.ANY)
HBM = pl.BlockSpec(memory_space=pltpu.HBM)
PIECES = 4


def call(body, operands, outs, scratch, flops, name, after=(), place=VMEM):
    nbytes = sum(v.size * v.dtype.itemsize for v in (*operands, *outs))
    held = sum(math.prod(v.shape) * v.dtype.itemsize for v in scratch if v.dtype in (F32, BF16))

    def kernel(*refs):
        body(*refs[len(after) :])

    return pl.pallas_call(
        kernel,
        out_shape=outs,
        in_specs=[ANY] * len(after) + [place] * len(operands),
        out_specs=[VMEM] * len(outs),
        scratch_shapes=scratch,
        compiler_params=pltpu.CompilerParams(vmem_limit_bytes=nbytes + held + (6 << 20)),
        cost_estimate=pl.CostEstimate(flops=flops, bytes_accessed=nbytes, transcendentals=0),
        name=name,
    )(*after, *operands)


def stacked(field):
    width = field.shape[1]
    lane = lax.broadcasted_iota(jnp.int32, field.shape, 1)
    zero = jnp.zeros_like(field)
    left = jnp.where(lane == 0, zero, pltpu.roll(field, 1, 1))
    right = jnp.where(lane == width - 1, zero, pltpu.roll(field, width - 1, 1))
    return jnp.concatenate([left, field, right], axis=0)


def put(ref, row, field):
    ref[row * STACK : (row + 1) * STACK, :] = stacked(field)


def middle(ref, row):
    return ref[row * STACK + CHAN : row * STACK + 2 * CHAN, :]


def one(ref, row):
    return ref[row * CHAN : (row + 1) * CHAN, :]


def stack_rows(ref, count, target, at):
    for row in range(count):
        put(target, row + at, one(ref, row))


def two_rows(target, index, column, value):
    width = value.shape[1]
    target[index, :CHAN, column : column + width] = value
    target[index, CHAN:, STACK + column : STACK + column + width] = value


def weights_kernel(kernels_ref, target):
    target[...] = jnp.zeros_like(target)
    line = lax.broadcasted_iota(jnp.int32, (CHAN, CHAN), 0)
    same = line == lax.broadcasted_iota(jnp.int32, (CHAN, CHAN), 1)
    unit = jnp.where(same, 1.0, 0.0).astype(BF16)
    for section in range(2):
        for which in range(2):
            index = 2 * (2 * section + which)
            two_rows(target, index, 0, kernels_ref[section, which])
            for tap in range(9):
                at = (8 - tap) * CHAN
                block = kernels_ref[section, which, :, at : at + CHAN]
                turned = lax.dot_general(
                    unit, block, (((1,), (1,)), ((), ())), preferred_element_type=F32
                )
                two_rows(target, index + 1, tap * CHAN, turned.astype(BF16))


def conv_rows(weight, source, count, finish):
    for row in range(0, count, 2):
        total = jnp.dot(
            weight,
            source[row * STACK : (row + 4) * STACK, :],
            preferred_element_type=F32,
        )
        finish(row, total[:CHAN])
        finish(row + 1, total[CHAN:])


def grad_rows(upper, upper_row, lower, lower_row, count):
    total = None
    for row in range(0, count, 2):
        left = upper[(row + upper_row) * STACK : (row + upper_row + 2) * STACK, :]
        right = lower[(row + lower_row) * CHAN : (row + lower_row + 4) * CHAN, :]
        term = lax.dot_general(
            left, right, (((1,), (1,)), ((), ())), preferred_element_type=F32
        )
        total = term if total is None else total + term
    return total[:STACK, :STACK] + total[STACK:, CHAN:]


def channels_first(wide, target):
    target[...] = jnp.swapaxes(wide[...], 0, 1).astype(BF16)


def odd_place():
    return lax.rem(lax.axis_index("space"), 2) == 1


def put_at(ref, row, field):
    ref[pl.ds(pl.multiple_of(row * STACK, CHAN), STACK), :] = stacked(field)


def halo_rows(near_ref, far_ref, count, rows, target):
    odd = odd_place()
    above, below = 0, rows + count
    near_at = jnp.where(odd, above, below)
    far_at = jnp.where(odd, below, above)
    for row in range(count):
        put_at(target, near_at + row, one(near_ref, row))
        put_at(target, far_at + row, one(far_ref, row))


def send_edges(rows_ref, edge, near_ref, far_ref):
    odd = odd_place()
    last = rows_ref.shape[0] - edge * CHAN
    near_at = jnp.where(odd, 0, last)
    far_at = jnp.where(odd, last, 0)
    near_ref[...] = rows_ref[pl.ds(pl.multiple_of(near_at, CHAN), edge * CHAN), :]
    far_ref[...] = rows_ref[pl.ds(pl.multiple_of(far_at, CHAN), edge * CHAN), :]


def entry_kernel(edge, tile_ref, rows_ref, near_ref, far_ref, held, arrived):
    piece = CHAN // PIECES
    copies = [
        pltpu.make_async_copy(
            tile_ref.at[i * piece : (i + 1) * piece],
            held.at[i * piece : (i + 1) * piece],
            arrived.at[i],
        )
        for i in range(PIECES)
    ]
    for copy in copies:
        copy.start()
    for i, copy in enumerate(copies):
        copy.wait()
        part = held[i * piece : (i + 1) * piece].astype(F32)
        turned = jnp.swapaxes(part, 0, 1).astype(BF16)
        for row in range(turned.shape[0]):
            at = row * CHAN + i * piece
            rows_ref[at : at + piece, :] = turned[row]
    send_edges(rows_ref, edge, near_ref, far_ref)


def channels_first(wide, target):
    target[...] = jnp.swapaxes(wide[...], 0, 1).astype(BF16)


def forward_kernel(
    rows, height, x_ref, near_ref, far_ref, w_ref, hid0_ref, x1_ref, hid1_ref, x3, h3, y3,
):
    first = lax.axis_index("space") * rows

    def inside(row, value):
        if 0 <= row < rows:
            return value
        keep = jnp.logical_and(first + row >= 0, first + row < height)
        return jnp.where(keep, value, 0.0)

    stack_rows(x_ref, rows, x3, 4)
    halo_rows(near_ref, far_ref, 4, rows, x3)

    def hidden0(row, total):
        value = inside(row - 3, jnp.maximum(total, 0.0)).astype(BF16)
        put(h3, row, value)
        if 2 <= row < rows + 4:
            hid0_ref[(row - 2) * CHAN : (row - 1) * CHAN, :] = value

    conv_rows(w_ref[0], x3, rows + 6, hidden0)

    def next_x(row, total):
        value = inside(row - 2, middle(x3, row + 2).astype(F32) + total).astype(BF16)
        put(y3, row, value)
        if 1 <= row < rows + 3:
            x1_ref[(row - 1) * CHAN : row * CHAN, :] = value

    conv_rows(w_ref[2], h3, rows + 4, next_x)

    def hidden1(row, total):
        value = inside(row - 1, jnp.maximum(total, 0.0)).astype(BF16)
        hid1_ref[row * CHAN : (row + 1) * CHAN, :] = value

    conv_rows(w_ref[4], y3, rows + 2, hidden1)


def backward1_kernel(
    rows, g_ref, near_ref, far_ref, hid1_ref, w_ref, g1_ref, next_near, next_far, dh1_ref, g3, d3,
):
    stack_rows(g_ref, rows, g3, 2)
    halo_rows(near_ref, far_ref, 2, rows, g3)

    def dhidden1(row, total):
        value = jnp.where(one(hid1_ref, row) > 0, total, 0.0).astype(BF16)
        put(d3, row, value)
        if 1 <= row < rows + 1:
            dh1_ref[(row - 1) * CHAN : row * CHAN, :] = value

    conv_rows(w_ref[7], g3, rows + 2, dhidden1)

    def next_g(row, total):
        value = (one(g_ref, row).astype(F32) + total).astype(BF16)
        g1_ref[row * CHAN : (row + 1) * CHAN, :] = value

    conv_rows(w_ref[5], d3, rows, next_g)
    send_edges(g1_ref, 2, next_near, next_far)


def grads1_kernel(rows, g_ref, hid1_ref, dh1_ref, x1_ref, grad10, grad11, s3):
    stack_rows(g_ref, rows, s3, 0)
    grad11[...] = grad_rows(s3, 0, hid1_ref, 0, rows)
    stack_rows(dh1_ref, rows, s3, 0)
    grad10[...] = grad_rows(s3, 0, x1_ref, 0, rows)


def output_kernel(rows, hid1_ref, x1_ref, w_ref, out_ref, token, k3, wide):
    token[...] = jnp.zeros_like(token)
    stack_rows(hid1_ref, rows + 2, k3, 0)

    def last_x(row, total):
        wide[row] = one(x1_ref, row + 1).astype(F32) + total

    conv_rows(w_ref[6], k3, rows, last_x)
    channels_first(wide, out_ref)


def backward0_kernel(
    rows, scale, g1_ref, near_ref, far_ref, hid0_ref, x_ref, xnear_ref, xfar_ref, w_ref, grad10, grad11,
    dh0_ref, keep_ref, send_ref, g3, d3, xs, both,
):
    stack_rows(g1_ref, rows, g3, 2)
    halo_rows(near_ref, far_ref, 2, rows, g3)

    def dhidden0(row, total):
        value = jnp.where(one(hid0_ref, row) > 0, total, 0.0).astype(BF16)
        dh0_ref[row * CHAN : (row + 1) * CHAN, :] = value
        put(d3, row, value)

    conv_rows(w_ref[3], g3, rows + 2, dhidden0)
    odd = odd_place()
    xs[CHAN : (rows + 1) * CHAN, :] = x_ref[...]
    near_at, far_at = jnp.where(odd, 0, rows + 1), jnp.where(odd, rows + 1, 0)
    near_row, far_row = jnp.where(odd, 3, 0), jnp.where(odd, 0, 3)
    for ref, at, row in ((xnear_ref, near_at, near_row), (xfar_ref, far_at, far_row)):
        source = pl.ds(pl.multiple_of(row * CHAN, CHAN), CHAN)
        xs[pl.ds(pl.multiple_of(at * CHAN, CHAN), CHAN), :] = ref[source, :]
    grad01 = grad_rows(g3, 2, hid0_ref, 0, rows)
    grad00 = grad_rows(d3, 1, xs, 0, rows)
    pairs = ((grad00, grad01), (grad10[...], grad11[...]))
    for section, pair in enumerate(pairs):
        for which, value in enumerate(pair):
            for a in range(3):
                for b in range(3):
                    block = value[(2 - b) * CHAN : (3 - b) * CHAN, a * CHAN : (a + 1) * CHAN]
                    at = which * 9 * CHAN + (3 * a + b) * CHAN
                    both[section, :, at : at + CHAN] = block * scale
    mine = lax.rem(lax.axis_index("space"), 2)
    keep_ref[...] = both[mine]
    send_ref[...] = both[1 - mine].astype(BF16)


def input_grad_kernel(rows, dh0_ref, g1_ref, w_ref, out_ref, token, d3, wide):
    token[...] = jnp.zeros_like(token)
    stack_rows(dh0_ref, rows + 2, d3, 0)

    def last_g(row, total):
        wide[row] = one(g1_ref, row).astype(F32) + total

    conv_rows(w_ref[1], d3, rows, last_g)
    channels_first(wide, out_ref)


def gathered_kernel(own_ref, other_ref, out_ref):
    mine = lax.rem(lax.axis_index("space"), 2)
    for section, ref in ((mine, own_ref), (1 - mine, other_ref)):
        for which in range(2):
            piece = ref[:, which * 9 * CHAN : (which + 1) * 9 * CHAN]
            out_ref[section, which] = piece.astype(F32)


def exchange(value, mask, count):
    return lax.ppermute(value, "space", [(d, d ^ mask) for d in range(count)])


def local(features, cotangent, kernels):
    rows, width = features.shape[1], features.shape[2]
    count = lax.axis_size("space")
    height = rows * count
    scale = 1.0 / math.sqrt(height * width)
    place = lax.axis_index("space")
    beyond = [(i, i + 1) for i in range(1, count - 1, 2)]
    beyond += [(target, source) for source, target in beyond]

    def shape(n, dtype=BF16):
        return jax.ShapeDtypeStruct((n * CHAN, width), dtype)

    def vmem(n):
        return pltpu.VMEM((n * STACK, width), BF16)

    def neighbours(near, far):
        return exchange(near, 1, count), lax.ppermute(far, "space", beyond)

    row_flops = 2 * CHAN * 9 * CHAN * width * 4
    grad = jax.ShapeDtypeStruct((STACK, STACK), F32)
    tile = jax.ShapeDtypeStruct((CHAN, rows, width), BF16)
    token = jax.ShapeDtypeStruct((8, 128), F32)
    wide = pltpu.VMEM((rows, CHAN, width), F32)
    half = (CHAN, 18 * CHAN)
    entry = [pltpu.VMEM((CHAN, rows, width), BF16), pltpu.SemaphoreType.DMA((PIECES,))]

    x, x_near, x_far = call(
        functools.partial(entry_kernel, 4), (features,), (shape(rows), shape(4), shape(4)),
        entry, 0, "x_rows", place=HBM,
    )
    xnear, xfar = neighbours(x_near, x_far)
    g, g_near, g_far = call(
        functools.partial(entry_kernel, 2), (cotangent,), (shape(rows), shape(2), shape(2)),
        entry, 0, "g_rows", after=(x_near,), place=HBM,
    )
    gnear, gfar = neighbours(g_near, g_far)
    (weights,) = call(
        weights_kernel, (kernels,), (jax.ShapeDtypeStruct((8, 2 * CHAN, 4 * STACK), BF16),), [],
        row_flops, "weights", after=(g_near,),
    )
    hid0, x1, hid1 = call(
        functools.partial(forward_kernel, rows, height), (x, xnear, xfar, weights),
        (shape(rows + 2),) * 3, [vmem(rows + 8), vmem(rows + 6), vmem(rows + 4)],
        36 * row_flops, "forward",
    )
    g1, g1_near, g1_far, dh1 = call(
        functools.partial(backward1_kernel, rows), (g, gnear, gfar, hid1, weights),
        (shape(rows), shape(2), shape(2), shape(rows)),
        [vmem(rows + 4), vmem(rows + 2)], 18 * row_flops, "backward1",
    )
    g1near, g1far = neighbours(g1_near, g1_far)
    grad10, grad11 = call(
        functools.partial(grads1_kernel, rows), (g, hid1, dh1, x1), (grad, grad), [vmem(rows)],
        16 * row_flops, "grads1",
    )
    dh0, part, send = call(
        functools.partial(backward0_kernel, rows, scale),
        (g1, g1near, g1far, hid0, x, xnear, xfar, weights, grad10, grad11),
        (shape(rows + 2), jax.ShapeDtypeStruct(half, F32), jax.ShapeDtypeStruct(half, BF16)),
        [vmem(rows + 4), vmem(rows + 2), pltpu.VMEM(((rows + 2) * CHAN, width), BF16),
         pltpu.VMEM((2, *half), F32)],
        26 * row_flops, "backward0",
    )

    part = part + exchange(send, 1, count).astype(F32)
    low, high = part[: CHAN // 2], part[CHAN // 2 :]
    bit = (place & 2) != 0
    send = jnp.where(bit, low, high).astype(BF16)
    part = jnp.where(bit, high, low)
    arrived = exchange(send, 2, count)
    section_output, mark = call(
        functools.partial(output_kernel, rows), (hid1, x1, weights), (tile, token),
        [vmem(rows + 2), wide], 8 * row_flops, "output", after=(send, dh0, g1),
    )
    part = part + (arrived.astype(F32) + mark[0, 0])
    step = 4
    input_grad = None
    while step < count:
        send = part.astype(BF16)
        masks = [step, 2 * step, 3 * step] if 2 * step < count else [step]
        arrived = [exchange(send, mask, count) for mask in masks]
        if input_grad is None:
            input_grad, mark = call(
                functools.partial(input_grad_kernel, rows), (dh0, g1, weights), (tile, token),
                [vmem(rows + 2), wide], 8 * row_flops, "input_grad", after=(send,),
            )
        own = send.astype(F32) + mark[0, 0]
        arrived = [value.astype(F32) for value in arrived]
        part = own + arrived[0]
        if len(masks) == 3:
            part = part + (arrived[1] + arrived[2])
        step *= len(masks) + 1
    done = part.astype(BF16)
    bit = (place & 2) != 0
    other = exchange(done, 2, count)
    done = jnp.where(bit, jnp.concatenate([other, done]), jnp.concatenate([done, other]))
    (kernel_grad,) = call(
        gathered_kernel, (done, exchange(done, 1, count)),
        (jax.ShapeDtypeStruct((2, 2, CHAN, 9 * CHAN), F32),), [], 0, "gathered",
    )
    return (section_output, input_grad, kernel_grad)


def solution(mesh):
    return jax.shard_map(
        local,
        mesh=mesh,
        in_specs=(P(None, "space", "groups"), P(None, "space", "groups"), P()),
        out_specs=(
            P(None, "space", "groups"),
            P(None, "space", "groups"),
            P("groups", None, None, None),
        ),
        check_vma=False,
    )
```

time: 81.5 us -> 75.1 us (0.921)
  local copies, waits for them, and re-layouts: 17.7 us -> 7.29 us
  starting transfers between devices: 27.8 us -> 35.3 us
  waiting for transfers between devices: 10.3 us -> 7.9 us
  Pallas kernels: 24.2 us -> 21.9 us
  other arithmetic: 0.18 us -> 1.44 us
    ppermute x7 -> x10, starting transfers between devices: 13.1 us -> 33.2 us  [exchange(): return lax.ppermute(value, 'space', [(d, d ^ mask) for d in range(count)])]
    ppermute x6 -> x3, starting transfers between devices: 14.6 us -> 2.19 us  [neighbours(): return (exchange(near, 1, count), lax.ppermute(far, 'space', beyond))]
    transpose x10 -> x0, local copies, waits for them, and re-layouts: 7.95 us -> none  [the longest x8 6.6 us: flipped(): return inner.transpose(3, 1, 2, 0).reshape(CHAN, 9 * CHAN)]
    reshape x4 -> x0, local copies, waits for them, and re-layouts: 3.26 us -> none  [flipped(): return inner.transpose(3, 1, 2, 0).reshape(CHAN, 9 * CHAN)]
    unnamed x26 -> x20, local copies, waits for them, and re-layouts: 3.66 us -> 6.27 us
    pallas_call x8 -> x10, Pallas kernels: 24.2 us -> 21.9 us  [call(): pl.pallas_call(kernel, out_shape=outs, in_specs=[ANY] * len(after) + [pla...]
    slice x5 -> x2, local copies, waits for them, and re-layouts: 2.8 us -> 1.02 us  [the longest x1 0.51 us: local(): part = part + (arrived.astype(F32) + mark[0, 0])]
    ppermute x6 -> x3, waiting for transfers between devices: 1.32 us -> 0.01 us  [neighbours(): return (exchange(near, 1, count), lax.ppermute(far, 'space', beyond))]
  transfers between devices with their start and end apart: 13 -> 13, of which waited for: 6 -> 5; matrix products, arithmetic and copies ran while one was open for 16% -> 1% of each run, Pallas kernels for 17% -> 18%
where the time goes in v1:
time: 75.1 us; the launch traced here: 74.8 us
  starting transfers between devices  35.3 us (47%)
  Pallas kernels  21.9 us (29%)
  waiting for transfers between devices  7.9 us (11%)
  local copies, waits for them, and re-layouts  7.29 us (10%)
  other arithmetic  1.44 us (2%)
  between operations  0.86 us (1%)
    ppermute x10, starting transfers between devices, exchange(): return lax.ppermute(value, 'space', [(d, d ^ mask) for d in range(count)])  33.2 us
    pallas_call x10, Pallas kernels, call(): pl.pallas_call(kernel, out_shape=outs, in_specs=[ANY] * len(after) + [pla...  21.9 us
    ppermute x10, waiting for transfers between devices, exchange(): return lax.ppermute(value, 'space', [(d, d ^ mask) for d in range(count)])  7.89 us
    unnamed x20, local copies, waits for them, and re-layouts  6.27 us
    ppermute x3, starting transfers between devices, neighbours(): return (exchange(near, 1, count), lax.ppermute(far, 'space', beyond))  2.19 us
  transfers between devices with their start and end apart: 13, of which 5 were waited for; matrix products, arithmetic and copies ran while one was open for 1% of the time, Pallas kernels for 18%

profile of v1, /device:TPU:0, one launch (start us, length us, event | category | flops | bytes accessed | tf_op | source)
XLA Modules:
  0.0 74.8 jit_solution(12078122496472445364)
XLA Ops:
  0.7 1.3 %copy-done.1 = bf16[64,8,1024]{2,1,0:T(8,128)(2,1)S(1)} copy-done((bf16[64,8,1024]{2,1,0:T(8,128)(2,1)S(1)}, bf16[64,8,1024]{2,1,0:T(8,128)(2,1)}, u32[]{:S(2)}) %copy-start.1) | copy-done | bytes 1048600
  4.5 3.9 %collective-permute-start = (bf16[128,1024]{1,0:T(8,128)(2,1)S(1)}, bf16[128,1024]{1,0:T(8,128)(2,1)S(1)}, u32[]{:S(2)}, u32[]{:S(2)}) collective-permute-start(bf16[128,1024]{1,0:T(8,128)(2,1)S(1)} %get-tuple-element.27.refs_0_), channel_id=1, source_target_pairs={{0,1},{1,0},{2,3},{3,2},{4,5},{5,4},{6,7},{7,6},{8,9},{9,8},{10,11... | collective-permute-start | bytes 786440 | tf_op jit(solution)/shard_map/ppermute | solution.py:302
  9.7 4.9 %forward.1 = (bf16[640,1024]{1,0:T(8,128)(2,1)S(1)}, bf16[640,1024]{1,0:T(8,128)(2,1)S(1)}, bf16[640,1024]{1,0:T(8,128)(2,1)S(1)}) custom-call(bf16[512,1024]{1,0:T(8,128)(2,1)S(1)} %get-tuple-element.29.refs_0_.refs_4_, bf16[256,1024]{1,0:T(8,128)(2,1)S(1)} %collective-permute-done.2.refs_1_.refs_5_, ...), custom_call_target="tpu_custom_call" | custom-call | flops 10871635968 | bytes 7602176 | tf_op jit(solution)/shard_map/forward/pallas_call | solution.py:28
  14.7 3.1 %backward1.1 = (bf16[512,1024]{1,0:T(8,128)(2,1)S(1)}, bf16[128,1024]{1,0:T(8,128)(2,1)S(1)}, bf16[128,1024]{1,0:T(8,128)(2,1)S(1)}, bf16[512,1024]{1,0:T(8,128)(2,1)S(1)}) custom-call(bf16[512,1024]{1,0:T(8,128)(2,1)S(1)} %get-tuple-element.26.refs_0_, bf16[128,1024]{1,0:T(8,128)(2,1)S(1)} %collective-permute-done.refs_1_, ...), custom_call_target="tpu_custom_call" | custom-call | flops 5435817984 | bytes 7077888 | tf_op jit(solution)/shard_map/backward1/pallas_call | solution.py:28
  17.8 12.4 %collective-permute-start.4 = (bf16[128,1024]{1,0:T(8,128)(2,1)S(1)}, bf16[128,1024]{1,0:T(8,128)(2,1)S(1)}, u32[]{:S(2)}, u32[]{:S(2)}) collective-permute-start(bf16[128,1024]{1,0:T(8,128)(2,1)S(1)} %get-tuple-element.33), channel_id=1, source_target_pairs={{0,1},{1,0},{2,3},{3,2},{4,5},{5,4},{6,7},{7,6},{8,9},{9,8},{10,11... | collective-permute-start | bytes 786440 | tf_op jit(solution)/shard_map/ppermute | solution.py:302
  31.1 2.0 %grads1.1 = (f32[192,192]{1,0:T(8,128)S(1)}, f32[192,192]{1,0:T(8,128)S(1)}) custom-call(bf16[512,1024]{1,0:T(8,128)(2,1)S(1)} %get-tuple-element.26.refs_0_, bf16[640,1024]{1,0:T(8,128)(2,1)S(1)} %get-tuple-element.31.refs_3_.refs_1_, bf16[512,1024]{1,0:T(8,128)(2,1)S(1)} %get-tuple-element.36.refs_2_, bf16[640,1024]{1,0:T(8,128)(2,1)S(1)} %get-tuple-element.37.refs_3_.refs_4_), custom_call_target="tpu_custom_call" | custom-call | flops 4831838208 | bytes 5013504 | tf_op jit(solution)/shard_map/grads1/pallas_call | solution.py:28
  33.1 4.0 %backward0.1 = (bf16[640,1024]{1,0:T(8,128)(2,1)S(1)}, f32[64,1152]{1,0:T(8,128)S(1)}, bf16[64,1152]{1,0:T(8,128)(2,1)S(1)}) custom-call(bf16[512,1024]{1,0:T(8,128)(2,1)S(1)} %get-tuple-element.32.refs_0_.refs_2_, bf16[128,1024]{1,0:T(8,128)(2,1)S(1)} %collective-permute-done.4.refs_1_, bf16[128,1024]{1,0:T(8,128)(2,1)S(1)} %collective-permute-done.5.refs_2_, ...), custom_call_target="tpu_custom_call" | custom-call | flops 7851737088 | bytes 8601600 | tf_op jit(solution)/shard_map/backward0/pallas_call | solution.py:28
  37.2 1.1 %copy-done.5 = bf16[640,1024]{1,0:T(8,128)(2,1)} copy-done((bf16[640,1024]{1,0:T(8,128)(2,1)}, bf16[640,1024]{1,0:T(8,128)(2,1)S(1)}, u32[]{:S(2)}) %copy-start.5) | copy-done | bytes 1310744
  38.2 7.7 %collective-permute-start.6 = (bf16[64,1152]{1,0:T(8,128)(2,1)S(1)}, bf16[64,1152]{1,0:T(8,128)(2,1)S(1)}, u32[]{:S(2)}, u32[]{:S(2)}) collective-permute-start(bf16[64,1152]{1,0:T(8,128)(2,1)S(1)} %get-tuple-element.41), channel_id=1, source_target_pairs={{0,1},{1,0},{2,3},{3,2},{4,5},{5,4},{6,7},{7,6},{8,9},{9,8},{10,11... | collective-permute-start | bytes 442376 | tf_op jit(solution)/shard_map/ppermute | solution.py:302
  45.9 1.0 %collective-permute-done.6 = bf16[64,1152]{1,0:T(8,128)(2,1)S(1)} collective-permute-done((bf16[64,1152]{1,0:T(8,128)(2,1)S(1)}, bf16[64,1152]{1,0:T(8,128)(2,1)S(1)}, u32[]{:S(2)}, u32[]{:S(2)}) %collective-permute-start.6) | collective-permute-done | bytes 147488 | tf_op jit(solution)/shard_map/ppermute | solution.py:302
  47.0 2.8 %collective-permute-start.7 = (bf16[32,1152]{1,0:T(8,128)(2,1)S(1)}, bf16[32,1152]{1,0:T(8,128)(2,1)S(1)}, u32[]{:S(2)}, u32[]{:S(2)}) collective-permute-start(bf16[32,1152]{1,0:T(8,128)(2,1)S(1)} %select_convert_fusion.refs_0_), channel_id=1, source_target_pairs={{0,2},{1,3},{2,0},{3,1},{4,6},{5,7},{6,4},{7,5},{8,10},{9,11},{10,... | collective-permute-start | bytes 221192 | tf_op jit(solution)/shard_map/ppermute | solution.py:302
  49.8 1.3 %copy-done.4 = bf16[640,1024]{1,0:T(8,128)(2,1)S(1)} copy-done((bf16[640,1024]{1,0:T(8,128)(2,1)S(1)}, bf16[640,1024]{1,0:T(8,128)(2,1)}, u32[]{:S(2)}) %copy-start.4) | copy-done | bytes 1310744
  51.1 1.3 %copy-done.6 = bf16[640,1024]{1,0:T(8,128)(2,1)S(1)} copy-done((bf16[640,1024]{1,0:T(8,128)(2,1)S(1)}, bf16[640,1024]{1,0:T(8,128)(2,1)}, u32[]{:S(2)}) %copy-start.6) | copy-done | bytes 1310744
  52.4 1.2 %copy-done.9 = bf16[512,1024]{1,0:T(8,128)(2,1)S(1)} copy-done((bf16[512,1024]{1,0:T(8,128)(2,1)S(1)}, bf16[512,1024]{1,0:T(8,128)(2,1)}, u32[]{:S(2)}) %copy-start.9) | copy-done | bytes 1048600
  53.7 2.5 %output.1 = (bf16[64,8,1024]{2,1,0:T(8,128)(2,1)}, f32[8,128]{1,0:T(8,128)S(1)}) custom-call(bf16[32,1152]{1,0:T(8,128)(2,1)S(1)} %select_convert_fusion.refs_0_, bf16[640,1024]{1,0:T(8,128)(2,1)S(1)} %copy-done.6, bf16[512,1024]{1,0:T(8,128)(2,1)S(1)} %copy-done.9, bf16[640,1024]{1,0:T(8,128)(2,1)S(1)} %copy-done.4, ...), custom_call_target="tpu_custom_call" | custom-call | flops 2415919104 | bytes 5246976 | tf_op jit(solution)/shard_map/output/pallas_call | solution.py:28
  57.4 2.3 %collective-permute-start.10 = (bf16[32,1152]{1,0:T(8,128)(2,1)S(1)}, bf16[32,1152]{1,0:T(8,128)(2,1)S(1)}, u32[]{:S(2)}, u32[]{:S(2)}) collective-permute-start(bf16[32,1152]{1,0:T(8,128)(2,1)S(1)} %add_convert_fusion.1.refs_0_), channel_id=1, source_target_pairs={{0,12},{1,13},{2,14},{3,15},{4,8},{5,9},{6,10},{7,11},{8,4},{9,5},... | collective-permute-start | bytes 221192 | tf_op jit(solution)/shard_map/ppermute | solution.py:302
  59.7 0.9 %collective-permute-start.8 = (bf16[32,1152]{1,0:T(8,128)(2,1)S(1)}, bf16[32,1152]{1,0:T(8,128)(2,1)S(1)}, u32[]{:S(2)}, u32[]{:S(2)}) collective-permute-start(bf16[32,1152]{1,0:T(8,128)(2,1)S(1)} %add_convert_fusion.1.refs_0_), channel_id=1, source_target_pairs={{0,4},{1,5},{2,6},{3,7},{4,0},{5,1},{6,2},{7,3},{8,12},{9,13},{10,... | collective-permute-start | bytes 221192 | tf_op jit(solution)/shard_map/ppermute | solution.py:302
  60.6 1.2 %collective-permute-start.9 = (bf16[32,1152]{1,0:T(8,128)(2,1)S(1)}, bf16[32,1152]{1,0:T(8,128)(2,1)S(1)}, u32[]{:S(2)}, u32[]{:S(2)}) collective-permute-start(bf16[32,1152]{1,0:T(8,128)(2,1)S(1)} %add_convert_fusion.1.refs_0_), channel_id=1, source_target_pairs={{0,8},{1,9},{2,10},{3,11},{4,12},{5,13},{6,14},{7,15},{8,0},{9,1},... | collective-permute-start | bytes 221192 | tf_op jit(solution)/shard_map/ppermute | solution.py:302
  61.8 2.5 %input_grad.1 = (bf16[64,8,1024]{2,1,0:T(8,128)(2,1)}, f32[8,128]{1,0:T(8,128)S(1)}) custom-call(bf16[32,1152]{1,0:T(8,128)(2,1)S(1)} %add_convert_fusion.1.refs_0_, bf16[640,1024]{1,0:T(8,128)(2,1)S(1)} %copy-done.7, bf16[512,1024]{1,0:T(8,128)(2,1)S(1)} %copy-done.9, bf16[8,128,768]{2,1,0:T(8,128)(2,1)S(1)} %weights.1.refs_3_.refs_4_.refs_7_.refs_5_), custom_call_target="tpu_custom_call" | custom-call | flops 2415919104 | bytes 4984832 | tf_op jit(solution)/shard_map/input_grad/pallas_call | solution.py:28
  65.7 1.6 %collective-permute-done.9 = bf16[32,1152]{1,0:T(8,128)(2,1)S(1)} collective-permute-done((bf16[32,1152]{1,0:T(8,128)(2,1)S(1)}, bf16[32,1152]{1,0:T(8,128)(2,1)S(1)}, u32[]{:S(2)}, u32[]{:S(2)}) %collective-permute-start.9) | collective-permute-done | bytes 73760 | tf_op jit(solution)/shard_map/ppermute | solution.py:302
  67.9 1.3 %collective-permute-start.11 = (bf16[32,1152]{1,0:T(8,128)(2,1)S(1)}, bf16[32,1152]{1,0:T(8,128)(2,1)S(1)}, u32[]{:S(2)}, u32[]{:S(2)}) collective-permute-start(bf16[32,1152]{1,0:T(8,128)(2,1)S(1)} %add_convert_fusion), channel_id=1, source_target_pairs={{0,2},{1,3},{2,0},{3,1},{4,6},{5,7},{6,4},{7,5},{8,10},{9,11},{10,... | collective-permute-start | bytes 221192 | tf_op jit(solution)/shard_map/ppermute | solution.py:302
  69.2 3.1 %collective-permute-done.11 = bf16[32,1152]{1,0:T(8,128)(2,1)S(1)} collective-permute-done((bf16[32,1152]{1,0:T(8,128)(2,1)S(1)}, bf16[32,1152]{1,0:T(8,128)(2,1)S(1)}, u32[]{:S(2)}, u32[]{:S(2)}) %collective-permute-start.11) | collective-permute-done | bytes 73760 | tf_op jit(solution)/shard_map/ppermute | solution.py:302
  72.4 1.4 %collective-permute-done.12.refs_1_ = bf16[64,1152]{1,0:T(8,128)(2,1)S(1)} collective-permute-done((bf16[64,1152]{1,0:T(8,128)(2,1)S(1)}, bf16[64,1152]{1,0:T(8,128)(2,1)S(1)}, u32[]{:S(2)}, u32[]{:S(2)}) %collective-permute-start.12) | collective-permute-done | bytes 147488 | tf_op jit(solution)/shard_map/ppermute | solution.py:302
  73.8 1.0 %gathered.1 = f32[2,2,64,576]{3,2,1,0:T(8,128)} custom-call(bf16[64,1152]{1,0:T(8,128)(2,1)S(1)} %maximum_select_fusion.refs_0_, bf16[64,1152]{1,0:T(8,128)(2,1)S(1)} %collective-permute-done.12.refs_1_), custom_call_target="tpu_custom_call" | custom-call | bytes 884736 | tf_op jit(solution)/shard_map/gathered/pallas_call | solution.py:28
  (39 shorter events, 8.0 us)
Async XLA Ops:
  0.6 3.2 %copy-start = (bf16[64,8,1024]{2,1,0:T(8,128)(2,1)S(1)}, bf16[64,8,1024]{2,1,0:T(8,128)(2,1)}, u32[]{:S(2)}) copy-start(bf16[64,8,1024]{2,1,0:T(8,128)(2,1)} %refs_1_.2) | copy-start | bytes 3145732
  0.6 1.3 %copy-start.1 = (bf16[64,8,1024]{2,1,0:T(8,128)(2,1)S(1)}, bf16[64,8,1024]{2,1,0:T(8,128)(2,1)}, u32[]{:S(2)}) copy-start(bf16[64,8,1024]{2,1,0:T(8,128)(2,1)} %refs_0_.1) | copy-start | bytes 3145732
  2.0 7.1 %copy-start.2 = (bf16[2,2,64,576]{3,2,1,0:T(8,128)(2,1)S(1)}, bf16[2,2,64,576]{3,2,1,0:T(8,128)(2,1)}, u32[]{:S(2)}) copy-start(bf16[2,2,64,576]{3,2,1,0:T(8,128)(2,1)} %refs_1_.3) | copy-start | bytes 884740
  2.6 7.1 %collective-permute-start.2 = (bf16[256,1024]{1,0:T(8,128)(2,1)S(1)}, bf16[256,1024]{1,0:T(8,128)(2,1)S(1)}, u32[]{:S(2)}, u32[]{:S(2)}) collective-permute-start(bf16[256,1024]{1,0:T(8,128)(2,1)S(1)} %get-tuple-element.25.refs_0_), channel_id=1, source_target_pairs={{0,1},{1,0},{2,3},{3,2},{4,5},{5,4},{6,7},{7,6},{8,9},{9,8},{10,11... | collective-permute-start | bytes 1572872 | tf_op jit(solution)/shard_map/ppermute | solution.py:302
  3.1 6.6 %collective-permute-start.3 = (bf16[256,1024]{1,0:T(8,128)(2,1)S(1)}, bf16[256,1024]{1,0:T(8,128)(2,1)S(1)}, u32[]{:S(2)}, u32[]{:S(2)}) collective-permute-start(bf16[256,1024]{1,0:T(8,128)(2,1)S(1)} %get-tuple-element.30), channel_id=1, source_target_pairs={{1,2},{3,4},{5,6},{7,8},{9,10},{11,12},{13,14},{2,1},{4,3},{6,5},{... | collective-permute-start | bytes 1572872 | tf_op jit(solution)/shard_map/ppermute | solution.py:321
  4.5 10.2 %collective-permute-start = (bf16[128,1024]{1,0:T(8,128)(2,1)S(1)}, bf16[128,1024]{1,0:T(8,128)(2,1)S(1)}, u32[]{:S(2)}, u32[]{:S(2)}) collective-permute-start(bf16[128,1024]{1,0:T(8,128)(2,1)S(1)} %get-tuple-element.27.refs_0_), channel_id=1, source_target_pairs={{0,1},{1,0},{2,3},{3,2},{4,5},{5,4},{6,7},{7,6},{8,9},{9,8},{10,11... | collective-permute-start | bytes 786440 | tf_op jit(solution)/shard_map/ppermute | solution.py:302
  8.4 6.3 %collective-permute-start.1 = (bf16[128,1024]{1,0:T(8,128)(2,1)S(1)}, bf16[128,1024]{1,0:T(8,128)(2,1)S(1)}, u32[]{:S(2)}, u32[]{:S(2)}) collective-permute-start(bf16[128,1024]{1,0:T(8,128)(2,1)S(1)} %get-tuple-element.28), channel_id=1, source_target_pairs={{1,2},{3,4},{5,6},{7,8},{9,10},{11,12},{13,14},{2,1},{4,3},{6,5},{... | collective-permute-start | bytes 786440 | tf_op jit(solution)/shard_map/ppermute | solution.py:321
  14.7 16.4 %copy-start.3 = (bf16[640,1024]{1,0:T(8,128)(2,1)}, bf16[640,1024]{1,0:T(8,128)(2,1)S(1)}, u32[]{:S(2)}) copy-start(bf16[640,1024]{1,0:T(8,128)(2,1)S(1)} %get-tuple-element.31.refs_3_.refs_1_) | copy-start | bytes 3932164
  17.8 15.3 %copy-start.8 = (bf16[512,1024]{1,0:T(8,128)(2,1)}, bf16[512,1024]{1,0:T(8,128)(2,1)S(1)}, u32[]{:S(2)}) copy-start(bf16[512,1024]{1,0:T(8,128)(2,1)S(1)} %get-tuple-element.32.refs_0_.refs_2_) | copy-start | bytes 3145732
  17.8 15.3 %collective-permute-start.4 = (bf16[128,1024]{1,0:T(8,128)(2,1)S(1)}, bf16[128,1024]{1,0:T(8,128)(2,1)S(1)}, u32[]{:S(2)}, u32[]{:S(2)}) collective-permute-start(bf16[128,1024]{1,0:T(8,128)(2,1)S(1)} %get-tuple-element.33), channel_id=1, source_target_pairs={{0,1},{1,0},{2,3},{3,2},{4,5},{5,4},{6,7},{7,6},{8,9},{9,8},{10,11... | collective-permute-start | bytes 786440 | tf_op jit(solution)/shard_map/ppermute | solution.py:302
  30.2 2.9 %collective-permute-start.5 = (bf16[128,1024]{1,0:T(8,128)(2,1)S(1)}, bf16[128,1024]{1,0:T(8,128)(2,1)S(1)}, u32[]{:S(2)}, u32[]{:S(2)}) collective-permute-start(bf16[128,1024]{1,0:T(8,128)(2,1)S(1)} %get-tuple-element.34), channel_id=1, source_target_pairs={{1,2},{3,4},{5,6},{7,8},{9,10},{11,12},{13,14},{2,1},{4,3},{6,5},{... | collective-permute-start | bytes 786440 | tf_op jit(solution)/shard_map/ppermute | solution.py:321
  37.1 1.1 %copy-start.5 = (bf16[640,1024]{1,0:T(8,128)(2,1)}, bf16[640,1024]{1,0:T(8,128)(2,1)S(1)}, u32[]{:S(2)}) copy-start(bf16[640,1024]{1,0:T(8,128)(2,1)S(1)} %get-tuple-element.42.refs_1_) | copy-start | bytes 3932164
  38.2 8.7 %collective-permute-start.6 = (bf16[64,1152]{1,0:T(8,128)(2,1)S(1)}, bf16[64,1152]{1,0:T(8,128)(2,1)S(1)}, u32[]{:S(2)}, u32[]{:S(2)}) collective-permute-start(bf16[64,1152]{1,0:T(8,128)(2,1)S(1)} %get-tuple-element.41), channel_id=1, source_target_pairs={{0,1},{1,0},{2,3},{3,2},{4,5},{5,4},{6,7},{7,6},{8,9},{9,8},{10,11... | collective-permute-start | bytes 442376 | tf_op jit(solution)/shard_map/ppermute | solution.py:302
  47.0 9.7 %collective-permute-start.7 = (bf16[32,1152]{1,0:T(8,128)(2,1)S(1)}, bf16[32,1152]{1,0:T(8,128)(2,1)S(1)}, u32[]{:S(2)}, u32[]{:S(2)}) collective-permute-start(bf16[32,1152]{1,0:T(8,128)(2,1)S(1)} %select_convert_fusion.refs_0_), channel_id=1, source_target_pairs={{0,2},{1,3},{2,0},{3,1},{4,6},{5,7},{6,4},{7,5},{8,10},{9,11},{10,... | collective-permute-start | bytes 221192 | tf_op jit(solution)/shard_map/ppermute | solution.py:302
  49.8 1.3 %copy-start.4 = (bf16[640,1024]{1,0:T(8,128)(2,1)S(1)}, bf16[640,1024]{1,0:T(8,128)(2,1)}, u32[]{:S(2)}) copy-start(bf16[640,1024]{1,0:T(8,128)(2,1)} %copy-done.3) | copy-start | bytes 3932164
  51.1 1.3 %copy-start.6 = (bf16[640,1024]{1,0:T(8,128)(2,1)S(1)}, bf16[640,1024]{1,0:T(8,128)(2,1)}, u32[]{:S(2)}) copy-start(bf16[640,1024]{1,0:T(8,128)(2,1)} %copy-done.5) | copy-start | bytes 3932164
  52.4 1.2 %copy-start.9 = (bf16[512,1024]{1,0:T(8,128)(2,1)S(1)}, bf16[512,1024]{1,0:T(8,128)(2,1)}, u32[]{:S(2)}) copy-start(bf16[512,1024]{1,0:T(8,128)(2,1)} %copy-done.8) | copy-start | bytes 3145732
  53.7 8.2 %copy-start.7 = (bf16[640,1024]{1,0:T(8,128)(2,1)S(1)}, bf16[640,1024]{1,0:T(8,128)(2,1)}, u32[]{:S(2)}) copy-start(bf16[640,1024]{1,0:T(8,128)(2,1)} %copy-done.5) | copy-start | bytes 3932164
  57.4 7.5 %collective-permute-start.10 = (bf16[32,1152]{1,0:T(8,128)(2,1)S(1)}, bf16[32,1152]{1,0:T(8,128)(2,1)S(1)}, u32[]{:S(2)}, u32[]{:S(2)}) collective-permute-start(bf16[32,1152]{1,0:T(8,128)(2,1)S(1)} %add_convert_fusion.1.refs_0_), channel_id=1, source_target_pairs={{0,12},{1,13},{2,14},{3,15},{4,8},{5,9},{6,10},{7,11},{8,4},{9,5},... | collective-permute-start | bytes 221192 | tf_op jit(solution)/shard_map/ppermute | solution.py:302
  59.7 6.0 %collective-permute-start.8 = (bf16[32,1152]{1,0:T(8,128)(2,1)S(1)}, bf16[32,1152]{1,0:T(8,128)(2,1)S(1)}, u32[]{:S(2)}, u32[]{:S(2)}) collective-permute-start(bf16[32,1152]{1,0:T(8,128)(2,1)S(1)} %add_convert_fusion.1.refs_0_), channel_id=1, source_target_pairs={{0,4},{1,5},{2,6},{3,7},{4,0},{5,1},{6,2},{7,3},{8,12},{9,13},{10,... | collective-permute-start | bytes 221192 | tf_op jit(solution)/shard_map/ppermute | solution.py:302
  60.6 6.6 %collective-permute-start.9 = (bf16[32,1152]{1,0:T(8,128)(2,1)S(1)}, bf16[32,1152]{1,0:T(8,128)(2,1)S(1)}, u32[]{:S(2)}, u32[]{:S(2)}) collective-permute-start(bf16[32,1152]{1,0:T(8,128)(2,1)S(1)} %add_convert_fusion.1.refs_0_), channel_id=1, source_target_pairs={{0,8},{1,9},{2,10},{3,11},{4,12},{5,13},{6,14},{7,15},{8,0},{9,1},... | collective-permute-start | bytes 221192 | tf_op jit(solution)/shard_map/ppermute | solution.py:302
  67.9 4.4 %collective-permute-start.11 = (bf16[32,1152]{1,0:T(8,128)(2,1)S(1)}, bf16[32,1152]{1,0:T(8,128)(2,1)S(1)}, u32[]{:S(2)}, u32[]{:S(2)}) collective-permute-start(bf16[32,1152]{1,0:T(8,128)(2,1)S(1)} %add_convert_fusion), channel_id=1, source_target_pairs={{0,2},{1,3},{2,0},{3,1},{4,6},{5,7},{6,4},{7,5},{8,10},{9,11},{10,... | collective-permute-start | bytes 221192 | tf_op jit(solution)/shard_map/ppermute | solution.py:302
  72.4 1.4 %collective-permute-start.12 = (bf16[64,1152]{1,0:T(8,128)(2,1)S(1)}, bf16[64,1152]{1,0:T(8,128)(2,1)S(1)}, u32[]{:S(2)}, u32[]{:S(2)}) collective-permute-start(bf16[64,1152]{1,0:T(8,128)(2,1)S(1)} %maximum_select_fusion.refs_0_), channel_id=1, source_target_pairs={{0,1},{1,0},{2,3},{3,2},{4,5},{5,4},{6,7},{7,6},{8,9},{9,8},{10,11... | collective-permute-start | bytes 442376 | tf_op jit(solution)/shard_map/ppermute | solution.py:302

commit v2 on v1

--- a/solution.py
+++ b/solution.py
@@ -58,9 +58,13 @@
     return ref[row * CHAN : (row + 1) * CHAN, :]
 
 
-def stack_rows(ref, count, target, at):
-    for row in range(count):
+def stack_rows(ref, rows, target, at):
+    for row in rows:
         put(target, row + at, one(ref, row))
+
+
+def copy_rows(ref, count, target, at):
+    target[at * CHAN : (at + count) * CHAN, :] = ref[: count * CHAN, :]
 
 
 def two_rows(target, index, column, value):
@@ -87,8 +91,8 @@
                 two_rows(target, index + 1, tap * CHAN, turned.astype(BF16))
 
 
-def conv_rows(weight, source, count, finish):
-    for row in range(0, count, 2):
+def conv_rows(weight, source, first, count, finish):
+    for row in range(first, first + count, 2):
         total = jnp.dot(
             weight,
             source[row * STACK : (row + 4) * STACK, :],
@@ -167,8 +171,32 @@
     target[...] = jnp.swapaxes(wide[...], 0, 1).astype(BF16)
 
 
+def inner_kernel(rows, x_ref, w_ref, hid0_ref, x1_ref, hid1_ref, x3, h3, y3):
+    stack_rows(x_ref, range(rows), x3, 0)
+
+    def hidden0(row, total):
+        value = jnp.maximum(total, 0.0).astype(BF16)
+        put(h3, row, value)
+        hid0_ref[row * CHAN : (row + 1) * CHAN, :] = value
+
+    conv_rows(w_ref[0], x3, 0, rows - 2, hidden0)
+
+    def next_x(row, total):
+        value = (one(x_ref, row + 2).astype(F32) + total).astype(BF16)
+        put(y3, row, value)
+        x1_ref[row * CHAN : (row + 1) * CHAN, :] = value
+
+    conv_rows(w_ref[2], h3, 0, rows - 4, next_x)
+
+    def hidden1(row, total):
+        hid1_ref[row * CHAN : (row + 1) * CHAN, :] = jnp.maximum(total, 0.0).astype(BF16)
+
+    conv_rows(w_ref[4], y3, 0, rows - 6, hidden1)
+
+
 def forward_kernel(
-    rows, height, x_ref, near_ref, far_ref, w_ref, hid0_ref, x1_ref, hid1_ref, x3, h3, y3,
+    rows, height, x_ref, near_ref, far_ref, w_ref, hid0_in, x1_in, hid1_in,
+    hid0_ref, x1_ref, hid1_ref, x3, h3, y3,
 ):
     first = lax.axis_index("space") * rows
 
@@ -178,8 +206,13 @@
         keep = jnp.logical_and(first + row >= 0, first + row < height)
         return jnp.where(keep, value, 0.0)
 
-    stack_rows(x_ref, rows, x3, 4)
     halo_rows(near_ref, far_ref, 4, rows, x3)
+    stack_rows(x_ref, (0, 1, rows - 2, rows - 1), x3, 4)
+    stack_rows(hid0_in, (0, 1, rows - 4, rows - 3), h3, 4)
+    stack_rows(x1_in, (0, 1, rows - 6, rows - 5), y3, 4)
+    copy_rows(hid0_in, rows - 2, hid0_ref, 2)
+    copy_rows(x1_in, rows - 4, x1_ref, 3)
+    copy_rows(hid1_in, rows - 6, hid1_ref, 4)
 
     def hidden0(row, total):
         value = inside(row - 3, jnp.maximum(total, 0.0)).astype(BF16)
@@ -187,27 +220,28 @@
         if 2 <= row < rows + 4:
             hid0_ref[(row - 2) * CHAN : (row - 1) * CHAN, :] = value
 
-    conv_rows(w_ref[0], x3, rows + 6, hidden0)
-
     def next_x(row, total):
         value = inside(row - 2, middle(x3, row + 2).astype(F32) + total).astype(BF16)
         put(y3, row, value)
         if 1 <= row < rows + 3:
             x1_ref[(row - 1) * CHAN : row * CHAN, :] = value
 
-    conv_rows(w_ref[2], h3, rows + 4, next_x)
-
     def hidden1(row, total):
         value = inside(row - 1, jnp.maximum(total, 0.0)).astype(BF16)
         hid1_ref[row * CHAN : (row + 1) * CHAN, :] = value
 
-    conv_rows(w_ref[4], y3, rows + 2, hidden1)
+    for at in (0, rows + 2):
+        conv_rows(w_ref[0], x3, at, 4, hidden0)
+    for at in (0, rows):
+        conv_rows(w_ref[2], h3, at, 4, next_x)
+    for at in (0, rows - 2):
+        conv_rows(w_ref[4], y3, at, 4, hidden1)
 
 
 def backward1_kernel(
     rows, g_ref, near_ref, far_ref, hid1_ref, w_ref, g1_ref, next_near, next_far, dh1_ref, g3, d3,
 ):
-    stack_rows(g_ref, rows, g3, 2)
+    stack_rows(g_ref, range(rows), g3, 2)
     halo_rows(near_ref, far_ref, 2, rows, g3)
 
     def dhidden1(row, total):
@@ -216,39 +250,42 @@
         if 1 <= row < rows + 1:
             dh1_ref[(row - 1) * CHAN : row * CHAN, :] = value
 
-    conv_rows(w_ref[7], g3, rows + 2, dhidden1)
+    conv_rows(w_ref[7], g3, 0, rows + 2, dhidden1)
 
     def next_g(row, total):
         value = (one(g_ref, row).astype(F32) + total).astype(BF16)
         g1_ref[row * CHAN : (row + 1) * CHAN, :] = value
 
-    conv_rows(w_ref[5], d3, rows, next_g)
+    conv_rows(w_ref[5], d3, 0, rows, next_g)
     send_edges(g1_ref, 2, next_near, next_far)
 
 
-def grads1_kernel(rows, g_ref, hid1_ref, dh1_ref, x1_ref, grad10, grad11, s3):
-    stack_rows(g_ref, rows, s3, 0)
+def grads1_kernel(
+    rows, g_ref, hid1_ref, dh1_ref, x1_ref, g1_ref, hid0_ref, grad01, grad10, grad11, s3, t3, u3
+):
+    stack_rows(g_ref, range(rows), s3, 0)
     grad11[...] = grad_rows(s3, 0, hid1_ref, 0, rows)
-    stack_rows(dh1_ref, rows, s3, 0)
-    grad10[...] = grad_rows(s3, 0, x1_ref, 0, rows)
-
-
-def output_kernel(rows, hid1_ref, x1_ref, w_ref, out_ref, token, k3, wide):
-    token[...] = jnp.zeros_like(token)
-    stack_rows(hid1_ref, rows + 2, k3, 0)
+    stack_rows(dh1_ref, range(rows), t3, 0)
+    grad10[...] = grad_rows(t3, 0, x1_ref, 0, rows)
+    stack_rows(g1_ref, range(rows), u3, 0)
+    grad01[...] = grad_rows(u3, 0, hid0_ref, 0, rows)
+
+
+def output_kernel(rows, hid1_ref, x1_ref, w_ref, out_ref, k3, wide):
+    stack_rows(hid1_ref, range(rows + 2), k3, 0)
 
     def last_x(row, total):
         wide[row] = one(x1_ref, row + 1).astype(F32) + total
 
-    conv_rows(w_ref[6], k3, rows, last_x)
+    conv_rows(w_ref[6], k3, 0, rows, last_x)
     channels_first(wide, out_ref)
 
 
 def backward0_kernel(
-    rows, scale, g1_ref, near_ref, far_ref, hid0_ref, x_ref, xnear_ref, xfar_ref, w_ref, grad10, grad11,
+    rows, scale, g1_ref, near_ref, far_ref, hid0_ref, x_ref, xnear_ref, xfar_ref, w_ref, grad01, grad10, grad11,
     dh0_ref, keep_ref, send_ref, g3, d3, xs, both,
 ):
-    stack_rows(g1_ref, rows, g3, 2)
+    stack_rows(g1_ref, range(rows), g3, 2)
     halo_rows(near_ref, far_ref, 2, rows, g3)
 
     def dhidden0(row, total):
@@ -256,7 +293,7 @@
         dh0_ref[row * CHAN : (row + 1) * CHAN, :] = value
         put(d3, row, value)
 
-    conv_rows(w_ref[3], g3, rows + 2, dhidden0)
+    conv_rows(w_ref[3], g3, 0, rows + 2, dhidden0)
     odd = odd_place()
     xs[CHAN : (rows + 1) * CHAN, :] = x_ref[...]
     near_at, far_at = jnp.where(odd, 0, rows + 1), jnp.where(odd, rows + 1, 0)
@@ -264,9 +301,8 @@
     for ref, at, row in ((xnear_ref, near_at, near_row), (xfar_ref, far_at, far_row)):
         source = pl.ds(pl.multiple_of(row * CHAN, CHAN), CHAN)
         xs[pl.ds(pl.multiple_of(at * CHAN, CHAN), CHAN), :] = ref[source, :]
-    grad01 = grad_rows(g3, 2, hid0_ref, 0, rows)
     grad00 = grad_rows(d3, 1, xs, 0, rows)
-    pairs = ((grad00, grad01), (grad10[...], grad11[...]))
+    pairs = ((grad00, grad01[...]), (grad10[...], grad11[...]))
     for section, pair in enumerate(pairs):
         for which, value in enumerate(pair):
             for a in range(3):
@@ -279,14 +315,13 @@
     send_ref[...] = both[1 - mine].astype(BF16)
 
 
-def input_grad_kernel(rows, dh0_ref, g1_ref, w_ref, out_ref, token, d3, wide):
-    token[...] = jnp.zeros_like(token)
-    stack_rows(dh0_ref, rows + 2, d3, 0)
+def input_grad_kernel(rows, dh0_ref, g1_ref, w_ref, out_ref, d3, wide):
+    stack_rows(dh0_ref, range(rows + 2), d3, 0)
 
     def last_g(row, total):
         wide[row] = one(g1_ref, row).astype(F32) + total
 
-    conv_rows(w_ref[1], d3, rows, last_g)
+    conv_rows(w_ref[1], d3, 0, rows, last_g)
     channels_first(wide, out_ref)
 
 
@@ -323,7 +358,6 @@
     row_flops = 2 * CHAN * 9 * CHAN * width * 4
     grad = jax.ShapeDtypeStruct((STACK, STACK), F32)
     tile = jax.ShapeDtypeStruct((CHAN, rows, width), BF16)
-    token = jax.ShapeDtypeStruct((8, 128), F32)
     wide = pltpu.VMEM((rows, CHAN, width), F32)
     half = (CHAN, 18 * CHAN)
     entry = [pltpu.VMEM((CHAN, rows, width), BF16), pltpu.SemaphoreType.DMA((PIECES,))]
@@ -333,19 +367,24 @@
         entry, 0, "x_rows", place=HBM,
     )
     xnear, xfar = neighbours(x_near, x_far)
+    (weights,) = call(
+        weights_kernel, (kernels,), (jax.ShapeDtypeStruct((8, 2 * CHAN, 4 * STACK), BF16),), [],
+        row_flops, "weights", after=(x_near,),
+    )
+    inner = call(
+        functools.partial(inner_kernel, rows), (x, weights),
+        (shape(rows - 2), shape(rows - 4), shape(rows - 6)),
+        [vmem(rows), vmem(rows - 2), vmem(rows - 4)], 12 * row_flops, "inner",
+    )
     g, g_near, g_far = call(
         functools.partial(entry_kernel, 2), (cotangent,), (shape(rows), shape(2), shape(2)),
-        entry, 0, "g_rows", after=(x_near,), place=HBM,
+        entry, 0, "g_rows", after=(inner[2],), place=HBM,
     )
     gnear, gfar = neighbours(g_near, g_far)
-    (weights,) = call(
-        weights_kernel, (kernels,), (jax.ShapeDtypeStruct((8, 2 * CHAN, 4 * STACK), BF16),), [],
-        row_flops, "weights", after=(g_near,),
-    )
     hid0, x1, hid1 = call(
-        functools.partial(forward_kernel, rows, height), (x, xnear, xfar, weights),
+        functools.partial(forward_kernel, rows, height), (x, xnear, xfar, weights, *inner),
         (shape(rows + 2),) * 3, [vmem(rows + 8), vmem(rows + 6), vmem(rows + 4)],
-        36 * row_flops, "forward",
+        24 * row_flops, "forward",
     )
     g1, g1_near, g1_far, dh1 = call(
         functools.partial(backward1_kernel, rows), (g, gnear, gfar, hid1, weights),
@@ -353,17 +392,22 @@
         [vmem(rows + 4), vmem(rows + 2)], 18 * row_flops, "backward1",
     )
     g1near, g1far = neighbours(g1_near, g1_far)
-    grad10, grad11 = call(
-        functools.partial(grads1_kernel, rows), (g, hid1, dh1, x1), (grad, grad), [vmem(rows)],
-        16 * row_flops, "grads1",
-    )
+    grad01, grad10, grad11 = call(
+        functools.partial(grads1_kernel, rows), (g, hid1, dh1, x1, g1, hid0), (grad,) * 3,
+        [vmem(rows)] * 3, 24 * row_flops, "grads1",
+    )
+    (section_output,) = call(
+        functools.partial(output_kernel, rows), (hid1, x1, weights), (tile,),
+        [vmem(rows + 2), wide], 8 * row_flops, "output", after=(g1_near,),
+    )
+    g1near, g1far, section_output = lax.optimization_barrier((g1near, g1far, section_output))
     dh0, part, send = call(
         functools.partial(backward0_kernel, rows, scale),
-        (g1, g1near, g1far, hid0, x, xnear, xfar, weights, grad10, grad11),
+        (g1, g1near, g1far, hid0, x, xnear, xfar, weights, grad01, grad10, grad11),
         (shape(rows + 2), jax.ShapeDtypeStruct(half, F32), jax.ShapeDtypeStruct(half, BF16)),
         [vmem(rows + 4), vmem(rows + 2), pltpu.VMEM(((rows + 2) * CHAN, width), BF16),
          pltpu.VMEM((2, *half), F32)],
-        26 * row_flops, "backward0",
+        18 * row_flops, "backward0",
     )
 
     part = part + exchange(send, 1, count).astype(F32)
@@ -372,11 +416,7 @@
     send = jnp.where(bit, low, high).astype(BF16)
     part = jnp.where(bit, high, low)
     arrived = exchange(send, 2, count)
-    section_output, mark = call(
-        functools.partial(output_kernel, rows), (hid1, x1, weights), (tile, token),
-        [vmem(rows + 2), wide], 8 * row_flops, "output", after=(send, dh0, g1),
-    )
-    part = part + (arrived.astype(F32) + mark[0, 0])
+    part = part + arrived.astype(F32)
     step = 4
     input_grad = None
     while step < count:
@@ -384,11 +424,12 @@
         masks = [step, 2 * step, 3 * step] if 2 * step < count else [step]
         arrived = [exchange(send, mask, count) for mask in masks]
         if input_grad is None:
-            input_grad, mark = call(
-                functools.partial(input_grad_kernel, rows), (dh0, g1, weights), (tile, token),
+            (input_grad,) = call(
+                functools.partial(input_grad_kernel, rows), (dh0, g1, weights), (tile,),
                 [vmem(rows + 2), wide], 8 * row_flops, "input_grad", after=(send,),
             )
-        own = send.astype(F32) + mark[0, 0]
+            arrived, input_grad = lax.optimization_barrier((arrived, input_grad))
+        own = send.astype(F32)
         arrived = [value.astype(F32) for value in arrived]
         part = own + arrived[0]
         if len(masks) == 3:

time: 75.1 us -> 66.2 us (0.88)
  starting transfers between devices: 35.3 us -> 29.2 us
  local copies, waits for them, and re-layouts: 7.29 us -> 2.2 us
  waiting for transfers between devices: 7.9 us -> 11.1 us
  other arithmetic: 1.44 us -> 0.14 us
    ppermute x10, starting transfers between devices: 33.2 us -> 27 us  [exchange(): return lax.ppermute(value, 'space', [(d, d ^ mask) for d in range(count)])]
    unnamed x20 -> x10, local copies, waits for them, and re-layouts: 6.27 us -> 2.2 us
    ppermute x10, waiting for transfers between devices: 7.89 us -> 11.1 us  [exchange(): return lax.ppermute(value, 'space', [(d, d ^ mask) for d in range(count)])]
    slice x2 -> x0, local copies, waits for them, and re-layouts: 1.02 us -> none  [the longest x1 0.51 us: local(): part = part + (arrived.astype(F32) + mark[0, 0])]
    pallas_call x10 -> x11, Pallas kernels: 21.9 us -> 22.5 us  [call(): pl.pallas_call(kernel, out_shape=outs, in_specs=[ANY] * len(after) + [pla...]
  transfers between devices with their start and end apart: 13 -> 13, of which waited for: 5 -> 5; matrix products, arithmetic and copies ran while one was open for 1% -> 0% of each run, Pallas kernels for 18% -> 22%
where the time goes in v2:
time: 66.2 us; the launch traced here: 66 us
  starting transfers between devices  29.2 us (44%)
  Pallas kernels  22.5 us (34%)
  waiting for transfers between devices  11.1 us (17%)
  local copies, waits for them, and re-layouts  2.2 us (3%)
  between operations  0.81 us (1%)
    ppermute x10, starting transfers between devices, exchange(): return lax.ppermute(value, 'space', [(d, d ^ mask) for d in range(count)])  27 us
    pallas_call x11, Pallas kernels, call(): pl.pallas_call(kernel, out_shape=outs, in_specs=[ANY] * len(after) + [pla...  22.5 us
    ppermute x10, waiting for transfers between devices, exchange(): return lax.ppermute(value, 'space', [(d, d ^ mask) for d in range(count)])  11.1 us
    unnamed x10, local copies, waits for them, and re-layouts  2.2 us
    ppermute x3, starting transfers between devices, neighbours(): return (exchange(near, 1, count), lax.ppermute(far, 'space', beyond))  2.19 us
  transfers between devices with their start and end apart: 13, of which 5 were waited for; matrix products, arithmetic and copies ran while one was open for 0% of the time, Pallas kernels for 22%

profile of v2, /device:TPU:0, one launch (start us, length us, event | category | flops | bytes accessed | tf_op | source)
XLA Modules:
  0.0 66.0 jit_solution(6708216525657870190)
XLA Ops:
  0.6 1.2 %copy-done.1 = bf16[64,8,1024]{2,1,0:T(8,128)(2,1)S(1)} copy-done((bf16[64,8,1024]{2,1,0:T(8,128)(2,1)S(1)}, bf16[64,8,1024]{2,1,0:T(8,128)(2,1)}, u32[]{:S(2)}) %copy-start.1) | copy-done | bytes 1048600
  3.0 0.7 %collective-permute-start.3 = (bf16[256,1024]{1,0:T(8,128)(2,1)S(1)}, bf16[256,1024]{1,0:T(8,128)(2,1)S(1)}, u32[]{:S(2)}, u32[]{:S(2)}) collective-permute-start(bf16[256,1024]{1,0:T(8,128)(2,1)S(1)} %get-tuple-element.38), channel_id=1, source_target_pairs={{1,2},{3,4},{5,6},{7,8},{9,10},{11,12},{13,14},{2,1},{4,3},{6,5},{... | collective-permute-start | bytes 1572872 | tf_op jit(solution)/shard_map/ppermute | solution.py:356
  3.7 1.0 %copy-done.2 = bf16[2,2,64,576]{3,2,1,0:T(8,128)(2,1)S(1)} copy-done((bf16[2,2,64,576]{3,2,1,0:T(8,128)(2,1)S(1)}, bf16[2,2,64,576]{3,2,1,0:T(8,128)(2,1)}, u32[]{:S(2)}) %copy-start.2) | copy-done | bytes 294936
  4.7 0.7 %weights.1.refs_1_.refs_3_.refs_4_.refs_7_ = bf16[8,128,768]{2,1,0:T(8,128)(2,1)S(1)} custom-call(bf16[256,1024]{1,0:T(8,128)(2,1)S(1)} %get-tuple-element.33.refs_0_, bf16[2,2,64,576]{3,2,1,0:T(8,128)(2,1)S(1)} %copy-done.2), custom_call_target="tpu_custom_call" | custom-call | flops 301989888 | bytes 1867776 | tf_op jit(solution)/shard_map/weights/pallas_call | solution.py:28
  5.4 1.7 %inner.1 = (bf16[384,1024]{1,0:T(8,128)(2,1)S(1)}, bf16[256,1024]{1,0:T(8,128)(2,1)S(1)}, bf16[128,1024]{1,0:T(8,128)(2,1)S(1)}) custom-call(bf16[512,1024]{1,0:T(8,128)(2,1)S(1)} %get-tuple-element.32.refs_0_.refs_4_, bf16[8,128,768]{2,1,0:T(8,128)(2,1)S(1)} %weights.1.refs_1_.refs_3_.refs_4_.refs_7_), custom_call_target="tpu_custom_call" | custom-call | flops 3623878656 | bytes 4194304 | tf_op jit(solution)/shard_map/inner/pallas_call | solution.py:28
  7.7 3.9 %collective-permute-start = (bf16[128,1024]{1,0:T(8,128)(2,1)S(1)}, bf16[128,1024]{1,0:T(8,128)(2,1)S(1)}, u32[]{:S(2)}, u32[]{:S(2)}) collective-permute-start(bf16[128,1024]{1,0:T(8,128)(2,1)S(1)} %get-tuple-element.36), channel_id=1, source_target_pairs={{0,1},{1,0},{2,3},{3,2},{4,5},{5,4},{6,7},{7,6},{8,9},{9,8},{10,11... | collective-permute-start | bytes 786440 | tf_op jit(solution)/shard_map/ppermute | solution.py:337
  12.3 3.8 %forward.1 = (bf16[640,1024]{1,0:T(8,128)(2,1)S(1)}, bf16[640,1024]{1,0:T(8,128)(2,1)S(1)}, bf16[640,1024]{1,0:T(8,128)(2,1)S(1)}) custom-call(bf16[512,1024]{1,0:T(8,128)(2,1)S(1)} %get-tuple-element.32.refs_0_.refs_4_, bf16[256,1024]{1,0:T(8,128)(2,1)S(1)} %collective-permute-done.2.refs_1_.refs_5_, ...), custom_call_target="tpu_custom_call" | custom-call | flops 7247757312 | bytes 9175040 | tf_op jit(solution)/shard_map/forward/pallas_call | solution.py:28
  16.2 3.1 %backward1.1 = (bf16[512,1024]{1,0:T(8,128)(2,1)S(1)}, bf16[128,1024]{1,0:T(8,128)(2,1)S(1)}, bf16[128,1024]{1,0:T(8,128)(2,1)S(1)}, bf16[512,1024]{1,0:T(8,128)(2,1)S(1)}) custom-call(bf16[512,1024]{1,0:T(8,128)(2,1)S(1)} %get-tuple-element.35.refs_0_, bf16[128,1024]{1,0:T(8,128)(2,1)S(1)} %collective-permute-done.refs_1_, ...), custom_call_target="tpu_custom_call" | custom-call | flops 5435817984 | bytes 7077888 | tf_op jit(solution)/shard_map/backward1/pallas_call | solution.py:28
  19.3 9.8 %collective-permute-start.4 = (bf16[128,1024]{1,0:T(8,128)(2,1)S(1)}, bf16[128,1024]{1,0:T(8,128)(2,1)S(1)}, u32[]{:S(2)}, u32[]{:S(2)}) collective-permute-start(bf16[128,1024]{1,0:T(8,128)(2,1)S(1)} %get-tuple-element.42.refs_0_), channel_id=1, source_target_pairs={{0,1},{1,0},{2,3},{3,2},{4,5},{5,4},{6,7},{7,6},{8,9},{9,8},{10,11... | collective-permute-start | bytes 786440 | tf_op jit(solution)/shard_map/ppermute | solution.py:337
  29.0 0.8 %collective-permute-start.5 = (bf16[128,1024]{1,0:T(8,128)(2,1)S(1)}, bf16[128,1024]{1,0:T(8,128)(2,1)S(1)}, u32[]{:S(2)}, u32[]{:S(2)}) collective-permute-start(bf16[128,1024]{1,0:T(8,128)(2,1)S(1)} %get-tuple-element.43), channel_id=1, source_target_pairs={{1,2},{3,4},{5,6},{7,8},{9,10},{11,12},{13,14},{2,1},{4,3},{6,5},{... | collective-permute-start | bytes 786440 | tf_op jit(solution)/shard_map/ppermute | solution.py:356
  29.9 2.8 %grads1.1 = (f32[192,192]{1,0:T(8,128)S(1)}, f32[192,192]{1,0:T(8,128)S(1)}, f32[192,192]{1,0:T(8,128)S(1)}) custom-call(bf16[512,1024]{1,0:T(8,128)(2,1)S(1)} %get-tuple-element.35.refs_0_, bf16[640,1024]{1,0:T(8,128)(2,1)S(1)} %get-tuple-element.41.refs_3_.refs_1_, bf16[512,1024]{1,0:T(8,128)(2,1)S(1)} %get-tuple-element.50.refs_2_, ...), custom_call_target="tpu_custom_call" | custom-call | flops 7247757312 | bytes 7520256 | tf_op jit(solution)/shard_map/grads1/pallas_call | solution.py:28
  32.7 2.5 %output.1 = bf16[64,8,1024]{2,1,0:T(8,128)(2,1)} custom-call(bf16[128,1024]{1,0:T(8,128)(2,1)S(1)} %get-tuple-element.42.refs_0_, bf16[640,1024]{1,0:T(8,128)(2,1)S(1)} %get-tuple-element.41.refs_3_.refs_1_, bf16[640,1024]{1,0:T(8,128)(2,1)S(1)} %get-tuple-element.44.refs_2_.refs_3_, bf16[8,128,768]{2,1,0:T(8,128)(2,1)S(1)} %weights.1.refs_1_.refs_3_.refs_4_.refs_7_), custom_call_target="tpu_custom_call" | custom-call | flops 2415919104 | bytes 5242880 | tf_op jit(solution)/shard_map/output/pallas_call | solution.py:28
  35.2 3.1 %backward0.1 = (bf16[640,1024]{1,0:T(8,128)(2,1)S(1)}, f32[64,1152]{1,0:T(8,128)S(1)}, bf16[64,1152]{1,0:T(8,128)(2,1)S(1)}) custom-call(bf16[512,1024]{1,0:T(8,128)(2,1)S(1)} %get-tuple-element.46.refs_4_.refs_0_.refs_2_, bf16[128,1024]{1,0:T(8,128)(2,1)S(1)} %collective-permute-done.4.refs_1_, bf16[128,1024]{1,0:T(8,128)(2,1)S(1)} %collective-permute-done.5.refs_2_, ...), custom_call_target="tpu_custom_call" | custom-call | flops 5435817984 | bytes 8749056 | tf_op jit(solution)/shard_map/backward0/pallas_call | solution.py:28
  38.4 4.4 %collective-permute-start.6 = (bf16[64,1152]{1,0:T(8,128)(2,1)S(1)}, bf16[64,1152]{1,0:T(8,128)(2,1)S(1)}, u32[]{:S(2)}, u32[]{:S(2)}) collective-permute-start(bf16[64,1152]{1,0:T(8,128)(2,1)S(1)} %get-tuple-element.55), channel_id=1, source_target_pairs={{0,1},{1,0},{2,3},{3,2},{4,5},{5,4},{6,7},{7,6},{8,9},{9,8},{10,11... | collective-permute-start | bytes 442376 | tf_op jit(solution)/shard_map/ppermute | solution.py:337
  42.8 1.0 %collective-permute-done.6 = bf16[64,1152]{1,0:T(8,128)(2,1)S(1)} collective-permute-done((bf16[64,1152]{1,0:T(8,128)(2,1)S(1)}, bf16[64,1152]{1,0:T(8,128)(2,1)S(1)}, u32[]{:S(2)}, u32[]{:S(2)}) %collective-permute-start.6) | collective-permute-done | bytes 147488 | tf_op jit(solution)/shard_map/ppermute | solution.py:337
  43.9 2.8 %collective-permute-start.7 = (bf16[32,1152]{1,0:T(8,128)(2,1)S(1)}, bf16[32,1152]{1,0:T(8,128)(2,1)S(1)}, u32[]{:S(2)}, u32[]{:S(2)}) collective-permute-start(bf16[32,1152]{1,0:T(8,128)(2,1)S(1)} %select_convert_fusion), channel_id=1, source_target_pairs={{0,2},{1,3},{2,0},{3,1},{4,6},{5,7},{6,4},{7,5},{8,10},{9,11},{10,... | collective-permute-start | bytes 221192 | tf_op jit(solution)/shard_map/ppermute | solution.py:337
  46.7 2.6 %collective-permute-done.7 = bf16[32,1152]{1,0:T(8,128)(2,1)S(1)} collective-permute-done((bf16[32,1152]{1,0:T(8,128)(2,1)S(1)}, bf16[32,1152]{1,0:T(8,128)(2,1)S(1)}, u32[]{:S(2)}, u32[]{:S(2)}) %collective-permute-start.7) | collective-permute-done | bytes 73760 | tf_op jit(solution)/shard_map/ppermute | solution.py:337
  49.3 4.2 %collective-permute-start.10 = (bf16[32,1152]{1,0:T(8,128)(2,1)S(1)}, bf16[32,1152]{1,0:T(8,128)(2,1)S(1)}, u32[]{:S(2)}, u32[]{:S(2)}) collective-permute-start(bf16[32,1152]{1,0:T(8,128)(2,1)S(1)} %add_convert_fusion.1.refs_0_), channel_id=1, source_target_pairs={{0,12},{1,13},{2,14},{3,15},{4,8},{5,9},{6,10},{7,11},{8,4},{9,5},... | collective-permute-start | bytes 221192 | tf_op jit(solution)/shard_map/ppermute | solution.py:337
  54.1 2.6 %input_grad.1 = bf16[64,8,1024]{2,1,0:T(8,128)(2,1)} custom-call(bf16[32,1152]{1,0:T(8,128)(2,1)S(1)} %add_convert_fusion.1.refs_0_, bf16[640,1024]{1,0:T(8,128)(2,1)S(1)} %get-tuple-element.56.refs_1_, bf16[512,1024]{1,0:T(8,128)(2,1)S(1)} %copy-done.4, bf16[8,128,768]{2,1,0:T(8,128)(2,1)S(1)} %weights.1.refs_1_.refs_3_.refs_4_.refs_7_), custom_call_target="tpu_custom_call" | custom-call | flops 2415919104 | bytes 4980736 | tf_op jit(solution)/shard_map/input_grad/pallas_call | solution.py:28
  56.7 2.4 %collective-permute-done.8 = bf16[32,1152]{1,0:T(8,128)(2,1)S(1)} collective-permute-done((bf16[32,1152]{1,0:T(8,128)(2,1)S(1)}, bf16[32,1152]{1,0:T(8,128)(2,1)S(1)}, u32[]{:S(2)}, u32[]{:S(2)}) %collective-permute-start.8) | collective-permute-done | bytes 73760 | tf_op jit(solution)/shard_map/ppermute | solution.py:337
  59.2 0.7 %collective-permute-start.11 = (bf16[32,1152]{1,0:T(8,128)(2,1)S(1)}, bf16[32,1152]{1,0:T(8,128)(2,1)S(1)}, u32[]{:S(2)}, u32[]{:S(2)}) collective-permute-start(bf16[32,1152]{1,0:T(8,128)(2,1)S(1)} %add_convert_fusion), channel_id=1, source_target_pairs={{0,2},{1,3},{2,0},{3,1},{4,6},{5,7},{6,4},{7,5},{8,10},{9,11},{10,... | collective-permute-start | bytes 221192 | tf_op jit(solution)/shard_map/ppermute | solution.py:337
  59.9 3.7 %collective-permute-done.11 = bf16[32,1152]{1,0:T(8,128)(2,1)S(1)} collective-permute-done((bf16[32,1152]{1,0:T(8,128)(2,1)S(1)}, bf16[32,1152]{1,0:T(8,128)(2,1)S(1)}, u32[]{:S(2)}, u32[]{:S(2)}) %collective-permute-start.11) | collective-permute-done | bytes 73760 | tf_op jit(solution)/shard_map/ppermute | solution.py:337
  63.7 1.4 %collective-permute-done.12.refs_1_ = bf16[64,1152]{1,0:T(8,128)(2,1)S(1)} collective-permute-done((bf16[64,1152]{1,0:T(8,128)(2,1)S(1)}, bf16[64,1152]{1,0:T(8,128)(2,1)S(1)}, u32[]{:S(2)}, u32[]{:S(2)}) %collective-permute-start.12) | collective-permute-done | bytes 147488 | tf_op jit(solution)/shard_map/ppermute | solution.py:337
  65.1 1.0 %gathered.1 = f32[2,2,64,576]{3,2,1,0:T(8,128)} custom-call(bf16[64,1152]{1,0:T(8,128)(2,1)S(1)} %maximum_select_fusion.refs_0_, bf16[64,1152]{1,0:T(8,128)(2,1)S(1)} %collective-permute-done.12.refs_1_), custom_call_target="tpu_custom_call" | custom-call | bytes 884736 | tf_op jit(solution)/shard_map/gathered/pallas_call | solution.py:28
  (28 shorter events, 3.3 us)
Async XLA Ops:
  0.6 1.2 %copy-start.1 = (bf16[64,8,1024]{2,1,0:T(8,128)(2,1)S(1)}, bf16[64,8,1024]{2,1,0:T(8,128)(2,1)}, u32[]{:S(2)}) copy-start(bf16[64,8,1024]{2,1,0:T(8,128)(2,1)} %refs_0_.1) | copy-start | bytes 3145732
  2.5 9.8 %collective-permute-start.2 = (bf16[256,1024]{1,0:T(8,128)(2,1)S(1)}, bf16[256,1024]{1,0:T(8,128)(2,1)S(1)}, u32[]{:S(2)}, u32[]{:S(2)}) collective-permute-start(bf16[256,1024]{1,0:T(8,128)(2,1)S(1)} %get-tuple-element.33.refs_0_), channel_id=1, source_target_pairs={{0,1},{1,0},{2,3},{3,2},{4,5},{5,4},{6,7},{7,6},{8,9},{9,8},{10,11... | collective-permute-start | bytes 1572872 | tf_op jit(solution)/shard_map/ppermute | solution.py:337
  3.0 9.3 %collective-permute-start.3 = (bf16[256,1024]{1,0:T(8,128)(2,1)S(1)}, bf16[256,1024]{1,0:T(8,128)(2,1)S(1)}, u32[]{:S(2)}, u32[]{:S(2)}) collective-permute-start(bf16[256,1024]{1,0:T(8,128)(2,1)S(1)} %get-tuple-element.38), channel_id=1, source_target_pairs={{1,2},{3,4},{5,6},{7,8},{9,10},{11,12},{13,14},{2,1},{4,3},{6,5},{... | collective-permute-start | bytes 1572872 | tf_op jit(solution)/shard_map/ppermute | solution.py:356
  3.7 1.0 %copy-start.2 = (bf16[2,2,64,576]{3,2,1,0:T(8,128)(2,1)S(1)}, bf16[2,2,64,576]{3,2,1,0:T(8,128)(2,1)}, u32[]{:S(2)}) copy-start(bf16[2,2,64,576]{3,2,1,0:T(8,128)(2,1)} %refs_1_.2) | copy-start | bytes 884740
  5.4 1.7 %copy-start = (bf16[64,8,1024]{2,1,0:T(8,128)(2,1)S(1)}, bf16[64,8,1024]{2,1,0:T(8,128)(2,1)}, u32[]{:S(2)}) copy-start(bf16[64,8,1024]{2,1,0:T(8,128)(2,1)} %refs_1_.3) | copy-start | bytes 3145732
  7.7 8.4 %collective-permute-start = (bf16[128,1024]{1,0:T(8,128)(2,1)S(1)}, bf16[128,1024]{1,0:T(8,128)(2,1)S(1)}, u32[]{:S(2)}, u32[]{:S(2)}) collective-permute-start(bf16[128,1024]{1,0:T(8,128)(2,1)S(1)} %get-tuple-element.36), channel_id=1, source_target_pairs={{0,1},{1,0},{2,3},{3,2},{4,5},{5,4},{6,7},{7,6},{8,9},{9,8},{10,11... | collective-permute-start | bytes 786440 | tf_op jit(solution)/shard_map/ppermute | solution.py:337
  11.6 4.6 %collective-permute-start.1 = (bf16[128,1024]{1,0:T(8,128)(2,1)S(1)}, bf16[128,1024]{1,0:T(8,128)(2,1)S(1)}, u32[]{:S(2)}, u32[]{:S(2)}) collective-permute-start(bf16[128,1024]{1,0:T(8,128)(2,1)S(1)} %get-tuple-element.37), channel_id=1, source_target_pairs={{1,2},{3,4},{5,6},{7,8},{9,10},{11,12},{13,14},{2,1},{4,3},{6,5},{... | collective-permute-start | bytes 786440 | tf_op jit(solution)/shard_map/ppermute | solution.py:356
  19.3 15.9 %copy-start.3 = (bf16[512,1024]{1,0:T(8,128)(2,1)}, bf16[512,1024]{1,0:T(8,128)(2,1)S(1)}, u32[]{:S(2)}) copy-start(bf16[512,1024]{1,0:T(8,128)(2,1)S(1)} %get-tuple-element.46.refs_4_.refs_0_.refs_2_) | copy-start | bytes 3145732
  19.3 15.9 %collective-permute-start.4 = (bf16[128,1024]{1,0:T(8,128)(2,1)S(1)}, bf16[128,1024]{1,0:T(8,128)(2,1)S(1)}, u32[]{:S(2)}, u32[]{:S(2)}) collective-permute-start(bf16[128,1024]{1,0:T(8,128)(2,1)S(1)} %get-tuple-element.42.refs_0_), channel_id=1, source_target_pairs={{0,1},{1,0},{2,3},{3,2},{4,5},{5,4},{6,7},{7,6},{8,9},{9,8},{10,11... | collective-permute-start | bytes 786440 | tf_op jit(solution)/shard_map/ppermute | solution.py:337
  29.0 6.2 %collective-permute-start.5 = (bf16[128,1024]{1,0:T(8,128)(2,1)S(1)}, bf16[128,1024]{1,0:T(8,128)(2,1)S(1)}, u32[]{:S(2)}, u32[]{:S(2)}) collective-permute-start(bf16[128,1024]{1,0:T(8,128)(2,1)S(1)} %get-tuple-element.43), channel_id=1, source_target_pairs={{1,2},{3,4},{5,6},{7,8},{9,10},{11,12},{13,14},{2,1},{4,3},{6,5},{... | collective-permute-start | bytes 786440 | tf_op jit(solution)/shard_map/ppermute | solution.py:356
  38.4 5.5 %collective-permute-start.6 = (bf16[64,1152]{1,0:T(8,128)(2,1)S(1)}, bf16[64,1152]{1,0:T(8,128)(2,1)S(1)}, u32[]{:S(2)}, u32[]{:S(2)}) collective-permute-start(bf16[64,1152]{1,0:T(8,128)(2,1)S(1)} %get-tuple-element.55), channel_id=1, source_target_pairs={{0,1},{1,0},{2,3},{3,2},{4,5},{5,4},{6,7},{7,6},{8,9},{9,8},{10,11... | collective-permute-start | bytes 442376 | tf_op jit(solution)/shard_map/ppermute | solution.py:337
  42.8 11.3 %copy-start.4 = (bf16[512,1024]{1,0:T(8,128)(2,1)S(1)}, bf16[512,1024]{1,0:T(8,128)(2,1)}, u32[]{:S(2)}) copy-start(bf16[512,1024]{1,0:T(8,128)(2,1)} %copy-done.3) | copy-start | bytes 3145732
  43.9 5.4 %collective-permute-start.7 = (bf16[32,1152]{1,0:T(8,128)(2,1)S(1)}, bf16[32,1152]{1,0:T(8,128)(2,1)S(1)}, u32[]{:S(2)}, u32[]{:S(2)}) collective-permute-start(bf16[32,1152]{1,0:T(8,128)(2,1)S(1)} %select_convert_fusion), channel_id=1, source_target_pairs={{0,2},{1,3},{2,0},{3,1},{4,6},{5,7},{6,4},{7,5},{8,10},{9,11},{10,... | collective-permute-start | bytes 221192 | tf_op jit(solution)/shard_map/ppermute | solution.py:337
  49.3 7.4 %collective-permute-start.10 = (bf16[32,1152]{1,0:T(8,128)(2,1)S(1)}, bf16[32,1152]{1,0:T(8,128)(2,1)S(1)}, u32[]{:S(2)}, u32[]{:S(2)}) collective-permute-start(bf16[32,1152]{1,0:T(8,128)(2,1)S(1)} %add_convert_fusion.1.refs_0_), channel_id=1, source_target_pairs={{0,12},{1,13},{2,14},{3,15},{4,8},{5,9},{6,10},{7,11},{8,4},{9,5},... | collective-permute-start | bytes 221192 | tf_op jit(solution)/shard_map/ppermute | solution.py:337
  53.5 5.7 %collective-permute-start.8 = (bf16[32,1152]{1,0:T(8,128)(2,1)S(1)}, bf16[32,1152]{1,0:T(8,128)(2,1)S(1)}, u32[]{:S(2)}, u32[]{:S(2)}) collective-permute-start(bf16[32,1152]{1,0:T(8,128)(2,1)S(1)} %add_convert_fusion.1.refs_0_), channel_id=1, source_target_pairs={{0,4},{1,5},{2,6},{3,7},{4,0},{5,1},{6,2},{7,3},{8,12},{9,13},{10,... | collective-permute-start | bytes 221192 | tf_op jit(solution)/shard_map/ppermute | solution.py:337
  53.5 5.7 %collective-permute-start.9 = (bf16[32,1152]{1,0:T(8,128)(2,1)S(1)}, bf16[32,1152]{1,0:T(8,128)(2,1)S(1)}, u32[]{:S(2)}, u32[]{:S(2)}) collective-permute-start(bf16[32,1152]{1,0:T(8,128)(2,1)S(1)} %add_convert_fusion.1.refs_0_), channel_id=1, source_target_pairs={{0,8},{1,9},{2,10},{3,11},{4,12},{5,13},{6,14},{7,15},{8,0},{9,1},... | collective-permute-start | bytes 221192 | tf_op jit(solution)/shard_map/ppermute | solution.py:337
  59.2 4.4 %collective-permute-start.11 = (bf16[32,1152]{1,0:T(8,128)(2,1)S(1)}, bf16[32,1152]{1,0:T(8,128)(2,1)S(1)}, u32[]{:S(2)}, u32[]{:S(2)}) collective-permute-start(bf16[32,1152]{1,0:T(8,128)(2,1)S(1)} %add_convert_fusion), channel_id=1, source_target_pairs={{0,2},{1,3},{2,0},{3,1},{4,6},{5,7},{6,4},{7,5},{8,10},{9,11},{10,... | collective-permute-start | bytes 221192 | tf_op jit(solution)/shard_map/ppermute | solution.py:337
  63.6 1.4 %collective-permute-start.12 = (bf16[64,1152]{1,0:T(8,128)(2,1)S(1)}, bf16[64,1152]{1,0:T(8,128)(2,1)S(1)}, u32[]{:S(2)}, u32[]{:S(2)}) collective-permute-start(bf16[64,1152]{1,0:T(8,128)(2,1)S(1)} %maximum_select_fusion.refs_0_), channel_id=1, source_target_pairs={{0,1},{1,0},{2,3},{3,2},{4,5},{5,4},{6,7},{7,6},{8,9},{9,8},{10,11... | collective-permute-start | bytes 442376 | tf_op jit(solution)/shard_map/ppermute | solution.py:337

commit v3 on v2

--- a/solution.py
+++ b/solution.py
@@ -28,7 +28,7 @@
     return pl.pallas_call(
         kernel,
         out_shape=outs,
-        in_specs=[ANY] * len(after) + [place] * len(operands),
+        in_specs=[ANY] * len(after) + [place] + [VMEM] * (len(operands) - 1),
         out_specs=[VMEM] * len(outs),
         scratch_shapes=scratch,
         compiler_params=pltpu.CompilerParams(vmem_limit_bytes=nbytes + held + (6 << 20)),
@@ -61,6 +61,19 @@
 def stack_rows(ref, rows, target, at):
     for row in rows:
         put(target, row + at, one(ref, row))
+
+
+def g_entry_kernel(
+    edge, tile_ref, w_ref, rows_ref, near_ref, far_ref, inner_ref, held, g3, arrived
+):
+    entry_kernel(edge, tile_ref, rows_ref, near_ref, far_ref, held, arrived)
+    rows = tile_ref.shape[1]
+    stack_rows(rows_ref, range(rows), g3, 0)
+
+    def keep(row, total):
+        inner_ref[row * CHAN : (row + 1) * CHAN, :] = total
+
+    conv_rows(w_ref[7], g3, 0, rows - 2, keep)
 
 
 def copy_rows(ref, count, target, at):
@@ -239,36 +252,60 @@
 
 
 def backward1_kernel(
-    rows, g_ref, near_ref, far_ref, hid1_ref, w_ref, g1_ref, next_near, next_far, dh1_ref, g3, d3,
+    rows, g_ref, near_ref, far_ref, hid1_ref, inner_ref, w_ref, next_near, next_far, edges_ref, dh1_ref,
+    g3, d3,
 ):
-    stack_rows(g_ref, range(rows), g3, 2)
     halo_rows(near_ref, far_ref, 2, rows, g3)
+    stack_rows(g_ref, (0, 1, rows - 2, rows - 1), g3, 2)
 
     def dhidden1(row, total):
         value = jnp.where(one(hid1_ref, row) > 0, total, 0.0).astype(BF16)
-        put(d3, row, value)
-        if 1 <= row < rows + 1:
-            dh1_ref[(row - 1) * CHAN : row * CHAN, :] = value
-
-    conv_rows(w_ref[7], g3, 0, rows + 2, dhidden1)
+        dh1_ref[row * CHAN : (row + 1) * CHAN, :] = value
+        if row < 4 or row >= rows - 2:
+            put(d3, row, value)
+
+    for row in range(2, rows):
+        dhidden1(row, one(inner_ref, row - 2))
+    for at in (0, rows):
+        conv_rows(w_ref[7], g3, at, 2, dhidden1)
+
+    def next_g(row, total):
+        value = (one(g_ref, row).astype(F32) + total).astype(BF16)
+        at = row if row < 2 else row - (rows - 4)
+        edges_ref[at * CHAN : (at + 1) * CHAN, :] = value
+
+    for at in (0, rows - 2):
+        conv_rows(w_ref[5], d3, at, 2, next_g)
+    send_edges(edges_ref, 2, next_near, next_far)
+
+
+def middle_kernel(
+    rows, g_ref, edges_ref, hid1_ref, dh1_ref, x1_ref, hid0_ref, x_ref, w_ref,
+    g1_ref, dh0_ref, grad00, grad01, grad10, grad11, s3, t3, u3, v3,
+):
+    stack_rows(dh1_ref, range(rows + 2), t3, 0)
+    copy_rows(edges_ref, 2, g1_ref, 0)
+    g1_ref[(rows - 2) * CHAN :, :] = edges_ref[2 * CHAN :, :]
 
     def next_g(row, total):
         value = (one(g_ref, row).astype(F32) + total).astype(BF16)
         g1_ref[row * CHAN : (row + 1) * CHAN, :] = value
-
-    conv_rows(w_ref[5], d3, 0, rows, next_g)
-    send_edges(g1_ref, 2, next_near, next_far)
-
-
-def grads1_kernel(
-    rows, g_ref, hid1_ref, dh1_ref, x1_ref, g1_ref, hid0_ref, grad01, grad10, grad11, s3, t3, u3
-):
+        put(u3, row, value)
+
+    conv_rows(w_ref[5], t3, 2, rows - 4, next_g)
+    stack_rows(g1_ref, (0, 1, rows - 2, rows - 1), u3, 0)
+
+    def dhidden0(row, total):
+        value = jnp.where(one(hid0_ref, row + 2) > 0, total, 0.0).astype(BF16)
+        dh0_ref[row * CHAN : (row + 1) * CHAN, :] = value
+        put(v3, row, value)
+
+    conv_rows(w_ref[3], u3, 0, rows - 2, dhidden0)
     stack_rows(g_ref, range(rows), s3, 0)
     grad11[...] = grad_rows(s3, 0, hid1_ref, 0, rows)
-    stack_rows(dh1_ref, range(rows), t3, 0)
-    grad10[...] = grad_rows(t3, 0, x1_ref, 0, rows)
-    stack_rows(g1_ref, range(rows), u3, 0)
+    grad10[...] = grad_rows(t3, 1, x1_ref, 0, rows)
     grad01[...] = grad_rows(u3, 0, hid0_ref, 0, rows)
+    grad00[...] = grad_rows(v3, 0, x_ref, 0, rows - 2)
 
 
 def output_kernel(rows, hid1_ref, x1_ref, w_ref, out_ref, k3, wide):
@@ -282,26 +319,39 @@
 
 
 def backward0_kernel(
-    rows, scale, g1_ref, near_ref, far_ref, hid0_ref, x_ref, xnear_ref, xfar_ref, w_ref, grad01, grad10, grad11,
-    dh0_ref, keep_ref, send_ref, g3, d3, xs, both,
+    rows, scale, g1_ref, near_ref, far_ref, hid0_ref, x_ref, xnear_ref, xfar_ref, w_ref, dh0_in,
+    inner00, grad01, grad10, grad11, dh0_ref, keep_ref, send_ref, g3, d3, xs, both,
 ):
-    stack_rows(g1_ref, range(rows), g3, 2)
     halo_rows(near_ref, far_ref, 2, rows, g3)
+    stack_rows(g1_ref, (0, 1, rows - 2, rows - 1), g3, 2)
+    copy_rows(dh0_in, rows - 2, dh0_ref, 2)
 
     def dhidden0(row, total):
         value = jnp.where(one(hid0_ref, row) > 0, total, 0.0).astype(BF16)
         dh0_ref[row * CHAN : (row + 1) * CHAN, :] = value
-        put(d3, row, value)
-
-    conv_rows(w_ref[3], g3, 0, rows + 2, dhidden0)
+        if row == 1:
+            put(d3, 0, value)
+        if row == rows:
+            put(d3, 1, value)
+
+    for at in (0, rows):
+        conv_rows(w_ref[3], g3, at, 2, dhidden0)
     odd = odd_place()
-    xs[CHAN : (rows + 1) * CHAN, :] = x_ref[...]
-    near_at, far_at = jnp.where(odd, 0, rows + 1), jnp.where(odd, rows + 1, 0)
+    copy_rows(x_ref, 2, xs, 1)
+    xs[3 * CHAN : 5 * CHAN, :] = x_ref[(rows - 2) * CHAN :, :]
+    near_at, far_at = jnp.where(odd, 0, 5), jnp.where(odd, 5, 0)
     near_row, far_row = jnp.where(odd, 3, 0), jnp.where(odd, 0, 3)
     for ref, at, row in ((xnear_ref, near_at, near_row), (xfar_ref, far_at, far_row)):
         source = pl.ds(pl.multiple_of(row * CHAN, CHAN), CHAN)
         xs[pl.ds(pl.multiple_of(at * CHAN, CHAN), CHAN), :] = ref[source, :]
-    grad00 = grad_rows(d3, 1, xs, 0, rows)
+    grad00 = inner00[...]
+    for end in range(2):
+        grad00 = grad00 + lax.dot_general(
+            d3[end * STACK : (end + 1) * STACK, :],
+            xs[end * STACK : (end + 1) * STACK, :],
+            (((1,), (1,)), ((), ())),
+            preferred_element_type=F32,
+        )
     pairs = ((grad00, grad01[...]), (grad10[...], grad11[...]))
     for section, pair in enumerate(pairs):
         for which, value in enumerate(pair):
@@ -376,9 +426,10 @@
         (shape(rows - 2), shape(rows - 4), shape(rows - 6)),
         [vmem(rows), vmem(rows - 2), vmem(rows - 4)], 12 * row_flops, "inner",
     )
-    g, g_near, g_far = call(
-        functools.partial(entry_kernel, 2), (cotangent,), (shape(rows), shape(2), shape(2)),
-        entry, 0, "g_rows", after=(inner[2],), place=HBM,
+    g, g_near, g_far, g_inner = call(
+        functools.partial(g_entry_kernel, 2), (cotangent, weights),
+        (shape(rows), shape(2), shape(2), shape(rows - 2, F32)),
+        [entry[0], vmem(rows), entry[1]], 6 * row_flops, "g_rows", after=(inner[2],), place=HBM,
     )
     gnear, gfar = neighbours(g_near, g_far)
     hid0, x1, hid1 = call(
@@ -386,28 +437,29 @@
         (shape(rows + 2),) * 3, [vmem(rows + 8), vmem(rows + 6), vmem(rows + 4)],
         24 * row_flops, "forward",
     )
-    g1, g1_near, g1_far, dh1 = call(
-        functools.partial(backward1_kernel, rows), (g, gnear, gfar, hid1, weights),
-        (shape(rows), shape(2), shape(2), shape(rows)),
-        [vmem(rows + 4), vmem(rows + 2)], 18 * row_flops, "backward1",
+    g1_near, g1_far, edges, dh1 = call(
+        functools.partial(backward1_kernel, rows), (g, gnear, gfar, hid1, g_inner, weights),
+        (shape(2), shape(2), shape(4), shape(rows + 2)),
+        [vmem(rows + 4), vmem(rows + 2)], 8 * row_flops, "backward1",
     )
     g1near, g1far = neighbours(g1_near, g1_far)
-    grad01, grad10, grad11 = call(
-        functools.partial(grads1_kernel, rows), (g, hid1, dh1, x1, g1, hid0), (grad,) * 3,
-        [vmem(rows)] * 3, 24 * row_flops, "grads1",
+    g1, dh0_inner, *grads = call(
+        functools.partial(middle_kernel, rows), (g, edges, hid1, dh1, x1, hid0, x, weights),
+        (shape(rows), shape(rows - 2)) + (grad,) * 4,
+        [vmem(rows), vmem(rows + 2), vmem(rows), vmem(rows - 2)], 40 * row_flops, "middle",
     )
     (section_output,) = call(
         functools.partial(output_kernel, rows), (hid1, x1, weights), (tile,),
-        [vmem(rows + 2), wide], 8 * row_flops, "output", after=(g1_near,),
+        [vmem(rows + 2), wide], 8 * row_flops, "output", after=(dh0_inner,),
     )
     g1near, g1far, section_output = lax.optimization_barrier((g1near, g1far, section_output))
     dh0, part, send = call(
         functools.partial(backward0_kernel, rows, scale),
-        (g1, g1near, g1far, hid0, x, xnear, xfar, weights, grad01, grad10, grad11),
+        (g1, g1near, g1far, hid0, x, xnear, xfar, weights, dh0_inner, *grads),
         (shape(rows + 2), jax.ShapeDtypeStruct(half, F32), jax.ShapeDtypeStruct(half, BF16)),
-        [vmem(rows + 4), vmem(rows + 2), pltpu.VMEM(((rows + 2) * CHAN, width), BF16),
+        [vmem(rows + 4), vmem(2), pltpu.VMEM((6 * CHAN, width), BF16),
          pltpu.VMEM((2, *half), F32)],
-        18 * row_flops, "backward0",
+        8 * row_flops, "backward0",
     )
 
     part = part + exchange(send, 1, count).astype(F32)

time: 66.2 us -> 65.4 us (0.988)
  starting transfers between devices: 29.2 us -> 27.2 us
  Pallas kernels: 22.5 us -> 23.3 us
    ppermute x10, starting transfers between devices: 27 us -> 25 us  [exchange(): return lax.ppermute(value, 'space', [(d, d ^ mask) for d in range(count)])]
    pallas_call x11, Pallas kernels: 22.5 us -> 23.3 us  [call(): pl.pallas_call(kernel, out_shape=outs, in_specs=[ANY] * len(after) + [pla...]
  transfers between devices with their start and end apart: 13 -> 13, of which waited for: 5 -> 6; matrix products, arithmetic and copies ran while one was open for 0% -> 0% of each run, Pallas kernels for 22% -> 27%
where the time goes in v3:
time: 65.4 us; the launch traced here: 65.2 us
  starting transfers between devices  27.2 us (42%)
  Pallas kernels  23.3 us (36%)
  waiting for transfers between devices  11.5 us (18%)
  local copies, waits for them, and re-layouts  2.2 us (3%)
  between operations  0.81 us (1%)
    ppermute x10, starting transfers between devices, exchange(): return lax.ppermute(value, 'space', [(d, d ^ mask) for d in range(count)])  25 us
    pallas_call x11, Pallas kernels, call(): pl.pallas_call(kernel, out_shape=outs, in_specs=[ANY] * len(after) + [pla...  23.3 us
    ppermute x10, waiting for transfers between devices, exchange(): return lax.ppermute(value, 'space', [(d, d ^ mask) for d in range(count)])  11.5 us
    unnamed x10, local copies, waits for them, and re-layouts  2.2 us
    ppermute x3, starting transfers between devices, neighbours(): return (exchange(near, 1, count), lax.ppermute(far, 'space', beyond))  2.19 us
  transfers between devices with their start and end apart: 13, of which 6 were waited for; matrix products, arithmetic and copies ran while one was open for 0% of the time, Pallas kernels for 27%

profile of v3, /device:TPU:0, one launch (start us, length us, event | category | flops | bytes accessed | tf_op | source)
XLA Modules:
  0.0 65.2 jit_solution(16651909066046226064)
XLA Ops:
  0.6 1.2 %copy-done = bf16[64,8,1024]{2,1,0:T(8,128)(2,1)S(1)} copy-done((bf16[64,8,1024]{2,1,0:T(8,128)(2,1)S(1)}, bf16[64,8,1024]{2,1,0:T(8,128)(2,1)}, u32[]{:S(2)}) %copy-start) | copy-done | bytes 1048600
  3.7 1.0 %copy-done.1 = bf16[2,2,64,576]{3,2,1,0:T(8,128)(2,1)S(1)} copy-done((bf16[2,2,64,576]{3,2,1,0:T(8,128)(2,1)S(1)}, bf16[2,2,64,576]{3,2,1,0:T(8,128)(2,1)}, u32[]{:S(2)}) %copy-start.1) | copy-done | bytes 294936
  5.4 1.7 %inner.1 = (bf16[384,1024]{1,0:T(8,128)(2,1)S(1)}, bf16[256,1024]{1,0:T(8,128)(2,1)S(1)}, bf16[128,1024]{1,0:T(8,128)(2,1)S(1)}) custom-call(bf16[512,1024]{1,0:T(8,128)(2,1)S(1)} %get-tuple-element.36.refs_0_.refs_6_.refs_4_, bf16[8,128,768]{2,1,0:T(8,128)(2,1)S(1)} %weights.1.refs_1_.refs_2_.refs_3_.refs_5_.refs_7_), custom_call_target="tpu_custom_call" | custom-call | flops 3623878656 | bytes 4194304 | tf_op jit(solution)/shard_map/inner/pallas_call | solution.py:28
  7.1 1.6 %g_rows.1 = (bf16[512,1024]{1,0:T(8,128)(2,1)S(1)}, bf16[128,1024]{1,0:T(8,128)(2,1)S(1)}, bf16[128,1024]{1,0:T(8,128)(2,1)S(1)}, f32[384,1024]{1,0:T(8,128)S(1)}) custom-call(bf16[128,1024]{1,0:T(8,128)(2,1)S(1)} %get-tuple-element.38.refs_0_.refs_6_, bf16[64,8,1024]{2,1,0:T(8,128)(2,1)S(1)} %copy-done.2, ...), custom_call_target="tpu_custom_call" | custom-call | flops 1811939328 | bytes 5767168 | tf_op jit(solution)/shard_map/g_rows/pallas_call | solution.py:28
  8.7 3.9 %collective-permute-start = (bf16[128,1024]{1,0:T(8,128)(2,1)S(1)}, bf16[128,1024]{1,0:T(8,128)(2,1)S(1)}, u32[]{:S(2)}, u32[]{:S(2)}) collective-permute-start(bf16[128,1024]{1,0:T(8,128)(2,1)S(1)} %get-tuple-element.40), channel_id=1, source_target_pairs={{0,1},{1,0},{2,3},{3,2},{4,5},{5,4},{6,7},{7,6},{8,9},{9,8},{10,11... | collective-permute-start | bytes 786440 | tf_op jit(solution)/shard_map/ppermute | solution.py:387
  13.3 3.8 %forward.1 = (bf16[640,1024]{1,0:T(8,128)(2,1)S(1)}, bf16[640,1024]{1,0:T(8,128)(2,1)S(1)}, bf16[640,1024]{1,0:T(8,128)(2,1)S(1)}) custom-call(bf16[512,1024]{1,0:T(8,128)(2,1)S(1)} %get-tuple-element.36.refs_0_.refs_6_.refs_4_, bf16[256,1024]{1,0:T(8,128)(2,1)S(1)} %collective-permute-done.2.refs_1_.refs_5_, ...), custom_call_target="tpu_custom_call" | custom-call | flops 7247757312 | bytes 9175040 | tf_op jit(solution)/shard_map/forward/pallas_call | solution.py:28
  17.1 2.3 %backward1.1 = (bf16[128,1024]{1,0:T(8,128)(2,1)S(1)}, bf16[128,1024]{1,0:T(8,128)(2,1)S(1)}, bf16[256,1024]{1,0:T(8,128)(2,1)S(1)}, bf16[640,1024]{1,0:T(8,128)(2,1)S(1)}) custom-call(bf16[512,1024]{1,0:T(8,128)(2,1)S(1)} %get-tuple-element.39.refs_0_, bf16[128,1024]{1,0:T(8,128)(2,1)S(1)} %collective-permute-done.refs_1_, ...), custom_call_target="tpu_custom_call" | custom-call | flops 2415919104 | bytes 8388608 | tf_op jit(solution)/shard_map/backward1/pallas_call | solution.py:28
  19.4 8.8 %collective-permute-start.4 = (bf16[128,1024]{1,0:T(8,128)(2,1)S(1)}, bf16[128,1024]{1,0:T(8,128)(2,1)S(1)}, u32[]{:S(2)}, u32[]{:S(2)}) collective-permute-start(bf16[128,1024]{1,0:T(8,128)(2,1)S(1)} %get-tuple-element.47), channel_id=1, source_target_pairs={{0,1},{1,0},{2,3},{3,2},{4,5},{5,4},{6,7},{7,6},{8,9},{9,8},{10,11... | collective-permute-start | bytes 786440 | tf_op jit(solution)/shard_map/ppermute | solution.py:387
  29.1 4.8 %middle.1 = (bf16[512,1024]{1,0:T(8,128)(2,1)S(1)}, bf16[384,1024]{1,0:T(8,128)(2,1)S(1)}, f32[192,192]{1,0:T(8,128)S(1)}, f32[192,192]{1,0:T(8,128)S(1)}, f32[1...) custom-call(bf16[512,1024]{1,0:T(8,128)(2,1)S(1)} %get-tuple-element.39.refs_0_, ...), custom_call_target="tpu_custom_call" | custom-call | flops 12079595520 | bytes 11862016 | tf_op jit(solution)/shard_map/middle/pallas_call | solution.py:28
  34.0 2.5 %output.1 = bf16[64,8,1024]{2,1,0:T(8,128)(2,1)} custom-call(bf16[384,1024]{1,0:T(8,128)(2,1)S(1)} %get-tuple-element.53.refs_0_.refs_8_, bf16[640,1024]{1,0:T(8,128)(2,1)S(1)} %get-tuple-element.45.refs_3_.refs_2_.refs_1_, bf16[640,1024]{1,0:T(8,128)(2,1)S(1)} %get-tuple-element.51.refs_4_.refs_2_, ...), custom_call_target="tpu_custom_call" | custom-call | flops 2415919104 | bytes 5242880 | tf_op jit(solution)/shard_map/output/pallas_call | solution.py:28
  36.5 1.7 %backward0.1 = (bf16[640,1024]{1,0:T(8,128)(2,1)S(1)}, f32[64,1152]{1,0:T(8,128)S(1)}, bf16[64,1152]{1,0:T(8,128)(2,1)S(1)}) custom-call(bf16[512,1024]{1,0:T(8,128)(2,1)S(1)} %get-tuple-element.55.refs_0_.refs_2_, bf16[128,1024]{1,0:T(8,128)(2,1)S(1)} %collective-permute-done.4.refs_1_, bf16[128,1024]{1,0:T(8,128)(2,1)S(1)} %collective-permute-done.5.refs_2_, ...), custom_call_target="tpu_custom_call" | custom-call | flops 2415919104 | bytes 9682944 | tf_op jit(solution)/shard_map/backward0/pallas_call | solution.py:28
  38.2 3.8 %collective-permute-start.6 = (bf16[64,1152]{1,0:T(8,128)(2,1)S(1)}, bf16[64,1152]{1,0:T(8,128)(2,1)S(1)}, u32[]{:S(2)}, u32[]{:S(2)}) collective-permute-start(bf16[64,1152]{1,0:T(8,128)(2,1)S(1)} %get-tuple-element.63), channel_id=1, source_target_pairs={{0,1},{1,0},{2,3},{3,2},{4,5},{5,4},{6,7},{7,6},{8,9},{9,8},{10,11... | collective-permute-start | bytes 442376 | tf_op jit(solution)/shard_map/ppermute | solution.py:387
  42.0 1.0 %collective-permute-done.6 = bf16[64,1152]{1,0:T(8,128)(2,1)S(1)} collective-permute-done((bf16[64,1152]{1,0:T(8,128)(2,1)S(1)}, bf16[64,1152]{1,0:T(8,128)(2,1)S(1)}, u32[]{:S(2)}, u32[]{:S(2)}) %collective-permute-start.6) | collective-permute-done | bytes 147488 | tf_op jit(solution)/shard_map/ppermute | solution.py:387
  43.1 2.0 %collective-permute-start.7 = (bf16[32,1152]{1,0:T(8,128)(2,1)S(1)}, bf16[32,1152]{1,0:T(8,128)(2,1)S(1)}, u32[]{:S(2)}, u32[]{:S(2)}) collective-permute-start(bf16[32,1152]{1,0:T(8,128)(2,1)S(1)} %select_convert_fusion), channel_id=1, source_target_pairs={{0,2},{1,3},{2,0},{3,1},{4,6},{5,7},{6,4},{7,5},{8,10},{9,11},{10,... | collective-permute-start | bytes 221192 | tf_op jit(solution)/shard_map/ppermute | solution.py:387
  45.1 2.8 %collective-permute-done.7 = bf16[32,1152]{1,0:T(8,128)(2,1)S(1)} collective-permute-done((bf16[32,1152]{1,0:T(8,128)(2,1)S(1)}, bf16[32,1152]{1,0:T(8,128)(2,1)S(1)}, u32[]{:S(2)}, u32[]{:S(2)}) %collective-permute-start.7) | collective-permute-done | bytes 73760 | tf_op jit(solution)/shard_map/ppermute | solution.py:387
  47.9 1.6 %collective-permute-start.8 = (bf16[32,1152]{1,0:T(8,128)(2,1)S(1)}, bf16[32,1152]{1,0:T(8,128)(2,1)S(1)}, u32[]{:S(2)}, u32[]{:S(2)}) collective-permute-start(bf16[32,1152]{1,0:T(8,128)(2,1)S(1)} %add_convert_fusion.1.refs_0_), channel_id=1, source_target_pairs={{0,4},{1,5},{2,6},{3,7},{4,0},{5,1},{6,2},{7,3},{8,12},{9,13},{10,... | collective-permute-start | bytes 221192 | tf_op jit(solution)/shard_map/ppermute | solution.py:387
  49.6 2.4 %collective-permute-start.9 = (bf16[32,1152]{1,0:T(8,128)(2,1)S(1)}, bf16[32,1152]{1,0:T(8,128)(2,1)S(1)}, u32[]{:S(2)}, u32[]{:S(2)}) collective-permute-start(bf16[32,1152]{1,0:T(8,128)(2,1)S(1)} %add_convert_fusion.1.refs_0_), channel_id=1, source_target_pairs={{0,8},{1,9},{2,10},{3,11},{4,12},{5,13},{6,14},{7,15},{8,0},{9,1},... | collective-permute-start | bytes 221192 | tf_op jit(solution)/shard_map/ppermute | solution.py:387
  52.4 2.6 %input_grad.1 = bf16[64,8,1024]{2,1,0:T(8,128)(2,1)} custom-call(bf16[32,1152]{1,0:T(8,128)(2,1)S(1)} %add_convert_fusion.1.refs_0_, bf16[640,1024]{1,0:T(8,128)(2,1)S(1)} %get-tuple-element.64.refs_1_, bf16[512,1024]{1,0:T(8,128)(2,1)S(1)} %copy-done.4, bf16[8,128,768]{2,1,0:T(8,128)(2,1)S(1)} %weights.1.refs_1_.refs_2_.refs_3_.refs_5_.refs_7_), custom_call_target="tpu_custom_call" | custom-call | flops 2415919104 | bytes 4980736 | tf_op jit(solution)/shard_map/input_grad/pallas_call | solution.py:28
  55.0 2.1 %collective-permute-done.9 = bf16[32,1152]{1,0:T(8,128)(2,1)S(1)} collective-permute-done((bf16[32,1152]{1,0:T(8,128)(2,1)S(1)}, bf16[32,1152]{1,0:T(8,128)(2,1)S(1)}, u32[]{:S(2)}, u32[]{:S(2)}) %collective-permute-start.9) | collective-permute-done | bytes 73760 | tf_op jit(solution)/shard_map/ppermute | solution.py:387
  57.0 1.2 %collective-permute-done.10 = bf16[32,1152]{1,0:T(8,128)(2,1)S(1)} collective-permute-done((bf16[32,1152]{1,0:T(8,128)(2,1)S(1)}, bf16[32,1152]{1,0:T(8,128)(2,1)S(1)}, u32[]{:S(2)}, u32[]{:S(2)}) %collective-permute-start.10) | collective-permute-done | bytes 73760 | tf_op jit(solution)/shard_map/ppermute | solution.py:387
  58.3 1.4 %collective-permute-start.11 = (bf16[32,1152]{1,0:T(8,128)(2,1)S(1)}, bf16[32,1152]{1,0:T(8,128)(2,1)S(1)}, u32[]{:S(2)}, u32[]{:S(2)}) collective-permute-start(bf16[32,1152]{1,0:T(8,128)(2,1)S(1)} %add_convert_fusion), channel_id=1, source_target_pairs={{0,2},{1,3},{2,0},{3,1},{4,6},{5,7},{6,4},{7,5},{8,10},{9,11},{10,... | collective-permute-start | bytes 221192 | tf_op jit(solution)/shard_map/ppermute | solution.py:387
  59.7 3.0 %collective-permute-done.11 = bf16[32,1152]{1,0:T(8,128)(2,1)S(1)} collective-permute-done((bf16[32,1152]{1,0:T(8,128)(2,1)S(1)}, bf16[32,1152]{1,0:T(8,128)(2,1)S(1)}, u32[]{:S(2)}, u32[]{:S(2)}) %collective-permute-start.11) | collective-permute-done | bytes 73760 | tf_op jit(solution)/shard_map/ppermute | solution.py:387
  62.9 1.4 %collective-permute-done.12.refs_1_ = bf16[64,1152]{1,0:T(8,128)(2,1)S(1)} collective-permute-done((bf16[64,1152]{1,0:T(8,128)(2,1)S(1)}, bf16[64,1152]{1,0:T(8,128)(2,1)S(1)}, u32[]{:S(2)}, u32[]{:S(2)}) %collective-permute-start.12) | collective-permute-done | bytes 147488 | tf_op jit(solution)/shard_map/ppermute | solution.py:387
  64.2 1.0 %gathered.1 = f32[2,2,64,576]{3,2,1,0:T(8,128)} custom-call(bf16[64,1152]{1,0:T(8,128)(2,1)S(1)} %maximum_select_fusion.refs_0_, bf16[64,1152]{1,0:T(8,128)(2,1)S(1)} %collective-permute-done.12.refs_1_), custom_call_target="tpu_custom_call" | custom-call | bytes 884736 | tf_op jit(solution)/shard_map/gathered/pallas_call | solution.py:28
  (28 shorter events, 4.7 us)
Async XLA Ops:
  0.6 1.2 %copy-start = (bf16[64,8,1024]{2,1,0:T(8,128)(2,1)S(1)}, bf16[64,8,1024]{2,1,0:T(8,128)(2,1)}, u32[]{:S(2)}) copy-start(bf16[64,8,1024]{2,1,0:T(8,128)(2,1)} %refs_0_.1) | copy-start | bytes 3145732
  2.5 10.7 %collective-permute-start.2 = (bf16[256,1024]{1,0:T(8,128)(2,1)S(1)}, bf16[256,1024]{1,0:T(8,128)(2,1)S(1)}, u32[]{:S(2)}, u32[]{:S(2)}) collective-permute-start(bf16[256,1024]{1,0:T(8,128)(2,1)S(1)} %get-tuple-element.37.refs_0_), channel_id=1, source_target_pairs={{0,1},{1,0},{2,3},{3,2},{4,5},{5,4},{6,7},{7,6},{8,9},{9,8},{10,11... | collective-permute-start | bytes 1572872 | tf_op jit(solution)/shard_map/ppermute | solution.py:387
  3.0 10.2 %collective-permute-start.3 = (bf16[256,1024]{1,0:T(8,128)(2,1)S(1)}, bf16[256,1024]{1,0:T(8,128)(2,1)S(1)}, u32[]{:S(2)}, u32[]{:S(2)}) collective-permute-start(bf16[256,1024]{1,0:T(8,128)(2,1)S(1)} %get-tuple-element.42), channel_id=1, source_target_pairs={{1,2},{3,4},{5,6},{7,8},{9,10},{11,12},{13,14},{2,1},{4,3},{6,5},{... | collective-permute-start | bytes 1572872 | tf_op jit(solution)/shard_map/ppermute | solution.py:406
  3.7 1.0 %copy-start.1 = (bf16[2,2,64,576]{3,2,1,0:T(8,128)(2,1)S(1)}, bf16[2,2,64,576]{3,2,1,0:T(8,128)(2,1)}, u32[]{:S(2)}) copy-start(bf16[2,2,64,576]{3,2,1,0:T(8,128)(2,1)} %refs_1_.2) | copy-start | bytes 884740
  5.4 1.7 %copy-start.2 = (bf16[64,8,1024]{2,1,0:T(8,128)(2,1)S(1)}, bf16[64,8,1024]{2,1,0:T(8,128)(2,1)}, u32[]{:S(2)}) copy-start(bf16[64,8,1024]{2,1,0:T(8,128)(2,1)} %refs_1_.3) | copy-start | bytes 3145732
  8.7 8.5 %collective-permute-start = (bf16[128,1024]{1,0:T(8,128)(2,1)S(1)}, bf16[128,1024]{1,0:T(8,128)(2,1)S(1)}, u32[]{:S(2)}, u32[]{:S(2)}) collective-permute-start(bf16[128,1024]{1,0:T(8,128)(2,1)S(1)} %get-tuple-element.40), channel_id=1, source_target_pairs={{0,1},{1,0},{2,3},{3,2},{4,5},{5,4},{6,7},{7,6},{8,9},{9,8},{10,11... | collective-permute-start | bytes 786440 | tf_op jit(solution)/shard_map/ppermute | solution.py:387
  12.6 4.6 %collective-permute-start.1 = (bf16[128,1024]{1,0:T(8,128)(2,1)S(1)}, bf16[128,1024]{1,0:T(8,128)(2,1)S(1)}, u32[]{:S(2)}, u32[]{:S(2)}) collective-permute-start(bf16[128,1024]{1,0:T(8,128)(2,1)S(1)} %get-tuple-element.41), channel_id=1, source_target_pairs={{1,2},{3,4},{5,6},{7,8},{9,10},{11,12},{13,14},{2,1},{4,3},{6,5},{... | collective-permute-start | bytes 786440 | tf_op jit(solution)/shard_map/ppermute | solution.py:406
  19.4 17.0 %collective-permute-start.4 = (bf16[128,1024]{1,0:T(8,128)(2,1)S(1)}, bf16[128,1024]{1,0:T(8,128)(2,1)S(1)}, u32[]{:S(2)}, u32[]{:S(2)}) collective-permute-start(bf16[128,1024]{1,0:T(8,128)(2,1)S(1)} %get-tuple-element.47), channel_id=1, source_target_pairs={{0,1},{1,0},{2,3},{3,2},{4,5},{5,4},{6,7},{7,6},{8,9},{9,8},{10,11... | collective-permute-start | bytes 786440 | tf_op jit(solution)/shard_map/ppermute | solution.py:387
  28.2 8.2 %collective-permute-start.5 = (bf16[128,1024]{1,0:T(8,128)(2,1)S(1)}, bf16[128,1024]{1,0:T(8,128)(2,1)S(1)}, u32[]{:S(2)}, u32[]{:S(2)}) collective-permute-start(bf16[128,1024]{1,0:T(8,128)(2,1)S(1)} %get-tuple-element.48), channel_id=1, source_target_pairs={{1,2},{3,4},{5,6},{7,8},{9,10},{11,12},{13,14},{2,1},{4,3},{6,5},{... | collective-permute-start | bytes 786440 | tf_op jit(solution)/shard_map/ppermute | solution.py:406
  33.9 2.5 %copy-start.3 = (bf16[512,1024]{1,0:T(8,128)(2,1)}, bf16[512,1024]{1,0:T(8,128)(2,1)S(1)}, u32[]{:S(2)}) copy-start(bf16[512,1024]{1,0:T(8,128)(2,1)S(1)} %get-tuple-element.55.refs_0_.refs_2_) | copy-start | bytes 3145732
  38.2 4.8 %collective-permute-start.6 = (bf16[64,1152]{1,0:T(8,128)(2,1)S(1)}, bf16[64,1152]{1,0:T(8,128)(2,1)S(1)}, u32[]{:S(2)}, u32[]{:S(2)}) collective-permute-start(bf16[64,1152]{1,0:T(8,128)(2,1)S(1)} %get-tuple-element.63), channel_id=1, source_target_pairs={{0,1},{1,0},{2,3},{3,2},{4,5},{5,4},{6,7},{7,6},{8,9},{9,8},{10,11... | collective-permute-start | bytes 442376 | tf_op jit(solution)/shard_map/ppermute | solution.py:387
  42.0 10.4 %copy-start.4 = (bf16[512,1024]{1,0:T(8,128)(2,1)S(1)}, bf16[512,1024]{1,0:T(8,128)(2,1)}, u32[]{:S(2)}) copy-start(bf16[512,1024]{1,0:T(8,128)(2,1)} %copy-done.3) | copy-start | bytes 3145732
  43.1 4.8 %collective-permute-start.7 = (bf16[32,1152]{1,0:T(8,128)(2,1)S(1)}, bf16[32,1152]{1,0:T(8,128)(2,1)S(1)}, u32[]{:S(2)}, u32[]{:S(2)}) collective-permute-start(bf16[32,1152]{1,0:T(8,128)(2,1)S(1)} %select_convert_fusion), channel_id=1, source_target_pairs={{0,2},{1,3},{2,0},{3,1},{4,6},{5,7},{6,4},{7,5},{8,10},{9,11},{10,... | collective-permute-start | bytes 221192 | tf_op jit(solution)/shard_map/ppermute | solution.py:387
  47.9 7.0 %collective-permute-start.8 = (bf16[32,1152]{1,0:T(8,128)(2,1)S(1)}, bf16[32,1152]{1,0:T(8,128)(2,1)S(1)}, u32[]{:S(2)}, u32[]{:S(2)}) collective-permute-start(bf16[32,1152]{1,0:T(8,128)(2,1)S(1)} %add_convert_fusion.1.refs_0_), channel_id=1, source_target_pairs={{0,4},{1,5},{2,6},{3,7},{4,0},{5,1},{6,2},{7,3},{8,12},{9,13},{10,... | collective-permute-start | bytes 221192 | tf_op jit(solution)/shard_map/ppermute | solution.py:387
  49.6 7.5 %collective-permute-start.9 = (bf16[32,1152]{1,0:T(8,128)(2,1)S(1)}, bf16[32,1152]{1,0:T(8,128)(2,1)S(1)}, u32[]{:S(2)}, u32[]{:S(2)}) collective-permute-start(bf16[32,1152]{1,0:T(8,128)(2,1)S(1)} %add_convert_fusion.1.refs_0_), channel_id=1, source_target_pairs={{0,8},{1,9},{2,10},{3,11},{4,12},{5,13},{6,14},{7,15},{8,0},{9,1},... | collective-permute-start | bytes 221192 | tf_op jit(solution)/shard_map/ppermute | solution.py:387
  52.0 6.3 %collective-permute-start.10 = (bf16[32,1152]{1,0:T(8,128)(2,1)S(1)}, bf16[32,1152]{1,0:T(8,128)(2,1)S(1)}, u32[]{:S(2)}, u32[]{:S(2)}) collective-permute-start(bf16[32,1152]{1,0:T(8,128)(2,1)S(1)} %add_convert_fusion.1.refs_0_), channel_id=1, source_target_pairs={{0,12},{1,13},{2,14},{3,15},{4,8},{5,9},{6,10},{7,11},{8,4},{9,5},... | collective-permute-start | bytes 221192 | tf_op jit(solution)/shard_map/ppermute | solution.py:387
  58.3 4.4 %collective-permute-start.11 = (bf16[32,1152]{1,0:T(8,128)(2,1)S(1)}, bf16[32,1152]{1,0:T(8,128)(2,1)S(1)}, u32[]{:S(2)}, u32[]{:S(2)}) collective-permute-start(bf16[32,1152]{1,0:T(8,128)(2,1)S(1)} %add_convert_fusion), channel_id=1, source_target_pairs={{0,2},{1,3},{2,0},{3,1},{4,6},{5,7},{6,4},{7,5},{8,10},{9,11},{10,... | collective-permute-start | bytes 221192 | tf_op jit(solution)/shard_map/ppermute | solution.py:387
  62.8 1.4 %collective-permute-start.12 = (bf16[64,1152]{1,0:T(8,128)(2,1)S(1)}, bf16[64,1152]{1,0:T(8,128)(2,1)S(1)}, u32[]{:S(2)}, u32[]{:S(2)}) collective-permute-start(bf16[64,1152]{1,0:T(8,128)(2,1)S(1)} %maximum_select_fusion.refs_0_), channel_id=1, source_target_pairs={{0,1},{1,0},{2,3},{3,2},{4,5},{5,4},{6,7},{7,6},{8,9},{9,8},{10,11... | collective-permute-start | bytes 442376 | tf_op jit(solution)/shard_map/ppermute | solution.py:387

commit v4 on v3

--- a/solution.py
+++ b/solution.py
@@ -276,7 +276,7 @@
 
     for at in (0, rows - 2):
         conv_rows(w_ref[5], d3, at, 2, next_g)
-    send_edges(edges_ref, 2, next_near, next_far)
+    send_edges(edges_ref, 1, next_near, next_far)
 
 
 def middle_kernel(
@@ -297,15 +297,15 @@
 
     def dhidden0(row, total):
         value = jnp.where(one(hid0_ref, row + 2) > 0, total, 0.0).astype(BF16)
-        dh0_ref[row * CHAN : (row + 1) * CHAN, :] = value
-        put(v3, row, value)
-
-    conv_rows(w_ref[3], u3, 0, rows - 2, dhidden0)
+        dh0_ref[(row - 1) * CHAN : row * CHAN, :] = value
+        put(v3, row - 1, value)
+
+    conv_rows(w_ref[3], u3, 1, rows - 4, dhidden0)
     stack_rows(g_ref, range(rows), s3, 0)
     grad11[...] = grad_rows(s3, 0, hid1_ref, 0, rows)
     grad10[...] = grad_rows(t3, 1, x1_ref, 0, rows)
     grad01[...] = grad_rows(u3, 0, hid0_ref, 0, rows)
-    grad00[...] = grad_rows(v3, 0, x_ref, 0, rows - 2)
+    grad00[...] = grad_rows(v3, 0, x_ref, 1, rows - 4)
 
 
 def output_kernel(rows, hid1_ref, x1_ref, w_ref, out_ref, k3, wide):
@@ -319,39 +319,31 @@
 
 
 def backward0_kernel(
-    rows, scale, g1_ref, near_ref, far_ref, hid0_ref, x_ref, xnear_ref, xfar_ref, w_ref, dh0_in,
-    inner00, grad01, grad10, grad11, dh0_ref, keep_ref, send_ref, g3, d3, xs, both,
+    rows, scale, g1_ref, near_ref, far_ref, hid0_ref, x_ref, xnear_ref, xfar_ref, w_ref, inner00,
+    grad01, grad10, grad11, dh0_ref, next_near, next_far, keep_ref, send_ref,
+    g3, d3, xs, both,
 ):
-    halo_rows(near_ref, far_ref, 2, rows, g3)
-    stack_rows(g1_ref, (0, 1, rows - 2, rows - 1), g3, 2)
-    copy_rows(dh0_in, rows - 2, dh0_ref, 2)
+    halo_rows(near_ref, far_ref, 1, rows, g3)
+    stack_rows(g1_ref, (0, 1, 2, rows - 3, rows - 2, rows - 1), g3, 1)
 
     def dhidden0(row, total):
-        value = jnp.where(one(hid0_ref, row) > 0, total, 0.0).astype(BF16)
-        dh0_ref[row * CHAN : (row + 1) * CHAN, :] = value
-        if row == 1:
-            put(d3, 0, value)
-        if row == rows:
-            put(d3, 1, value)
-
-    for at in (0, rows):
+        value = jnp.where(one(hid0_ref, row + 1) > 0, total, 0.0).astype(BF16)
+        at = row if row < 2 else row - (rows - 4)
+        dh0_ref[at * CHAN : (at + 1) * CHAN, :] = value
+        put(d3, at, value)
+
+    for at in (0, rows - 2):
         conv_rows(w_ref[3], g3, at, 2, dhidden0)
+    send_edges(dh0_ref, 1, next_near, next_far)
     odd = odd_place()
-    copy_rows(x_ref, 2, xs, 1)
-    xs[3 * CHAN : 5 * CHAN, :] = x_ref[(rows - 2) * CHAN :, :]
-    near_at, far_at = jnp.where(odd, 0, 5), jnp.where(odd, 5, 0)
+    copy_rows(x_ref, 3, xs, 1)
+    xs[4 * CHAN : 7 * CHAN, :] = x_ref[(rows - 3) * CHAN :, :]
+    near_at, far_at = jnp.where(odd, 0, 7), jnp.where(odd, 7, 0)
     near_row, far_row = jnp.where(odd, 3, 0), jnp.where(odd, 0, 3)
     for ref, at, row in ((xnear_ref, near_at, near_row), (xfar_ref, far_at, far_row)):
         source = pl.ds(pl.multiple_of(row * CHAN, CHAN), CHAN)
         xs[pl.ds(pl.multiple_of(at * CHAN, CHAN), CHAN), :] = ref[source, :]
-    grad00 = inner00[...]
-    for end in range(2):
-        grad00 = grad00 + lax.dot_general(
-            d3[end * STACK : (end + 1) * STACK, :],
-            xs[end * STACK : (end + 1) * STACK, :],
-            (((1,), (1,)), ((), ())),
-            preferred_element_type=F32,
-        )
+    grad00 = inner00[...] + grad_rows(d3, 0, xs, 0, 2) + grad_rows(d3, 2, xs, 4, 2)
     pairs = ((grad00, grad01[...]), (grad10[...], grad11[...]))
     for section, pair in enumerate(pairs):
         for which, value in enumerate(pair):
@@ -365,8 +357,11 @@
     send_ref[...] = both[1 - mine].astype(BF16)
 
 
-def input_grad_kernel(rows, dh0_ref, g1_ref, w_ref, out_ref, d3, wide):
-    stack_rows(dh0_ref, range(rows + 2), d3, 0)
+def input_grad_kernel(rows, dh0_in, dh0_ref, near_ref, far_ref, g1_ref, w_ref, out_ref, d3, wide):
+    halo_rows(near_ref, far_ref, 1, rows, d3)
+    stack_rows(dh0_in, range(rows - 4), d3, 3)
+    stack_rows(dh0_ref, (0, 1), d3, 1)
+    stack_rows(dh0_ref, (2, 3), d3, rows - 3)
 
     def last_g(row, total):
         wide[row] = one(g1_ref, row).astype(F32) + total
@@ -403,7 +398,8 @@
         return pltpu.VMEM((n * STACK, width), BF16)
 
     def neighbours(near, far):
-        return exchange(near, 1, count), lax.ppermute(far, "space", beyond)
+        from_far = lax.ppermute(far, "space", beyond)
+        return exchange(near, 1, count), from_far
 
     row_flops = 2 * CHAN * 9 * CHAN * width * 4
     grad = jax.ShapeDtypeStruct((STACK, STACK), F32)
@@ -419,7 +415,7 @@
     xnear, xfar = neighbours(x_near, x_far)
     (weights,) = call(
         weights_kernel, (kernels,), (jax.ShapeDtypeStruct((8, 2 * CHAN, 4 * STACK), BF16),), [],
-        row_flops, "weights", after=(x_near,),
+        row_flops, "weights", after=(x_far,),
     )
     inner = call(
         functools.partial(inner_kernel, rows), (x, weights),
@@ -439,25 +435,21 @@
     )
     g1_near, g1_far, edges, dh1 = call(
         functools.partial(backward1_kernel, rows), (g, gnear, gfar, hid1, g_inner, weights),
-        (shape(2), shape(2), shape(4), shape(rows + 2)),
+        (shape(1), shape(1), shape(4), shape(rows + 2)),
         [vmem(rows + 4), vmem(rows + 2)], 8 * row_flops, "backward1",
     )
     g1near, g1far = neighbours(g1_near, g1_far)
     g1, dh0_inner, *grads = call(
         functools.partial(middle_kernel, rows), (g, edges, hid1, dh1, x1, hid0, x, weights),
-        (shape(rows), shape(rows - 2)) + (grad,) * 4,
-        [vmem(rows), vmem(rows + 2), vmem(rows), vmem(rows - 2)], 40 * row_flops, "middle",
-    )
-    (section_output,) = call(
-        functools.partial(output_kernel, rows), (hid1, x1, weights), (tile,),
-        [vmem(rows + 2), wide], 8 * row_flops, "output", after=(dh0_inner,),
-    )
-    g1near, g1far, section_output = lax.optimization_barrier((g1near, g1far, section_output))
-    dh0, part, send = call(
+        (shape(rows), shape(rows - 4)) + (grad,) * 4,
+        [vmem(rows), vmem(rows + 2), vmem(rows), vmem(rows - 4)], 36 * row_flops, "middle",
+    )
+    dh0, dh0_near, dh0_far, part, send = call(
         functools.partial(backward0_kernel, rows, scale),
-        (g1, g1near, g1far, hid0, x, xnear, xfar, weights, dh0_inner, *grads),
-        (shape(rows + 2), jax.ShapeDtypeStruct(half, F32), jax.ShapeDtypeStruct(half, BF16)),
-        [vmem(rows + 4), vmem(2), pltpu.VMEM((6 * CHAN, width), BF16),
+        (g1, g1near, g1far, hid0, x, xnear, xfar, weights, *grads),
+        (shape(4), shape(1), shape(1), jax.ShapeDtypeStruct(half, F32),
+         jax.ShapeDtypeStruct(half, BF16)),
+        [vmem(rows + 2), vmem(4), pltpu.VMEM((8 * CHAN, width), BF16),
          pltpu.VMEM((2, *half), F32)],
         8 * row_flops, "backward0",
     )
@@ -468,6 +460,8 @@
     send = jnp.where(bit, low, high).astype(BF16)
     part = jnp.where(bit, high, low)
     arrived = exchange(send, 2, count)
+    dh0_near, dh0_far, _ = lax.optimization_barrier((dh0_near, dh0_far, send))
+    dh0near, dh0far = neighbours(dh0_near, dh0_far)
     part = part + arrived.astype(F32)
     step = 4
     input_grad = None
@@ -477,7 +471,8 @@
         arrived = [exchange(send, mask, count) for mask in masks]
         if input_grad is None:
             (input_grad,) = call(
-                functools.partial(input_grad_kernel, rows), (dh0, g1, weights), (tile,),
+                functools.partial(input_grad_kernel, rows), (dh0_inner, dh0, dh0near, dh0far, g1, weights),
+                (tile,),
                 [vmem(rows + 2), wide], 8 * row_flops, "input_grad", after=(send,),
             )
             arrived, input_grad = lax.optimization_barrier((arrived, input_grad))
@@ -490,6 +485,11 @@
     done = part.astype(BF16)
     bit = (place & 2) != 0
     other = exchange(done, 2, count)
+    (section_output,) = call(
+        functools.partial(output_kernel, rows), (hid1, x1, weights), (tile,),
+        [vmem(rows + 2), wide], 8 * row_flops, "output", after=(done,),
+    )
+    other, section_output = lax.optimization_barrier((other, section_output))
     done = jnp.where(bit, jnp.concatenate([other, done]), jnp.concatenate([done, other]))
     (kernel_grad,) = call(
         gathered_kernel, (done, exchange(done, 1, count)),

time: 65.4 us -> 64.7 us (0.989)
  waiting for transfers between devices: 11.5 us -> 9.76 us
  local copies, waits for them, and re-layouts: 2.2 us -> 3.79 us
    ppermute x10 -> x11, waiting for transfers between devices: 11.5 us -> 9.75 us  [exchange(): return lax.ppermute(value, 'space', [(d, d ^ mask) for d in range(count)])]
    unnamed x10 -> x22, local copies, waits for them, and re-layouts: 2.2 us -> 3.79 us
    ppermute x10 -> x11, starting transfers between devices: 25 us -> 23.8 us  [exchange(): return lax.ppermute(value, 'space', [(d, d ^ mask) for d in range(count)])]
    ppermute x3 -> x4, starting transfers between devices: 2.19 us -> 2.86 us  [neighbours(): from_far = lax.ppermute(far, 'space', beyond)]
  transfers between devices with their start and end apart: 13 -> 15, of which waited for: 6 -> 7; matrix products, arithmetic and copies ran while one was open for 0% -> 0% of each run, Pallas kernels for 27% -> 27%
where the time goes in v4:
time: 64.7 us; the launch traced here: 64.4 us
  starting transfers between devices  26.7 us (41%)
  Pallas kernels  23.2 us (36%)
  waiting for transfers between devices  9.76 us (15%)
  local copies, waits for them, and re-layouts  3.79 us (6%)
  between operations  0.88 us (1%)
    ppermute x11, starting transfers between devices, exchange(): return lax.ppermute(value, 'space', [(d, d ^ mask) for d in range(count)])  23.8 us
    pallas_call x11, Pallas kernels, call(): pl.pallas_call(kernel, out_shape=outs, in_specs=[ANY] * len(after) + [pla...  23.2 us
    ppermute x11, waiting for transfers between devices, exchange(): return lax.ppermute(value, 'space', [(d, d ^ mask) for d in range(count)])  9.75 us
    unnamed x22, local copies, waits for them, and re-layouts  3.79 us
    ppermute x4, starting transfers between devices, neighbours(): from_far = lax.ppermute(far, 'space', beyond)  2.86 us
  transfers between devices with their start and end apart: 15, of which 7 were waited for; matrix products, arithmetic and copies ran while one was open for 0% of the time, Pallas kernels for 27%

profile of v4, /device:TPU:0, one launch (start us, length us, event | category | flops | bytes accessed | tf_op | source)
XLA Modules:
  0.0 64.4 jit_solution(8393633957950993721)
XLA Ops:
  0.6 1.2 %copy-done = bf16[64,8,1024]{2,1,0:T(8,128)(2,1)S(1)} copy-done((bf16[64,8,1024]{2,1,0:T(8,128)(2,1)S(1)}, bf16[64,8,1024]{2,1,0:T(8,128)(2,1)}, u32[]{:S(2)}) %copy-start) | copy-done | bytes 1048600
  3.2 4.3 %collective-permute-start.2 = (bf16[256,1024]{1,0:T(8,128)(2,1)S(1)}, bf16[256,1024]{1,0:T(8,128)(2,1)S(1)}, u32[]{:S(2)}, u32[]{:S(2)}) collective-permute-start(bf16[256,1024]{1,0:T(8,128)(2,1)S(1)} %get-tuple-element.45), channel_id=1, source_target_pairs={{0,1},{1,0},{2,3},{3,2},{4,5},{5,4},{6,7},{7,6},{8,9},{9,8},{10,11... | collective-permute-start | bytes 1572872 | tf_op jit(solution)/shard_map/ppermute | solution.py:382
  7.5 1.0 %copy-done.1 = bf16[2,2,64,576]{3,2,1,0:T(8,128)(2,1)S(1)} copy-done((bf16[2,2,64,576]{3,2,1,0:T(8,128)(2,1)S(1)}, bf16[2,2,64,576]{3,2,1,0:T(8,128)(2,1)}, u32[]{:S(2)}) %copy-start.1) | copy-done | bytes 294936
  9.2 1.7 %inner.1 = (bf16[384,1024]{1,0:T(8,128)(2,1)S(1)}, bf16[256,1024]{1,0:T(8,128)(2,1)S(1)}, bf16[128,1024]{1,0:T(8,128)(2,1)S(1)}) custom-call(bf16[512,1024]{1,0:T(8,128)(2,1)S(1)} %get-tuple-element.39.refs_0_.refs_6_.refs_4_, bf16[8,128,768]{2,1,0:T(8,128)(2,1)S(1)} %weights.1.refs_1_.refs_2_.refs_3_.refs_5_.refs_7_.refs_6_), custom_call_target="tpu_custom_call" | custom-call | flops 3623878656 | bytes 4194304 | tf_op jit(solution)/shard_map/inner/pallas_call | solution.py:28
  10.9 1.6 %g_rows.1 = (bf16[512,1024]{1,0:T(8,128)(2,1)S(1)}, bf16[128,1024]{1,0:T(8,128)(2,1)S(1)}, bf16[128,1024]{1,0:T(8,128)(2,1)S(1)}, f32[384,1024]{1,0:T(8,128)S(1)}) custom-call(bf16[128,1024]{1,0:T(8,128)(2,1)S(1)} %get-tuple-element.41.refs_0_.refs_6_, bf16[64,8,1024]{2,1,0:T(8,128)(2,1)S(1)} %copy-done.2, ...), custom_call_target="tpu_custom_call" | custom-call | flops 1811939328 | bytes 5767168 | tf_op jit(solution)/shard_map/g_rows/pallas_call | solution.py:28
  13.3 3.8 %forward.1 = (bf16[640,1024]{1,0:T(8,128)(2,1)S(1)}, bf16[640,1024]{1,0:T(8,128)(2,1)S(1)}, bf16[640,1024]{1,0:T(8,128)(2,1)S(1)}) custom-call(bf16[512,1024]{1,0:T(8,128)(2,1)S(1)} %get-tuple-element.39.refs_0_.refs_6_.refs_4_, bf16[256,1024]{1,0:T(8,128)(2,1)S(1)} %collective-permute-done.2.refs_1_.refs_5_, ...), custom_call_target="tpu_custom_call" | custom-call | flops 7247757312 | bytes 9175040 | tf_op jit(solution)/shard_map/forward/pallas_call | solution.py:28
  17.2 2.3 %backward1.1 = (bf16[64,1024]{1,0:T(8,128)(2,1)S(1)}, bf16[64,1024]{1,0:T(8,128)(2,1)S(1)}, bf16[256,1024]{1,0:T(8,128)(2,1)S(1)}, bf16[640,1024]{1,0:T(8,128)(2,1)S(1)}) custom-call(bf16[512,1024]{1,0:T(8,128)(2,1)S(1)} %get-tuple-element.42.refs_0_, bf16[128,1024]{1,0:T(8,128)(2,1)S(1)} %collective-permute-done.refs_1_, ...), custom_call_target="tpu_custom_call" | custom-call | flops 2415919104 | bytes 8126464 | tf_op jit(solution)/shard_map/backward1/pallas_call | solution.py:28
  19.4 8.7 %collective-permute-start.4 = (bf16[64,1024]{1,0:T(8,128)(2,1)S(1)}, bf16[64,1024]{1,0:T(8,128)(2,1)S(1)}, u32[]{:S(2)}, u32[]{:S(2)}) collective-permute-start(bf16[64,1024]{1,0:T(8,128)(2,1)S(1)} %get-tuple-element.55), channel_id=1, source_target_pairs={{0,1},{1,0},{2,3},{3,2},{4,5},{5,4},{6,7},{7,6},{8,9},{9,8},{10,11... | collective-permute-start | bytes 393224 | tf_op jit(solution)/shard_map/ppermute | solution.py:382
  28.2 0.8 %collective-permute-start.5 = (bf16[64,1024]{1,0:T(8,128)(2,1)S(1)}, bf16[64,1024]{1,0:T(8,128)(2,1)S(1)}, u32[]{:S(2)}, u32[]{:S(2)}) collective-permute-start(bf16[64,1024]{1,0:T(8,128)(2,1)S(1)} %get-tuple-element.56), channel_id=1, source_target_pairs={{1,2},{3,4},{5,6},{7,8},{9,10},{11,12},{13,14},{2,1},{4,3},{6,5},{... | collective-permute-start | bytes 393224 | tf_op jit(solution)/shard_map/ppermute | solution.py:401
  29.0 4.4 %middle.1 = (bf16[512,1024]{1,0:T(8,128)(2,1)S(1)}, bf16[256,1024]{1,0:T(8,128)(2,1)S(1)}, f32[192,192]{1,0:T(8,128)S(1)}, f32[192,192]{1,0:T(8,128)S(1)}, f32[1...) custom-call(bf16[512,1024]{1,0:T(8,128)(2,1)S(1)} %get-tuple-element.42.refs_0_, ...), custom_call_target="tpu_custom_call" | custom-call | flops 10871635968 | bytes 11599872 | tf_op jit(solution)/shard_map/middle/pallas_call | solution.py:28
  34.3 1.8 %backward0.1 = (bf16[256,1024]{1,0:T(8,128)(2,1)S(1)}, bf16[64,1024]{1,0:T(8,128)(2,1)S(1)}, bf16[64,1024]{1,0:T(8,128)(2,1)S(1)}, f32[64,1152]{1,0:T(8,128)S(1)}, bf16[64,1152]{1,0:T(8,128)(2,1)S(1)}) custom-call(bf16[512,1024]{1,0:T(8,128)(2,1)S(1)} %get-tuple-element.54.refs_0_.refs_5_, bf16[64,1024]{1,0:T(8,128)(2,1)S(1)} %collective-permute-done.4.refs_1_, ...), custom_call_target="tpu_custom_call" | custom-call | flops 2415919104 | bytes 8110080 | tf_op jit(solution)/shard_map/backward0/pallas_call | solution.py:28
  36.9 3.8 %collective-permute-start.6 = (bf16[64,1152]{1,0:T(8,128)(2,1)S(1)}, bf16[64,1152]{1,0:T(8,128)(2,1)S(1)}, u32[]{:S(2)}, u32[]{:S(2)}) collective-permute-start(bf16[64,1152]{1,0:T(8,128)(2,1)S(1)} %get-tuple-element.62), channel_id=1, source_target_pairs={{0,1},{1,0},{2,3},{3,2},{4,5},{5,4},{6,7},{7,6},{8,9},{9,8},{10,11... | collective-permute-start | bytes 442376 | tf_op jit(solution)/shard_map/ppermute | solution.py:382
  40.7 1.0 %collective-permute-done.6 = bf16[64,1152]{1,0:T(8,128)(2,1)S(1)} collective-permute-done((bf16[64,1152]{1,0:T(8,128)(2,1)S(1)}, bf16[64,1152]{1,0:T(8,128)(2,1)S(1)}, u32[]{:S(2)}, u32[]{:S(2)}) %collective-permute-start.6) | collective-permute-done | bytes 147488 | tf_op jit(solution)/shard_map/ppermute | solution.py:382
  41.7 1.4 %collective-permute-start.7 = (bf16[32,1152]{1,0:T(8,128)(2,1)S(1)}, bf16[32,1152]{1,0:T(8,128)(2,1)S(1)}, u32[]{:S(2)}, u32[]{:S(2)}) collective-permute-start(bf16[32,1152]{1,0:T(8,128)(2,1)S(1)} %select_convert_fusion), channel_id=1, source_target_pairs={{0,2},{1,3},{2,0},{3,1},{4,6},{5,7},{6,4},{7,5},{8,10},{9,11},{10,... | collective-permute-start | bytes 221192 | tf_op jit(solution)/shard_map/ppermute | solution.py:382
  43.9 2.4 %collective-permute-done.7 = bf16[32,1152]{1,0:T(8,128)(2,1)S(1)} collective-permute-done((bf16[32,1152]{1,0:T(8,128)(2,1)S(1)}, bf16[32,1152]{1,0:T(8,128)(2,1)S(1)}, u32[]{:S(2)}, u32[]{:S(2)}) %collective-permute-start.7) | collective-permute-done | bytes 73760 | tf_op jit(solution)/shard_map/ppermute | solution.py:382
  46.4 3.7 %collective-permute-start.10 = (bf16[32,1152]{1,0:T(8,128)(2,1)S(1)}, bf16[32,1152]{1,0:T(8,128)(2,1)S(1)}, u32[]{:S(2)}, u32[]{:S(2)}) collective-permute-start(bf16[32,1152]{1,0:T(8,128)(2,1)S(1)} %add_convert_fusion.1.refs_0_), channel_id=1, source_target_pairs={{0,12},{1,13},{2,14},{3,15},{4,8},{5,9},{6,10},{7,11},{8,4},{9,5},... | collective-permute-start | bytes 221192 | tf_op jit(solution)/shard_map/ppermute | solution.py:382
  50.9 2.8 %input_grad.1 = bf16[64,8,1024]{2,1,0:T(8,128)(2,1)} custom-call(bf16[32,1152]{1,0:T(8,128)(2,1)S(1)} %add_convert_fusion.1.refs_0_, bf16[256,1024]{1,0:T(8,128)(2,1)S(1)} %copy-done.10, bf16[256,1024]{1,0:T(8,128)(2,1)S(1)} %copy-done.6, bf16[64,1024]{1,0:T(8,128)(2,1)S(1)} %collective-permute-done.11.refs_3_, ...), custom_call_target="tpu_custom_call" | custom-call | flops 2415919104 | bytes 4980736 | tf_op jit(solution)/shard_map/input_grad/pallas_call | solution.py:28
  53.6 1.1 %collective-permute-done.10 = bf16[32,1152]{1,0:T(8,128)(2,1)S(1)} collective-permute-done((bf16[32,1152]{1,0:T(8,128)(2,1)S(1)}, bf16[32,1152]{1,0:T(8,128)(2,1)S(1)}, u32[]{:S(2)}, u32[]{:S(2)}) %collective-permute-start.10) | collective-permute-done | bytes 73760 | tf_op jit(solution)/shard_map/ppermute | solution.py:382
  55.5 2.1 %collective-permute-done.9 = bf16[32,1152]{1,0:T(8,128)(2,1)S(1)} collective-permute-done((bf16[32,1152]{1,0:T(8,128)(2,1)S(1)}, bf16[32,1152]{1,0:T(8,128)(2,1)S(1)}, u32[]{:S(2)}, u32[]{:S(2)}) %collective-permute-start.9) | collective-permute-done | bytes 73760 | tf_op jit(solution)/shard_map/ppermute | solution.py:382
  57.6 0.9 %collective-permute-start.13 = (bf16[32,1152]{1,0:T(8,128)(2,1)S(1)}, bf16[32,1152]{1,0:T(8,128)(2,1)S(1)}, u32[]{:S(2)}, u32[]{:S(2)}) collective-permute-start(bf16[32,1152]{1,0:T(8,128)(2,1)S(1)} %add_convert_fusion.refs_0_), channel_id=1, source_target_pairs={{0,2},{1,3},{2,0},{3,1},{4,6},{5,7},{6,4},{7,5},{8,10},{9,11},{10,... | collective-permute-start | bytes 221192 | tf_op jit(solution)/shard_map/ppermute | solution.py:382
  58.4 2.5 %output.1 = bf16[64,8,1024]{2,1,0:T(8,128)(2,1)} custom-call(bf16[32,1152]{1,0:T(8,128)(2,1)S(1)} %add_convert_fusion.refs_0_, bf16[640,1024]{1,0:T(8,128)(2,1)S(1)} %copy-done.4, bf16[640,1024]{1,0:T(8,128)(2,1)S(1)} %copy-done.8, bf16[8,128,768]{2,1,0:T(8,128)(2,1)S(1)} %weights.1.refs_1_.refs_2_.refs_3_.refs_5_.refs_7_.refs_6_), custom_call_target="tpu_custom_call" | custom-call | flops 2415919104 | bytes 5242880 | tf_op jit(solution)/shard_map/output/pallas_call | solution.py:28
  61.0 1.0 %collective-permute-done.13 = bf16[32,1152]{1,0:T(8,128)(2,1)S(1)} collective-permute-done((bf16[32,1152]{1,0:T(8,128)(2,1)S(1)}, bf16[32,1152]{1,0:T(8,128)(2,1)S(1)}, u32[]{:S(2)}, u32[]{:S(2)}) %collective-permute-start.13) | collective-permute-done | bytes 73760 | tf_op jit(solution)/shard_map/ppermute | solution.py:382
  62.1 1.4 %collective-permute-done.14.refs_1_ = bf16[64,1152]{1,0:T(8,128)(2,1)S(1)} collective-permute-done((bf16[64,1152]{1,0:T(8,128)(2,1)S(1)}, bf16[64,1152]{1,0:T(8,128)(2,1)S(1)}, u32[]{:S(2)}, u32[]{:S(2)}) %collective-permute-start.14) | collective-permute-done | bytes 147488 | tf_op jit(solution)/shard_map/ppermute | solution.py:382
  63.5 1.0 %gathered.1 = f32[2,2,64,576]{3,2,1,0:T(8,128)} custom-call(bf16[64,1152]{1,0:T(8,128)(2,1)S(1)} %maximum_select_fusion.refs_0_, bf16[64,1152]{1,0:T(8,128)(2,1)S(1)} %collective-permute-done.14.refs_1_), custom_call_target="tpu_custom_call" | custom-call | bytes 884736 | tf_op jit(solution)/shard_map/gathered/pallas_call | solution.py:28
  (44 shorter events, 6.8 us)
Async XLA Ops:
  0.6 1.2 %copy-start = (bf16[64,8,1024]{2,1,0:T(8,128)(2,1)S(1)}, bf16[64,8,1024]{2,1,0:T(8,128)(2,1)}, u32[]{:S(2)}) copy-start(bf16[64,8,1024]{2,1,0:T(8,128)(2,1)} %refs_0_.1) | copy-start | bytes 3145732
  2.5 10.8 %collective-permute-start.3 = (bf16[256,1024]{1,0:T(8,128)(2,1)S(1)}, bf16[256,1024]{1,0:T(8,128)(2,1)S(1)}, u32[]{:S(2)}, u32[]{:S(2)}) collective-permute-start(bf16[256,1024]{1,0:T(8,128)(2,1)S(1)} %get-tuple-element.40.refs_0_), channel_id=1, source_target_pairs={{1,2},{3,4},{5,6},{7,8},{9,10},{11,12},{13,14},{2,1},{4,3},{6,5},{... | collective-permute-start | bytes 1572872 | tf_op jit(solution)/shard_map/ppermute | solution.py:401
  3.2 10.1 %collective-permute-start.2 = (bf16[256,1024]{1,0:T(8,128)(2,1)S(1)}, bf16[256,1024]{1,0:T(8,128)(2,1)S(1)}, u32[]{:S(2)}, u32[]{:S(2)}) collective-permute-start(bf16[256,1024]{1,0:T(8,128)(2,1)S(1)} %get-tuple-element.45), channel_id=1, source_target_pairs={{0,1},{1,0},{2,3},{3,2},{4,5},{5,4},{6,7},{7,6},{8,9},{9,8},{10,11... | collective-permute-start | bytes 1572872 | tf_op jit(solution)/shard_map/ppermute | solution.py:382
  7.5 1.0 %copy-start.1 = (bf16[2,2,64,576]{3,2,1,0:T(8,128)(2,1)S(1)}, bf16[2,2,64,576]{3,2,1,0:T(8,128)(2,1)}, u32[]{:S(2)}) copy-start(bf16[2,2,64,576]{3,2,1,0:T(8,128)(2,1)} %refs_1_.2) | copy-start | bytes 884740
  9.2 1.7 %copy-start.2 = (bf16[64,8,1024]{2,1,0:T(8,128)(2,1)S(1)}, bf16[64,8,1024]{2,1,0:T(8,128)(2,1)}, u32[]{:S(2)}) copy-start(bf16[64,8,1024]{2,1,0:T(8,128)(2,1)} %refs_1_.3) | copy-start | bytes 3145732
  12.5 4.7 %collective-permute-start = (bf16[128,1024]{1,0:T(8,128)(2,1)S(1)}, bf16[128,1024]{1,0:T(8,128)(2,1)S(1)}, u32[]{:S(2)}, u32[]{:S(2)}) collective-permute-start(bf16[128,1024]{1,0:T(8,128)(2,1)S(1)} %get-tuple-element.43), channel_id=1, source_target_pairs={{0,1},{1,0},{2,3},{3,2},{4,5},{5,4},{6,7},{7,6},{8,9},{9,8},{10,11... | collective-permute-start | bytes 786440 | tf_op jit(solution)/shard_map/ppermute | solution.py:382
  12.6 4.6 %collective-permute-start.1 = (bf16[128,1024]{1,0:T(8,128)(2,1)S(1)}, bf16[128,1024]{1,0:T(8,128)(2,1)S(1)}, u32[]{:S(2)}, u32[]{:S(2)}) collective-permute-start(bf16[128,1024]{1,0:T(8,128)(2,1)S(1)} %get-tuple-element.44), channel_id=1, source_target_pairs={{1,2},{3,4},{5,6},{7,8},{9,10},{11,12},{13,14},{2,1},{4,3},{6,5},{... | collective-permute-start | bytes 786440 | tf_op jit(solution)/shard_map/ppermute | solution.py:401
  17.1 11.9 %copy-start.3 = (bf16[640,1024]{1,0:T(8,128)(2,1)}, bf16[640,1024]{1,0:T(8,128)(2,1)S(1)}, u32[]{:S(2)}) copy-start(bf16[640,1024]{1,0:T(8,128)(2,1)S(1)} %get-tuple-element.48.refs_3_.refs_2_.refs_1_) | copy-start | bytes 3932164
  17.1 11.9 %copy-start.7 = (bf16[640,1024]{1,0:T(8,128)(2,1)}, bf16[640,1024]{1,0:T(8,128)(2,1)S(1)}, u32[]{:S(2)}) copy-start(bf16[640,1024]{1,0:T(8,128)(2,1)S(1)} %get-tuple-element.52.refs_4_.refs_2_) | copy-start | bytes 3932164
  19.4 14.8 %collective-permute-start.4 = (bf16[64,1024]{1,0:T(8,128)(2,1)S(1)}, bf16[64,1024]{1,0:T(8,128)(2,1)S(1)}, u32[]{:S(2)}, u32[]{:S(2)}) collective-permute-start(bf16[64,1024]{1,0:T(8,128)(2,1)S(1)} %get-tuple-element.55), channel_id=1, source_target_pairs={{0,1},{1,0},{2,3},{3,2},{4,5},{5,4},{6,7},{7,6},{8,9},{9,8},{10,11... | collective-permute-start | bytes 393224 | tf_op jit(solution)/shard_map/ppermute | solution.py:382
  28.2 6.1 %collective-permute-start.5 = (bf16[64,1024]{1,0:T(8,128)(2,1)S(1)}, bf16[64,1024]{1,0:T(8,128)(2,1)S(1)}, u32[]{:S(2)}, u32[]{:S(2)}) collective-permute-start(bf16[64,1024]{1,0:T(8,128)(2,1)S(1)} %get-tuple-element.56), channel_id=1, source_target_pairs={{1,2},{3,4},{5,6},{7,8},{9,10},{11,12},{13,14},{2,1},{4,3},{6,5},{... | collective-permute-start | bytes 393224 | tf_op jit(solution)/shard_map/ppermute | solution.py:401
  36.9 4.8 %collective-permute-start.6 = (bf16[64,1152]{1,0:T(8,128)(2,1)S(1)}, bf16[64,1152]{1,0:T(8,128)(2,1)S(1)}, u32[]{:S(2)}, u32[]{:S(2)}) collective-permute-start(bf16[64,1152]{1,0:T(8,128)(2,1)S(1)} %get-tuple-element.62), channel_id=1, source_target_pairs={{0,1},{1,0},{2,3},{3,2},{4,5},{5,4},{6,7},{7,6},{8,9},{9,8},{10,11... | collective-permute-start | bytes 442376 | tf_op jit(solution)/shard_map/ppermute | solution.py:382
  40.7 10.2 %copy-start.6 = (bf16[256,1024]{1,0:T(8,128)(2,1)S(1)}, bf16[256,1024]{1,0:T(8,128)(2,1)}, u32[]{:S(2)}) copy-start(bf16[256,1024]{1,0:T(8,128)(2,1)} %copy-done.5) | copy-start | bytes 1572868
  40.7 10.2 %copy-start.10 = (bf16[256,1024]{1,0:T(8,128)(2,1)S(1)}, bf16[256,1024]{1,0:T(8,128)(2,1)}, u32[]{:S(2)}) copy-start(bf16[256,1024]{1,0:T(8,128)(2,1)} %copy-done.9) | copy-start | bytes 1572868
  41.7 4.6 %collective-permute-start.7 = (bf16[32,1152]{1,0:T(8,128)(2,1)S(1)}, bf16[32,1152]{1,0:T(8,128)(2,1)S(1)}, u32[]{:S(2)}, u32[]{:S(2)}) collective-permute-start(bf16[32,1152]{1,0:T(8,128)(2,1)S(1)} %select_convert_fusion), channel_id=1, source_target_pairs={{0,2},{1,3},{2,0},{3,1},{4,6},{5,7},{6,4},{7,5},{8,10},{9,11},{10,... | collective-permute-start | bytes 221192 | tf_op jit(solution)/shard_map/ppermute | solution.py:382
  43.2 7.7 %collective-permute-start.11 = (bf16[64,1024]{1,0:T(8,128)(2,1)S(1)}, bf16[64,1024]{1,0:T(8,128)(2,1)S(1)}, u32[]{:S(2)}, u32[]{:S(2)}) collective-permute-start(bf16[64,1024]{1,0:T(8,128)(2,1)S(1)} %get-tuple-element.67), channel_id=1, source_target_pairs={{0,1},{1,0},{2,3},{3,2},{4,5},{5,4},{6,7},{7,6},{8,9},{9,8},{10,11... | collective-permute-start | bytes 393224 | tf_op jit(solution)/shard_map/ppermute | solution.py:382
  43.2 7.6 %collective-permute-start.12 = (bf16[64,1024]{1,0:T(8,128)(2,1)S(1)}, bf16[64,1024]{1,0:T(8,128)(2,1)S(1)}, u32[]{:S(2)}, u32[]{:S(2)}) collective-permute-start(bf16[64,1024]{1,0:T(8,128)(2,1)S(1)} %get-tuple-element.68), channel_id=1, source_target_pairs={{1,2},{3,4},{5,6},{7,8},{9,10},{11,12},{13,14},{2,1},{4,3},{6,5},{... | collective-permute-start | bytes 393224 | tf_op jit(solution)/shard_map/ppermute | solution.py:401
  46.4 8.4 %collective-permute-start.10 = (bf16[32,1152]{1,0:T(8,128)(2,1)S(1)}, bf16[32,1152]{1,0:T(8,128)(2,1)S(1)}, u32[]{:S(2)}, u32[]{:S(2)}) collective-permute-start(bf16[32,1152]{1,0:T(8,128)(2,1)S(1)} %add_convert_fusion.1.refs_0_), channel_id=1, source_target_pairs={{0,12},{1,13},{2,14},{3,15},{4,8},{5,9},{6,10},{7,11},{8,4},{9,5},... | collective-permute-start | bytes 221192 | tf_op jit(solution)/shard_map/ppermute | solution.py:382
  50.1 5.4 %collective-permute-start.8 = (bf16[32,1152]{1,0:T(8,128)(2,1)S(1)}, bf16[32,1152]{1,0:T(8,128)(2,1)S(1)}, u32[]{:S(2)}, u32[]{:S(2)}) collective-permute-start(bf16[32,1152]{1,0:T(8,128)(2,1)S(1)} %add_convert_fusion.1.refs_0_), channel_id=1, source_target_pairs={{0,4},{1,5},{2,6},{3,7},{4,0},{5,1},{6,2},{7,3},{8,12},{9,13},{10,... | collective-permute-start | bytes 221192 | tf_op jit(solution)/shard_map/ppermute | solution.py:382
  50.1 7.4 %collective-permute-start.9 = (bf16[32,1152]{1,0:T(8,128)(2,1)S(1)}, bf16[32,1152]{1,0:T(8,128)(2,1)S(1)}, u32[]{:S(2)}, u32[]{:S(2)}) collective-permute-start(bf16[32,1152]{1,0:T(8,128)(2,1)S(1)} %add_convert_fusion.1.refs_0_), channel_id=1, source_target_pairs={{0,8},{1,9},{2,10},{3,11},{4,12},{5,13},{6,14},{7,15},{8,0},{9,1},... | collective-permute-start | bytes 221192 | tf_op jit(solution)/shard_map/ppermute | solution.py:382
  50.8 7.6 %copy-start.4 = (bf16[640,1024]{1,0:T(8,128)(2,1)S(1)}, bf16[640,1024]{1,0:T(8,128)(2,1)}, u32[]{:S(2)}) copy-start(bf16[640,1024]{1,0:T(8,128)(2,1)} %copy-done.3) | copy-start | bytes 3932164
  50.8 7.6 %copy-start.8 = (bf16[640,1024]{1,0:T(8,128)(2,1)S(1)}, bf16[640,1024]{1,0:T(8,128)(2,1)}, u32[]{:S(2)}) copy-start(bf16[640,1024]{1,0:T(8,128)(2,1)} %copy-done.7) | copy-start | bytes 3932164
  57.6 4.4 %collective-permute-start.13 = (bf16[32,1152]{1,0:T(8,128)(2,1)S(1)}, bf16[32,1152]{1,0:T(8,128)(2,1)S(1)}, u32[]{:S(2)}, u32[]{:S(2)}) collective-permute-start(bf16[32,1152]{1,0:T(8,128)(2,1)S(1)} %add_convert_fusion.refs_0_), channel_id=1, source_target_pairs={{0,2},{1,3},{2,0},{3,1},{4,6},{5,7},{6,4},{7,5},{8,10},{9,11},{10,... | collective-permute-start | bytes 221192 | tf_op jit(solution)/shard_map/ppermute | solution.py:382
  62.0 1.4 %collective-permute-start.14 = (bf16[64,1152]{1,0:T(8,128)(2,1)S(1)}, bf16[64,1152]{1,0:T(8,128)(2,1)S(1)}, u32[]{:S(2)}, u32[]{:S(2)}) collective-permute-start(bf16[64,1152]{1,0:T(8,128)(2,1)S(1)} %maximum_select_fusion.refs_0_), channel_id=1, source_target_pairs={{0,1},{1,0},{2,3},{3,2},{4,5},{5,4},{6,7},{7,6},{8,9},{9,8},{10,11... | collective-permute-start | bytes 442376 | tf_op jit(solution)/shard_map/ppermute | solution.py:382
  (2 other events, 1.6 us)

commit v5 on v4

--- a/solution.py
+++ b/solution.py
@@ -18,7 +18,7 @@
 PIECES = 4
 
 
-def call(body, operands, outs, scratch, flops, name, after=(), place=VMEM):
+def call(body, operands, outs, scratch, flops, name, after=(), place=VMEM, to_hbm=()):
     nbytes = sum(v.size * v.dtype.itemsize for v in (*operands, *outs))
     held = sum(math.prod(v.shape) * v.dtype.itemsize for v in scratch if v.dtype in (F32, BF16))
 
@@ -29,7 +29,7 @@
         kernel,
         out_shape=outs,
         in_specs=[ANY] * len(after) + [place] + [VMEM] * (len(operands) - 1),
-        out_specs=[VMEM] * len(outs),
+        out_specs=[HBM if i in to_hbm else VMEM for i in range(len(outs))],
         scratch_shapes=scratch,
         compiler_params=pltpu.CompilerParams(vmem_limit_bytes=nbytes + held + (6 << 20)),
         cost_estimate=pl.CostEstimate(flops=flops, bytes_accessed=nbytes, transcendentals=0),
@@ -207,48 +207,72 @@
     conv_rows(w_ref[4], y3, 0, rows - 6, hidden1)
 
 
-def forward_kernel(
-    rows, height, x_ref, near_ref, far_ref, w_ref, hid0_in, x1_in, hid1_in,
-    hid0_ref, x1_ref, hid1_ref, x3, h3, y3,
-):
+def at_row(ref, row, count=1):
+    return ref.at[pl.ds(pl.multiple_of(row * CHAN, CHAN), count * CHAN), :]
+
+
+def side_rows(rows, height, top, x_ref, halo_ref, w_ref, hid0_in, x1_in, hid0, x1, hid1, x3, h3, y3):
     first = lax.axis_index("space") * rows
+    own = jnp.where(top, 0, 2)
+    rest = jnp.where(top, 4, 0)
 
     def inside(row, value):
-        if 0 <= row < rows:
-            return value
         keep = jnp.logical_and(first + row >= 0, first + row < height)
         return jnp.where(keep, value, 0.0)
 
-    halo_rows(near_ref, far_ref, 4, rows, x3)
-    stack_rows(x_ref, (0, 1, rows - 2, rows - 1), x3, 4)
-    stack_rows(hid0_in, (0, 1, rows - 4, rows - 3), h3, 4)
-    stack_rows(x1_in, (0, 1, rows - 6, rows - 5), y3, 4)
+    for i in range(4):
+        put_at(x3, own + i, one(halo_ref, i))
+    for i in range(2):
+        put_at(x3, rest + i, at_row(x_ref, jnp.where(top, 0, rows - 2) + i)[...])
+        put_at(h3, rest + i, at_row(hid0_in, jnp.where(top, 0, rows - 4) + i)[...])
+        put_at(y3, rest + i, at_row(x1_in, jnp.where(top, 0, rows - 6) + i)[...])
+
+    def hidden0(row, total):
+        at = jnp.where(top, -3, rows - 1) + row
+        value = inside(at, jnp.maximum(total, 0.0)).astype(BF16)
+        hid0[row * CHAN : (row + 1) * CHAN, :] = value
+        put_at(h3, own + row, value)
+
+    conv_rows(w_ref[0], x3, 0, 4, hidden0)
+
+    def next_x(row, total):
+        at = jnp.where(top, -2, rows - 2) + row
+        start = pl.multiple_of((jnp.where(top, 2, 0) + row) * STACK + CHAN, CHAN)
+        value = inside(at, x3[pl.ds(start, CHAN), :].astype(F32) + total).astype(BF16)
+        x1[row * CHAN : (row + 1) * CHAN, :] = value
+        put_at(y3, own + row, value)
+
+    conv_rows(w_ref[2], h3, 0, 4, next_x)
+
+    def hidden1(row, total):
+        at = jnp.where(top, -1, rows - 3) + row
+        value = inside(at, jnp.maximum(total, 0.0)).astype(BF16)
+        hid1[row * CHAN : (row + 1) * CHAN, :] = value
+
+    conv_rows(w_ref[4], y3, 0, 4, hidden1)
+
+
+def near_kernel(rows, height, *refs):
+    side_rows(rows, height, odd_place(), *refs)
+
+
+def far_kernel(
+    rows, height, x_ref, far_ref, w_ref, hid0_in, x1_in, hid1_in, near0, near1, near2,
+    hid0_ref, x1_ref, hid1_ref, far0, far1, far2, *scratch,
+):
+    odd = odd_place()
+    side_rows(
+        rows, height, jnp.logical_not(odd), x_ref, far_ref, w_ref, hid0_in, x1_in, far0, far1, far2,
+        *scratch,
+    )
     copy_rows(hid0_in, rows - 2, hid0_ref, 2)
     copy_rows(x1_in, rows - 4, x1_ref, 3)
     copy_rows(hid1_in, rows - 6, hid1_ref, 4)
-
-    def hidden0(row, total):
-        value = inside(row - 3, jnp.maximum(total, 0.0)).astype(BF16)
-        put(h3, row, value)
-        if 2 <= row < rows + 4:
-            hid0_ref[(row - 2) * CHAN : (row - 1) * CHAN, :] = value
-
-    def next_x(row, total):
-        value = inside(row - 2, middle(x3, row + 2).astype(F32) + total).astype(BF16)
-        put(y3, row, value)
-        if 1 <= row < rows + 3:
-            x1_ref[(row - 1) * CHAN : row * CHAN, :] = value
-
-    def hidden1(row, total):
-        value = inside(row - 1, jnp.maximum(total, 0.0)).astype(BF16)
-        hid1_ref[row * CHAN : (row + 1) * CHAN, :] = value
-
-    for at in (0, rows + 2):
-        conv_rows(w_ref[0], x3, at, 4, hidden0)
-    for at in (0, rows):
-        conv_rows(w_ref[2], h3, at, 4, next_x)
-    for at in (0, rows - 2):
-        conv_rows(w_ref[4], y3, at, 4, hidden1)
+    sides = ((odd, near0, near1, near2), (jnp.logical_not(odd), far0, far1, far2))
+    for top, hid0, x1, hid1 in sides:
+        for target, source, count in ((hid0_ref, hid0, 2), (x1_ref, x1, 3), (hid1_ref, hid1, 4)):
+            to = at_row(target, jnp.where(top, 0, rows + 2 - count), count)
+            to[...] = at_row(source, jnp.where(top, 4 - count, 0), count)[...]
 
 
 def backward1_kernel(
@@ -281,7 +305,7 @@
 
 def middle_kernel(
     rows, g_ref, edges_ref, hid1_ref, dh1_ref, x1_ref, hid0_ref, x_ref, w_ref,
-    g1_ref, dh0_ref, grad00, grad01, grad10, grad11, s3, t3, u3, v3,
+    g1_ref, dh0_out, grad00, grad01, grad10, grad11, s3, t3, u3, v3, dh0_ref, copied,
 ):
     stack_rows(dh1_ref, range(rows + 2), t3, 0)
     copy_rows(edges_ref, 2, g1_ref, 0)
@@ -301,11 +325,14 @@
         put(v3, row - 1, value)
 
     conv_rows(w_ref[3], u3, 1, rows - 4, dhidden0)
+    copy = pltpu.make_async_copy(dh0_ref, dh0_out, copied)
+    copy.start()
     stack_rows(g_ref, range(rows), s3, 0)
     grad11[...] = grad_rows(s3, 0, hid1_ref, 0, rows)
     grad10[...] = grad_rows(t3, 1, x1_ref, 0, rows)
     grad01[...] = grad_rows(u3, 0, hid0_ref, 0, rows)
     grad00[...] = grad_rows(v3, 0, x_ref, 1, rows - 4)
+    copy.wait()
 
 
 def output_kernel(rows, hid1_ref, x1_ref, w_ref, out_ref, k3, wide):
@@ -320,8 +347,8 @@
 
 def backward0_kernel(
     rows, scale, g1_ref, near_ref, far_ref, hid0_ref, x_ref, xnear_ref, xfar_ref, w_ref, inner00,
-    grad01, grad10, grad11, dh0_ref, next_near, next_far, keep_ref, send_ref,
-    g3, d3, xs, both,
+    grad01, grad10, grad11, dh0_out, next_near, next_far, keep_ref, send_ref,
+    g3, d3, xs, both, dh0_ref, copied,
 ):
     halo_rows(near_ref, far_ref, 1, rows, g3)
     stack_rows(g1_ref, (0, 1, 2, rows - 3, rows - 2, rows - 1), g3, 1)
@@ -334,6 +361,8 @@
 
     for at in (0, rows - 2):
         conv_rows(w_ref[3], g3, at, 2, dhidden0)
+    copy = pltpu.make_async_copy(dh0_ref, dh0_out, copied)
+    copy.start()
     send_edges(dh0_ref, 1, next_near, next_far)
     odd = odd_place()
     copy_rows(x_ref, 3, xs, 1)
@@ -355,6 +384,7 @@
     mine = lax.rem(lax.axis_index("space"), 2)
     keep_ref[...] = both[mine]
     send_ref[...] = both[1 - mine].astype(BF16)
+    copy.wait()
 
 
 def input_grad_kernel(rows, dh0_in, dh0_ref, near_ref, far_ref, g1_ref, w_ref, out_ref, d3, wide):
@@ -397,6 +427,11 @@
     def vmem(n):
         return pltpu.VMEM((n * STACK, width), BF16)
 
+    def plain(n):
+        return pltpu.VMEM((n * CHAN, width), BF16)
+
+    one_copy = pltpu.SemaphoreType.DMA
+
     def neighbours(near, far):
         from_far = lax.ppermute(far, "space", beyond)
         return exchange(near, 1, count), from_far
@@ -428,10 +463,13 @@
         [entry[0], vmem(rows), entry[1]], 6 * row_flops, "g_rows", after=(inner[2],), place=HBM,
     )
     gnear, gfar = neighbours(g_near, g_far)
+    near = call(
+        functools.partial(near_kernel, rows, height), (x, xnear, weights, inner[0], inner[1]),
+        (shape(4),) * 3, [vmem(6)] * 3, 12 * row_flops, "forward_near", after=(g_near,),
+    )
     hid0, x1, hid1 = call(
-        functools.partial(forward_kernel, rows, height), (x, xnear, xfar, weights, *inner),
-        (shape(rows + 2),) * 3, [vmem(rows + 8), vmem(rows + 6), vmem(rows + 4)],
-        24 * row_flops, "forward",
+        functools.partial(far_kernel, rows, height), (x, xfar, weights, *inner, *near),
+        (shape(rows + 2),) * 3, [plain(4)] * 3 + [vmem(6)] * 3, 12 * row_flops, "forward_far",
     )
     g1_near, g1_far, edges, dh1 = call(
         functools.partial(backward1_kernel, rows), (g, gnear, gfar, hid1, g_inner, weights),
@@ -442,7 +480,8 @@
     g1, dh0_inner, *grads = call(
         functools.partial(middle_kernel, rows), (g, edges, hid1, dh1, x1, hid0, x, weights),
         (shape(rows), shape(rows - 4)) + (grad,) * 4,
-        [vmem(rows), vmem(rows + 2), vmem(rows), vmem(rows - 4)], 36 * row_flops, "middle",
+        [vmem(rows), vmem(rows + 2), vmem(rows), vmem(rows - 4), plain(rows - 4), one_copy],
+        36 * row_flops, "middle", to_hbm=(1,),
     )
     dh0, dh0_near, dh0_far, part, send = call(
         functools.partial(backward0_kernel, rows, scale),
@@ -450,8 +489,8 @@
         (shape(4), shape(1), shape(1), jax.ShapeDtypeStruct(half, F32),
          jax.ShapeDtypeStruct(half, BF16)),
         [vmem(rows + 2), vmem(4), pltpu.VMEM((8 * CHAN, width), BF16),
-         pltpu.VMEM((2, *half), F32)],
-        8 * row_flops, "backward0",
+         pltpu.VMEM((2, *half), F32), plain(4), one_copy],
+        8 * row_flops, "backward0", to_hbm=(0,),
     )
 
     part = part + exchange(send, 1, count).astype(F32)

time: 64.7 us -> 64.7 us (level)
  Pallas kernels: 23.2 us -> 26.9 us
  starting transfers between devices: 26.7 us -> 24.8 us
  waiting for transfers between devices: 9.76 us -> 8.78 us
  local copies, waits for them, and re-layouts: 3.79 us -> 3.01 us
    pallas_call x11 -> x12, Pallas kernels: 23.2 us -> 26.9 us  [call(): pl.pallas_call(kernel, out_shape=outs, in_specs=[ANY] * len(after) + [pla...]
    ppermute x11, starting transfers between devices: 23.8 us -> 21.7 us  [exchange(): return lax.ppermute(value, 'space', [(d, d ^ mask) for d in range(count)])]
    ppermute x11, waiting for transfers between devices: 9.75 us -> 8.77 us  [exchange(): return lax.ppermute(value, 'space', [(d, d ^ mask) for d in range(count)])]
    unnamed x22, local copies, waits for them, and re-layouts: 3.79 us -> 3.01 us
  transfers between devices with their start and end apart: 15 -> 15, of which waited for: 7 -> 7; matrix products, arithmetic and copies ran while one was open for 0% -> 0% of each run, Pallas kernels for 27% -> 32%
where the time goes in v5:
time: 64.7 us; the launch traced here: 64.5 us
  Pallas kernels  26.9 us (42%)
  starting transfers between devices  24.8 us (38%)
  waiting for transfers between devices  8.78 us (14%)
  local copies, waits for them, and re-layouts  3.01 us (5%)
  between operations  0.92 us (1%)
    pallas_call x12, Pallas kernels, call(): pl.pallas_call(kernel, out_shape=outs, in_specs=[ANY] * len(after) + [pla...  26.9 us
    ppermute x11, starting transfers between devices, exchange(): return lax.ppermute(value, 'space', [(d, d ^ mask) for d in range(count)])  21.7 us
    ppermute x11, waiting for transfers between devices, exchange(): return lax.ppermute(value, 'space', [(d, d ^ mask) for d in range(count)])  8.77 us
    ppermute x4, starting transfers between devices, neighbours(): from_far = lax.ppermute(far, 'space', beyond)  3.06 us
    unnamed x22, local copies, waits for them, and re-layouts  3.01 us
  transfers between devices with their start and end apart: 15, of which 7 were waited for; matrix products, arithmetic and copies ran while one was open for 0% of the time, Pallas kernels for 32%

profile of v5, /device:TPU:0, one launch (start us, length us, event | category | flops | bytes accessed | tf_op | source)
XLA Modules:
  0.0 64.5 jit_solution(839438577398635043)
XLA Ops:
  0.6 1.2 %copy-done = bf16[64,8,1024]{2,1,0:T(8,128)(2,1)S(1)} copy-done((bf16[64,8,1024]{2,1,0:T(8,128)(2,1)S(1)}, bf16[64,8,1024]{2,1,0:T(8,128)(2,1)}, u32[]{:S(2)}) %copy-start) | copy-done | bytes 1048600
  3.7 1.0 %copy-done.1 = bf16[2,2,64,576]{3,2,1,0:T(8,128)(2,1)S(1)} copy-done((bf16[2,2,64,576]{3,2,1,0:T(8,128)(2,1)S(1)}, bf16[2,2,64,576]{3,2,1,0:T(8,128)(2,1)}, u32[]{:S(2)}) %copy-start.1) | copy-done | bytes 294936
  5.4 1.7 %inner.1 = (bf16[384,1024]{1,0:T(8,128)(2,1)S(1)}, bf16[256,1024]{1,0:T(8,128)(2,1)S(1)}, bf16[128,1024]{1,0:T(8,128)(2,1)S(1)}) custom-call(bf16[512,1024]{1,0:T(8,128)(2,1)S(1)} %get-tuple-element.42.refs_0_.refs_1_.refs_6_.refs_4_, bf16[8,128,768]{2,1,0:T(8,128)(2,1)S(1)} %weights.1.refs_1_.refs_2_.refs_3_.refs_5_.refs_7_.refs_6_), custom_call_target="tpu_custom_call" | custom-call | flops 3623878656 | bytes 4194304 | tf_op jit(solution)/shard_map/inner/pallas_call | solution.py:28
  7.1 1.6 %g_rows.1 = (bf16[512,1024]{1,0:T(8,128)(2,1)S(1)}, bf16[128,1024]{1,0:T(8,128)(2,1)S(1)}, bf16[128,1024]{1,0:T(8,128)(2,1)S(1)}, f32[384,1024]{1,0:T(8,128)S(1)}) custom-call(bf16[128,1024]{1,0:T(8,128)(2,1)S(1)} %get-tuple-element.44.refs_0_.refs_5_, bf16[64,8,1024]{2,1,0:T(8,128)(2,1)S(1)} %copy-done.2, ...), custom_call_target="tpu_custom_call" | custom-call | flops 1811939328 | bytes 5767168 | tf_op jit(solution)/shard_map/g_rows/pallas_call | solution.py:28
  8.7 3.9 %collective-permute-start = (bf16[128,1024]{1,0:T(8,128)(2,1)S(1)}, bf16[128,1024]{1,0:T(8,128)(2,1)S(1)}, u32[]{:S(2)}, u32[]{:S(2)}) collective-permute-start(bf16[128,1024]{1,0:T(8,128)(2,1)S(1)} %get-tuple-element.46.refs_0_), channel_id=1, source_target_pairs={{0,1},{1,0},{2,3},{3,2},{4,5},{5,4},{6,7},{7,6},{8,9},{9,8},{10,11... | collective-permute-start | bytes 786440 | tf_op jit(solution)/shard_map/ppermute | solution.py:412
  13.4 3.1 %forward_near.1 = (bf16[256,1024]{1,0:T(8,128)(2,1)S(1)}, bf16[256,1024]{1,0:T(8,128)(2,1)S(1)}, bf16[256,1024]{1,0:T(8,128)(2,1)S(1)}) custom-call(bf16[128,1024]{1,0:T(8,128)(2,1)S(1)} %get-tuple-element.46.refs_0_, bf16[512,1024]{1,0:T(8,128)(2,1)S(1)} %get-tuple-element.42.refs_0_.refs_1_.refs_6_.refs_4_, ...), custom_call_target="tpu_custom_call" | custom-call | flops 3623878656 | bytes 6029312 | tf_op jit(solution)/shard_map/forward_near/pallas_call | solution.py:28
  16.6 3.3 %forward_far.1 = (bf16[640,1024]{1,0:T(8,128)(2,1)S(1)}, bf16[640,1024]{1,0:T(8,128)(2,1)S(1)}, bf16[640,1024]{1,0:T(8,128)(2,1)S(1)}) custom-call(bf16[512,1024]{1,0:T(8,128)(2,1)S(1)} %get-tuple-element.42.refs_0_.refs_1_.refs_6_.refs_4_, bf16[256,1024]{1,0:T(8,128)(2,1)S(1)} %collective-permute-done.2.refs_1_.refs_6_, ...), custom_call_target="tpu_custom_call" | custom-call | flops 3623878656 | bytes 10223616 | tf_op jit(solution)/shard_map/forward_far/pallas_call | solution.py:28
  19.9 2.3 %backward1.1 = (bf16[64,1024]{1,0:T(8,128)(2,1)S(1)}, bf16[64,1024]{1,0:T(8,128)(2,1)S(1)}, bf16[256,1024]{1,0:T(8,128)(2,1)S(1)}, bf16[640,1024]{1,0:T(8,128)(2,1)S(1)}) custom-call(bf16[512,1024]{1,0:T(8,128)(2,1)S(1)} %get-tuple-element.45.refs_0_, bf16[128,1024]{1,0:T(8,128)(2,1)S(1)} %collective-permute-done.refs_1_, ...), custom_call_target="tpu_custom_call" | custom-call | flops 2415919104 | bytes 8126464 | tf_op jit(solution)/shard_map/backward1/pallas_call | solution.py:28
  22.2 5.5 %collective-permute-start.4 = (bf16[64,1024]{1,0:T(8,128)(2,1)S(1)}, bf16[64,1024]{1,0:T(8,128)(2,1)S(1)}, u32[]{:S(2)}, u32[]{:S(2)}) collective-permute-start(bf16[64,1024]{1,0:T(8,128)(2,1)S(1)} %get-tuple-element.61), channel_id=1, source_target_pairs={{0,1},{1,0},{2,3},{3,2},{4,5},{5,4},{6,7},{7,6},{8,9},{9,8},{10,11... | collective-permute-start | bytes 393224 | tf_op jit(solution)/shard_map/ppermute | solution.py:412
  28.6 5.3 %middle.1 = (bf16[512,1024]{1,0:T(8,128)(2,1)S(1)}, bf16[256,1024]{1,0:T(8,128)(2,1)S(1)}, f32[192,192]{1,0:T(8,128)S(1)}, f32[192,192]{1,0:T(8,128)S(1)}, f32[1...) custom-call(bf16[512,1024]{1,0:T(8,128)(2,1)S(1)} %get-tuple-element.45.refs_0_, ...), custom_call_target="tpu_custom_call" | custom-call | flops 10871635968 | bytes 11599872 | tf_op jit(solution)/shard_map/middle/pallas_call | solution.py:28
  33.9 2.1 %backward0.1 = (bf16[256,1024]{1,0:T(8,128)(2,1)S(1)}, bf16[64,1024]{1,0:T(8,128)(2,1)S(1)}, bf16[64,1024]{1,0:T(8,128)(2,1)S(1)}, f32[64,1152]{1,0:T(8,128)S(1)}, bf16[64,1152]{1,0:T(8,128)(2,1)S(1)}) custom-call(bf16[512,1024]{1,0:T(8,128)(2,1)S(1)} %get-tuple-element.60.refs_0_.refs_5_, bf16[64,1024]{1,0:T(8,128)(2,1)S(1)} %collective-permute-done.4.refs_1_, ...), custom_call_target="tpu_custom_call" | custom-call | flops 2415919104 | bytes 8110080 | tf_op jit(solution)/shard_map/backward0/pallas_call | solution.py:28
  36.8 3.8 %collective-permute-start.6 = (bf16[64,1152]{1,0:T(8,128)(2,1)S(1)}, bf16[64,1152]{1,0:T(8,128)(2,1)S(1)}, u32[]{:S(2)}, u32[]{:S(2)}) collective-permute-start(bf16[64,1152]{1,0:T(8,128)(2,1)S(1)} %get-tuple-element.68), channel_id=1, source_target_pairs={{0,1},{1,0},{2,3},{3,2},{4,5},{5,4},{6,7},{7,6},{8,9},{9,8},{10,11... | collective-permute-start | bytes 442376 | tf_op jit(solution)/shard_map/ppermute | solution.py:412
  40.6 1.0 %collective-permute-done.6 = bf16[64,1152]{1,0:T(8,128)(2,1)S(1)} collective-permute-done((bf16[64,1152]{1,0:T(8,128)(2,1)S(1)}, bf16[64,1152]{1,0:T(8,128)(2,1)S(1)}, u32[]{:S(2)}, u32[]{:S(2)}) %collective-permute-start.6) | collective-permute-done | bytes 147488 | tf_op jit(solution)/shard_map/ppermute | solution.py:412
  41.6 2.1 %collective-permute-start.7 = (bf16[32,1152]{1,0:T(8,128)(2,1)S(1)}, bf16[32,1152]{1,0:T(8,128)(2,1)S(1)}, u32[]{:S(2)}, u32[]{:S(2)}) collective-permute-start(bf16[32,1152]{1,0:T(8,128)(2,1)S(1)} %select_convert_fusion), channel_id=1, source_target_pairs={{0,2},{1,3},{2,0},{3,1},{4,6},{5,7},{6,4},{7,5},{8,10},{9,11},{10,... | collective-permute-start | bytes 221192 | tf_op jit(solution)/shard_map/ppermute | solution.py:412
  44.4 2.0 %collective-permute-done.7 = bf16[32,1152]{1,0:T(8,128)(2,1)S(1)} collective-permute-done((bf16[32,1152]{1,0:T(8,128)(2,1)S(1)}, bf16[32,1152]{1,0:T(8,128)(2,1)S(1)}, u32[]{:S(2)}, u32[]{:S(2)}) %collective-permute-start.7) | collective-permute-done | bytes 73760 | tf_op jit(solution)/shard_map/ppermute | solution.py:412
  46.5 3.5 %collective-permute-start.10 = (bf16[32,1152]{1,0:T(8,128)(2,1)S(1)}, bf16[32,1152]{1,0:T(8,128)(2,1)S(1)}, u32[]{:S(2)}, u32[]{:S(2)}) collective-permute-start(bf16[32,1152]{1,0:T(8,128)(2,1)S(1)} %add_convert_fusion.1.refs_0_), channel_id=1, source_target_pairs={{0,12},{1,13},{2,14},{3,15},{4,8},{5,9},{6,10},{7,11},{8,4},{9,5},... | collective-permute-start | bytes 221192 | tf_op jit(solution)/shard_map/ppermute | solution.py:412
  50.0 1.0 %collective-permute-start.9 = (bf16[32,1152]{1,0:T(8,128)(2,1)S(1)}, bf16[32,1152]{1,0:T(8,128)(2,1)S(1)}, u32[]{:S(2)}, u32[]{:S(2)}) collective-permute-start(bf16[32,1152]{1,0:T(8,128)(2,1)S(1)} %add_convert_fusion.1.refs_0_), channel_id=1, source_target_pairs={{0,8},{1,9},{2,10},{3,11},{4,12},{5,13},{6,14},{7,15},{8,0},{9,1},... | collective-permute-start | bytes 221192 | tf_op jit(solution)/shard_map/ppermute | solution.py:412
  51.0 2.8 %input_grad.1 = bf16[64,8,1024]{2,1,0:T(8,128)(2,1)} custom-call(bf16[32,1152]{1,0:T(8,128)(2,1)S(1)} %add_convert_fusion.1.refs_0_, bf16[256,1024]{1,0:T(8,128)(2,1)S(1)} %copy-done.10, bf16[256,1024]{1,0:T(8,128)(2,1)S(1)} %copy-done.6, bf16[64,1024]{1,0:T(8,128)(2,1)S(1)} %collective-permute-done.11.refs_3_, ...), custom_call_target="tpu_custom_call" | custom-call | flops 2415919104 | bytes 4980736 | tf_op jit(solution)/shard_map/input_grad/pallas_call | solution.py:28
  53.8 1.3 %collective-permute-done.10 = bf16[32,1152]{1,0:T(8,128)(2,1)S(1)} collective-permute-done((bf16[32,1152]{1,0:T(8,128)(2,1)S(1)}, bf16[32,1152]{1,0:T(8,128)(2,1)S(1)}, u32[]{:S(2)}, u32[]{:S(2)}) %collective-permute-start.10) | collective-permute-done | bytes 73760 | tf_op jit(solution)/shard_map/ppermute | solution.py:412
  55.3 2.2 %collective-permute-done.9 = bf16[32,1152]{1,0:T(8,128)(2,1)S(1)} collective-permute-done((bf16[32,1152]{1,0:T(8,128)(2,1)S(1)}, bf16[32,1152]{1,0:T(8,128)(2,1)S(1)}, u32[]{:S(2)}, u32[]{:S(2)}) %collective-permute-start.9) | collective-permute-done | bytes 73760 | tf_op jit(solution)/shard_map/ppermute | solution.py:412
  57.6 1.3 %collective-permute-start.13 = (bf16[32,1152]{1,0:T(8,128)(2,1)S(1)}, bf16[32,1152]{1,0:T(8,128)(2,1)S(1)}, u32[]{:S(2)}, u32[]{:S(2)}) collective-permute-start(bf16[32,1152]{1,0:T(8,128)(2,1)S(1)} %add_convert_fusion.refs_0_), channel_id=1, source_target_pairs={{0,2},{1,3},{2,0},{3,1},{4,6},{5,7},{6,4},{7,5},{8,10},{9,11},{10,... | collective-permute-start | bytes 221192 | tf_op jit(solution)/shard_map/ppermute | solution.py:412
  59.0 2.5 %output.1 = bf16[64,8,1024]{2,1,0:T(8,128)(2,1)} custom-call(bf16[32,1152]{1,0:T(8,128)(2,1)S(1)} %add_convert_fusion.refs_0_, bf16[640,1024]{1,0:T(8,128)(2,1)S(1)} %copy-done.4, bf16[640,1024]{1,0:T(8,128)(2,1)S(1)} %copy-done.8, bf16[8,128,768]{2,1,0:T(8,128)(2,1)S(1)} %weights.1.refs_1_.refs_2_.refs_3_.refs_5_.refs_7_.refs_6_), custom_call_target="tpu_custom_call" | custom-call | flops 2415919104 | bytes 5242880 | tf_op jit(solution)/shard_map/output/pallas_call | solution.py:28
  62.2 1.4 %collective-permute-done.14.refs_1_ = bf16[64,1152]{1,0:T(8,128)(2,1)S(1)} collective-permute-done((bf16[64,1152]{1,0:T(8,128)(2,1)S(1)}, bf16[64,1152]{1,0:T(8,128)(2,1)S(1)}, u32[]{:S(2)}, u32[]{:S(2)}) %collective-permute-start.14) | collective-permute-done | bytes 147488 | tf_op jit(solution)/shard_map/ppermute | solution.py:412
  63.5 1.0 %gathered.1 = f32[2,2,64,576]{3,2,1,0:T(8,128)} custom-call(bf16[64,1152]{1,0:T(8,128)(2,1)S(1)} %maximum_select_fusion.refs_0_, bf16[64,1152]{1,0:T(8,128)(2,1)S(1)} %collective-permute-done.14.refs_1_), custom_call_target="tpu_custom_call" | custom-call | bytes 884736 | tf_op jit(solution)/shard_map/gathered/pallas_call | solution.py:28
  (45 shorter events, 6.8 us)
Async XLA Ops:
  0.6 1.2 %copy-start = (bf16[64,8,1024]{2,1,0:T(8,128)(2,1)S(1)}, bf16[64,8,1024]{2,1,0:T(8,128)(2,1)}, u32[]{:S(2)}) copy-start(bf16[64,8,1024]{2,1,0:T(8,128)(2,1)} %refs_0_.1) | copy-start | bytes 3145732
  2.5 10.9 %collective-permute-start.3 = (bf16[256,1024]{1,0:T(8,128)(2,1)S(1)}, bf16[256,1024]{1,0:T(8,128)(2,1)S(1)}, u32[]{:S(2)}, u32[]{:S(2)}) collective-permute-start(bf16[256,1024]{1,0:T(8,128)(2,1)S(1)} %get-tuple-element.50), channel_id=1, source_target_pairs={{0,1},{1,0},{2,3},{3,2},{4,5},{5,4},{6,7},{7,6},{8,9},{9,8},{10,11... | collective-permute-start | bytes 1572872 | tf_op jit(solution)/shard_map/ppermute | solution.py:412
  3.0 13.6 %collective-permute-start.2 = (bf16[256,1024]{1,0:T(8,128)(2,1)S(1)}, bf16[256,1024]{1,0:T(8,128)(2,1)S(1)}, u32[]{:S(2)}, u32[]{:S(2)}) collective-permute-start(bf16[256,1024]{1,0:T(8,128)(2,1)S(1)} %get-tuple-element.43.refs_0_), channel_id=1, source_target_pairs={{1,2},{3,4},{5,6},{7,8},{9,10},{11,12},{13,14},{2,1},{4,3},{6,5},{... | collective-permute-start | bytes 1572872 | tf_op jit(solution)/shard_map/ppermute | solution.py:436
  5.4 1.7 %copy-start.2 = (bf16[64,8,1024]{2,1,0:T(8,128)(2,1)S(1)}, bf16[64,8,1024]{2,1,0:T(8,128)(2,1)}, u32[]{:S(2)}) copy-start(bf16[64,8,1024]{2,1,0:T(8,128)(2,1)} %refs_1_.3) | copy-start | bytes 3145732
  8.7 11.3 %collective-permute-start = (bf16[128,1024]{1,0:T(8,128)(2,1)S(1)}, bf16[128,1024]{1,0:T(8,128)(2,1)S(1)}, u32[]{:S(2)}, u32[]{:S(2)}) collective-permute-start(bf16[128,1024]{1,0:T(8,128)(2,1)S(1)} %get-tuple-element.46.refs_0_), channel_id=1, source_target_pairs={{0,1},{1,0},{2,3},{3,2},{4,5},{5,4},{6,7},{7,6},{8,9},{9,8},{10,11... | collective-permute-start | bytes 786440 | tf_op jit(solution)/shard_map/ppermute | solution.py:412
  12.6 7.4 %collective-permute-start.1 = (bf16[128,1024]{1,0:T(8,128)(2,1)S(1)}, bf16[128,1024]{1,0:T(8,128)(2,1)S(1)}, u32[]{:S(2)}, u32[]{:S(2)}) collective-permute-start(bf16[128,1024]{1,0:T(8,128)(2,1)S(1)} %get-tuple-element.47), channel_id=1, source_target_pairs={{1,2},{3,4},{5,6},{7,8},{9,10},{11,12},{13,14},{2,1},{4,3},{6,5},{... | collective-permute-start | bytes 786440 | tf_op jit(solution)/shard_map/ppermute | solution.py:436
  19.9 8.7 %copy-start.3 = (bf16[640,1024]{1,0:T(8,128)(2,1)}, bf16[640,1024]{1,0:T(8,128)(2,1)S(1)}, u32[]{:S(2)}) copy-start(bf16[640,1024]{1,0:T(8,128)(2,1)S(1)} %get-tuple-element.54.refs_3_.refs_2_.refs_1_) | copy-start | bytes 3932164
  19.9 8.7 %copy-start.7 = (bf16[640,1024]{1,0:T(8,128)(2,1)}, bf16[640,1024]{1,0:T(8,128)(2,1)S(1)}, u32[]{:S(2)}) copy-start(bf16[640,1024]{1,0:T(8,128)(2,1)S(1)} %get-tuple-element.58.refs_4_.refs_2_) | copy-start | bytes 3932164
  22.2 11.7 %collective-permute-start.4 = (bf16[64,1024]{1,0:T(8,128)(2,1)S(1)}, bf16[64,1024]{1,0:T(8,128)(2,1)S(1)}, u32[]{:S(2)}, u32[]{:S(2)}) collective-permute-start(bf16[64,1024]{1,0:T(8,128)(2,1)S(1)} %get-tuple-element.61), channel_id=1, source_target_pairs={{0,1},{1,0},{2,3},{3,2},{4,5},{5,4},{6,7},{7,6},{8,9},{9,8},{10,11... | collective-permute-start | bytes 393224 | tf_op jit(solution)/shard_map/ppermute | solution.py:412
  27.7 6.2 %collective-permute-start.5 = (bf16[64,1024]{1,0:T(8,128)(2,1)S(1)}, bf16[64,1024]{1,0:T(8,128)(2,1)S(1)}, u32[]{:S(2)}, u32[]{:S(2)}) collective-permute-start(bf16[64,1024]{1,0:T(8,128)(2,1)S(1)} %get-tuple-element.62), channel_id=1, source_target_pairs={{1,2},{3,4},{5,6},{7,8},{9,10},{11,12},{13,14},{2,1},{4,3},{6,5},{... | collective-permute-start | bytes 393224 | tf_op jit(solution)/shard_map/ppermute | solution.py:436
  33.9 2.1 %copy-start.9 = (bf16[256,1024]{1,0:T(8,128)(2,1)}, bf16[256,1024]{1,0:T(8,128)(2,1)S(1)}, u32[]{:S(2)}) copy-start(bf16[256,1024]{1,0:T(8,128)(2,1)S(1)} %get-tuple-element.69.refs_1_) | copy-start | bytes 1572868
  36.8 4.8 %collective-permute-start.6 = (bf16[64,1152]{1,0:T(8,128)(2,1)S(1)}, bf16[64,1152]{1,0:T(8,128)(2,1)S(1)}, u32[]{:S(2)}, u32[]{:S(2)}) collective-permute-start(bf16[64,1152]{1,0:T(8,128)(2,1)S(1)} %get-tuple-element.68), channel_id=1, source_target_pairs={{0,1},{1,0},{2,3},{3,2},{4,5},{5,4},{6,7},{7,6},{8,9},{9,8},{10,11... | collective-permute-start | bytes 442376 | tf_op jit(solution)/shard_map/ppermute | solution.py:412
  40.6 10.4 %copy-start.6 = (bf16[256,1024]{1,0:T(8,128)(2,1)S(1)}, bf16[256,1024]{1,0:T(8,128)(2,1)}, u32[]{:S(2)}) copy-start(bf16[256,1024]{1,0:T(8,128)(2,1)} %copy-done.5) | copy-start | bytes 1572868
  40.6 10.4 %copy-start.10 = (bf16[256,1024]{1,0:T(8,128)(2,1)S(1)}, bf16[256,1024]{1,0:T(8,128)(2,1)}, u32[]{:S(2)}) copy-start(bf16[256,1024]{1,0:T(8,128)(2,1)} %copy-done.9) | copy-start | bytes 1572868
  41.6 4.8 %collective-permute-start.7 = (bf16[32,1152]{1,0:T(8,128)(2,1)S(1)}, bf16[32,1152]{1,0:T(8,128)(2,1)S(1)}, u32[]{:S(2)}, u32[]{:S(2)}) collective-permute-start(bf16[32,1152]{1,0:T(8,128)(2,1)S(1)} %select_convert_fusion), channel_id=1, source_target_pairs={{0,2},{1,3},{2,0},{3,1},{4,6},{5,7},{6,4},{7,5},{8,10},{9,11},{10,... | collective-permute-start | bytes 221192 | tf_op jit(solution)/shard_map/ppermute | solution.py:412
  43.7 7.3 %collective-permute-start.11 = (bf16[64,1024]{1,0:T(8,128)(2,1)S(1)}, bf16[64,1024]{1,0:T(8,128)(2,1)S(1)}, u32[]{:S(2)}, u32[]{:S(2)}) collective-permute-start(bf16[64,1024]{1,0:T(8,128)(2,1)S(1)} %get-tuple-element.73), channel_id=1, source_target_pairs={{0,1},{1,0},{2,3},{3,2},{4,5},{5,4},{6,7},{7,6},{8,9},{9,8},{10,11... | collective-permute-start | bytes 393224 | tf_op jit(solution)/shard_map/ppermute | solution.py:412
  43.8 7.2 %collective-permute-start.12 = (bf16[64,1024]{1,0:T(8,128)(2,1)S(1)}, bf16[64,1024]{1,0:T(8,128)(2,1)S(1)}, u32[]{:S(2)}, u32[]{:S(2)}) collective-permute-start(bf16[64,1024]{1,0:T(8,128)(2,1)S(1)} %get-tuple-element.74), channel_id=1, source_target_pairs={{1,2},{3,4},{5,6},{7,8},{9,10},{11,12},{13,14},{2,1},{4,3},{6,5},{... | collective-permute-start | bytes 393224 | tf_op jit(solution)/shard_map/ppermute | solution.py:436
  46.5 8.6 %collective-permute-start.10 = (bf16[32,1152]{1,0:T(8,128)(2,1)S(1)}, bf16[32,1152]{1,0:T(8,128)(2,1)S(1)}, u32[]{:S(2)}, u32[]{:S(2)}) collective-permute-start(bf16[32,1152]{1,0:T(8,128)(2,1)S(1)} %add_convert_fusion.1.refs_0_), channel_id=1, source_target_pairs={{0,12},{1,13},{2,14},{3,15},{4,8},{5,9},{6,10},{7,11},{8,4},{9,5},... | collective-permute-start | bytes 221192 | tf_op jit(solution)/shard_map/ppermute | solution.py:412
  50.0 5.4 %collective-permute-start.8 = (bf16[32,1152]{1,0:T(8,128)(2,1)S(1)}, bf16[32,1152]{1,0:T(8,128)(2,1)S(1)}, u32[]{:S(2)}, u32[]{:S(2)}) collective-permute-start(bf16[32,1152]{1,0:T(8,128)(2,1)S(1)} %add_convert_fusion.1.refs_0_), channel_id=1, source_target_pairs={{0,4},{1,5},{2,6},{3,7},{4,0},{5,1},{6,2},{7,3},{8,12},{9,13},{10,... | collective-permute-start | bytes 221192 | tf_op jit(solution)/shard_map/ppermute | solution.py:412
  50.0 7.6 %collective-permute-start.9 = (bf16[32,1152]{1,0:T(8,128)(2,1)S(1)}, bf16[32,1152]{1,0:T(8,128)(2,1)S(1)}, u32[]{:S(2)}, u32[]{:S(2)}) collective-permute-start(bf16[32,1152]{1,0:T(8,128)(2,1)S(1)} %add_convert_fusion.1.refs_0_), channel_id=1, source_target_pairs={{0,8},{1,9},{2,10},{3,11},{4,12},{5,13},{6,14},{7,15},{8,0},{9,1},... | collective-permute-start | bytes 221192 | tf_op jit(solution)/shard_map/ppermute | solution.py:412
  51.0 8.0 %copy-start.4 = (bf16[640,1024]{1,0:T(8,128)(2,1)S(1)}, bf16[640,1024]{1,0:T(8,128)(2,1)}, u32[]{:S(2)}) copy-start(bf16[640,1024]{1,0:T(8,128)(2,1)} %copy-done.3) | copy-start | bytes 3932164
  51.0 8.0 %copy-start.8 = (bf16[640,1024]{1,0:T(8,128)(2,1)S(1)}, bf16[640,1024]{1,0:T(8,128)(2,1)}, u32[]{:S(2)}) copy-start(bf16[640,1024]{1,0:T(8,128)(2,1)} %copy-done.7) | copy-start | bytes 3932164
  57.6 4.4 %collective-permute-start.13 = (bf16[32,1152]{1,0:T(8,128)(2,1)S(1)}, bf16[32,1152]{1,0:T(8,128)(2,1)S(1)}, u32[]{:S(2)}, u32[]{:S(2)}) collective-permute-start(bf16[32,1152]{1,0:T(8,128)(2,1)S(1)} %add_convert_fusion.refs_0_), channel_id=1, source_target_pairs={{0,2},{1,3},{2,0},{3,1},{4,6},{5,7},{6,4},{7,5},{8,10},{9,11},{10,... | collective-permute-start | bytes 221192 | tf_op jit(solution)/shard_map/ppermute | solution.py:412
  62.1 1.4 %collective-permute-start.14 = (bf16[64,1152]{1,0:T(8,128)(2,1)S(1)}, bf16[64,1152]{1,0:T(8,128)(2,1)S(1)}, u32[]{:S(2)}, u32[]{:S(2)}) collective-permute-start(bf16[64,1152]{1,0:T(8,128)(2,1)S(1)} %maximum_select_fusion.refs_0_), channel_id=1, source_target_pairs={{0,1},{1,0},{2,3},{3,2},{4,5},{5,4},{6,7},{7,6},{8,9},{9,8},{10,11... | collective-permute-start | bytes 442376 | tf_op jit(solution)/shard_map/ppermute | solution.py:412
  (2 other events, 1.8 us)

commit v6 on v5

--- a/solution.py
+++ b/solution.py
@@ -18,7 +18,7 @@
 PIECES = 4
 
 
-def call(body, operands, outs, scratch, flops, name, after=(), place=VMEM, to_hbm=()):
+def call(body, operands, outs, scratch, flops, name, after=(), place=VMEM):
     nbytes = sum(v.size * v.dtype.itemsize for v in (*operands, *outs))
     held = sum(math.prod(v.shape) * v.dtype.itemsize for v in scratch if v.dtype in (F32, BF16))
 
@@ -29,7 +29,7 @@
         kernel,
         out_shape=outs,
         in_specs=[ANY] * len(after) + [place] + [VMEM] * (len(operands) - 1),
-        out_specs=[HBM if i in to_hbm else VMEM for i in range(len(outs))],
+        out_specs=[VMEM] * len(outs),
         scratch_shapes=scratch,
         compiler_params=pltpu.CompilerParams(vmem_limit_bytes=nbytes + held + (6 << 20)),
         cost_estimate=pl.CostEstimate(flops=flops, bytes_accessed=nbytes, transcendentals=0),
@@ -207,45 +207,42 @@
     conv_rows(w_ref[4], y3, 0, rows - 6, hidden1)
 
 
-def at_row(ref, row, count=1):
-    return ref.at[pl.ds(pl.multiple_of(row * CHAN, CHAN), count * CHAN), :]
-
-
 def side_rows(rows, height, top, x_ref, halo_ref, w_ref, hid0_in, x1_in, hid0, x1, hid1, x3, h3, y3):
     first = lax.axis_index("space") * rows
-    own = jnp.where(top, 0, 2)
-    rest = jnp.where(top, 4, 0)
+    own, rest = (0, 4) if top else (2, 0)
 
     def inside(row, value):
+        if 0 <= row < rows:
+            return value
         keep = jnp.logical_and(first + row >= 0, first + row < height)
         return jnp.where(keep, value, 0.0)
 
     for i in range(4):
-        put_at(x3, own + i, one(halo_ref, i))
+        put(x3, own + i, one(halo_ref, i))
     for i in range(2):
-        put_at(x3, rest + i, at_row(x_ref, jnp.where(top, 0, rows - 2) + i)[...])
-        put_at(h3, rest + i, at_row(hid0_in, jnp.where(top, 0, rows - 4) + i)[...])
-        put_at(y3, rest + i, at_row(x1_in, jnp.where(top, 0, rows - 6) + i)[...])
+        put(x3, rest + i, one(x_ref, (0 if top else rows - 2) + i))
+        put(h3, rest + i, one(hid0_in, (0 if top else rows - 4) + i))
+        put(y3, rest + i, one(x1_in, (0 if top else rows - 6) + i))
 
     def hidden0(row, total):
-        at = jnp.where(top, -3, rows - 1) + row
+        at = (-3 if top else rows - 1) + row
         value = inside(at, jnp.maximum(total, 0.0)).astype(BF16)
         hid0[row * CHAN : (row + 1) * CHAN, :] = value
-        put_at(h3, own + row, value)
+        put(h3, own + row, value)
 
     conv_rows(w_ref[0], x3, 0, 4, hidden0)
 
     def next_x(row, total):
-        at = jnp.where(top, -2, rows - 2) + row
-        start = pl.multiple_of((jnp.where(top, 2, 0) + row) * STACK + CHAN, CHAN)
-        value = inside(at, x3[pl.ds(start, CHAN), :].astype(F32) + total).astype(BF16)
+        at = (-2 if top else rows - 2) + row
+        value = middle(x3, (2 if top else 0) + row).astype(F32) + total
+        value = inside(at, value).astype(BF16)
         x1[row * CHAN : (row + 1) * CHAN, :] = value
-        put_at(y3, own + row, value)
+        put(y3, own + row, value)
 
     conv_rows(w_ref[2], h3, 0, 4, next_x)
 
     def hidden1(row, total):
-        at = jnp.where(top, -1, rows - 3) + row
+        at = (-1 if top else rows - 3) + row
         value = inside(at, jnp.maximum(total, 0.0)).astype(BF16)
         hid1[row * CHAN : (row + 1) * CHAN, :] = value
 
@@ -253,26 +250,31 @@
 
 
 def near_kernel(rows, height, *refs):
-    side_rows(rows, height, odd_place(), *refs)
+    odd = odd_place()
+    for top in (True, False):
+        pl.when(odd == top)(functools.partial(side_rows, rows, height, top, *refs))
 
 
 def far_kernel(
     rows, height, x_ref, far_ref, w_ref, hid0_in, x1_in, hid1_in, near0, near1, near2,
     hid0_ref, x1_ref, hid1_ref, far0, far1, far2, *scratch,
 ):
-    odd = odd_place()
-    side_rows(
-        rows, height, jnp.logical_not(odd), x_ref, far_ref, w_ref, hid0_in, x1_in, far0, far1, far2,
-        *scratch,
-    )
+    def far_side(top):
+        side_rows(
+            rows, height, top, x_ref, far_ref, w_ref, hid0_in, x1_in, far0, far1, far2, *scratch
+        )
+        for edge, hid0, x1, hid1 in ((top, far0, far1, far2), (not top, near0, near1, near2)):
+            for target, source, count in ((hid0_ref, hid0, 2), (x1_ref, x1, 3), (hid1_ref, hid1, 4)):
+                to = 0 if edge else rows + 2 - count
+                at = 4 - count if edge else 0
+                target[to * CHAN : (to + count) * CHAN, :] = source[at * CHAN : (at + count) * CHAN, :]
+
     copy_rows(hid0_in, rows - 2, hid0_ref, 2)
     copy_rows(x1_in, rows - 4, x1_ref, 3)
     copy_rows(hid1_in, rows - 6, hid1_ref, 4)
-    sides = ((odd, near0, near1, near2), (jnp.logical_not(odd), far0, far1, far2))
-    for top, hid0, x1, hid1 in sides:
-        for target, source, count in ((hid0_ref, hid0, 2), (x1_ref, x1, 3), (hid1_ref, hid1, 4)):
-            to = at_row(target, jnp.where(top, 0, rows + 2 - count), count)
-            to[...] = at_row(source, jnp.where(top, 4 - count, 0), count)[...]
+    odd = odd_place()
+    for top in (True, False):
+        pl.when(odd != top)(functools.partial(far_side, top))
 
 
 def backward1_kernel(
@@ -305,7 +307,7 @@
 
 def middle_kernel(
     rows, g_ref, edges_ref, hid1_ref, dh1_ref, x1_ref, hid0_ref, x_ref, w_ref,
-    g1_ref, dh0_out, grad00, grad01, grad10, grad11, s3, t3, u3, v3, dh0_ref, copied,
+    g1_ref, dh0_ref, grad00, grad01, grad10, grad11, s3, t3, u3, v3,
 ):
     stack_rows(dh1_ref, range(rows + 2), t3, 0)
     copy_rows(edges_ref, 2, g1_ref, 0)
@@ -325,14 +327,11 @@
         put(v3, row - 1, value)
 
     conv_rows(w_ref[3], u3, 1, rows - 4, dhidden0)
-    copy = pltpu.make_async_copy(dh0_ref, dh0_out, copied)
-    copy.start()
     stack_rows(g_ref, range(rows), s3, 0)
     grad11[...] = grad_rows(s3, 0, hid1_ref, 0, rows)
     grad10[...] = grad_rows(t3, 1, x1_ref, 0, rows)
     grad01[...] = grad_rows(u3, 0, hid0_ref, 0, rows)
     grad00[...] = grad_rows(v3, 0, x_ref, 1, rows - 4)
-    copy.wait()
 
 
 def output_kernel(rows, hid1_ref, x1_ref, w_ref, out_ref, k3, wide):
@@ -347,8 +346,8 @@
 
 def backward0_kernel(
     rows, scale, g1_ref, near_ref, far_ref, hid0_ref, x_ref, xnear_ref, xfar_ref, w_ref, inner00,
-    grad01, grad10, grad11, dh0_out, next_near, next_far, keep_ref, send_ref,
-    g3, d3, xs, both, dh0_ref, copied,
+    grad01, grad10, grad11, dh0_ref, next_near, next_far, keep_ref, send_ref,
+    g3, d3, xs, both,
 ):
     halo_rows(near_ref, far_ref, 1, rows, g3)
     stack_rows(g1_ref, (0, 1, 2, rows - 3, rows - 2, rows - 1), g3, 1)
@@ -361,8 +360,6 @@
 
     for at in (0, rows - 2):
         conv_rows(w_ref[3], g3, at, 2, dhidden0)
-    copy = pltpu.make_async_copy(dh0_ref, dh0_out, copied)
-    copy.start()
     send_edges(dh0_ref, 1, next_near, next_far)
     odd = odd_place()
     copy_rows(x_ref, 3, xs, 1)
@@ -384,7 +381,6 @@
     mine = lax.rem(lax.axis_index("space"), 2)
     keep_ref[...] = both[mine]
     send_ref[...] = both[1 - mine].astype(BF16)
-    copy.wait()
 
 
 def input_grad_kernel(rows, dh0_in, dh0_ref, near_ref, far_ref, g1_ref, w_ref, out_ref, d3, wide):
@@ -430,8 +426,6 @@
     def plain(n):
         return pltpu.VMEM((n * CHAN, width), BF16)
 
-    one_copy = pltpu.SemaphoreType.DMA
-
     def neighbours(near, far):
         from_far = lax.ppermute(far, "space", beyond)
         return exchange(near, 1, count), from_far
@@ -480,8 +474,8 @@
     g1, dh0_inner, *grads = call(
         functools.partial(middle_kernel, rows), (g, edges, hid1, dh1, x1, hid0, x, weights),
         (shape(rows), shape(rows - 4)) + (grad,) * 4,
-        [vmem(rows), vmem(rows + 2), vmem(rows), vmem(rows - 4), plain(rows - 4), one_copy],
-        36 * row_flops, "middle", to_hbm=(1,),
+        [vmem(rows), vmem(rows + 2), vmem(rows), vmem(rows - 4)],
+        36 * row_flops, "middle",
     )
     dh0, dh0_near, dh0_far, part, send = call(
         functools.partial(backward0_kernel, rows, scale),
@@ -489,8 +483,8 @@
         (shape(4), shape(1), shape(1), jax.ShapeDtypeStruct(half, F32),
          jax.ShapeDtypeStruct(half, BF16)),
         [vmem(rows + 2), vmem(4), pltpu.VMEM((8 * CHAN, width), BF16),
-         pltpu.VMEM((2, *half), F32), plain(4), one_copy],
-        8 * row_flops, "backward0", to_hbm=(0,),
+         pltpu.VMEM((2, *half), F32)],
+        8 * row_flops, "backward0",
     )
 
     part = part + exchange(send, 1, count).astype(F32)

time: 64.7 us -> 63 us (0.974)
  Pallas kernels: 26.9 us -> 23.5 us
  starting transfers between devices: 24.8 us -> 26.6 us
    pallas_call x12, Pallas kernels: 26.9 us -> 23.5 us  [call(): pl.pallas_call(kernel, out_shape=outs, in_specs=[ANY] * len(after) + [pla...]
    ppermute x11, starting transfers between devices: 21.7 us -> 23.7 us  [exchange(): return lax.ppermute(value, 'space', [(d, d ^ mask) for d in range(count)])]
  transfers between devices with their start and end apart: 15 -> 15, of which waited for: 7 -> 7; matrix products, arithmetic and copies ran while one was open for 0% -> 0% of each run, Pallas kernels for 32% -> 28%
where the time goes in v6:
time: 63 us; the launch traced here: 62.8 us
  starting transfers between devices  26.6 us (42%)
  Pallas kernels  23.5 us (37%)
  waiting for transfers between devices  8.57 us (14%)
  local copies, waits for them, and re-layouts  3.01 us (5%)
  between operations  0.91 us (1%)
    ppermute x11, starting transfers between devices, exchange(): return lax.ppermute(value, 'space', [(d, d ^ mask) for d in range(count)])  23.7 us
    pallas_call x12, Pallas kernels, call(): pl.pallas_call(kernel, out_shape=outs, in_specs=[ANY] * len(after) + [pla...  23.5 us
    ppermute x11, waiting for transfers between devices, exchange(): return lax.ppermute(value, 'space', [(d, d ^ mask) for d in range(count)])  8.56 us
    unnamed x22, local copies, waits for them, and re-layouts  3.01 us
    ppermute x4, starting transfers between devices, neighbours(): from_far = lax.ppermute(far, 'space', beyond)  2.88 us
  transfers between devices with their start and end apart: 15, of which 7 were waited for; matrix products, arithmetic and copies ran while one was open for 0% of the time, Pallas kernels for 28%

profile of v6, /device:TPU:0, one launch (start us, length us, event | category | flops | bytes accessed | tf_op | source)
XLA Modules:
  0.0 62.8 jit_solution(15040259397915526950)
XLA Ops:
  0.6 1.2 %copy-done = bf16[64,8,1024]{2,1,0:T(8,128)(2,1)S(1)} copy-done((bf16[64,8,1024]{2,1,0:T(8,128)(2,1)S(1)}, bf16[64,8,1024]{2,1,0:T(8,128)(2,1)}, u32[]{:S(2)}) %copy-start) | copy-done | bytes 1048600
  3.7 1.0 %copy-done.1 = bf16[2,2,64,576]{3,2,1,0:T(8,128)(2,1)S(1)} copy-done((bf16[2,2,64,576]{3,2,1,0:T(8,128)(2,1)S(1)}, bf16[2,2,64,576]{3,2,1,0:T(8,128)(2,1)}, u32[]{:S(2)}) %copy-start.1) | copy-done | bytes 294936
  5.4 1.7 %inner.1 = (bf16[384,1024]{1,0:T(8,128)(2,1)S(1)}, bf16[256,1024]{1,0:T(8,128)(2,1)S(1)}, bf16[128,1024]{1,0:T(8,128)(2,1)S(1)}) custom-call(bf16[512,1024]{1,0:T(8,128)(2,1)S(1)} %get-tuple-element.42.refs_0_.refs_1_.refs_6_.refs_4_, bf16[8,128,768]{2,1,0:T(8,128)(2,1)S(1)} %weights.1.refs_1_.refs_2_.refs_3_.refs_5_.refs_7_.refs_6_), custom_call_target="tpu_custom_call" | custom-call | flops 3623878656 | bytes 4194304 | tf_op jit(solution)/shard_map/inner/pallas_call | solution.py:28
  7.1 1.6 %g_rows.1 = (bf16[512,1024]{1,0:T(8,128)(2,1)S(1)}, bf16[128,1024]{1,0:T(8,128)(2,1)S(1)}, bf16[128,1024]{1,0:T(8,128)(2,1)S(1)}, f32[384,1024]{1,0:T(8,128)S(1)}) custom-call(bf16[128,1024]{1,0:T(8,128)(2,1)S(1)} %get-tuple-element.44.refs_0_.refs_5_, bf16[64,8,1024]{2,1,0:T(8,128)(2,1)S(1)} %copy-done.2, ...), custom_call_target="tpu_custom_call" | custom-call | flops 1811939328 | bytes 5767168 | tf_op jit(solution)/shard_map/g_rows/pallas_call | solution.py:28
  8.7 3.9 %collective-permute-start = (bf16[128,1024]{1,0:T(8,128)(2,1)S(1)}, bf16[128,1024]{1,0:T(8,128)(2,1)S(1)}, u32[]{:S(2)}, u32[]{:S(2)}) collective-permute-start(bf16[128,1024]{1,0:T(8,128)(2,1)S(1)} %get-tuple-element.46.refs_0_), channel_id=1, source_target_pairs={{0,1},{1,0},{2,3},{3,2},{4,5},{5,4},{6,7},{7,6},{8,9},{9,8},{10,11... | collective-permute-start | bytes 786440 | tf_op jit(solution)/shard_map/ppermute | solution.py:408
  13.3 1.9 %forward_near.1 = (bf16[256,1024]{1,0:T(8,128)(2,1)S(1)}, bf16[256,1024]{1,0:T(8,128)(2,1)S(1)}, bf16[256,1024]{1,0:T(8,128)(2,1)S(1)}) custom-call(bf16[128,1024]{1,0:T(8,128)(2,1)S(1)} %get-tuple-element.46.refs_0_, bf16[512,1024]{1,0:T(8,128)(2,1)S(1)} %get-tuple-element.42.refs_0_.refs_1_.refs_6_.refs_4_, ...), custom_call_target="tpu_custom_call" | custom-call | flops 3623878656 | bytes 6029312 | tf_op jit(solution)/shard_map/forward_near/pallas_call | solution.py:28
  15.1 2.3 %forward_far.1 = (bf16[640,1024]{1,0:T(8,128)(2,1)S(1)}, bf16[640,1024]{1,0:T(8,128)(2,1)S(1)}, bf16[640,1024]{1,0:T(8,128)(2,1)S(1)}) custom-call(bf16[512,1024]{1,0:T(8,128)(2,1)S(1)} %get-tuple-element.42.refs_0_.refs_1_.refs_6_.refs_4_, bf16[256,1024]{1,0:T(8,128)(2,1)S(1)} %collective-permute-done.2.refs_1_.refs_6_, ...), custom_call_target="tpu_custom_call" | custom-call | flops 3623878656 | bytes 10223616 | tf_op jit(solution)/shard_map/forward_far/pallas_call | solution.py:28
  17.5 2.3 %backward1.1 = (bf16[64,1024]{1,0:T(8,128)(2,1)S(1)}, bf16[64,1024]{1,0:T(8,128)(2,1)S(1)}, bf16[256,1024]{1,0:T(8,128)(2,1)S(1)}, bf16[640,1024]{1,0:T(8,128)(2,1)S(1)}) custom-call(bf16[512,1024]{1,0:T(8,128)(2,1)S(1)} %get-tuple-element.45.refs_0_, bf16[128,1024]{1,0:T(8,128)(2,1)S(1)} %collective-permute-done.refs_1_, ...), custom_call_target="tpu_custom_call" | custom-call | flops 2415919104 | bytes 8126464 | tf_op jit(solution)/shard_map/backward1/pallas_call | solution.py:28
  19.7 7.5 %collective-permute-start.4 = (bf16[64,1024]{1,0:T(8,128)(2,1)S(1)}, bf16[64,1024]{1,0:T(8,128)(2,1)S(1)}, u32[]{:S(2)}, u32[]{:S(2)}) collective-permute-start(bf16[64,1024]{1,0:T(8,128)(2,1)S(1)} %get-tuple-element.61), channel_id=1, source_target_pairs={{0,1},{1,0},{2,3},{3,2},{4,5},{5,4},{6,7},{7,6},{8,9},{9,8},{10,11... | collective-permute-start | bytes 393224 | tf_op jit(solution)/shard_map/ppermute | solution.py:408
  27.9 4.4 %middle.1 = (bf16[512,1024]{1,0:T(8,128)(2,1)S(1)}, bf16[256,1024]{1,0:T(8,128)(2,1)S(1)}, f32[192,192]{1,0:T(8,128)S(1)}, f32[192,192]{1,0:T(8,128)S(1)}, f32[1...) custom-call(bf16[512,1024]{1,0:T(8,128)(2,1)S(1)} %get-tuple-element.45.refs_0_, ...), custom_call_target="tpu_custom_call" | custom-call | flops 10871635968 | bytes 11599872 | tf_op jit(solution)/shard_map/middle/pallas_call | solution.py:28
  32.3 1.8 %backward0.1 = (bf16[256,1024]{1,0:T(8,128)(2,1)S(1)}, bf16[64,1024]{1,0:T(8,128)(2,1)S(1)}, bf16[64,1024]{1,0:T(8,128)(2,1)S(1)}, f32[64,1152]{1,0:T(8,128)S(1)}, bf16[64,1152]{1,0:T(8,128)(2,1)S(1)}) custom-call(bf16[512,1024]{1,0:T(8,128)(2,1)S(1)} %get-tuple-element.60.refs_0_.refs_5_, bf16[64,1024]{1,0:T(8,128)(2,1)S(1)} %collective-permute-done.4.refs_1_, ...), custom_call_target="tpu_custom_call" | custom-call | flops 2415919104 | bytes 8110080 | tf_op jit(solution)/shard_map/backward0/pallas_call | solution.py:28
  35.0 3.7 %collective-permute-start.6 = (bf16[64,1152]{1,0:T(8,128)(2,1)S(1)}, bf16[64,1152]{1,0:T(8,128)(2,1)S(1)}, u32[]{:S(2)}, u32[]{:S(2)}) collective-permute-start(bf16[64,1152]{1,0:T(8,128)(2,1)S(1)} %get-tuple-element.68), channel_id=1, source_target_pairs={{0,1},{1,0},{2,3},{3,2},{4,5},{5,4},{6,7},{7,6},{8,9},{9,8},{10,11... | collective-permute-start | bytes 442376 | tf_op jit(solution)/shard_map/ppermute | solution.py:408
  38.7 1.0 %collective-permute-done.6 = bf16[64,1152]{1,0:T(8,128)(2,1)S(1)} collective-permute-done((bf16[64,1152]{1,0:T(8,128)(2,1)S(1)}, bf16[64,1152]{1,0:T(8,128)(2,1)S(1)}, u32[]{:S(2)}, u32[]{:S(2)}) %collective-permute-start.6) | collective-permute-done | bytes 147488 | tf_op jit(solution)/shard_map/ppermute | solution.py:408
  39.8 2.1 %collective-permute-start.7 = (bf16[32,1152]{1,0:T(8,128)(2,1)S(1)}, bf16[32,1152]{1,0:T(8,128)(2,1)S(1)}, u32[]{:S(2)}, u32[]{:S(2)}) collective-permute-start(bf16[32,1152]{1,0:T(8,128)(2,1)S(1)} %select_convert_fusion), channel_id=1, source_target_pairs={{0,2},{1,3},{2,0},{3,1},{4,6},{5,7},{6,4},{7,5},{8,10},{9,11},{10,... | collective-permute-start | bytes 221192 | tf_op jit(solution)/shard_map/ppermute | solution.py:408
  42.8 1.8 %collective-permute-done.7 = bf16[32,1152]{1,0:T(8,128)(2,1)S(1)} collective-permute-done((bf16[32,1152]{1,0:T(8,128)(2,1)S(1)}, bf16[32,1152]{1,0:T(8,128)(2,1)S(1)}, u32[]{:S(2)}, u32[]{:S(2)}) %collective-permute-start.7) | collective-permute-done | bytes 73760 | tf_op jit(solution)/shard_map/ppermute | solution.py:408
  44.7 3.6 %collective-permute-start.10 = (bf16[32,1152]{1,0:T(8,128)(2,1)S(1)}, bf16[32,1152]{1,0:T(8,128)(2,1)S(1)}, u32[]{:S(2)}, u32[]{:S(2)}) collective-permute-start(bf16[32,1152]{1,0:T(8,128)(2,1)S(1)} %add_convert_fusion.1.refs_0_), channel_id=1, source_target_pairs={{0,12},{1,13},{2,14},{3,15},{4,8},{5,9},{6,10},{7,11},{8,4},{9,5},... | collective-permute-start | bytes 221192 | tf_op jit(solution)/shard_map/ppermute | solution.py:408
  48.3 0.9 %collective-permute-start.9 = (bf16[32,1152]{1,0:T(8,128)(2,1)S(1)}, bf16[32,1152]{1,0:T(8,128)(2,1)S(1)}, u32[]{:S(2)}, u32[]{:S(2)}) collective-permute-start(bf16[32,1152]{1,0:T(8,128)(2,1)S(1)} %add_convert_fusion.1.refs_0_), channel_id=1, source_target_pairs={{0,8},{1,9},{2,10},{3,11},{4,12},{5,13},{6,14},{7,15},{8,0},{9,1},... | collective-permute-start | bytes 221192 | tf_op jit(solution)/shard_map/ppermute | solution.py:408
  49.2 2.8 %input_grad.1 = bf16[64,8,1024]{2,1,0:T(8,128)(2,1)} custom-call(bf16[32,1152]{1,0:T(8,128)(2,1)S(1)} %add_convert_fusion.1.refs_0_, bf16[256,1024]{1,0:T(8,128)(2,1)S(1)} %copy-done.10, bf16[256,1024]{1,0:T(8,128)(2,1)S(1)} %copy-done.6, bf16[64,1024]{1,0:T(8,128)(2,1)S(1)} %collective-permute-done.11.refs_3_, ...), custom_call_target="tpu_custom_call" | custom-call | flops 2415919104 | bytes 4980736 | tf_op jit(solution)/shard_map/input_grad/pallas_call | solution.py:28
  52.0 1.2 %collective-permute-done.10 = bf16[32,1152]{1,0:T(8,128)(2,1)S(1)} collective-permute-done((bf16[32,1152]{1,0:T(8,128)(2,1)S(1)}, bf16[32,1152]{1,0:T(8,128)(2,1)S(1)}, u32[]{:S(2)}, u32[]{:S(2)}) %collective-permute-start.10) | collective-permute-done | bytes 73760 | tf_op jit(solution)/shard_map/ppermute | solution.py:408
  53.7 2.2 %collective-permute-done.9 = bf16[32,1152]{1,0:T(8,128)(2,1)S(1)} collective-permute-done((bf16[32,1152]{1,0:T(8,128)(2,1)S(1)}, bf16[32,1152]{1,0:T(8,128)(2,1)S(1)}, u32[]{:S(2)}, u32[]{:S(2)}) %collective-permute-start.9) | collective-permute-done | bytes 73760 | tf_op jit(solution)/shard_map/ppermute | solution.py:408
  55.9 1.4 %collective-permute-start.13 = (bf16[32,1152]{1,0:T(8,128)(2,1)S(1)}, bf16[32,1152]{1,0:T(8,128)(2,1)S(1)}, u32[]{:S(2)}, u32[]{:S(2)}) collective-permute-start(bf16[32,1152]{1,0:T(8,128)(2,1)S(1)} %add_convert_fusion.refs_0_), channel_id=1, source_target_pairs={{0,2},{1,3},{2,0},{3,1},{4,6},{5,7},{6,4},{7,5},{8,10},{9,11},{10,... | collective-permute-start | bytes 221192 | tf_op jit(solution)/shard_map/ppermute | solution.py:408
  57.4 2.5 %output.1 = bf16[64,8,1024]{2,1,0:T(8,128)(2,1)} custom-call(bf16[32,1152]{1,0:T(8,128)(2,1)S(1)} %add_convert_fusion.refs_0_, bf16[640,1024]{1,0:T(8,128)(2,1)S(1)} %copy-done.4, bf16[640,1024]{1,0:T(8,128)(2,1)S(1)} %copy-done.8, bf16[8,128,768]{2,1,0:T(8,128)(2,1)S(1)} %weights.1.refs_1_.refs_2_.refs_3_.refs_5_.refs_7_.refs_6_), custom_call_target="tpu_custom_call" | custom-call | flops 2415919104 | bytes 5242880 | tf_op jit(solution)/shard_map/output/pallas_call | solution.py:28
  60.5 1.4 %collective-permute-done.14.refs_1_ = bf16[64,1152]{1,0:T(8,128)(2,1)S(1)} collective-permute-done((bf16[64,1152]{1,0:T(8,128)(2,1)S(1)}, bf16[64,1152]{1,0:T(8,128)(2,1)S(1)}, u32[]{:S(2)}, u32[]{:S(2)}) %collective-permute-start.14) | collective-permute-done | bytes 147488 | tf_op jit(solution)/shard_map/ppermute | solution.py:408
  61.8 1.0 %gathered.1 = f32[2,2,64,576]{3,2,1,0:T(8,128)} custom-call(bf16[64,1152]{1,0:T(8,128)(2,1)S(1)} %maximum_select_fusion.refs_0_, bf16[64,1152]{1,0:T(8,128)(2,1)S(1)} %collective-permute-done.14.refs_1_), custom_call_target="tpu_custom_call" | custom-call | bytes 884736 | tf_op jit(solution)/shard_map/gathered/pallas_call | solution.py:28
  (45 shorter events, 6.8 us)
Async XLA Ops:
  0.6 1.2 %copy-start = (bf16[64,8,1024]{2,1,0:T(8,128)(2,1)S(1)}, bf16[64,8,1024]{2,1,0:T(8,128)(2,1)}, u32[]{:S(2)}) copy-start(bf16[64,8,1024]{2,1,0:T(8,128)(2,1)} %refs_0_.1) | copy-start | bytes 3145732
  2.5 10.7 %collective-permute-start.3 = (bf16[256,1024]{1,0:T(8,128)(2,1)S(1)}, bf16[256,1024]{1,0:T(8,128)(2,1)S(1)}, u32[]{:S(2)}, u32[]{:S(2)}) collective-permute-start(bf16[256,1024]{1,0:T(8,128)(2,1)S(1)} %get-tuple-element.50), channel_id=1, source_target_pairs={{0,1},{1,0},{2,3},{3,2},{4,5},{5,4},{6,7},{7,6},{8,9},{9,8},{10,11... | collective-permute-start | bytes 1572872 | tf_op jit(solution)/shard_map/ppermute | solution.py:408
  3.0 12.1 %collective-permute-start.2 = (bf16[256,1024]{1,0:T(8,128)(2,1)S(1)}, bf16[256,1024]{1,0:T(8,128)(2,1)S(1)}, u32[]{:S(2)}, u32[]{:S(2)}) collective-permute-start(bf16[256,1024]{1,0:T(8,128)(2,1)S(1)} %get-tuple-element.43.refs_0_), channel_id=1, source_target_pairs={{1,2},{3,4},{5,6},{7,8},{9,10},{11,12},{13,14},{2,1},{4,3},{6,5},{... | collective-permute-start | bytes 1572872 | tf_op jit(solution)/shard_map/ppermute | solution.py:430
  5.4 1.7 %copy-start.2 = (bf16[64,8,1024]{2,1,0:T(8,128)(2,1)S(1)}, bf16[64,8,1024]{2,1,0:T(8,128)(2,1)}, u32[]{:S(2)}) copy-start(bf16[64,8,1024]{2,1,0:T(8,128)(2,1)} %refs_1_.3) | copy-start | bytes 3145732
  8.7 8.8 %collective-permute-start = (bf16[128,1024]{1,0:T(8,128)(2,1)S(1)}, bf16[128,1024]{1,0:T(8,128)(2,1)S(1)}, u32[]{:S(2)}, u32[]{:S(2)}) collective-permute-start(bf16[128,1024]{1,0:T(8,128)(2,1)S(1)} %get-tuple-element.46.refs_0_), channel_id=1, source_target_pairs={{0,1},{1,0},{2,3},{3,2},{4,5},{5,4},{6,7},{7,6},{8,9},{9,8},{10,11... | collective-permute-start | bytes 786440 | tf_op jit(solution)/shard_map/ppermute | solution.py:408
  12.6 4.9 %collective-permute-start.1 = (bf16[128,1024]{1,0:T(8,128)(2,1)S(1)}, bf16[128,1024]{1,0:T(8,128)(2,1)S(1)}, u32[]{:S(2)}, u32[]{:S(2)}) collective-permute-start(bf16[128,1024]{1,0:T(8,128)(2,1)S(1)} %get-tuple-element.47), channel_id=1, source_target_pairs={{1,2},{3,4},{5,6},{7,8},{9,10},{11,12},{13,14},{2,1},{4,3},{6,5},{... | collective-permute-start | bytes 786440 | tf_op jit(solution)/shard_map/ppermute | solution.py:430
  17.4 10.4 %copy-start.3 = (bf16[640,1024]{1,0:T(8,128)(2,1)}, bf16[640,1024]{1,0:T(8,128)(2,1)S(1)}, u32[]{:S(2)}) copy-start(bf16[640,1024]{1,0:T(8,128)(2,1)S(1)} %get-tuple-element.54.refs_3_.refs_2_.refs_1_) | copy-start | bytes 3932164
  17.5 10.4 %copy-start.7 = (bf16[640,1024]{1,0:T(8,128)(2,1)}, bf16[640,1024]{1,0:T(8,128)(2,1)S(1)}, u32[]{:S(2)}) copy-start(bf16[640,1024]{1,0:T(8,128)(2,1)S(1)} %get-tuple-element.58.refs_4_.refs_2_) | copy-start | bytes 3932164
  19.7 12.6 %collective-permute-start.4 = (bf16[64,1024]{1,0:T(8,128)(2,1)S(1)}, bf16[64,1024]{1,0:T(8,128)(2,1)S(1)}, u32[]{:S(2)}, u32[]{:S(2)}) collective-permute-start(bf16[64,1024]{1,0:T(8,128)(2,1)S(1)} %get-tuple-element.61), channel_id=1, source_target_pairs={{0,1},{1,0},{2,3},{3,2},{4,5},{5,4},{6,7},{7,6},{8,9},{9,8},{10,11... | collective-permute-start | bytes 393224 | tf_op jit(solution)/shard_map/ppermute | solution.py:408
  27.2 5.1 %collective-permute-start.5 = (bf16[64,1024]{1,0:T(8,128)(2,1)S(1)}, bf16[64,1024]{1,0:T(8,128)(2,1)S(1)}, u32[]{:S(2)}, u32[]{:S(2)}) collective-permute-start(bf16[64,1024]{1,0:T(8,128)(2,1)S(1)} %get-tuple-element.62), channel_id=1, source_target_pairs={{1,2},{3,4},{5,6},{7,8},{9,10},{11,12},{13,14},{2,1},{4,3},{6,5},{... | collective-permute-start | bytes 393224 | tf_op jit(solution)/shard_map/ppermute | solution.py:430
  32.3 1.9 %copy-start.9 = (bf16[256,1024]{1,0:T(8,128)(2,1)}, bf16[256,1024]{1,0:T(8,128)(2,1)S(1)}, u32[]{:S(2)}) copy-start(bf16[256,1024]{1,0:T(8,128)(2,1)S(1)} %get-tuple-element.69.refs_1_) | copy-start | bytes 1572868
  35.0 4.7 %collective-permute-start.6 = (bf16[64,1152]{1,0:T(8,128)(2,1)S(1)}, bf16[64,1152]{1,0:T(8,128)(2,1)S(1)}, u32[]{:S(2)}, u32[]{:S(2)}) collective-permute-start(bf16[64,1152]{1,0:T(8,128)(2,1)S(1)} %get-tuple-element.68), channel_id=1, source_target_pairs={{0,1},{1,0},{2,3},{3,2},{4,5},{5,4},{6,7},{7,6},{8,9},{9,8},{10,11... | collective-permute-start | bytes 442376 | tf_op jit(solution)/shard_map/ppermute | solution.py:408
  38.7 10.4 %copy-start.6 = (bf16[256,1024]{1,0:T(8,128)(2,1)S(1)}, bf16[256,1024]{1,0:T(8,128)(2,1)}, u32[]{:S(2)}) copy-start(bf16[256,1024]{1,0:T(8,128)(2,1)} %copy-done.5) | copy-start | bytes 1572868
  38.7 10.4 %copy-start.10 = (bf16[256,1024]{1,0:T(8,128)(2,1)S(1)}, bf16[256,1024]{1,0:T(8,128)(2,1)}, u32[]{:S(2)}) copy-start(bf16[256,1024]{1,0:T(8,128)(2,1)} %copy-done.9) | copy-start | bytes 1572868
  39.8 4.9 %collective-permute-start.7 = (bf16[32,1152]{1,0:T(8,128)(2,1)S(1)}, bf16[32,1152]{1,0:T(8,128)(2,1)S(1)}, u32[]{:S(2)}, u32[]{:S(2)}) collective-permute-start(bf16[32,1152]{1,0:T(8,128)(2,1)S(1)} %select_convert_fusion), channel_id=1, source_target_pairs={{0,2},{1,3},{2,0},{3,1},{4,6},{5,7},{6,4},{7,5},{8,10},{9,11},{10,... | collective-permute-start | bytes 221192 | tf_op jit(solution)/shard_map/ppermute | solution.py:408
  41.9 7.3 %collective-permute-start.11 = (bf16[64,1024]{1,0:T(8,128)(2,1)S(1)}, bf16[64,1024]{1,0:T(8,128)(2,1)S(1)}, u32[]{:S(2)}, u32[]{:S(2)}) collective-permute-start(bf16[64,1024]{1,0:T(8,128)(2,1)S(1)} %get-tuple-element.73), channel_id=1, source_target_pairs={{0,1},{1,0},{2,3},{3,2},{4,5},{5,4},{6,7},{7,6},{8,9},{9,8},{10,11... | collective-permute-start | bytes 393224 | tf_op jit(solution)/shard_map/ppermute | solution.py:408
  42.0 7.2 %collective-permute-start.12 = (bf16[64,1024]{1,0:T(8,128)(2,1)S(1)}, bf16[64,1024]{1,0:T(8,128)(2,1)S(1)}, u32[]{:S(2)}, u32[]{:S(2)}) collective-permute-start(bf16[64,1024]{1,0:T(8,128)(2,1)S(1)} %get-tuple-element.74), channel_id=1, source_target_pairs={{1,2},{3,4},{5,6},{7,8},{9,10},{11,12},{13,14},{2,1},{4,3},{6,5},{... | collective-permute-start | bytes 393224 | tf_op jit(solution)/shard_map/ppermute | solution.py:430
  44.7 8.5 %collective-permute-start.10 = (bf16[32,1152]{1,0:T(8,128)(2,1)S(1)}, bf16[32,1152]{1,0:T(8,128)(2,1)S(1)}, u32[]{:S(2)}, u32[]{:S(2)}) collective-permute-start(bf16[32,1152]{1,0:T(8,128)(2,1)S(1)} %add_convert_fusion.1.refs_0_), channel_id=1, source_target_pairs={{0,12},{1,13},{2,14},{3,15},{4,8},{5,9},{6,10},{7,11},{8,4},{9,5},... | collective-permute-start | bytes 221192 | tf_op jit(solution)/shard_map/ppermute | solution.py:408
  48.3 5.4 %collective-permute-start.8 = (bf16[32,1152]{1,0:T(8,128)(2,1)S(1)}, bf16[32,1152]{1,0:T(8,128)(2,1)S(1)}, u32[]{:S(2)}, u32[]{:S(2)}) collective-permute-start(bf16[32,1152]{1,0:T(8,128)(2,1)S(1)} %add_convert_fusion.1.refs_0_), channel_id=1, source_target_pairs={{0,4},{1,5},{2,6},{3,7},{4,0},{5,1},{6,2},{7,3},{8,12},{9,13},{10,... | collective-permute-start | bytes 221192 | tf_op jit(solution)/shard_map/ppermute | solution.py:408
  48.3 7.6 %collective-permute-start.9 = (bf16[32,1152]{1,0:T(8,128)(2,1)S(1)}, bf16[32,1152]{1,0:T(8,128)(2,1)S(1)}, u32[]{:S(2)}, u32[]{:S(2)}) collective-permute-start(bf16[32,1152]{1,0:T(8,128)(2,1)S(1)} %add_convert_fusion.1.refs_0_), channel_id=1, source_target_pairs={{0,8},{1,9},{2,10},{3,11},{4,12},{5,13},{6,14},{7,15},{8,0},{9,1},... | collective-permute-start | bytes 221192 | tf_op jit(solution)/shard_map/ppermute | solution.py:408
  49.2 8.2 %copy-start.4 = (bf16[640,1024]{1,0:T(8,128)(2,1)S(1)}, bf16[640,1024]{1,0:T(8,128)(2,1)}, u32[]{:S(2)}) copy-start(bf16[640,1024]{1,0:T(8,128)(2,1)} %copy-done.3) | copy-start | bytes 3932164
  49.2 8.2 %copy-start.8 = (bf16[640,1024]{1,0:T(8,128)(2,1)S(1)}, bf16[640,1024]{1,0:T(8,128)(2,1)}, u32[]{:S(2)}) copy-start(bf16[640,1024]{1,0:T(8,128)(2,1)} %copy-done.7) | copy-start | bytes 3932164
  55.9 4.4 %collective-permute-start.13 = (bf16[32,1152]{1,0:T(8,128)(2,1)S(1)}, bf16[32,1152]{1,0:T(8,128)(2,1)S(1)}, u32[]{:S(2)}, u32[]{:S(2)}) collective-permute-start(bf16[32,1152]{1,0:T(8,128)(2,1)S(1)} %add_convert_fusion.refs_0_), channel_id=1, source_target_pairs={{0,2},{1,3},{2,0},{3,1},{4,6},{5,7},{6,4},{7,5},{8,10},{9,11},{10,... | collective-permute-start | bytes 221192 | tf_op jit(solution)/shard_map/ppermute | solution.py:408
  60.4 1.4 %collective-permute-start.14 = (bf16[64,1152]{1,0:T(8,128)(2,1)S(1)}, bf16[64,1152]{1,0:T(8,128)(2,1)S(1)}, u32[]{:S(2)}, u32[]{:S(2)}) collective-permute-start(bf16[64,1152]{1,0:T(8,128)(2,1)S(1)} %maximum_select_fusion.refs_0_), channel_id=1, source_target_pairs={{0,1},{1,0},{2,3},{3,2},{4,5},{5,4},{6,7},{7,6},{8,9},{9,8},{10,11... | collective-permute-start | bytes 442376 | tf_op jit(solution)/shard_map/ppermute | solution.py:408
  (2 other events, 1.8 us)

commit v7 on v6

--- a/solution.py
+++ b/solution.py
@@ -277,31 +277,81 @@
         pl.when(odd != top)(functools.partial(far_side, top))
 
 
-def backward1_kernel(
-    rows, g_ref, near_ref, far_ref, hid1_ref, inner_ref, w_ref, next_near, next_far, edges_ref, dh1_ref,
-    g3, d3,
+def backward_side(
+    rows, top, g_ref, halo_ref, hid1_row, inner_ref, w_ref, inner_rows, keep_dh1, keep_edge, g3, d3
 ):
-    halo_rows(near_ref, far_ref, 2, rows, g3)
-    stack_rows(g_ref, (0, 1, rows - 2, rows - 1), g3, 2)
+    start = 0 if top else rows - 2
+    for i in range(2):
+        put(g3, (0 if top else 2) + i, one(halo_ref, i))
+        put(g3, (2 if top else 0) + i, one(g_ref, start + i))
 
     def dhidden1(row, total):
-        value = jnp.where(one(hid1_ref, row) > 0, total, 0.0).astype(BF16)
-        dh1_ref[row * CHAN : (row + 1) * CHAN, :] = value
-        if row < 4 or row >= rows - 2:
-            put(d3, row, value)
-
-    for row in range(2, rows):
-        dhidden1(row, one(inner_ref, row - 2))
-    for at in (0, rows):
-        conv_rows(w_ref[7], g3, at, 2, dhidden1)
+        value = jnp.where(hid1_row(row) > 0, total, 0.0).astype(BF16)
+        keep_dh1(row, value)
+        at = row + 1 if top else row - (rows - 3)
+        if 0 <= at < 4:
+            put(d3, at, value)
+
+    for row in inner_rows:
+        dhidden1(row, one(inner_ref, row - 1))
+    edge = -1 if top else rows - 1
+    conv_rows(w_ref[7], g3, 0, 2, lambda row, total: dhidden1(edge + row, total))
 
     def next_g(row, total):
-        value = (one(g_ref, row).astype(F32) + total).astype(BF16)
-        at = row if row < 2 else row - (rows - 4)
-        edges_ref[at * CHAN : (at + 1) * CHAN, :] = value
-
-    for at in (0, rows - 2):
-        conv_rows(w_ref[5], d3, at, 2, next_g)
+        keep_edge(row, (one(g_ref, start + row).astype(F32) + total).astype(BF16))
+
+    conv_rows(w_ref[5], d3, 0, 2, next_g)
+
+
+def backward1_near_kernel(
+    rows, g_ref, near_ref, hid1_near, hid1_in, inner_ref, w_ref, dh1_ref, edge_ref, g3, d3
+):
+    def near_side(top):
+        def hid1_row(row):
+            if 3 <= row < rows - 3:
+                return one(hid1_in, row - 3)
+            return one(hid1_near, row + 1 if top else row - (rows - 3))
+
+        def keep_dh1(row, value):
+            at = row + 1 if top else row - 3
+            dh1_ref[at * CHAN : (at + 1) * CHAN, :] = value
+
+        def keep_edge(row, value):
+            edge_ref[row * CHAN : (row + 1) * CHAN, :] = value
+
+        inner_rows = range(1, rows - 3) if top else range(3, rows - 1)
+        backward_side(
+            rows, top, g_ref, near_ref, hid1_row, inner_ref, w_ref, inner_rows, keep_dh1, keep_edge, g3, d3
+        )
+
+    odd = odd_place()
+    for top in (True, False):
+        pl.when(odd == top)(functools.partial(near_side, top))
+
+
+def backward1_far_kernel(
+    rows, g_ref, far_ref, hid1_ref, inner_ref, w_ref, dh1_near, edge_near,
+    next_near, next_far, edges_ref, dh1_ref, g3, d3,
+):
+    def far_side(top):
+        def keep_dh1(row, value):
+            dh1_ref[(row + 1) * CHAN : (row + 2) * CHAN, :] = value
+
+        def keep_edge(row, value):
+            at = row if top else 2 + row
+            edges_ref[at * CHAN : (at + 1) * CHAN, :] = value
+
+        inner_rows = (1, 2) if top else (rows - 3, rows - 2)
+        backward_side(
+            rows, top, g_ref, far_ref, lambda row: one(hid1_ref, row + 1), inner_ref, w_ref, inner_rows,
+            keep_dh1, keep_edge, g3, d3,
+        )
+        copy_rows(dh1_near, rows - 2, dh1_ref, 4 if top else 0)
+        copy_rows(edge_near, 2, edges_ref, 2 if top else 0)
+
+    odd = odd_place()
+    for top in (True, False):
+        pl.when(odd != top)(functools.partial(far_side, top))
     send_edges(edges_ref, 1, next_near, next_far)
 
 
@@ -323,15 +373,15 @@
 
     def dhidden0(row, total):
         value = jnp.where(one(hid0_ref, row + 2) > 0, total, 0.0).astype(BF16)
-        dh0_ref[(row - 1) * CHAN : row * CHAN, :] = value
-        put(v3, row - 1, value)
-
-    conv_rows(w_ref[3], u3, 1, rows - 4, dhidden0)
+        dh0_ref[row * CHAN : (row + 1) * CHAN, :] = value
+        put(v3, row, value)
+
+    conv_rows(w_ref[3], u3, 0, rows - 2, dhidden0)
     stack_rows(g_ref, range(rows), s3, 0)
     grad11[...] = grad_rows(s3, 0, hid1_ref, 0, rows)
     grad10[...] = grad_rows(t3, 1, x1_ref, 0, rows)
     grad01[...] = grad_rows(u3, 0, hid0_ref, 0, rows)
-    grad00[...] = grad_rows(v3, 0, x_ref, 1, rows - 4)
+    grad00[...] = grad_rows(v3, 0, x_ref, 0, rows - 2)
 
 
 def output_kernel(rows, hid1_ref, x1_ref, w_ref, out_ref, k3, wide):
@@ -346,30 +396,39 @@
 
 def backward0_kernel(
     rows, scale, g1_ref, near_ref, far_ref, hid0_ref, x_ref, xnear_ref, xfar_ref, w_ref, inner00,
-    grad01, grad10, grad11, dh0_ref, next_near, next_far, keep_ref, send_ref,
-    g3, d3, xs, both,
+    grad01, grad10, grad11, next_near, next_far, keep_ref, send_ref,
+    d0, g3, d3, xs, both,
 ):
-    halo_rows(near_ref, far_ref, 1, rows, g3)
-    stack_rows(g1_ref, (0, 1, 2, rows - 3, rows - 2, rows - 1), g3, 1)
-
-    def dhidden0(row, total):
-        value = jnp.where(one(hid0_ref, row + 1) > 0, total, 0.0).astype(BF16)
-        at = row if row < 2 else row - (rows - 4)
-        dh0_ref[at * CHAN : (at + 1) * CHAN, :] = value
-        put(d3, at, value)
-
-    for at in (0, rows - 2):
-        conv_rows(w_ref[3], g3, at, 2, dhidden0)
-    send_edges(dh0_ref, 1, next_near, next_far)
-    odd = odd_place()
-    copy_rows(x_ref, 3, xs, 1)
-    xs[4 * CHAN : 7 * CHAN, :] = x_ref[(rows - 3) * CHAN :, :]
-    near_at, far_at = jnp.where(odd, 0, 7), jnp.where(odd, 7, 0)
+    odd = odd_place()
+    near_at, far_at = jnp.where(odd, 0, 5), jnp.where(odd, 5, 0)
+    put_at(g3, near_at, one(near_ref, 0))
+    put_at(g3, far_at, one(far_ref, 0))
+    stack_rows(g1_ref, (0, 1), g3, 1)
+    stack_rows(g1_ref, (rows - 2, rows - 1), g3, 5 - rows)
+    copy_rows(x_ref, 2, xs, 1)
+    xs[3 * CHAN : 5 * CHAN, :] = x_ref[(rows - 2) * CHAN :, :]
     near_row, far_row = jnp.where(odd, 3, 0), jnp.where(odd, 0, 3)
     for ref, at, row in ((xnear_ref, near_at, near_row), (xfar_ref, far_at, far_row)):
         source = pl.ds(pl.multiple_of(row * CHAN, CHAN), CHAN)
         xs[pl.ds(pl.multiple_of(at * CHAN, CHAN), CHAN), :] = ref[source, :]
-    grad00 = inner00[...] + grad_rows(d3, 0, xs, 0, 2) + grad_rows(d3, 2, xs, 4, 2)
+    grad00 = inner00[...]
+    for end, row in ((0, 0), (1, rows - 1)):
+        total = jnp.dot(
+            w_ref[3, :CHAN, : 3 * STACK],
+            g3[3 * end * STACK : 3 * (end + 1) * STACK, :],
+            preferred_element_type=F32,
+        )
+        value = jnp.where(one(hid0_ref, row + 1) > 0, total, 0.0).astype(BF16)
+        d0[end * CHAN : (end + 1) * CHAN, :] = value
+        put(d3, end, value)
+    for end in range(2):
+        grad00 = grad00 + lax.dot_general(
+            d3[end * STACK : (end + 1) * STACK, :],
+            xs[end * STACK : (end + 1) * STACK, :],
+            (((1,), (1,)), ((), ())),
+            preferred_element_type=F32,
+        )
+    send_edges(d0, 1, next_near, next_far)
     pairs = ((grad00, grad01[...]), (grad10[...], grad11[...]))
     for section, pair in enumerate(pairs):
         for which, value in enumerate(pair):
@@ -383,11 +442,12 @@
     send_ref[...] = both[1 - mine].astype(BF16)
 
 
-def input_grad_kernel(rows, dh0_in, dh0_ref, near_ref, far_ref, g1_ref, w_ref, out_ref, d3, wide):
+def input_grad_kernel(rows, dh0_in, own_near, own_far, near_ref, far_ref, g1_ref, w_ref, out_ref, d3, wide):
     halo_rows(near_ref, far_ref, 1, rows, d3)
-    stack_rows(dh0_in, range(rows - 4), d3, 3)
-    stack_rows(dh0_ref, (0, 1), d3, 1)
-    stack_rows(dh0_ref, (2, 3), d3, rows - 3)
+    stack_rows(dh0_in, range(rows - 2), d3, 2)
+    odd = odd_place()
+    put_at(d3, jnp.where(odd, 1, rows), one(own_near, 0))
+    put_at(d3, jnp.where(odd, rows, 1), one(own_far, 0))
 
     def last_g(row, total):
         wide[row] = one(g1_ref, row).astype(F32) + total
@@ -461,28 +521,33 @@
         functools.partial(near_kernel, rows, height), (x, xnear, weights, inner[0], inner[1]),
         (shape(4),) * 3, [vmem(6)] * 3, 12 * row_flops, "forward_near", after=(g_near,),
     )
+    dh1_near, edge_near = call(
+        functools.partial(backward1_near_kernel, rows),
+        (g, gnear, near[2], inner[2], g_inner, weights), (shape(rows - 2), shape(2)),
+        [vmem(4)] * 2, 4 * row_flops, "backward1_near",
+    )
     hid0, x1, hid1 = call(
         functools.partial(far_kernel, rows, height), (x, xfar, weights, *inner, *near),
         (shape(rows + 2),) * 3, [plain(4)] * 3 + [vmem(6)] * 3, 12 * row_flops, "forward_far",
     )
     g1_near, g1_far, edges, dh1 = call(
-        functools.partial(backward1_kernel, rows), (g, gnear, gfar, hid1, g_inner, weights),
-        (shape(1), shape(1), shape(4), shape(rows + 2)),
-        [vmem(rows + 4), vmem(rows + 2)], 8 * row_flops, "backward1",
+        functools.partial(backward1_far_kernel, rows),
+        (g, gfar, hid1, g_inner, weights, dh1_near, edge_near),
+        (shape(1), shape(1), shape(4), shape(rows + 2)), [vmem(4)] * 2, 4 * row_flops, "backward1_far",
     )
     g1near, g1far = neighbours(g1_near, g1_far)
     g1, dh0_inner, *grads = call(
         functools.partial(middle_kernel, rows), (g, edges, hid1, dh1, x1, hid0, x, weights),
-        (shape(rows), shape(rows - 4)) + (grad,) * 4,
-        [vmem(rows), vmem(rows + 2), vmem(rows), vmem(rows - 4)],
+        (shape(rows), shape(rows - 2)) + (grad,) * 4,
+        [vmem(rows), vmem(rows + 2), vmem(rows), vmem(rows - 2)],
         36 * row_flops, "middle",
     )
-    dh0, dh0_near, dh0_far, part, send = call(
+    dh0_near, dh0_far, part, send = call(
         functools.partial(backward0_kernel, rows, scale),
         (g1, g1near, g1far, hid0, x, xnear, xfar, weights, *grads),
-        (shape(4), shape(1), shape(1), jax.ShapeDtypeStruct(half, F32),
+        (shape(1), shape(1), jax.ShapeDtypeStruct(half, F32),
          jax.ShapeDtypeStruct(half, BF16)),
-        [vmem(rows + 2), vmem(4), pltpu.VMEM((8 * CHAN, width), BF16),
+        [plain(2), vmem(6), vmem(2), plain(6),
          pltpu.VMEM((2, *half), F32)],
         8 * row_flops, "backward0",
     )
@@ -504,7 +569,7 @@
         arrived = [exchange(send, mask, count) for mask in masks]
         if input_grad is None:
             (input_grad,) = call(
-                functools.partial(input_grad_kernel, rows), (dh0_inner, dh0, dh0near, dh0far, g1, weights),
+                functools.partial(input_grad_kernel, rows), (dh0_inner, dh0_near, dh0_far, dh0near, dh0far, g1, weights),
                 (tile,),
                 [vmem(rows + 2), wide], 8 * row_flops, "input_grad", after=(send,),
             )

time: 63 us -> 61.6 us (0.978)
  starting transfers between devices: 26.6 us -> 24.5 us
  other arithmetic: 0.14 us -> 1.05 us
  waiting for transfers between devices: 8.57 us -> 7.9 us
    ppermute x11, starting transfers between devices: 23.7 us -> 21.6 us  [exchange(): return lax.ppermute(value, 'space', [(d, d ^ mask) for d in range(count)])]
    add x1, other arithmetic: 0.03 us -> 0.94 us  [local(): part = part + exchange(send, 1, count).astype(F32)]
    ppermute x11, waiting for transfers between devices: 8.56 us -> 7.88 us  [exchange(): return lax.ppermute(value, 'space', [(d, d ^ mask) for d in range(count)])]
    pallas_call x12 -> x13, Pallas kernels: 23.5 us -> 23.5 us  [call(): pl.pallas_call(kernel, out_shape=outs, in_specs=[ANY] * len(after) + [pla...]
  transfers between devices with their start and end apart: 15 -> 15, of which waited for: 7 -> 6; matrix products, arithmetic and copies ran while one was open for 0% -> 0% of each run, Pallas kernels for 28% -> 32%
where the time goes in v7:
time: 61.6 us; the launch traced here: 61.2 us
  starting transfers between devices  24.5 us (40%)
  Pallas kernels  23.5 us (38%)
  waiting for transfers between devices  7.9 us (13%)
  local copies, waits for them, and re-layouts  3.36 us (5%)
  other arithmetic  1.05 us (2%)
  between operations  0.91 us (1%)
    pallas_call x13, Pallas kernels, call(): pl.pallas_call(kernel, out_shape=outs, in_specs=[ANY] * len(after) + [pla...  23.5 us
    ppermute x11, starting transfers between devices, exchange(): return lax.ppermute(value, 'space', [(d, d ^ mask) for d in range(count)])  21.6 us
    ppermute x11, waiting for transfers between devices, exchange(): return lax.ppermute(value, 'space', [(d, d ^ mask) for d in range(count)])  7.88 us
    unnamed x22, local copies, waits for them, and re-layouts  3.36 us
    ppermute x4, starting transfers between devices, neighbours(): from_far = lax.ppermute(far, 'space', beyond)  2.91 us
  transfers between devices with their start and end apart: 15, of which 6 were waited for; matrix products, arithmetic and copies ran while one was open for 0% of the time, Pallas kernels for 32%

profile of v7, /device:TPU:0, one launch (start us, length us, event | category | flops | bytes accessed | tf_op | source)
XLA Modules:
  0.0 61.2 jit_solution(8855296881900679478)
XLA Ops:
  0.6 1.2 %copy-done = bf16[64,8,1024]{2,1,0:T(8,128)(2,1)S(1)} copy-done((bf16[64,8,1024]{2,1,0:T(8,128)(2,1)S(1)}, bf16[64,8,1024]{2,1,0:T(8,128)(2,1)}, u32[]{:S(2)}) %copy-start) | copy-done | bytes 1048600
  3.2 4.3 %collective-permute-start.2 = (bf16[256,1024]{1,0:T(8,128)(2,1)S(1)}, bf16[256,1024]{1,0:T(8,128)(2,1)S(1)}, u32[]{:S(2)}, u32[]{:S(2)}) collective-permute-start(bf16[256,1024]{1,0:T(8,128)(2,1)S(1)} %get-tuple-element.51), channel_id=1, source_target_pairs={{0,1},{1,0},{2,3},{3,2},{4,5},{5,4},{6,7},{7,6},{8,9},{9,8},{10,11... | collective-permute-start | bytes 1572872 | tf_op jit(solution)/shard_map/ppermute | solution.py:468
  9.2 1.7 %inner.1 = (bf16[384,1024]{1,0:T(8,128)(2,1)S(1)}, bf16[256,1024]{1,0:T(8,128)(2,1)S(1)}, bf16[128,1024]{1,0:T(8,128)(2,1)S(1)}) custom-call(bf16[512,1024]{1,0:T(8,128)(2,1)S(1)} %get-tuple-element.43.refs_0_.refs_1_.refs_6_.refs_4_, bf16[8,128,768]{2,1,0:T(8,128)(2,1)S(1)} %weights.1.refs_1_.refs_2_.refs_3_.refs_5_.refs_4_.refs_7_), custom_call_target="tpu_custom_call" | custom-call | flops 3623878656 | bytes 4194304 | tf_op jit(solution)/shard_map/inner/pallas_call | solution.py:28
  10.9 1.6 %g_rows.1 = (bf16[512,1024]{1,0:T(8,128)(2,1)S(1)}, bf16[128,1024]{1,0:T(8,128)(2,1)S(1)}, bf16[128,1024]{1,0:T(8,128)(2,1)S(1)}, f32[384,1024]{1,0:T(8,128)S(1)}) custom-call(bf16[128,1024]{1,0:T(8,128)(2,1)S(1)} %get-tuple-element.45.refs_0_.refs_5_.refs_3_, bf16[64,8,1024]{2,1,0:T(8,128)(2,1)S(1)} %copy-done.2, ...), custom_call_target="tpu_custom_call" | custom-call | flops 1811939328 | bytes 5767168 | tf_op jit(solution)/shard_map/g_rows/pallas_call | solution.py:28
  13.2 3.0 %collective-permute-start.3 = (bf16[128,1024]{1,0:T(8,128)(2,1)S(1)}, bf16[128,1024]{1,0:T(8,128)(2,1)S(1)}, u32[]{:S(2)}, u32[]{:S(2)}) collective-permute-start(bf16[128,1024]{1,0:T(8,128)(2,1)S(1)} %get-tuple-element.50.refs_0_), channel_id=1, source_target_pairs={{0,1},{1,0},{2,3},{3,2},{4,5},{5,4},{6,7},{7,6},{8,9},{9,8},{10,11... | collective-permute-start | bytes 786440 | tf_op jit(solution)/shard_map/ppermute | solution.py:468
  16.1 1.8 %forward_near.1 = (bf16[256,1024]{1,0:T(8,128)(2,1)S(1)}, bf16[256,1024]{1,0:T(8,128)(2,1)S(1)}, bf16[256,1024]{1,0:T(8,128)(2,1)S(1)}) custom-call(bf16[128,1024]{1,0:T(8,128)(2,1)S(1)} %get-tuple-element.50.refs_0_, bf16[512,1024]{1,0:T(8,128)(2,1)S(1)} %get-tuple-element.43.refs_0_.refs_1_.refs_6_.refs_4_, ...), custom_call_target="tpu_custom_call" | custom-call | flops 3623878656 | bytes 6029312 | tf_op jit(solution)/shard_map/forward_near/pallas_call | solution.py:28
  18.0 1.1 %backward1_near.1 = (bf16[384,1024]{1,0:T(8,128)(2,1)S(1)}, bf16[128,1024]{1,0:T(8,128)(2,1)S(1)}) custom-call(bf16[512,1024]{1,0:T(8,128)(2,1)S(1)} %get-tuple-element.46.refs_0_, bf16[128,1024]{1,0:T(8,128)(2,1)S(1)} %collective-permute-done.3.refs_1_, bf16[256,1024]{1,0:T(8,128)(2,1)S(1)} %get-tuple-element.54.refs_8_.refs_2_, ...), custom_call_target="tpu_custom_call" | custom-call | flops 1207959552 | bytes 6291456 | tf_op jit(solution)/shard_map/backward1_near/pallas_call | solution.py:28
  19.1 2.3 %forward_far.1 = (bf16[640,1024]{1,0:T(8,128)(2,1)S(1)}, bf16[640,1024]{1,0:T(8,128)(2,1)S(1)}, bf16[640,1024]{1,0:T(8,128)(2,1)S(1)}) custom-call(bf16[512,1024]{1,0:T(8,128)(2,1)S(1)} %get-tuple-element.43.refs_0_.refs_1_.refs_6_.refs_4_, bf16[256,1024]{1,0:T(8,128)(2,1)S(1)} %collective-permute-done.1.refs_1_.refs_6_, ...), custom_call_target="tpu_custom_call" | custom-call | flops 3623878656 | bytes 10223616 | tf_op jit(solution)/shard_map/forward_far/pallas_call | solution.py:28
  21.4 1.0 %backward1_far.1 = (bf16[64,1024]{1,0:T(8,128)(2,1)S(1)}, bf16[64,1024]{1,0:T(8,128)(2,1)S(1)}, bf16[256,1024]{1,0:T(8,128)(2,1)S(1)}, bf16[640,1024]{1,0:T(8,128)(2,1)S(1)}) custom-call(bf16[512,1024]{1,0:T(8,128)(2,1)S(1)} %get-tuple-element.46.refs_0_, bf16[128,1024]{1,0:T(8,128)(2,1)S(1)} %collective-permute-done.refs_1_, ...), custom_call_target="tpu_custom_call" | custom-call | flops 1207959552 | bytes 8912896 | tf_op jit(solution)/shard_map/backward1_far/pallas_call | solution.py:28
  22.4 3.4 %collective-permute-start.4 = (bf16[64,1024]{1,0:T(8,128)(2,1)S(1)}, bf16[64,1024]{1,0:T(8,128)(2,1)S(1)}, u32[]{:S(2)}, u32[]{:S(2)}) collective-permute-start(bf16[64,1024]{1,0:T(8,128)(2,1)S(1)} %get-tuple-element.64), channel_id=1, source_target_pairs={{0,1},{1,0},{2,3},{3,2},{4,5},{5,4},{6,7},{7,6},{8,9},{9,8},{10,11... | collective-permute-start | bytes 393224 | tf_op jit(solution)/shard_map/ppermute | solution.py:468
  26.5 4.8 %middle.1 = (bf16[512,1024]{1,0:T(8,128)(2,1)S(1)}, bf16[384,1024]{1,0:T(8,128)(2,1)S(1)}, f32[192,192]{1,0:T(8,128)S(1)}, f32[192,192]{1,0:T(8,128)S(1)}, f32[1...) custom-call(bf16[512,1024]{1,0:T(8,128)(2,1)S(1)} %get-tuple-element.46.refs_0_, ...), custom_call_target="tpu_custom_call" | custom-call | flops 10871635968 | bytes 11862016 | tf_op jit(solution)/shard_map/middle/pallas_call | solution.py:28
  31.4 1.4 %backward0.1 = (bf16[64,1024]{1,0:T(8,128)(2,1)S(1)}, bf16[64,1024]{1,0:T(8,128)(2,1)S(1)}, f32[64,1152]{1,0:T(8,128)S(1)}, bf16[64,1152]{1,0:T(8,128)(2,1)S(1)}) custom-call(bf16[512,1024]{1,0:T(8,128)(2,1)S(1)} %get-tuple-element.63.refs_0_.refs_6_, bf16[64,1024]{1,0:T(8,128)(2,1)S(1)} %collective-permute-done.4.refs_1_, ...), custom_call_target="tpu_custom_call" | custom-call | flops 2415919104 | bytes 7585792 | tf_op jit(solution)/shard_map/backward0/pallas_call | solution.py:28
  32.9 3.8 %collective-permute-start.6 = (bf16[64,1152]{1,0:T(8,128)(2,1)S(1)}, bf16[64,1152]{1,0:T(8,128)(2,1)}, u32[]{:S(2)}, u32[]{:S(2)}) collective-permute-start(bf16[64,1152]{1,0:T(8,128)(2,1)S(1)} %get-tuple-element.71), channel_id=1, source_target_pairs={{0,1},{1,0},{2,3},{3,2},{4,5},{5,4},{6,7},{7,6},{8,9},{9,8},{10,11... | collective-permute-start | bytes 442376 | tf_op jit(solution)/shard_map/ppermute | solution.py:468
  36.7 1.1 %collective-permute-done.6 = bf16[64,1152]{1,0:T(8,128)(2,1)} collective-permute-done((bf16[64,1152]{1,0:T(8,128)(2,1)S(1)}, bf16[64,1152]{1,0:T(8,128)(2,1)}, u32[]{:S(2)}, u32[]{:S(2)}) %collective-permute-start.6) | collective-permute-done | bytes 147488 | tf_op jit(solution)/shard_map/ppermute | solution.py:468
  38.8 1.5 %collective-permute-start.7 = (bf16[32,1152]{1,0:T(8,128)(2,1)S(1)}, bf16[32,1152]{1,0:T(8,128)(2,1)S(1)}, u32[]{:S(2)}, u32[]{:S(2)}) collective-permute-start(bf16[32,1152]{1,0:T(8,128)(2,1)S(1)} %select_convert_fusion), channel_id=1, source_target_pairs={{0,2},{1,3},{2,0},{3,1},{4,6},{5,7},{6,4},{7,5},{8,10},{9,11},{10,... | collective-permute-start | bytes 221192 | tf_op jit(solution)/shard_map/ppermute | solution.py:468
  41.2 2.2 %collective-permute-done.7 = bf16[32,1152]{1,0:T(8,128)(2,1)S(1)} collective-permute-done((bf16[32,1152]{1,0:T(8,128)(2,1)S(1)}, bf16[32,1152]{1,0:T(8,128)(2,1)S(1)}, u32[]{:S(2)}, u32[]{:S(2)}) %collective-permute-start.7) | collective-permute-done | bytes 73760 | tf_op jit(solution)/shard_map/ppermute | solution.py:468
  43.4 1.7 %collective-permute-start.8 = (bf16[32,1152]{1,0:T(8,128)(2,1)S(1)}, bf16[32,1152]{1,0:T(8,128)(2,1)S(1)}, u32[]{:S(2)}, u32[]{:S(2)}) collective-permute-start(bf16[32,1152]{1,0:T(8,128)(2,1)S(1)} %add_convert_fusion.1.refs_0_), channel_id=1, source_target_pairs={{0,4},{1,5},{2,6},{3,7},{4,0},{5,1},{6,2},{7,3},{8,12},{9,13},{10,... | collective-permute-start | bytes 221192 | tf_op jit(solution)/shard_map/ppermute | solution.py:468
  45.1 2.6 %collective-permute-start.9 = (bf16[32,1152]{1,0:T(8,128)(2,1)S(1)}, bf16[32,1152]{1,0:T(8,128)(2,1)S(1)}, u32[]{:S(2)}, u32[]{:S(2)}) collective-permute-start(bf16[32,1152]{1,0:T(8,128)(2,1)S(1)} %add_convert_fusion.1.refs_0_), channel_id=1, source_target_pairs={{0,8},{1,9},{2,10},{3,11},{4,12},{5,13},{6,14},{7,15},{8,0},{9,1},... | collective-permute-start | bytes 221192 | tf_op jit(solution)/shard_map/ppermute | solution.py:468
  47.9 1.1 %copy-done.10 = bf16[384,1024]{1,0:T(8,128)(2,1)S(1)} copy-done((bf16[384,1024]{1,0:T(8,128)(2,1)S(1)}, bf16[384,1024]{1,0:T(8,128)(2,1)}, u32[]{:S(2)}) %copy-start.10) | copy-done | bytes 786456
  49.0 2.9 %input_grad.1 = bf16[64,8,1024]{2,1,0:T(8,128)(2,1)} custom-call(bf16[32,1152]{1,0:T(8,128)(2,1)S(1)} %add_convert_fusion.1.refs_0_, bf16[384,1024]{1,0:T(8,128)(2,1)S(1)} %copy-done.10, bf16[64,1024]{1,0:T(8,128)(2,1)S(1)} %get-tuple-element.75.refs_2_, bf16[64,1024]{1,0:T(8,128)(2,1)S(1)} %copy-done.4, ...), custom_call_target="tpu_custom_call" | custom-call | flops 2415919104 | bytes 4980736 | tf_op jit(solution)/shard_map/input_grad/pallas_call | solution.py:28
  52.2 2.1 %collective-permute-done.10 = bf16[32,1152]{1,0:T(8,128)(2,1)S(1)} collective-permute-done((bf16[32,1152]{1,0:T(8,128)(2,1)S(1)}, bf16[32,1152]{1,0:T(8,128)(2,1)S(1)}, u32[]{:S(2)}, u32[]{:S(2)}) %collective-permute-start.10) | collective-permute-done | bytes 73760 | tf_op jit(solution)/shard_map/ppermute | solution.py:468
  54.4 1.0 %collective-permute-start.13 = (bf16[32,1152]{1,0:T(8,128)(2,1)S(1)}, bf16[32,1152]{1,0:T(8,128)(2,1)S(1)}, u32[]{:S(2)}, u32[]{:S(2)}) collective-permute-start(bf16[32,1152]{1,0:T(8,128)(2,1)S(1)} %add_convert_fusion.refs_0_), channel_id=1, source_target_pairs={{0,2},{1,3},{2,0},{3,1},{4,6},{5,7},{6,4},{7,5},{8,10},{9,11},{10,... | collective-permute-start | bytes 221192 | tf_op jit(solution)/shard_map/ppermute | solution.py:468
  55.4 2.6 %output.1 = bf16[64,8,1024]{2,1,0:T(8,128)(2,1)} custom-call(bf16[32,1152]{1,0:T(8,128)(2,1)S(1)} %add_convert_fusion.refs_0_, bf16[640,1024]{1,0:T(8,128)(2,1)S(1)} %get-tuple-element.55.refs_2_.refs_1_, bf16[640,1024]{1,0:T(8,128)(2,1)S(1)} %copy-done.8, bf16[8,128,768]{2,1,0:T(8,128)(2,1)S(1)} %weights.1.refs_1_.refs_2_.refs_3_.refs_5_.refs_4_.refs_7_), custom_call_target="tpu_custom_call" | custom-call | flops 2415919104 | bytes 5242880 | tf_op jit(solution)/shard_map/output/pallas_call | solution.py:28
  58.9 1.4 %collective-permute-done.14.refs_1_ = bf16[64,1152]{1,0:T(8,128)(2,1)S(1)} collective-permute-done((bf16[64,1152]{1,0:T(8,128)(2,1)S(1)}, bf16[64,1152]{1,0:T(8,128)(2,1)S(1)}, u32[]{:S(2)}, u32[]{:S(2)}) %collective-permute-start.14) | collective-permute-done | bytes 147488 | tf_op jit(solution)/shard_map/ppermute | solution.py:468
  (46 shorter events, 8.6 us)
Async XLA Ops:
  0.6 1.2 %copy-start = (bf16[64,8,1024]{2,1,0:T(8,128)(2,1)S(1)}, bf16[64,8,1024]{2,1,0:T(8,128)(2,1)}, u32[]{:S(2)}) copy-start(bf16[64,8,1024]{2,1,0:T(8,128)(2,1)} %refs_0_.1) | copy-start | bytes 3145732
  2.5 16.6 %collective-permute-start.1 = (bf16[256,1024]{1,0:T(8,128)(2,1)S(1)}, bf16[256,1024]{1,0:T(8,128)(2,1)S(1)}, u32[]{:S(2)}, u32[]{:S(2)}) collective-permute-start(bf16[256,1024]{1,0:T(8,128)(2,1)S(1)} %get-tuple-element.44.refs_0_), channel_id=1, source_target_pairs={{1,2},{3,4},{5,6},{7,8},{9,10},{11,12},{13,14},{2,1},{4,3},{6,5},{... | collective-permute-start | bytes 1572872 | tf_op jit(solution)/shard_map/ppermute | solution.py:490
  3.2 12.9 %collective-permute-start.2 = (bf16[256,1024]{1,0:T(8,128)(2,1)S(1)}, bf16[256,1024]{1,0:T(8,128)(2,1)S(1)}, u32[]{:S(2)}, u32[]{:S(2)}) collective-permute-start(bf16[256,1024]{1,0:T(8,128)(2,1)S(1)} %get-tuple-element.51), channel_id=1, source_target_pairs={{0,1},{1,0},{2,3},{3,2},{4,5},{5,4},{6,7},{7,6},{8,9},{9,8},{10,11... | collective-permute-start | bytes 1572872 | tf_op jit(solution)/shard_map/ppermute | solution.py:468
  9.2 1.7 %copy-start.2 = (bf16[64,8,1024]{2,1,0:T(8,128)(2,1)S(1)}, bf16[64,8,1024]{2,1,0:T(8,128)(2,1)}, u32[]{:S(2)}) copy-start(bf16[64,8,1024]{2,1,0:T(8,128)(2,1)} %refs_1_.3) | copy-start | bytes 3145732
  12.5 8.9 %collective-permute-start = (bf16[128,1024]{1,0:T(8,128)(2,1)S(1)}, bf16[128,1024]{1,0:T(8,128)(2,1)S(1)}, u32[]{:S(2)}, u32[]{:S(2)}) collective-permute-start(bf16[128,1024]{1,0:T(8,128)(2,1)S(1)} %get-tuple-element.47), channel_id=1, source_target_pairs={{1,2},{3,4},{5,6},{7,8},{9,10},{11,12},{13,14},{2,1},{4,3},{6,5},{... | collective-permute-start | bytes 786440 | tf_op jit(solution)/shard_map/ppermute | solution.py:490
  13.2 4.8 %collective-permute-start.3 = (bf16[128,1024]{1,0:T(8,128)(2,1)S(1)}, bf16[128,1024]{1,0:T(8,128)(2,1)S(1)}, u32[]{:S(2)}, u32[]{:S(2)}) collective-permute-start(bf16[128,1024]{1,0:T(8,128)(2,1)S(1)} %get-tuple-element.50.refs_0_), channel_id=1, source_target_pairs={{0,1},{1,0},{2,3},{3,2},{4,5},{5,4},{6,7},{7,6},{8,9},{9,8},{10,11... | collective-permute-start | bytes 786440 | tf_op jit(solution)/shard_map/ppermute | solution.py:468
  21.4 5.1 %copy-start.7 = (bf16[640,1024]{1,0:T(8,128)(2,1)}, bf16[640,1024]{1,0:T(8,128)(2,1)S(1)}, u32[]{:S(2)}) copy-start(bf16[640,1024]{1,0:T(8,128)(2,1)S(1)} %get-tuple-element.61.refs_4_.refs_2_) | copy-start | bytes 3932164
  22.4 9.0 %collective-permute-start.4 = (bf16[64,1024]{1,0:T(8,128)(2,1)S(1)}, bf16[64,1024]{1,0:T(8,128)(2,1)S(1)}, u32[]{:S(2)}, u32[]{:S(2)}) collective-permute-start(bf16[64,1024]{1,0:T(8,128)(2,1)S(1)} %get-tuple-element.64), channel_id=1, source_target_pairs={{0,1},{1,0},{2,3},{3,2},{4,5},{5,4},{6,7},{7,6},{8,9},{9,8},{10,11... | collective-permute-start | bytes 393224 | tf_op jit(solution)/shard_map/ppermute | solution.py:468
  25.8 5.5 %collective-permute-start.5 = (bf16[64,1024]{1,0:T(8,128)(2,1)S(1)}, bf16[64,1024]{1,0:T(8,128)(2,1)S(1)}, u32[]{:S(2)}, u32[]{:S(2)}) collective-permute-start(bf16[64,1024]{1,0:T(8,128)(2,1)S(1)} %get-tuple-element.65), channel_id=1, source_target_pairs={{1,2},{3,4},{5,6},{7,8},{9,10},{11,12},{13,14},{2,1},{4,3},{6,5},{... | collective-permute-start | bytes 393224 | tf_op jit(solution)/shard_map/ppermute | solution.py:490
  31.3 1.5 %copy-start.5 = (bf16[512,1024]{1,0:T(8,128)(2,1)}, bf16[512,1024]{1,0:T(8,128)(2,1)S(1)}, u32[]{:S(2)}) copy-start(bf16[512,1024]{1,0:T(8,128)(2,1)S(1)} %get-tuple-element.63.refs_0_.refs_6_) | copy-start | bytes 3145732
  31.4 1.5 %copy-start.9 = (bf16[384,1024]{1,0:T(8,128)(2,1)}, bf16[384,1024]{1,0:T(8,128)(2,1)S(1)}, u32[]{:S(2)}) copy-start(bf16[384,1024]{1,0:T(8,128)(2,1)S(1)} %get-tuple-element.72.refs_1_) | copy-start | bytes 2359300
  32.9 3.8 %copy-start.3 = (bf16[64,1024]{1,0:T(8,128)(2,1)}, bf16[64,1024]{1,0:T(8,128)(2,1)S(1)}, u32[]{:S(2)}) copy-start(bf16[64,1024]{1,0:T(8,128)(2,1)S(1)} %get-tuple-element.76.refs_3_) | copy-start | bytes 393220
  32.9 4.9 %collective-permute-start.6 = (bf16[64,1152]{1,0:T(8,128)(2,1)S(1)}, bf16[64,1152]{1,0:T(8,128)(2,1)}, u32[]{:S(2)}, u32[]{:S(2)}) collective-permute-start(bf16[64,1152]{1,0:T(8,128)(2,1)S(1)} %get-tuple-element.71), channel_id=1, source_target_pairs={{0,1},{1,0},{2,3},{3,2},{4,5},{5,4},{6,7},{7,6},{8,9},{9,8},{10,11... | collective-permute-start | bytes 442376 | tf_op jit(solution)/shard_map/ppermute | solution.py:468
  36.7 11.2 %copy-start.4 = (bf16[64,1024]{1,0:T(8,128)(2,1)S(1)}, bf16[64,1024]{1,0:T(8,128)(2,1)}, u32[]{:S(2)}) copy-start(bf16[64,1024]{1,0:T(8,128)(2,1)} %copy-done.3) | copy-start | bytes 393220
  36.7 11.2 %copy-start.6 = (bf16[512,1024]{1,0:T(8,128)(2,1)S(1)}, bf16[512,1024]{1,0:T(8,128)(2,1)}, u32[]{:S(2)}) copy-start(bf16[512,1024]{1,0:T(8,128)(2,1)} %copy-done.5) | copy-start | bytes 3145732
  38.8 4.6 %collective-permute-start.7 = (bf16[32,1152]{1,0:T(8,128)(2,1)S(1)}, bf16[32,1152]{1,0:T(8,128)(2,1)S(1)}, u32[]{:S(2)}, u32[]{:S(2)}) collective-permute-start(bf16[32,1152]{1,0:T(8,128)(2,1)S(1)} %select_convert_fusion), channel_id=1, source_target_pairs={{0,2},{1,3},{2,0},{3,1},{4,6},{5,7},{6,4},{7,5},{8,10},{9,11},{10,... | collective-permute-start | bytes 221192 | tf_op jit(solution)/shard_map/ppermute | solution.py:468
  40.2 7.6 %collective-permute-start.11 = (bf16[64,1024]{1,0:T(8,128)(2,1)S(1)}, bf16[64,1024]{1,0:T(8,128)(2,1)S(1)}, u32[]{:S(2)}, u32[]{:S(2)}) collective-permute-start(bf16[64,1024]{1,0:T(8,128)(2,1)S(1)} %get-tuple-element.75.refs_2_), channel_id=1, source_target_pairs={{0,1},{1,0},{2,3},{3,2},{4,5},{5,4},{6,7},{7,6},{8,9},{9,8},{10,11... | collective-permute-start | bytes 393224 | tf_op jit(solution)/shard_map/ppermute | solution.py:468
  40.3 7.6 %collective-permute-start.12 = (bf16[64,1024]{1,0:T(8,128)(2,1)}, bf16[64,1024]{1,0:T(8,128)(2,1)S(1)}, u32[]{:S(2)}, u32[]{:S(2)}) collective-permute-start(bf16[64,1024]{1,0:T(8,128)(2,1)} %copy-done.3), channel_id=1, source_target_pairs={{1,2},{3,4},{5,6},{7,8},{9,10},{11,12},{13,14},{2,1},{4,3},{6,5},{... | collective-permute-start | bytes 393224 | tf_op jit(solution)/shard_map/ppermute | solution.py:490
  43.4 8.6 %collective-permute-start.8 = (bf16[32,1152]{1,0:T(8,128)(2,1)S(1)}, bf16[32,1152]{1,0:T(8,128)(2,1)S(1)}, u32[]{:S(2)}, u32[]{:S(2)}) collective-permute-start(bf16[32,1152]{1,0:T(8,128)(2,1)S(1)} %add_convert_fusion.1.refs_0_), channel_id=1, source_target_pairs={{0,4},{1,5},{2,6},{3,7},{4,0},{5,1},{6,2},{7,3},{8,12},{9,13},{10,... | collective-permute-start | bytes 221192 | tf_op jit(solution)/shard_map/ppermute | solution.py:468
  45.1 7.1 %collective-permute-start.9 = (bf16[32,1152]{1,0:T(8,128)(2,1)S(1)}, bf16[32,1152]{1,0:T(8,128)(2,1)S(1)}, u32[]{:S(2)}, u32[]{:S(2)}) collective-permute-start(bf16[32,1152]{1,0:T(8,128)(2,1)S(1)} %add_convert_fusion.1.refs_0_), channel_id=1, source_target_pairs={{0,8},{1,9},{2,10},{3,11},{4,12},{5,13},{6,14},{7,15},{8,0},{9,1},... | collective-permute-start | bytes 221192 | tf_op jit(solution)/shard_map/ppermute | solution.py:468
  47.7 6.6 %collective-permute-start.10 = (bf16[32,1152]{1,0:T(8,128)(2,1)S(1)}, bf16[32,1152]{1,0:T(8,128)(2,1)S(1)}, u32[]{:S(2)}, u32[]{:S(2)}) collective-permute-start(bf16[32,1152]{1,0:T(8,128)(2,1)S(1)} %add_convert_fusion.1.refs_0_), channel_id=1, source_target_pairs={{0,12},{1,13},{2,14},{3,15},{4,8},{5,9},{6,10},{7,11},{8,4},{9,5},... | collective-permute-start | bytes 221192 | tf_op jit(solution)/shard_map/ppermute | solution.py:468
  49.0 6.4 %copy-start.8 = (bf16[640,1024]{1,0:T(8,128)(2,1)S(1)}, bf16[640,1024]{1,0:T(8,128)(2,1)}, u32[]{:S(2)}) copy-start(bf16[640,1024]{1,0:T(8,128)(2,1)} %copy-done.7) | copy-start | bytes 3932164
  54.4 4.4 %collective-permute-start.13 = (bf16[32,1152]{1,0:T(8,128)(2,1)S(1)}, bf16[32,1152]{1,0:T(8,128)(2,1)S(1)}, u32[]{:S(2)}, u32[]{:S(2)}) collective-permute-start(bf16[32,1152]{1,0:T(8,128)(2,1)S(1)} %add_convert_fusion.refs_0_), channel_id=1, source_target_pairs={{0,2},{1,3},{2,0},{3,1},{4,6},{5,7},{6,4},{7,5},{8,10},{9,11},{10,... | collective-permute-start | bytes 221192 | tf_op jit(solution)/shard_map/ppermute | solution.py:468
  58.9 1.4 %collective-permute-start.14 = (bf16[64,1152]{1,0:T(8,128)(2,1)S(1)}, bf16[64,1152]{1,0:T(8,128)(2,1)S(1)}, u32[]{:S(2)}, u32[]{:S(2)}) collective-permute-start(bf16[64,1152]{1,0:T(8,128)(2,1)S(1)} %maximum_select_fusion.refs_0_), channel_id=1, source_target_pairs={{0,1},{1,0},{2,3},{3,2},{4,5},{5,4},{6,7},{7,6},{8,9},{9,8},{10,11... | collective-permute-start | bytes 442376 | tf_op jit(solution)/shard_map/ppermute | solution.py:468
  (2 other events, 2.1 us)

commit v8 on v7

--- a/solution.py
+++ b/solution.py
@@ -456,13 +456,22 @@
     channels_first(wide, out_ref)
 
 
+def halved_kernel(part_ref, other_ref, keep_ref, send_ref):
+    low, high = (
+        part_ref[at : at + CHAN // 2, :] + other_ref[at : at + CHAN // 2, :].astype(F32)
+        for at in (0, CHAN // 2)
+    )
+    bit = lax.rem(lax.axis_index("space"), 4) >= 2
+    keep_ref[...] = jnp.where(bit, high, low)
+    send_ref[...] = jnp.where(bit, low, high).astype(BF16)
+
+
 def gathered_kernel(own_ref, other_ref, out_ref):
     mine = lax.rem(lax.axis_index("space"), 2)
     for section, ref in ((mine, own_ref), (1 - mine, other_ref)):
         for which in range(2):
             piece = ref[:, which * 9 * CHAN : (which + 1) * 9 * CHAN]
             out_ref[section, which] = piece.astype(F32)
-
 
 def exchange(value, mask, count):
     return lax.ppermute(value, "space", [(d, d ^ mask) for d in range(count)])
@@ -552,11 +561,11 @@
         8 * row_flops, "backward0",
     )
 
-    part = part + exchange(send, 1, count).astype(F32)
-    low, high = part[: CHAN // 2], part[CHAN // 2 :]
-    bit = (place & 2) != 0
-    send = jnp.where(bit, low, high).astype(BF16)
-    part = jnp.where(bit, high, low)
+    quarter = (CHAN // 2, 18 * CHAN)
+    part, send = call(
+        halved_kernel, (part, exchange(send, 1, count)),
+        (jax.ShapeDtypeStruct(quarter, F32), jax.ShapeDtypeStruct(quarter, BF16)), [], 0, "halved",
+    )
     arrived = exchange(send, 2, count)
     dh0_near, dh0_far, _ = lax.optimization_barrier((dh0_near, dh0_far, send))
     dh0near, dh0far = neighbours(dh0_near, dh0_far)

time: 61.6 us -> 60.5 us (0.982)
  waiting for transfers between devices: 7.9 us -> 6.57 us
  local copies, waits for them, and re-layouts: 3.36 us -> 4.57 us
  other arithmetic: 1.05 us -> 0.09 us
    ppermute x11, waiting for transfers between devices: 7.88 us -> 6.55 us  [exchange(): return lax.ppermute(value, 'space', [(d, d ^ mask) for d in range(count)])]
    unnamed x22 -> x18, local copies, waits for them, and re-layouts: 3.36 us -> 4.57 us
    add x1 -> x0, other arithmetic: 0.94 us -> none  [local(): part = part + exchange(send, 1, count).astype(F32)]
    pallas_call x13 -> x14, Pallas kernels: 23.5 us -> 23.5 us  [call(): pl.pallas_call(kernel, out_shape=outs, in_specs=[ANY] * len(after) + [pla...]
  transfers between devices with their start and end apart: 15 -> 15, of which waited for: 6 -> 5; matrix products, arithmetic and copies ran while one was open for 0% -> 0% of each run, Pallas kernels for 32% -> 32%
where the time goes in v8:
time: 60.5 us; the launch traced here: 60.2 us
  starting transfers between devices  24.5 us (40%)
  Pallas kernels  23.5 us (39%)
  waiting for transfers between devices  6.57 us (11%)
  local copies, waits for them, and re-layouts  4.57 us (8%)
  between operations  0.87 us (1%)
    pallas_call x14, Pallas kernels, call(): pl.pallas_call(kernel, out_shape=outs, in_specs=[ANY] * len(after) + [pla...  23.5 us
    ppermute x11, starting transfers between devices, exchange(): return lax.ppermute(value, 'space', [(d, d ^ mask) for d in range(count)])  21.6 us
    ppermute x11, waiting for transfers between devices, exchange(): return lax.ppermute(value, 'space', [(d, d ^ mask) for d in range(count)])  6.55 us
    unnamed x18, local copies, waits for them, and re-layouts  4.57 us
    ppermute x4, starting transfers between devices, neighbours(): from_far = lax.ppermute(far, 'space', beyond)  2.91 us
  transfers between devices with their start and end apart: 15, of which 5 were waited for; matrix products, arithmetic and copies ran while one was open for 0% of the time, Pallas kernels for 32%

profile of v8, /device:TPU:0, one launch (start us, length us, event | category | flops | bytes accessed | tf_op | source)
XLA Modules:
  0.0 60.2 jit_solution(17267873817194965942)
XLA Ops:
  0.6 1.2 %copy-done = bf16[64,8,1024]{2,1,0:T(8,128)(2,1)S(1)} copy-done((bf16[64,8,1024]{2,1,0:T(8,128)(2,1)S(1)}, bf16[64,8,1024]{2,1,0:T(8,128)(2,1)}, u32[]{:S(2)}) %copy-start) | copy-done | bytes 1048600
  3.2 4.3 %collective-permute-start.2 = (bf16[256,1024]{1,0:T(8,128)(2,1)S(1)}, bf16[256,1024]{1,0:T(8,128)(2,1)S(1)}, u32[]{:S(2)}, u32[]{:S(2)}) collective-permute-start(bf16[256,1024]{1,0:T(8,128)(2,1)S(1)} %get-tuple-element.53), channel_id=1, source_target_pairs={{0,1},{1,0},{2,3},{3,2},{4,5},{5,4},{6,7},{7,6},{8,9},{9,8},{10,11... | collective-permute-start | bytes 1572872 | tf_op jit(solution)/shard_map/ppermute | solution.py:477
  9.2 1.7 %inner.1 = (bf16[384,1024]{1,0:T(8,128)(2,1)S(1)}, bf16[256,1024]{1,0:T(8,128)(2,1)S(1)}, bf16[128,1024]{1,0:T(8,128)(2,1)S(1)}) custom-call(bf16[512,1024]{1,0:T(8,128)(2,1)S(1)} %get-tuple-element.45.refs_0_.refs_1_.refs_6_.refs_4_, bf16[8,128,768]{2,1,0:T(8,128)(2,1)S(1)} %weights.1.refs_1_.refs_2_.refs_3_.refs_5_.refs_4_.refs_7_), custom_call_target="tpu_custom_call" | custom-call | flops 3623878656 | bytes 4194304 | tf_op jit(solution)/shard_map/inner/pallas_call | solution.py:28
  10.9 1.6 %g_rows.1 = (bf16[512,1024]{1,0:T(8,128)(2,1)S(1)}, bf16[128,1024]{1,0:T(8,128)(2,1)S(1)}, bf16[128,1024]{1,0:T(8,128)(2,1)S(1)}, f32[384,1024]{1,0:T(8,128)S(1)}) custom-call(bf16[128,1024]{1,0:T(8,128)(2,1)S(1)} %get-tuple-element.47.refs_0_.refs_5_.refs_3_, bf16[64,8,1024]{2,1,0:T(8,128)(2,1)S(1)} %copy-done.2, ...), custom_call_target="tpu_custom_call" | custom-call | flops 1811939328 | bytes 5767168 | tf_op jit(solution)/shard_map/g_rows/pallas_call | solution.py:28
  13.2 3.0 %collective-permute-start.3 = (bf16[128,1024]{1,0:T(8,128)(2,1)S(1)}, bf16[128,1024]{1,0:T(8,128)(2,1)S(1)}, u32[]{:S(2)}, u32[]{:S(2)}) collective-permute-start(bf16[128,1024]{1,0:T(8,128)(2,1)S(1)} %get-tuple-element.52.refs_0_), channel_id=1, source_target_pairs={{0,1},{1,0},{2,3},{3,2},{4,5},{5,4},{6,7},{7,6},{8,9},{9,8},{10,11... | collective-permute-start | bytes 786440 | tf_op jit(solution)/shard_map/ppermute | solution.py:477
  16.1 1.8 %forward_near.1 = (bf16[256,1024]{1,0:T(8,128)(2,1)S(1)}, bf16[256,1024]{1,0:T(8,128)(2,1)S(1)}, bf16[256,1024]{1,0:T(8,128)(2,1)S(1)}) custom-call(bf16[128,1024]{1,0:T(8,128)(2,1)S(1)} %get-tuple-element.52.refs_0_, bf16[512,1024]{1,0:T(8,128)(2,1)S(1)} %get-tuple-element.45.refs_0_.refs_1_.refs_6_.refs_4_, ...), custom_call_target="tpu_custom_call" | custom-call | flops 3623878656 | bytes 6029312 | tf_op jit(solution)/shard_map/forward_near/pallas_call | solution.py:28
  18.0 1.1 %backward1_near.1 = (bf16[384,1024]{1,0:T(8,128)(2,1)S(1)}, bf16[128,1024]{1,0:T(8,128)(2,1)S(1)}) custom-call(bf16[512,1024]{1,0:T(8,128)(2,1)S(1)} %get-tuple-element.48.refs_0_, bf16[128,1024]{1,0:T(8,128)(2,1)S(1)} %collective-permute-done.3.refs_1_, bf16[256,1024]{1,0:T(8,128)(2,1)S(1)} %get-tuple-element.56.refs_8_.refs_2_, ...), custom_call_target="tpu_custom_call" | custom-call | flops 1207959552 | bytes 6291456 | tf_op jit(solution)/shard_map/backward1_near/pallas_call | solution.py:28
  19.1 2.3 %forward_far.1 = (bf16[640,1024]{1,0:T(8,128)(2,1)S(1)}, bf16[640,1024]{1,0:T(8,128)(2,1)S(1)}, bf16[640,1024]{1,0:T(8,128)(2,1)S(1)}) custom-call(bf16[512,1024]{1,0:T(8,128)(2,1)S(1)} %get-tuple-element.45.refs_0_.refs_1_.refs_6_.refs_4_, bf16[256,1024]{1,0:T(8,128)(2,1)S(1)} %collective-permute-done.1.refs_1_.refs_6_, ...), custom_call_target="tpu_custom_call" | custom-call | flops 3623878656 | bytes 10223616 | tf_op jit(solution)/shard_map/forward_far/pallas_call | solution.py:28
  22.4 3.4 %collective-permute-start.4 = (bf16[64,1024]{1,0:T(8,128)(2,1)S(1)}, bf16[64,1024]{1,0:T(8,128)(2,1)S(1)}, u32[]{:S(2)}, u32[]{:S(2)}) collective-permute-start(bf16[64,1024]{1,0:T(8,128)(2,1)S(1)} %get-tuple-element.66), channel_id=1, source_target_pairs={{0,1},{1,0},{2,3},{3,2},{4,5},{5,4},{6,7},{7,6},{8,9},{9,8},{10,11... | collective-permute-start | bytes 393224 | tf_op jit(solution)/shard_map/ppermute | solution.py:477
  26.5 4.8 %middle.1 = (bf16[512,1024]{1,0:T(8,128)(2,1)S(1)}, bf16[384,1024]{1,0:T(8,128)(2,1)S(1)}, f32[192,192]{1,0:T(8,128)S(1)}, f32[192,192]{1,0:T(8,128)S(1)}, f32[1...) custom-call(bf16[512,1024]{1,0:T(8,128)(2,1)S(1)} %get-tuple-element.48.refs_0_, ...), custom_call_target="tpu_custom_call" | custom-call | flops 10871635968 | bytes 11862016 | tf_op jit(solution)/shard_map/middle/pallas_call | solution.py:28
  31.4 1.4 %backward0.1 = (bf16[64,1024]{1,0:T(8,128)(2,1)S(1)}, bf16[64,1024]{1,0:T(8,128)(2,1)S(1)}, f32[64,1152]{1,0:T(8,128)S(1)}, bf16[64,1152]{1,0:T(8,128)(2,1)S(1)}) custom-call(bf16[512,1024]{1,0:T(8,128)(2,1)S(1)} %get-tuple-element.65.refs_0_.refs_6_, bf16[64,1024]{1,0:T(8,128)(2,1)S(1)} %collective-permute-done.4.refs_1_, ...), custom_call_target="tpu_custom_call" | custom-call | flops 2415919104 | bytes 7585792 | tf_op jit(solution)/shard_map/backward0/pallas_call | solution.py:28
  32.9 3.8 %collective-permute-start.6 = (bf16[64,1152]{1,0:T(8,128)(2,1)S(1)}, bf16[64,1152]{1,0:T(8,128)(2,1)S(1)}, u32[]{:S(2)}, u32[]{:S(2)}) collective-permute-start(bf16[64,1152]{1,0:T(8,128)(2,1)S(1)} %get-tuple-element.73), channel_id=1, source_target_pairs={{0,1},{1,0},{2,3},{3,2},{4,5},{5,4},{6,7},{7,6},{8,9},{9,8},{10,11... | collective-permute-start | bytes 442376 | tf_op jit(solution)/shard_map/ppermute | solution.py:477
  36.7 1.0 %collective-permute-done.6.refs_1_ = bf16[64,1152]{1,0:T(8,128)(2,1)S(1)} collective-permute-done((bf16[64,1152]{1,0:T(8,128)(2,1)S(1)}, bf16[64,1152]{1,0:T(8,128)(2,1)S(1)}, u32[]{:S(2)}, u32[]{:S(2)}) %collective-permute-start.6) | collective-permute-done | bytes 147488 | tf_op jit(solution)/shard_map/ppermute | solution.py:477
  37.7 1.5 %collective-permute-start.7 = (bf16[32,1152]{1,0:T(8,128)(2,1)S(1)}, bf16[32,1152]{1,0:T(8,128)(2,1)S(1)}, u32[]{:S(2)}, u32[]{:S(2)}) collective-permute-start(bf16[32,1152]{1,0:T(8,128)(2,1)S(1)} %get-tuple-element.75), channel_id=1, source_target_pairs={{0,2},{1,3},{2,0},{3,1},{4,6},{5,7},{6,4},{7,5},{8,10},{9,11},{10,... | collective-permute-start | bytes 221192 | tf_op jit(solution)/shard_map/ppermute | solution.py:477
  40.1 2.2 %collective-permute-done.7 = bf16[32,1152]{1,0:T(8,128)(2,1)S(1)} collective-permute-done((bf16[32,1152]{1,0:T(8,128)(2,1)S(1)}, bf16[32,1152]{1,0:T(8,128)(2,1)S(1)}, u32[]{:S(2)}, u32[]{:S(2)}) %collective-permute-start.7) | collective-permute-done | bytes 73760 | tf_op jit(solution)/shard_map/ppermute | solution.py:477
  42.3 1.7 %collective-permute-start.8 = (bf16[32,1152]{1,0:T(8,128)(2,1)S(1)}, bf16[32,1152]{1,0:T(8,128)(2,1)S(1)}, u32[]{:S(2)}, u32[]{:S(2)}) collective-permute-start(bf16[32,1152]{1,0:T(8,128)(2,1)S(1)} %add_convert_fusion.1.refs_0_), channel_id=1, source_target_pairs={{0,4},{1,5},{2,6},{3,7},{4,0},{5,1},{6,2},{7,3},{8,12},{9,13},{10,... | collective-permute-start | bytes 221192 | tf_op jit(solution)/shard_map/ppermute | solution.py:477
  44.0 2.6 %collective-permute-start.9 = (bf16[32,1152]{1,0:T(8,128)(2,1)S(1)}, bf16[32,1152]{1,0:T(8,128)(2,1)S(1)}, u32[]{:S(2)}, u32[]{:S(2)}) collective-permute-start(bf16[32,1152]{1,0:T(8,128)(2,1)S(1)} %add_convert_fusion.1.refs_0_), channel_id=1, source_target_pairs={{0,8},{1,9},{2,10},{3,11},{4,12},{5,13},{6,14},{7,15},{8,0},{9,1},... | collective-permute-start | bytes 221192 | tf_op jit(solution)/shard_map/ppermute | solution.py:477
  46.8 1.2 %copy-done.4 = bf16[512,1024]{1,0:T(8,128)(2,1)S(1)} copy-done((bf16[512,1024]{1,0:T(8,128)(2,1)S(1)}, bf16[512,1024]{1,0:T(8,128)(2,1)}, u32[]{:S(2)}) %copy-start.4) | copy-done | bytes 1048600
  48.0 1.1 %copy-done.8 = bf16[384,1024]{1,0:T(8,128)(2,1)S(1)} copy-done((bf16[384,1024]{1,0:T(8,128)(2,1)S(1)}, bf16[384,1024]{1,0:T(8,128)(2,1)}, u32[]{:S(2)}) %copy-start.8) | copy-done | bytes 786456
  49.2 3.0 %input_grad.1 = bf16[64,8,1024]{2,1,0:T(8,128)(2,1)} custom-call(bf16[32,1152]{1,0:T(8,128)(2,1)S(1)} %add_convert_fusion.1.refs_0_, bf16[384,1024]{1,0:T(8,128)(2,1)S(1)} %copy-done.8, bf16[64,1024]{1,0:T(8,128)(2,1)S(1)} %get-tuple-element.79.refs_2_, bf16[64,1024]{1,0:T(8,128)(2,1)S(1)} %get-tuple-element.80.refs_3_, ...), custom_call_target="tpu_custom_call" | custom-call | flops 2415919104 | bytes 4980736 | tf_op jit(solution)/shard_map/input_grad/pallas_call | solution.py:28
  52.1 1.2 %collective-permute-done.10 = bf16[32,1152]{1,0:T(8,128)(2,1)S(1)} collective-permute-done((bf16[32,1152]{1,0:T(8,128)(2,1)S(1)}, bf16[32,1152]{1,0:T(8,128)(2,1)S(1)}, u32[]{:S(2)}, u32[]{:S(2)}) %collective-permute-start.10) | collective-permute-done | bytes 73760 | tf_op jit(solution)/shard_map/ppermute | solution.py:477
  53.3 1.0 %collective-permute-start.13 = (bf16[32,1152]{1,0:T(8,128)(2,1)S(1)}, bf16[32,1152]{1,0:T(8,128)(2,1)S(1)}, u32[]{:S(2)}, u32[]{:S(2)}) collective-permute-start(bf16[32,1152]{1,0:T(8,128)(2,1)S(1)} %add_convert_fusion.refs_0_), channel_id=1, source_target_pairs={{0,2},{1,3},{2,0},{3,1},{4,6},{5,7},{6,4},{7,5},{8,10},{9,11},{10,... | collective-permute-start | bytes 221192 | tf_op jit(solution)/shard_map/ppermute | solution.py:477
  54.4 2.6 %output.1 = bf16[64,8,1024]{2,1,0:T(8,128)(2,1)} custom-call(bf16[32,1152]{1,0:T(8,128)(2,1)S(1)} %add_convert_fusion.refs_0_, bf16[640,1024]{1,0:T(8,128)(2,1)S(1)} %get-tuple-element.57.refs_2_.refs_1_, bf16[640,1024]{1,0:T(8,128)(2,1)S(1)} %copy-done.6, bf16[8,128,768]{2,1,0:T(8,128)(2,1)S(1)} %weights.1.refs_1_.refs_2_.refs_3_.refs_5_.refs_4_.refs_7_), custom_call_target="tpu_custom_call" | custom-call | flops 2415919104 | bytes 5242880 | tf_op jit(solution)/shard_map/output/pallas_call | solution.py:28
  57.9 1.4 %collective-permute-done.14.refs_1_ = bf16[64,1152]{1,0:T(8,128)(2,1)S(1)} collective-permute-done((bf16[64,1152]{1,0:T(8,128)(2,1)S(1)}, bf16[64,1152]{1,0:T(8,128)(2,1)S(1)}, u32[]{:S(2)}, u32[]{:S(2)}) %collective-permute-start.14) | collective-permute-done | bytes 147488 | tf_op jit(solution)/shard_map/ppermute | solution.py:477
  (41 shorter events, 8.4 us)
Async XLA Ops:
  0.6 1.2 %copy-start = (bf16[64,8,1024]{2,1,0:T(8,128)(2,1)S(1)}, bf16[64,8,1024]{2,1,0:T(8,128)(2,1)}, u32[]{:S(2)}) copy-start(bf16[64,8,1024]{2,1,0:T(8,128)(2,1)} %refs_0_.1) | copy-start | bytes 3145732
  2.5 16.6 %collective-permute-start.1 = (bf16[256,1024]{1,0:T(8,128)(2,1)S(1)}, bf16[256,1024]{1,0:T(8,128)(2,1)S(1)}, u32[]{:S(2)}, u32[]{:S(2)}) collective-permute-start(bf16[256,1024]{1,0:T(8,128)(2,1)S(1)} %get-tuple-element.46.refs_0_), channel_id=1, source_target_pairs={{1,2},{3,4},{5,6},{7,8},{9,10},{11,12},{13,14},{2,1},{4,3},{6,5},{... | collective-permute-start | bytes 1572872 | tf_op jit(solution)/shard_map/ppermute | solution.py:499
  3.2 12.9 %collective-permute-start.2 = (bf16[256,1024]{1,0:T(8,128)(2,1)S(1)}, bf16[256,1024]{1,0:T(8,128)(2,1)S(1)}, u32[]{:S(2)}, u32[]{:S(2)}) collective-permute-start(bf16[256,1024]{1,0:T(8,128)(2,1)S(1)} %get-tuple-element.53), channel_id=1, source_target_pairs={{0,1},{1,0},{2,3},{3,2},{4,5},{5,4},{6,7},{7,6},{8,9},{9,8},{10,11... | collective-permute-start | bytes 1572872 | tf_op jit(solution)/shard_map/ppermute | solution.py:477
  7.5 1.0 %copy-start.1 = (bf16[2,2,64,576]{3,2,1,0:T(8,128)(2,1)S(1)}, bf16[2,2,64,576]{3,2,1,0:T(8,128)(2,1)}, u32[]{:S(2)}) copy-start(bf16[2,2,64,576]{3,2,1,0:T(8,128)(2,1)} %refs_1_.2) | copy-start | bytes 884740
  9.2 1.7 %copy-start.2 = (bf16[64,8,1024]{2,1,0:T(8,128)(2,1)S(1)}, bf16[64,8,1024]{2,1,0:T(8,128)(2,1)}, u32[]{:S(2)}) copy-start(bf16[64,8,1024]{2,1,0:T(8,128)(2,1)} %refs_1_.3) | copy-start | bytes 3145732
  12.5 8.9 %collective-permute-start = (bf16[128,1024]{1,0:T(8,128)(2,1)S(1)}, bf16[128,1024]{1,0:T(8,128)(2,1)S(1)}, u32[]{:S(2)}, u32[]{:S(2)}) collective-permute-start(bf16[128,1024]{1,0:T(8,128)(2,1)S(1)} %get-tuple-element.49), channel_id=1, source_target_pairs={{1,2},{3,4},{5,6},{7,8},{9,10},{11,12},{13,14},{2,1},{4,3},{6,5},{... | collective-permute-start | bytes 786440 | tf_op jit(solution)/shard_map/ppermute | solution.py:499
  13.2 4.8 %collective-permute-start.3 = (bf16[128,1024]{1,0:T(8,128)(2,1)S(1)}, bf16[128,1024]{1,0:T(8,128)(2,1)S(1)}, u32[]{:S(2)}, u32[]{:S(2)}) collective-permute-start(bf16[128,1024]{1,0:T(8,128)(2,1)S(1)} %get-tuple-element.52.refs_0_), channel_id=1, source_target_pairs={{0,1},{1,0},{2,3},{3,2},{4,5},{5,4},{6,7},{7,6},{8,9},{9,8},{10,11... | collective-permute-start | bytes 786440 | tf_op jit(solution)/shard_map/ppermute | solution.py:477
  21.4 5.1 %copy-start.5 = (bf16[640,1024]{1,0:T(8,128)(2,1)}, bf16[640,1024]{1,0:T(8,128)(2,1)S(1)}, u32[]{:S(2)}) copy-start(bf16[640,1024]{1,0:T(8,128)(2,1)S(1)} %get-tuple-element.63.refs_4_.refs_2_) | copy-start | bytes 3932164
  22.4 9.0 %collective-permute-start.4 = (bf16[64,1024]{1,0:T(8,128)(2,1)S(1)}, bf16[64,1024]{1,0:T(8,128)(2,1)S(1)}, u32[]{:S(2)}, u32[]{:S(2)}) collective-permute-start(bf16[64,1024]{1,0:T(8,128)(2,1)S(1)} %get-tuple-element.66), channel_id=1, source_target_pairs={{0,1},{1,0},{2,3},{3,2},{4,5},{5,4},{6,7},{7,6},{8,9},{9,8},{10,11... | collective-permute-start | bytes 393224 | tf_op jit(solution)/shard_map/ppermute | solution.py:477
  25.8 5.5 %collective-permute-start.5 = (bf16[64,1024]{1,0:T(8,128)(2,1)S(1)}, bf16[64,1024]{1,0:T(8,128)(2,1)S(1)}, u32[]{:S(2)}, u32[]{:S(2)}) collective-permute-start(bf16[64,1024]{1,0:T(8,128)(2,1)S(1)} %get-tuple-element.67), channel_id=1, source_target_pairs={{1,2},{3,4},{5,6},{7,8},{9,10},{11,12},{13,14},{2,1},{4,3},{6,5},{... | collective-permute-start | bytes 393224 | tf_op jit(solution)/shard_map/ppermute | solution.py:499
  31.3 1.5 %copy-start.3 = (bf16[512,1024]{1,0:T(8,128)(2,1)}, bf16[512,1024]{1,0:T(8,128)(2,1)S(1)}, u32[]{:S(2)}) copy-start(bf16[512,1024]{1,0:T(8,128)(2,1)S(1)} %get-tuple-element.65.refs_0_.refs_6_) | copy-start | bytes 3145732
  31.4 1.5 %copy-start.7 = (bf16[384,1024]{1,0:T(8,128)(2,1)}, bf16[384,1024]{1,0:T(8,128)(2,1)S(1)}, u32[]{:S(2)}) copy-start(bf16[384,1024]{1,0:T(8,128)(2,1)S(1)} %get-tuple-element.76.refs_1_) | copy-start | bytes 2359300
  32.9 4.8 %collective-permute-start.6 = (bf16[64,1152]{1,0:T(8,128)(2,1)S(1)}, bf16[64,1152]{1,0:T(8,128)(2,1)S(1)}, u32[]{:S(2)}, u32[]{:S(2)}) collective-permute-start(bf16[64,1152]{1,0:T(8,128)(2,1)S(1)} %get-tuple-element.73), channel_id=1, source_target_pairs={{0,1},{1,0},{2,3},{3,2},{4,5},{5,4},{6,7},{7,6},{8,9},{9,8},{10,11... | collective-permute-start | bytes 442376 | tf_op jit(solution)/shard_map/ppermute | solution.py:477
  37.7 4.6 %collective-permute-start.7 = (bf16[32,1152]{1,0:T(8,128)(2,1)S(1)}, bf16[32,1152]{1,0:T(8,128)(2,1)S(1)}, u32[]{:S(2)}, u32[]{:S(2)}) collective-permute-start(bf16[32,1152]{1,0:T(8,128)(2,1)S(1)} %get-tuple-element.75), channel_id=1, source_target_pairs={{0,2},{1,3},{2,0},{3,1},{4,6},{5,7},{6,4},{7,5},{8,10},{9,11},{10,... | collective-permute-start | bytes 221192 | tf_op jit(solution)/shard_map/ppermute | solution.py:477
  39.2 7.6 %collective-permute-start.11 = (bf16[64,1024]{1,0:T(8,128)(2,1)S(1)}, bf16[64,1024]{1,0:T(8,128)(2,1)S(1)}, u32[]{:S(2)}, u32[]{:S(2)}) collective-permute-start(bf16[64,1024]{1,0:T(8,128)(2,1)S(1)} %get-tuple-element.79.refs_2_), channel_id=1, source_target_pairs={{0,1},{1,0},{2,3},{3,2},{4,5},{5,4},{6,7},{7,6},{8,9},{9,8},{10,11... | collective-permute-start | bytes 393224 | tf_op jit(solution)/shard_map/ppermute | solution.py:477
  39.2 7.6 %collective-permute-start.12 = (bf16[64,1024]{1,0:T(8,128)(2,1)S(1)}, bf16[64,1024]{1,0:T(8,128)(2,1)S(1)}, u32[]{:S(2)}, u32[]{:S(2)}) collective-permute-start(bf16[64,1024]{1,0:T(8,128)(2,1)S(1)} %get-tuple-element.80.refs_3_), channel_id=1, source_target_pairs={{1,2},{3,4},{5,6},{7,8},{9,10},{11,12},{13,14},{2,1},{4,3},{6,5},{... | collective-permute-start | bytes 393224 | tf_op jit(solution)/shard_map/ppermute | solution.py:499
  42.3 9.8 %collective-permute-start.8 = (bf16[32,1152]{1,0:T(8,128)(2,1)S(1)}, bf16[32,1152]{1,0:T(8,128)(2,1)S(1)}, u32[]{:S(2)}, u32[]{:S(2)}) collective-permute-start(bf16[32,1152]{1,0:T(8,128)(2,1)S(1)} %add_convert_fusion.1.refs_0_), channel_id=1, source_target_pairs={{0,4},{1,5},{2,6},{3,7},{4,0},{5,1},{6,2},{7,3},{8,12},{9,13},{10,... | collective-permute-start | bytes 221192 | tf_op jit(solution)/shard_map/ppermute | solution.py:477
  44.0 8.1 %collective-permute-start.9 = (bf16[32,1152]{1,0:T(8,128)(2,1)S(1)}, bf16[32,1152]{1,0:T(8,128)(2,1)S(1)}, u32[]{:S(2)}, u32[]{:S(2)}) collective-permute-start(bf16[32,1152]{1,0:T(8,128)(2,1)S(1)} %add_convert_fusion.1.refs_0_), channel_id=1, source_target_pairs={{0,8},{1,9},{2,10},{3,11},{4,12},{5,13},{6,14},{7,15},{8,0},{9,1},... | collective-permute-start | bytes 221192 | tf_op jit(solution)/shard_map/ppermute | solution.py:477
  46.7 6.6 %collective-permute-start.10 = (bf16[32,1152]{1,0:T(8,128)(2,1)S(1)}, bf16[32,1152]{1,0:T(8,128)(2,1)S(1)}, u32[]{:S(2)}, u32[]{:S(2)}) collective-permute-start(bf16[32,1152]{1,0:T(8,128)(2,1)S(1)} %add_convert_fusion.1.refs_0_), channel_id=1, source_target_pairs={{0,12},{1,13},{2,14},{3,15},{4,8},{5,9},{6,10},{7,11},{8,4},{9,5},... | collective-permute-start | bytes 221192 | tf_op jit(solution)/shard_map/ppermute | solution.py:477
  46.8 1.2 %copy-start.4 = (bf16[512,1024]{1,0:T(8,128)(2,1)S(1)}, bf16[512,1024]{1,0:T(8,128)(2,1)}, u32[]{:S(2)}) copy-start(bf16[512,1024]{1,0:T(8,128)(2,1)} %copy-done.3) | copy-start | bytes 3145732
  48.0 1.1 %copy-start.8 = (bf16[384,1024]{1,0:T(8,128)(2,1)S(1)}, bf16[384,1024]{1,0:T(8,128)(2,1)}, u32[]{:S(2)}) copy-start(bf16[384,1024]{1,0:T(8,128)(2,1)} %copy-done.7) | copy-start | bytes 2359300
  49.2 5.2 %copy-start.6 = (bf16[640,1024]{1,0:T(8,128)(2,1)S(1)}, bf16[640,1024]{1,0:T(8,128)(2,1)}, u32[]{:S(2)}) copy-start(bf16[640,1024]{1,0:T(8,128)(2,1)} %copy-done.5) | copy-start | bytes 3932164
  53.3 4.4 %collective-permute-start.13 = (bf16[32,1152]{1,0:T(8,128)(2,1)S(1)}, bf16[32,1152]{1,0:T(8,128)(2,1)S(1)}, u32[]{:S(2)}, u32[]{:S(2)}) collective-permute-start(bf16[32,1152]{1,0:T(8,128)(2,1)S(1)} %add_convert_fusion.refs_0_), channel_id=1, source_target_pairs={{0,2},{1,3},{2,0},{3,1},{4,6},{5,7},{6,4},{7,5},{8,10},{9,11},{10,... | collective-permute-start | bytes 221192 | tf_op jit(solution)/shard_map/ppermute | solution.py:477
  57.8 1.4 %collective-permute-start.14 = (bf16[64,1152]{1,0:T(8,128)(2,1)S(1)}, bf16[64,1152]{1,0:T(8,128)(2,1)S(1)}, u32[]{:S(2)}, u32[]{:S(2)}) collective-permute-start(bf16[64,1152]{1,0:T(8,128)(2,1)S(1)} %maximum_select_fusion.refs_0_), channel_id=1, source_target_pairs={{0,1},{1,0},{2,3},{3,2},{4,5},{5,4},{6,7},{7,6},{8,9},{9,8},{10,11... | collective-permute-start | bytes 442376 | tf_op jit(solution)/shard_map/ppermute | solution.py:477

commit v9 on v8

--- a/solution.py
+++ b/solution.py
@@ -355,11 +355,51 @@
     send_edges(edges_ref, 1, next_near, next_far)
 
 
+def grads_near_kernel(
+    rows, g_ref, hid1_near, hid1_in, dh1_near, x1_near, x1_in, grad11, grad10, s3, t3, hid1, x1
+):
+    def near_side(top):
+        start = 0 if top else rows - 4
+        for i in range(4):
+            put(s3, i, one(g_ref, start + i))
+            put(t3, i, one(dh1_near, start + i + 1 if top else start + i - 3))
+        for i in range(6):
+            row = start - 1 + i
+            if 3 <= row < rows - 3:
+                value = one(hid1_in, row - 3)
+            else:
+                value = one(hid1_near, row + 1 if top else row - (rows - 3))
+            hid1[i * CHAN : (i + 1) * CHAN, :] = value
+            if 2 <= row < rows - 2:
+                value = one(x1_in, row - 2)
+            else:
+                value = one(x1_near, row + 2 if top else row - (rows - 2))
+            x1[i * CHAN : (i + 1) * CHAN, :] = value
+        grad11[...] = grad_rows(s3, 0, hid1, 0, 4)
+        grad10[...] = grad_rows(t3, 0, x1, 0, 4)
+
+    odd = odd_place()
+    for top in (True, False):
+        pl.when(odd == top)(functools.partial(near_side, top))
+
+
+def grad_rows_from(upper, upper_row, lower, lower_row, count):
+    total = None
+    for row in range(0, count, 2):
+        left = pl.ds(pl.multiple_of((row + upper_row) * STACK, CHAN), 2 * STACK)
+        right = pl.ds(pl.multiple_of((row + lower_row) * CHAN, CHAN), 4 * CHAN)
+        term = lax.dot_general(
+            upper[left, :], lower[right, :], (((1,), (1,)), ((), ())), preferred_element_type=F32
+        )
+        total = term if total is None else total + term
+    return total[:STACK, :STACK] + total[STACK:, CHAN:]
+
+
 def middle_kernel(
-    rows, g_ref, edges_ref, hid1_ref, dh1_ref, x1_ref, hid0_ref, x_ref, w_ref,
+    rows, g_ref, edges_ref, hid1_ref, dh1_ref, x1_ref, hid0_ref, x_ref, w_ref, near11, near10,
     g1_ref, dh0_ref, grad00, grad01, grad10, grad11, s3, t3, u3, v3,
 ):
-    stack_rows(dh1_ref, range(rows + 2), t3, 0)
+    stack_rows(dh1_ref, range(1, rows + 1), t3, 0)
     copy_rows(edges_ref, 2, g1_ref, 0)
     g1_ref[(rows - 2) * CHAN :, :] = edges_ref[2 * CHAN :, :]
 
@@ -377,9 +417,12 @@
         put(v3, row, value)
 
     conv_rows(w_ref[3], u3, 0, rows - 2, dhidden0)
-    stack_rows(g_ref, range(rows), s3, 0)
-    grad11[...] = grad_rows(s3, 0, hid1_ref, 0, rows)
-    grad10[...] = grad_rows(t3, 1, x1_ref, 0, rows)
+    start = jnp.where(odd_place(), 4, 0)
+    for row in range(rows - 4):
+        source = pl.ds(pl.multiple_of((start + row) * CHAN, CHAN), CHAN)
+        put(s3, row, g_ref[source, :])
+    grad11[...] = near11[...] + grad_rows_from(s3, 0, hid1_ref, start, rows - 4)
+    grad10[...] = near10[...] + grad_rows_from(t3, start + 1, x1_ref, start, rows - 4)
     grad01[...] = grad_rows(u3, 0, hid0_ref, 0, rows)
     grad00[...] = grad_rows(v3, 0, x_ref, 0, rows - 2)
 
@@ -535,9 +578,15 @@
         (g, gnear, near[2], inner[2], g_inner, weights), (shape(rows - 2), shape(2)),
         [vmem(4)] * 2, 4 * row_flops, "backward1_near",
     )
+    near_grads = call(
+        functools.partial(grads_near_kernel, rows),
+        (g, near[2], inner[2], dh1_near, near[1], inner[1]), (grad, grad),
+        [vmem(4), vmem(4), plain(6), plain(6)], 8 * row_flops, "grads_near", after=(edge_near,),
+    )
     hid0, x1, hid1 = call(
         functools.partial(far_kernel, rows, height), (x, xfar, weights, *inner, *near),
         (shape(rows + 2),) * 3, [plain(4)] * 3 + [vmem(6)] * 3, 12 * row_flops, "forward_far",
+        after=(near_grads[1],),
     )
     g1_near, g1_far, edges, dh1 = call(
         functools.partial(backward1_far_kernel, rows),
@@ -546,9 +595,9 @@
     )
     g1near, g1far = neighbours(g1_near, g1_far)
     g1, dh0_inner, *grads = call(
-        functools.partial(middle_kernel, rows), (g, edges, hid1, dh1, x1, hid0, x, weights),
+        functools.partial(middle_kernel, rows), (g, edges, hid1, dh1, x1, hid0, x, weights, *near_grads),
         (shape(rows), shape(rows - 2)) + (grad,) * 4,
-        [vmem(rows), vmem(rows + 2), vmem(rows), vmem(rows - 2)],
+        [vmem(rows - 4), vmem(rows + 2), vmem(rows), vmem(rows - 2)],
         36 * row_flops, "middle",
     )
     dh0_near, dh0_far, part, send = call(

time: 60.5 us -> 60 us (level)
  waiting for transfers between devices: 6.57 us -> 5.63 us
    ppermute x11, waiting for transfers between devices: 6.55 us -> 5.62 us  [exchange(): return lax.ppermute(value, 'space', [(d, d ^ mask) for d in range(count)])]
    pallas_call x14 -> x15, Pallas kernels: 23.5 us -> 24 us  [call(): pl.pallas_call(kernel, out_shape=outs, in_specs=[ANY] * len(after) + [pla...]
  transfers between devices with their start and end apart: 15 -> 15, of which waited for: 5 -> 5; matrix products, arithmetic and copies ran while one was open for 0% -> 0% of each run, Pallas kernels for 32% -> 33%
where the time goes in v9:
time: 60 us; the launch traced here: 59.7 us
  starting transfers between devices  24.5 us (41%)
  Pallas kernels  24 us (40%)
  waiting for transfers between devices  5.63 us (9%)
  local copies, waits for them, and re-layouts  4.57 us (8%)
  between operations  0.89 us (1%)
    pallas_call x15, Pallas kernels, call(): pl.pallas_call(kernel, out_shape=outs, in_specs=[ANY] * len(after) + [pla...  24 us
    ppermute x11, starting transfers between devices, exchange(): return lax.ppermute(value, 'space', [(d, d ^ mask) for d in range(count)])  21.6 us
    ppermute x11, waiting for transfers between devices, exchange(): return lax.ppermute(value, 'space', [(d, d ^ mask) for d in range(count)])  5.62 us
    unnamed x18, local copies, waits for them, and re-layouts  4.57 us
    ppermute x4, starting transfers between devices, neighbours(): from_far = lax.ppermute(far, 'space', beyond)  2.89 us
  transfers between devices with their start and end apart: 15, of which 5 were waited for; matrix products, arithmetic and copies ran while one was open for 0% of the time, Pallas kernels for 33%

profile of v9, /device:TPU:0, one launch (start us, length us, event | category | flops | bytes accessed | tf_op | source)
XLA Modules:
  0.0 59.7 jit_solution(11643178555075690982)
XLA Ops:
  0.6 1.2 %copy-done = bf16[64,8,1024]{2,1,0:T(8,128)(2,1)S(1)} copy-done((bf16[64,8,1024]{2,1,0:T(8,128)(2,1)S(1)}, bf16[64,8,1024]{2,1,0:T(8,128)(2,1)}, u32[]{:S(2)}) %copy-start) | copy-done | bytes 1048600
  5.4 1.7 %inner.1 = (bf16[384,1024]{1,0:T(8,128)(2,1)S(1)}, bf16[256,1024]{1,0:T(8,128)(2,1)S(1)}, bf16[128,1024]{1,0:T(8,128)(2,1)S(1)}) custom-call(bf16[512,1024]{1,0:T(8,128)(2,1)S(1)} %get-tuple-element.47.refs_0_.refs_1_.refs_6_.refs_4_, bf16[8,128,768]{2,1,0:T(8,128)(2,1)S(1)} %weights.1.refs_1_.refs_2_.refs_3_.refs_5_.refs_4_.refs_7_), custom_call_target="tpu_custom_call" | custom-call | flops 3623878656 | bytes 4194304 | tf_op jit(solution)/shard_map/inner/pallas_call | solution.py:28
  7.1 1.6 %g_rows.1 = (bf16[512,1024]{1,0:T(8,128)(2,1)S(1)}, bf16[128,1024]{1,0:T(8,128)(2,1)S(1)}, bf16[128,1024]{1,0:T(8,128)(2,1)S(1)}, f32[384,1024]{1,0:T(8,128)S(1)}) custom-call(bf16[128,1024]{1,0:T(8,128)(2,1)S(1)} %get-tuple-element.49.refs_0_.refs_3_.refs_6_, bf16[64,8,1024]{2,1,0:T(8,128)(2,1)S(1)} %copy-done.2, ...), custom_call_target="tpu_custom_call" | custom-call | flops 1811939328 | bytes 5767168 | tf_op jit(solution)/shard_map/g_rows/pallas_call | solution.py:28
  9.3 5.2 %collective-permute-start.1 = (bf16[128,1024]{1,0:T(8,128)(2,1)S(1)}, bf16[128,1024]{1,0:T(8,128)(2,1)S(1)}, u32[]{:S(2)}, u32[]{:S(2)}) collective-permute-start(bf16[128,1024]{1,0:T(8,128)(2,1)S(1)} %get-tuple-element.52.refs_0_), channel_id=1, source_target_pairs={{0,1},{1,0},{2,3},{3,2},{4,5},{5,4},{6,7},{7,6},{8,9},{9,8},{10,11... | collective-permute-start | bytes 786440 | tf_op jit(solution)/shard_map/ppermute | solution.py:520
  14.5 1.8 %forward_near.1 = (bf16[256,1024]{1,0:T(8,128)(2,1)S(1)}, bf16[256,1024]{1,0:T(8,128)(2,1)S(1)}, bf16[256,1024]{1,0:T(8,128)(2,1)S(1)}) custom-call(bf16[128,1024]{1,0:T(8,128)(2,1)S(1)} %get-tuple-element.52.refs_0_, bf16[512,1024]{1,0:T(8,128)(2,1)S(1)} %get-tuple-element.47.refs_0_.refs_1_.refs_6_.refs_4_, ...), custom_call_target="tpu_custom_call" | custom-call | flops 3623878656 | bytes 6029312 | tf_op jit(solution)/shard_map/forward_near/pallas_call | solution.py:28
  16.4 1.1 %backward1_near.1 = (bf16[384,1024]{1,0:T(8,128)(2,1)S(1)}, bf16[128,1024]{1,0:T(8,128)(2,1)S(1)}) custom-call(bf16[512,1024]{1,0:T(8,128)(2,1)S(1)} %get-tuple-element.50.refs_0_.refs_1_, bf16[128,1024]{1,0:T(8,128)(2,1)S(1)} %collective-permute-done.1.refs_1_, bf16[256,1024]{1,0:T(8,128)(2,1)S(1)} %get-tuple-element.56.refs_2_.refs_9_, ...), custom_call_target="tpu_custom_call" | custom-call | flops 1207959552 | bytes 6291456 | tf_op jit(solution)/shard_map/backward1_near/pallas_call | solution.py:28
  17.4 1.4 %grads_near.1 = (f32[192,192]{1,0:T(8,128)S(1)}, f32[192,192]{1,0:T(8,128)S(1)}) custom-call(bf16[128,1024]{1,0:T(8,128)(2,1)S(1)} %get-tuple-element.58.refs_0_.refs_6_, bf16[512,1024]{1,0:T(8,128)(2,1)S(1)} %get-tuple-element.50.refs_0_.refs_1_, bf16[256,1024]{1,0:T(8,128)(2,1)S(1)} %get-tuple-element.56.refs_2_.refs_9_, ...), custom_call_target="tpu_custom_call" | custom-call | flops 2415919104 | bytes 3964928 | tf_op jit(solution)/shard_map/grads_near/pallas_call | solution.py:28
  18.9 2.1 %forward_far.1 = (bf16[640,1024]{1,0:T(8,128)(2,1)S(1)}, bf16[640,1024]{1,0:T(8,128)(2,1)S(1)}, bf16[640,1024]{1,0:T(8,128)(2,1)S(1)}) custom-call(f32[192,192]{1,0:T(8,128)S(1)} %get-tuple-element.61.refs_0_.refs_9_, bf16[512,1024]{1,0:T(8,128)(2,1)S(1)} %get-tuple-element.47.refs_0_.refs_1_.refs_6_.refs_4_, ...), custom_call_target="tpu_custom_call" | custom-call | flops 3623878656 | bytes 10223616 | tf_op jit(solution)/shard_map/forward_far/pallas_call | solution.py:28
  21.0 1.0 %backward1_far.1 = (bf16[64,1024]{1,0:T(8,128)(2,1)S(1)}, bf16[64,1024]{1,0:T(8,128)(2,1)S(1)}, bf16[256,1024]{1,0:T(8,128)(2,1)S(1)}, bf16[640,1024]{1,0:T(8,128)(2,1)S(1)}) custom-call(bf16[512,1024]{1,0:T(8,128)(2,1)S(1)} %get-tuple-element.50.refs_0_.refs_1_, bf16[128,1024]{1,0:T(8,128)(2,1)S(1)} %collective-permute-done.refs_1_, ...), custom_call_target="tpu_custom_call" | custom-call | flops 1207959552 | bytes 8912896 | tf_op jit(solution)/shard_map/backward1_far/pallas_call | solution.py:28
  22.0 3.9 %collective-permute-start.4 = (bf16[64,1024]{1,0:T(8,128)(2,1)S(1)}, bf16[64,1024]{1,0:T(8,128)(2,1)S(1)}, u32[]{:S(2)}, u32[]{:S(2)}) collective-permute-start(bf16[64,1024]{1,0:T(8,128)(2,1)S(1)} %get-tuple-element.70), channel_id=1, source_target_pairs={{0,1},{1,0},{2,3},{3,2},{4,5},{5,4},{6,7},{7,6},{8,9},{9,8},{10,11... | collective-permute-start | bytes 393224 | tf_op jit(solution)/shard_map/ppermute | solution.py:520
  26.8 4.1 %middle.1 = (bf16[512,1024]{1,0:T(8,128)(2,1)S(1)}, bf16[384,1024]{1,0:T(8,128)(2,1)S(1)}, f32[192,192]{1,0:T(8,128)S(1)}, f32[192,192]{1,0:T(8,128)S(1)}, f32[1...) custom-call(bf16[512,1024]{1,0:T(8,128)(2,1)S(1)} %get-tuple-element.50.refs_0_.refs_1_, ...), custom_call_target="tpu_custom_call" | custom-call | flops 10871635968 | bytes 12156928 | tf_op jit(solution)/shard_map/middle/pallas_call | solution.py:28
  31.0 1.4 %backward0.1 = (bf16[64,1024]{1,0:T(8,128)(2,1)S(1)}, bf16[64,1024]{1,0:T(8,128)(2,1)S(1)}, f32[64,1152]{1,0:T(8,128)S(1)}, bf16[64,1152]{1,0:T(8,128)(2,1)S(1)}) custom-call(bf16[512,1024]{1,0:T(8,128)(2,1)S(1)} %get-tuple-element.69.refs_0_.refs_6_, bf16[64,1024]{1,0:T(8,128)(2,1)S(1)} %collective-permute-done.4.refs_1_, ...), custom_call_target="tpu_custom_call" | custom-call | flops 2415919104 | bytes 7585792 | tf_op jit(solution)/shard_map/backward0/pallas_call | solution.py:28
  32.4 3.8 %collective-permute-start.6 = (bf16[64,1152]{1,0:T(8,128)(2,1)S(1)}, bf16[64,1152]{1,0:T(8,128)(2,1)S(1)}, u32[]{:S(2)}, u32[]{:S(2)}) collective-permute-start(bf16[64,1152]{1,0:T(8,128)(2,1)S(1)} %get-tuple-element.77), channel_id=1, source_target_pairs={{0,1},{1,0},{2,3},{3,2},{4,5},{5,4},{6,7},{7,6},{8,9},{9,8},{10,11... | collective-permute-start | bytes 442376 | tf_op jit(solution)/shard_map/ppermute | solution.py:520
  36.2 1.0 %collective-permute-done.6.refs_1_ = bf16[64,1152]{1,0:T(8,128)(2,1)S(1)} collective-permute-done((bf16[64,1152]{1,0:T(8,128)(2,1)S(1)}, bf16[64,1152]{1,0:T(8,128)(2,1)S(1)}, u32[]{:S(2)}, u32[]{:S(2)}) %collective-permute-start.6) | collective-permute-done | bytes 147488 | tf_op jit(solution)/shard_map/ppermute | solution.py:520
  37.3 2.1 %collective-permute-start.7 = (bf16[32,1152]{1,0:T(8,128)(2,1)S(1)}, bf16[32,1152]{1,0:T(8,128)(2,1)S(1)}, u32[]{:S(2)}, u32[]{:S(2)}) collective-permute-start(bf16[32,1152]{1,0:T(8,128)(2,1)S(1)} %get-tuple-element.79), channel_id=1, source_target_pairs={{0,2},{1,3},{2,0},{3,1},{4,6},{5,7},{6,4},{7,5},{8,10},{9,11},{10,... | collective-permute-start | bytes 221192 | tf_op jit(solution)/shard_map/ppermute | solution.py:520
  40.1 2.0 %collective-permute-done.7 = bf16[32,1152]{1,0:T(8,128)(2,1)S(1)} collective-permute-done((bf16[32,1152]{1,0:T(8,128)(2,1)S(1)}, bf16[32,1152]{1,0:T(8,128)(2,1)S(1)}, u32[]{:S(2)}, u32[]{:S(2)}) %collective-permute-start.7) | collective-permute-done | bytes 73760 | tf_op jit(solution)/shard_map/ppermute | solution.py:520
  42.2 1.6 %collective-permute-start.8 = (bf16[32,1152]{1,0:T(8,128)(2,1)S(1)}, bf16[32,1152]{1,0:T(8,128)(2,1)S(1)}, u32[]{:S(2)}, u32[]{:S(2)}) collective-permute-start(bf16[32,1152]{1,0:T(8,128)(2,1)S(1)} %add_convert_fusion.1.refs_0_), channel_id=1, source_target_pairs={{0,4},{1,5},{2,6},{3,7},{4,0},{5,1},{6,2},{7,3},{8,12},{9,13},{10,... | collective-permute-start | bytes 221192 | tf_op jit(solution)/shard_map/ppermute | solution.py:520
  43.8 2.6 %collective-permute-start.9 = (bf16[32,1152]{1,0:T(8,128)(2,1)S(1)}, bf16[32,1152]{1,0:T(8,128)(2,1)S(1)}, u32[]{:S(2)}, u32[]{:S(2)}) collective-permute-start(bf16[32,1152]{1,0:T(8,128)(2,1)S(1)} %add_convert_fusion.1.refs_0_), channel_id=1, source_target_pairs={{0,8},{1,9},{2,10},{3,11},{4,12},{5,13},{6,14},{7,15},{8,0},{9,1},... | collective-permute-start | bytes 221192 | tf_op jit(solution)/shard_map/ppermute | solution.py:520
  46.6 1.2 %copy-done.4 = bf16[512,1024]{1,0:T(8,128)(2,1)S(1)} copy-done((bf16[512,1024]{1,0:T(8,128)(2,1)S(1)}, bf16[512,1024]{1,0:T(8,128)(2,1)}, u32[]{:S(2)}) %copy-start.4) | copy-done | bytes 1048600
  47.9 1.1 %copy-done.8 = bf16[384,1024]{1,0:T(8,128)(2,1)S(1)} copy-done((bf16[384,1024]{1,0:T(8,128)(2,1)S(1)}, bf16[384,1024]{1,0:T(8,128)(2,1)}, u32[]{:S(2)}) %copy-start.8) | copy-done | bytes 786456
  49.0 2.9 %input_grad.1 = bf16[64,8,1024]{2,1,0:T(8,128)(2,1)} custom-call(bf16[32,1152]{1,0:T(8,128)(2,1)S(1)} %add_convert_fusion.1.refs_0_, bf16[384,1024]{1,0:T(8,128)(2,1)S(1)} %copy-done.8, bf16[64,1024]{1,0:T(8,128)(2,1)S(1)} %get-tuple-element.83.refs_2_, bf16[64,1024]{1,0:T(8,128)(2,1)S(1)} %get-tuple-element.84.refs_3_, ...), custom_call_target="tpu_custom_call" | custom-call | flops 2415919104 | bytes 4980736 | tf_op jit(solution)/shard_map/input_grad/pallas_call | solution.py:28
  52.8 1.5 %collective-permute-start.13 = (bf16[32,1152]{1,0:T(8,128)(2,1)S(1)}, bf16[32,1152]{1,0:T(8,128)(2,1)S(1)}, u32[]{:S(2)}, u32[]{:S(2)}) collective-permute-start(bf16[32,1152]{1,0:T(8,128)(2,1)S(1)} %add_convert_fusion.refs_0_), channel_id=1, source_target_pairs={{0,2},{1,3},{2,0},{3,1},{4,6},{5,7},{6,4},{7,5},{8,10},{9,11},{10,... | collective-permute-start | bytes 221192 | tf_op jit(solution)/shard_map/ppermute | solution.py:520
  54.3 2.6 %output.1 = bf16[64,8,1024]{2,1,0:T(8,128)(2,1)} custom-call(bf16[32,1152]{1,0:T(8,128)(2,1)S(1)} %add_convert_fusion.refs_0_, bf16[640,1024]{1,0:T(8,128)(2,1)S(1)} %get-tuple-element.63.refs_2_.refs_1_, bf16[640,1024]{1,0:T(8,128)(2,1)S(1)} %copy-done.6, bf16[8,128,768]{2,1,0:T(8,128)(2,1)S(1)} %weights.1.refs_1_.refs_2_.refs_3_.refs_5_.refs_4_.refs_7_), custom_call_target="tpu_custom_call" | custom-call | flops 2415919104 | bytes 5242880 | tf_op jit(solution)/shard_map/output/pallas_call | solution.py:28
  57.4 1.4 %collective-permute-done.14.refs_1_ = bf16[64,1152]{1,0:T(8,128)(2,1)S(1)} collective-permute-done((bf16[64,1152]{1,0:T(8,128)(2,1)S(1)}, bf16[64,1152]{1,0:T(8,128)(2,1)S(1)}, u32[]{:S(2)}, u32[]{:S(2)}) %collective-permute-start.14) | collective-permute-done | bytes 147488 | tf_op jit(solution)/shard_map/ppermute | solution.py:520
  (42 shorter events, 8.4 us)
Async XLA Ops:
  0.6 1.2 %copy-start = (bf16[64,8,1024]{2,1,0:T(8,128)(2,1)S(1)}, bf16[64,8,1024]{2,1,0:T(8,128)(2,1)}, u32[]{:S(2)}) copy-start(bf16[64,8,1024]{2,1,0:T(8,128)(2,1)} %refs_0_.1) | copy-start | bytes 3145732
  2.5 12.0 %collective-permute-start.2 = (bf16[256,1024]{1,0:T(8,128)(2,1)S(1)}, bf16[256,1024]{1,0:T(8,128)(2,1)S(1)}, u32[]{:S(2)}, u32[]{:S(2)}) collective-permute-start(bf16[256,1024]{1,0:T(8,128)(2,1)S(1)} %get-tuple-element.53), channel_id=1, source_target_pairs={{0,1},{1,0},{2,3},{3,2},{4,5},{5,4},{6,7},{7,6},{8,9},{9,8},{10,11... | collective-permute-start | bytes 1572872 | tf_op jit(solution)/shard_map/ppermute | solution.py:520
  3.0 15.8 %collective-permute-start.3 = (bf16[256,1024]{1,0:T(8,128)(2,1)S(1)}, bf16[256,1024]{1,0:T(8,128)(2,1)S(1)}, u32[]{:S(2)}, u32[]{:S(2)}) collective-permute-start(bf16[256,1024]{1,0:T(8,128)(2,1)S(1)} %get-tuple-element.48.refs_0_), channel_id=1, source_target_pairs={{1,2},{3,4},{5,6},{7,8},{9,10},{11,12},{13,14},{2,1},{4,3},{6,5},{... | collective-permute-start | bytes 1572872 | tf_op jit(solution)/shard_map/ppermute | solution.py:542
  3.7 1.0 %copy-start.1 = (bf16[2,2,64,576]{3,2,1,0:T(8,128)(2,1)S(1)}, bf16[2,2,64,576]{3,2,1,0:T(8,128)(2,1)}, u32[]{:S(2)}) copy-start(bf16[2,2,64,576]{3,2,1,0:T(8,128)(2,1)} %refs_1_.2) | copy-start | bytes 884740
  5.4 1.7 %copy-start.2 = (bf16[64,8,1024]{2,1,0:T(8,128)(2,1)S(1)}, bf16[64,8,1024]{2,1,0:T(8,128)(2,1)}, u32[]{:S(2)}) copy-start(bf16[64,8,1024]{2,1,0:T(8,128)(2,1)} %refs_1_.3) | copy-start | bytes 3145732
  8.7 12.3 %collective-permute-start = (bf16[128,1024]{1,0:T(8,128)(2,1)S(1)}, bf16[128,1024]{1,0:T(8,128)(2,1)S(1)}, u32[]{:S(2)}, u32[]{:S(2)}) collective-permute-start(bf16[128,1024]{1,0:T(8,128)(2,1)S(1)} %get-tuple-element.51), channel_id=1, source_target_pairs={{1,2},{3,4},{5,6},{7,8},{9,10},{11,12},{13,14},{2,1},{4,3},{6,5},{... | collective-permute-start | bytes 786440 | tf_op jit(solution)/shard_map/ppermute | solution.py:542
  9.3 7.0 %collective-permute-start.1 = (bf16[128,1024]{1,0:T(8,128)(2,1)S(1)}, bf16[128,1024]{1,0:T(8,128)(2,1)S(1)}, u32[]{:S(2)}, u32[]{:S(2)}) collective-permute-start(bf16[128,1024]{1,0:T(8,128)(2,1)S(1)} %get-tuple-element.52.refs_0_), channel_id=1, source_target_pairs={{0,1},{1,0},{2,3},{3,2},{4,5},{5,4},{6,7},{7,6},{8,9},{9,8},{10,11... | collective-permute-start | bytes 786440 | tf_op jit(solution)/shard_map/ppermute | solution.py:520
  21.0 5.8 %copy-start.5 = (bf16[640,1024]{1,0:T(8,128)(2,1)}, bf16[640,1024]{1,0:T(8,128)(2,1)S(1)}, u32[]{:S(2)}) copy-start(bf16[640,1024]{1,0:T(8,128)(2,1)S(1)} %get-tuple-element.66.refs_4_.refs_2_) | copy-start | bytes 3932164
  22.0 8.9 %collective-permute-start.4 = (bf16[64,1024]{1,0:T(8,128)(2,1)S(1)}, bf16[64,1024]{1,0:T(8,128)(2,1)S(1)}, u32[]{:S(2)}, u32[]{:S(2)}) collective-permute-start(bf16[64,1024]{1,0:T(8,128)(2,1)S(1)} %get-tuple-element.70), channel_id=1, source_target_pairs={{0,1},{1,0},{2,3},{3,2},{4,5},{5,4},{6,7},{7,6},{8,9},{9,8},{10,11... | collective-permute-start | bytes 393224 | tf_op jit(solution)/shard_map/ppermute | solution.py:520
  25.9 5.0 %collective-permute-start.5 = (bf16[64,1024]{1,0:T(8,128)(2,1)S(1)}, bf16[64,1024]{1,0:T(8,128)(2,1)S(1)}, u32[]{:S(2)}, u32[]{:S(2)}) collective-permute-start(bf16[64,1024]{1,0:T(8,128)(2,1)S(1)} %get-tuple-element.71), channel_id=1, source_target_pairs={{1,2},{3,4},{5,6},{7,8},{9,10},{11,12},{13,14},{2,1},{4,3},{6,5},{... | collective-permute-start | bytes 393224 | tf_op jit(solution)/shard_map/ppermute | solution.py:542
  30.9 1.5 %copy-start.3 = (bf16[512,1024]{1,0:T(8,128)(2,1)}, bf16[512,1024]{1,0:T(8,128)(2,1)S(1)}, u32[]{:S(2)}) copy-start(bf16[512,1024]{1,0:T(8,128)(2,1)S(1)} %get-tuple-element.69.refs_0_.refs_6_) | copy-start | bytes 3145732
  30.9 1.5 %copy-start.7 = (bf16[384,1024]{1,0:T(8,128)(2,1)}, bf16[384,1024]{1,0:T(8,128)(2,1)S(1)}, u32[]{:S(2)}) copy-start(bf16[384,1024]{1,0:T(8,128)(2,1)S(1)} %get-tuple-element.80.refs_1_) | copy-start | bytes 2359300
  32.4 4.8 %collective-permute-start.6 = (bf16[64,1152]{1,0:T(8,128)(2,1)S(1)}, bf16[64,1152]{1,0:T(8,128)(2,1)S(1)}, u32[]{:S(2)}, u32[]{:S(2)}) collective-permute-start(bf16[64,1152]{1,0:T(8,128)(2,1)S(1)} %get-tuple-element.77), channel_id=1, source_target_pairs={{0,1},{1,0},{2,3},{3,2},{4,5},{5,4},{6,7},{7,6},{8,9},{9,8},{10,11... | collective-permute-start | bytes 442376 | tf_op jit(solution)/shard_map/ppermute | solution.py:520
  37.3 4.9 %collective-permute-start.7 = (bf16[32,1152]{1,0:T(8,128)(2,1)S(1)}, bf16[32,1152]{1,0:T(8,128)(2,1)S(1)}, u32[]{:S(2)}, u32[]{:S(2)}) collective-permute-start(bf16[32,1152]{1,0:T(8,128)(2,1)S(1)} %get-tuple-element.79), channel_id=1, source_target_pairs={{0,2},{1,3},{2,0},{3,1},{4,6},{5,7},{6,4},{7,5},{8,10},{9,11},{10,... | collective-permute-start | bytes 221192 | tf_op jit(solution)/shard_map/ppermute | solution.py:520
  39.4 7.3 %collective-permute-start.11 = (bf16[64,1024]{1,0:T(8,128)(2,1)S(1)}, bf16[64,1024]{1,0:T(8,128)(2,1)S(1)}, u32[]{:S(2)}, u32[]{:S(2)}) collective-permute-start(bf16[64,1024]{1,0:T(8,128)(2,1)S(1)} %get-tuple-element.83.refs_2_), channel_id=1, source_target_pairs={{0,1},{1,0},{2,3},{3,2},{4,5},{5,4},{6,7},{7,6},{8,9},{9,8},{10,11... | collective-permute-start | bytes 393224 | tf_op jit(solution)/shard_map/ppermute | solution.py:520
  39.4 7.2 %collective-permute-start.12 = (bf16[64,1024]{1,0:T(8,128)(2,1)S(1)}, bf16[64,1024]{1,0:T(8,128)(2,1)S(1)}, u32[]{:S(2)}, u32[]{:S(2)}) collective-permute-start(bf16[64,1024]{1,0:T(8,128)(2,1)S(1)} %get-tuple-element.84.refs_3_), channel_id=1, source_target_pairs={{1,2},{3,4},{5,6},{7,8},{9,10},{11,12},{13,14},{2,1},{4,3},{6,5},{... | collective-permute-start | bytes 393224 | tf_op jit(solution)/shard_map/ppermute | solution.py:542
  42.2 9.8 %collective-permute-start.8 = (bf16[32,1152]{1,0:T(8,128)(2,1)S(1)}, bf16[32,1152]{1,0:T(8,128)(2,1)S(1)}, u32[]{:S(2)}, u32[]{:S(2)}) collective-permute-start(bf16[32,1152]{1,0:T(8,128)(2,1)S(1)} %add_convert_fusion.1.refs_0_), channel_id=1, source_target_pairs={{0,4},{1,5},{2,6},{3,7},{4,0},{5,1},{6,2},{7,3},{8,12},{9,13},{10,... | collective-permute-start | bytes 221192 | tf_op jit(solution)/shard_map/ppermute | solution.py:520
  43.8 8.1 %collective-permute-start.9 = (bf16[32,1152]{1,0:T(8,128)(2,1)S(1)}, bf16[32,1152]{1,0:T(8,128)(2,1)S(1)}, u32[]{:S(2)}, u32[]{:S(2)}) collective-permute-start(bf16[32,1152]{1,0:T(8,128)(2,1)S(1)} %add_convert_fusion.1.refs_0_), channel_id=1, source_target_pairs={{0,8},{1,9},{2,10},{3,11},{4,12},{5,13},{6,14},{7,15},{8,0},{9,1},... | collective-permute-start | bytes 221192 | tf_op jit(solution)/shard_map/ppermute | solution.py:520
  46.4 6.4 %collective-permute-start.10 = (bf16[32,1152]{1,0:T(8,128)(2,1)S(1)}, bf16[32,1152]{1,0:T(8,128)(2,1)S(1)}, u32[]{:S(2)}, u32[]{:S(2)}) collective-permute-start(bf16[32,1152]{1,0:T(8,128)(2,1)S(1)} %add_convert_fusion.1.refs_0_), channel_id=1, source_target_pairs={{0,12},{1,13},{2,14},{3,15},{4,8},{5,9},{6,10},{7,11},{8,4},{9,5},... | collective-permute-start | bytes 221192 | tf_op jit(solution)/shard_map/ppermute | solution.py:520
  46.6 1.2 %copy-start.4 = (bf16[512,1024]{1,0:T(8,128)(2,1)S(1)}, bf16[512,1024]{1,0:T(8,128)(2,1)}, u32[]{:S(2)}) copy-start(bf16[512,1024]{1,0:T(8,128)(2,1)} %copy-done.3) | copy-start | bytes 3145732
  47.9 1.1 %copy-start.8 = (bf16[384,1024]{1,0:T(8,128)(2,1)S(1)}, bf16[384,1024]{1,0:T(8,128)(2,1)}, u32[]{:S(2)}) copy-start(bf16[384,1024]{1,0:T(8,128)(2,1)} %copy-done.7) | copy-start | bytes 2359300
  49.0 5.4 %copy-start.6 = (bf16[640,1024]{1,0:T(8,128)(2,1)S(1)}, bf16[640,1024]{1,0:T(8,128)(2,1)}, u32[]{:S(2)}) copy-start(bf16[640,1024]{1,0:T(8,128)(2,1)} %copy-done.5) | copy-start | bytes 3932164
  52.8 4.4 %collective-permute-start.13 = (bf16[32,1152]{1,0:T(8,128)(2,1)S(1)}, bf16[32,1152]{1,0:T(8,128)(2,1)S(1)}, u32[]{:S(2)}, u32[]{:S(2)}) collective-permute-start(bf16[32,1152]{1,0:T(8,128)(2,1)S(1)} %add_convert_fusion.refs_0_), channel_id=1, source_target_pairs={{0,2},{1,3},{2,0},{3,1},{4,6},{5,7},{6,4},{7,5},{8,10},{9,11},{10,... | collective-permute-start | bytes 221192 | tf_op jit(solution)/shard_map/ppermute | solution.py:520
  57.3 1.4 %collective-permute-start.14 = (bf16[64,1152]{1,0:T(8,128)(2,1)S(1)}, bf16[64,1152]{1,0:T(8,128)(2,1)S(1)}, u32[]{:S(2)}, u32[]{:S(2)}) collective-permute-start(bf16[64,1152]{1,0:T(8,128)(2,1)S(1)} %maximum_select_fusion.refs_0_), channel_id=1, source_target_pairs={{0,1},{1,0},{2,3},{3,2},{4,5},{5,4},{6,7},{7,6},{8,9},{9,8},{10,11... | collective-permute-start | bytes 442376 | tf_op jit(solution)/shard_map/ppermute | solution.py:520

commit v10 on v9

--- a/solution.py
+++ b/solution.py
@@ -620,18 +620,17 @@
     dh0near, dh0far = neighbours(dh0_near, dh0_far)
     part = part + arrived.astype(F32)
     step = 4
-    input_grad = None
+    section_output = None
     while step < count:
         send = part.astype(BF16)
         masks = [step, 2 * step, 3 * step] if 2 * step < count else [step]
         arrived = [exchange(send, mask, count) for mask in masks]
-        if input_grad is None:
-            (input_grad,) = call(
-                functools.partial(input_grad_kernel, rows), (dh0_inner, dh0_near, dh0_far, dh0near, dh0far, g1, weights),
-                (tile,),
-                [vmem(rows + 2), wide], 8 * row_flops, "input_grad", after=(send,),
+        if section_output is None:
+            (section_output,) = call(
+                functools.partial(output_kernel, rows), (hid1, x1, weights), (tile,),
+                [vmem(rows + 2), wide], 8 * row_flops, "output", after=(send,),
             )
-            arrived, input_grad = lax.optimization_barrier((arrived, input_grad))
+            arrived, section_output = lax.optimization_barrier((arrived, section_output))
         own = send.astype(F32)
         arrived = [value.astype(F32) for value in arrived]
         part = own + arrived[0]
@@ -641,11 +640,12 @@
     done = part.astype(BF16)
     bit = (place & 2) != 0
     other = exchange(done, 2, count)
-    (section_output,) = call(
-        functools.partial(output_kernel, rows), (hid1, x1, weights), (tile,),
-        [vmem(rows + 2), wide], 8 * row_flops, "output", after=(done,),
-    )
-    other, section_output = lax.optimization_barrier((other, section_output))
+    (input_grad,) = call(
+        functools.partial(input_grad_kernel, rows), (dh0_inner, dh0_near, dh0_far, dh0near, dh0far, g1, weights),
+        (tile,),
+        [vmem(rows + 2), wide], 8 * row_flops, "input_grad", after=(done,),
+    )
+    other, input_grad = lax.optimization_barrier((other, input_grad))
     done = jnp.where(bit, jnp.concatenate([other, done]), jnp.concatenate([done, other]))
     (kernel_grad,) = call(
         gathered_kernel, (done, exchange(done, 1, count)),

time: 60 us -> 60 us (level)
  waiting for transfers between devices: 5.63 us -> 6.77 us
  local copies, waits for them, and re-layouts: 4.57 us -> 3.53 us
    ppermute x11, waiting for transfers between devices: 5.62 us -> 6.76 us  [exchange(): return lax.ppermute(value, 'space', [(d, d ^ mask) for d in range(count)])]
    unnamed x18, local copies, waits for them, and re-layouts: 4.57 us -> 3.53 us
where the time goes in v10:
time: 60 us; the launch traced here: 59.7 us
  starting transfers between devices  24.5 us (41%)
  Pallas kernels  23.9 us (40%)
  waiting for transfers between devices  6.77 us (11%)
  local copies, waits for them, and re-layouts  3.53 us (6%)
  between operations  0.9 us (2%)
    pallas_call x15, Pallas kernels, call(): pl.pallas_call(kernel, out_shape=outs, in_specs=[ANY] * len(after) + [pla...  23.9 us
    ppermute x11, starting transfers between devices, exchange(): return lax.ppermute(value, 'space', [(d, d ^ mask) for d in range(count)])  21.6 us
    ppermute x11, waiting for transfers between devices, exchange(): return lax.ppermute(value, 'space', [(d, d ^ mask) for d in range(count)])  6.76 us
    unnamed x18, local copies, waits for them, and re-layouts  3.53 us
    ppermute x4, starting transfers between devices, neighbours(): from_far = lax.ppermute(far, 'space', beyond)  2.89 us
  transfers between devices with their start and end apart: 15, of which 5 were waited for; matrix products, arithmetic and copies ran while one was open for 0% of the time, Pallas kernels for 33%

profile of v10, /device:TPU:0, one launch (start us, length us, event | category | flops | bytes accessed | tf_op | source)
XLA Modules:
  0.0 59.7 jit_solution(11900651458037730939)
XLA Ops:
  0.6 1.2 %copy-done = bf16[64,8,1024]{2,1,0:T(8,128)(2,1)S(1)} copy-done((bf16[64,8,1024]{2,1,0:T(8,128)(2,1)S(1)}, bf16[64,8,1024]{2,1,0:T(8,128)(2,1)}, u32[]{:S(2)}) %copy-start) | copy-done | bytes 1048600
  5.4 1.7 %inner.1 = (bf16[384,1024]{1,0:T(8,128)(2,1)S(1)}, bf16[256,1024]{1,0:T(8,128)(2,1)S(1)}, bf16[128,1024]{1,0:T(8,128)(2,1)S(1)}) custom-call(bf16[512,1024]{1,0:T(8,128)(2,1)S(1)} %get-tuple-element.47.refs_0_.refs_1_.refs_6_.refs_4_, bf16[8,128,768]{2,1,0:T(8,128)(2,1)S(1)} %weights.1.refs_1_.refs_2_.refs_3_.refs_5_.refs_4_.refs_7_), custom_call_target="tpu_custom_call" | custom-call | flops 3623878656 | bytes 4194304 | tf_op jit(solution)/shard_map/inner/pallas_call | solution.py:28
  7.1 1.6 %g_rows.1 = (bf16[512,1024]{1,0:T(8,128)(2,1)S(1)}, bf16[128,1024]{1,0:T(8,128)(2,1)S(1)}, bf16[128,1024]{1,0:T(8,128)(2,1)S(1)}, f32[384,1024]{1,0:T(8,128)S(1)}) custom-call(bf16[128,1024]{1,0:T(8,128)(2,1)S(1)} %get-tuple-element.49.refs_0_.refs_3_.refs_6_, bf16[64,8,1024]{2,1,0:T(8,128)(2,1)S(1)} %copy-done.2, ...), custom_call_target="tpu_custom_call" | custom-call | flops 1811939328 | bytes 5767168 | tf_op jit(solution)/shard_map/g_rows/pallas_call | solution.py:28
  9.3 5.2 %collective-permute-start.1 = (bf16[128,1024]{1,0:T(8,128)(2,1)S(1)}, bf16[128,1024]{1,0:T(8,128)(2,1)S(1)}, u32[]{:S(2)}, u32[]{:S(2)}) collective-permute-start(bf16[128,1024]{1,0:T(8,128)(2,1)S(1)} %get-tuple-element.52.refs_0_), channel_id=1, source_target_pairs={{0,1},{1,0},{2,3},{3,2},{4,5},{5,4},{6,7},{7,6},{8,9},{9,8},{10,11... | collective-permute-start | bytes 786440 | tf_op jit(solution)/shard_map/ppermute | solution.py:520
  14.5 1.8 %forward_near.1 = (bf16[256,1024]{1,0:T(8,128)(2,1)S(1)}, bf16[256,1024]{1,0:T(8,128)(2,1)S(1)}, bf16[256,1024]{1,0:T(8,128)(2,1)S(1)}) custom-call(bf16[128,1024]{1,0:T(8,128)(2,1)S(1)} %get-tuple-element.52.refs_0_, bf16[512,1024]{1,0:T(8,128)(2,1)S(1)} %get-tuple-element.47.refs_0_.refs_1_.refs_6_.refs_4_, ...), custom_call_target="tpu_custom_call" | custom-call | flops 3623878656 | bytes 6029312 | tf_op jit(solution)/shard_map/forward_near/pallas_call | solution.py:28
  16.4 1.1 %backward1_near.1 = (bf16[384,1024]{1,0:T(8,128)(2,1)S(1)}, bf16[128,1024]{1,0:T(8,128)(2,1)S(1)}) custom-call(bf16[512,1024]{1,0:T(8,128)(2,1)S(1)} %get-tuple-element.50.refs_0_.refs_1_, bf16[128,1024]{1,0:T(8,128)(2,1)S(1)} %collective-permute-done.1.refs_1_, bf16[256,1024]{1,0:T(8,128)(2,1)S(1)} %get-tuple-element.56.refs_2_.refs_9_, ...), custom_call_target="tpu_custom_call" | custom-call | flops 1207959552 | bytes 6291456 | tf_op jit(solution)/shard_map/backward1_near/pallas_call | solution.py:28
  17.4 1.4 %grads_near.1 = (f32[192,192]{1,0:T(8,128)S(1)}, f32[192,192]{1,0:T(8,128)S(1)}) custom-call(bf16[128,1024]{1,0:T(8,128)(2,1)S(1)} %get-tuple-element.58.refs_0_.refs_6_, bf16[512,1024]{1,0:T(8,128)(2,1)S(1)} %get-tuple-element.50.refs_0_.refs_1_, bf16[256,1024]{1,0:T(8,128)(2,1)S(1)} %get-tuple-element.56.refs_2_.refs_9_, ...), custom_call_target="tpu_custom_call" | custom-call | flops 2415919104 | bytes 3964928 | tf_op jit(solution)/shard_map/grads_near/pallas_call | solution.py:28
  18.9 2.1 %forward_far.1 = (bf16[640,1024]{1,0:T(8,128)(2,1)S(1)}, bf16[640,1024]{1,0:T(8,128)(2,1)S(1)}, bf16[640,1024]{1,0:T(8,128)(2,1)S(1)}) custom-call(f32[192,192]{1,0:T(8,128)S(1)} %get-tuple-element.61.refs_0_.refs_9_, bf16[512,1024]{1,0:T(8,128)(2,1)S(1)} %get-tuple-element.47.refs_0_.refs_1_.refs_6_.refs_4_, ...), custom_call_target="tpu_custom_call" | custom-call | flops 3623878656 | bytes 10223616 | tf_op jit(solution)/shard_map/forward_far/pallas_call | solution.py:28
  21.0 1.0 %backward1_far.1 = (bf16[64,1024]{1,0:T(8,128)(2,1)S(1)}, bf16[64,1024]{1,0:T(8,128)(2,1)S(1)}, bf16[256,1024]{1,0:T(8,128)(2,1)S(1)}, bf16[640,1024]{1,0:T(8,128)(2,1)S(1)}) custom-call(bf16[512,1024]{1,0:T(8,128)(2,1)S(1)} %get-tuple-element.50.refs_0_.refs_1_, bf16[128,1024]{1,0:T(8,128)(2,1)S(1)} %collective-permute-done.refs_1_, ...), custom_call_target="tpu_custom_call" | custom-call | flops 1207959552 | bytes 8912896 | tf_op jit(solution)/shard_map/backward1_far/pallas_call | solution.py:28
  22.0 3.9 %collective-permute-start.4 = (bf16[64,1024]{1,0:T(8,128)(2,1)S(1)}, bf16[64,1024]{1,0:T(8,128)(2,1)S(1)}, u32[]{:S(2)}, u32[]{:S(2)}) collective-permute-start(bf16[64,1024]{1,0:T(8,128)(2,1)S(1)} %get-tuple-element.70), channel_id=1, source_target_pairs={{0,1},{1,0},{2,3},{3,2},{4,5},{5,4},{6,7},{7,6},{8,9},{9,8},{10,11... | collective-permute-start | bytes 393224 | tf_op jit(solution)/shard_map/ppermute | solution.py:520
  26.8 4.1 %middle.1 = (bf16[512,1024]{1,0:T(8,128)(2,1)S(1)}, bf16[384,1024]{1,0:T(8,128)(2,1)S(1)}, f32[192,192]{1,0:T(8,128)S(1)}, f32[192,192]{1,0:T(8,128)S(1)}, f32[1...) custom-call(bf16[512,1024]{1,0:T(8,128)(2,1)S(1)} %get-tuple-element.50.refs_0_.refs_1_, ...), custom_call_target="tpu_custom_call" | custom-call | flops 10871635968 | bytes 12156928 | tf_op jit(solution)/shard_map/middle/pallas_call | solution.py:28
  31.0 1.4 %backward0.1 = (bf16[64,1024]{1,0:T(8,128)(2,1)S(1)}, bf16[64,1024]{1,0:T(8,128)(2,1)S(1)}, f32[64,1152]{1,0:T(8,128)S(1)}, bf16[64,1152]{1,0:T(8,128)(2,1)S(1)}) custom-call(bf16[512,1024]{1,0:T(8,128)(2,1)S(1)} %get-tuple-element.69.refs_0_.refs_6_, bf16[64,1024]{1,0:T(8,128)(2,1)S(1)} %collective-permute-done.4.refs_1_, ...), custom_call_target="tpu_custom_call" | custom-call | flops 2415919104 | bytes 7585792 | tf_op jit(solution)/shard_map/backward0/pallas_call | solution.py:28
  32.4 3.8 %collective-permute-start.6 = (bf16[64,1152]{1,0:T(8,128)(2,1)S(1)}, bf16[64,1152]{1,0:T(8,128)(2,1)S(1)}, u32[]{:S(2)}, u32[]{:S(2)}) collective-permute-start(bf16[64,1152]{1,0:T(8,128)(2,1)S(1)} %get-tuple-element.77), channel_id=1, source_target_pairs={{0,1},{1,0},{2,3},{3,2},{4,5},{5,4},{6,7},{7,6},{8,9},{9,8},{10,11... | collective-permute-start | bytes 442376 | tf_op jit(solution)/shard_map/ppermute | solution.py:520
  36.2 1.0 %collective-permute-done.6.refs_1_ = bf16[64,1152]{1,0:T(8,128)(2,1)S(1)} collective-permute-done((bf16[64,1152]{1,0:T(8,128)(2,1)S(1)}, bf16[64,1152]{1,0:T(8,128)(2,1)S(1)}, u32[]{:S(2)}, u32[]{:S(2)}) %collective-permute-start.6) | collective-permute-done | bytes 147488 | tf_op jit(solution)/shard_map/ppermute | solution.py:520
  37.3 2.1 %collective-permute-start.7 = (bf16[32,1152]{1,0:T(8,128)(2,1)S(1)}, bf16[32,1152]{1,0:T(8,128)(2,1)S(1)}, u32[]{:S(2)}, u32[]{:S(2)}) collective-permute-start(bf16[32,1152]{1,0:T(8,128)(2,1)S(1)} %get-tuple-element.79), channel_id=1, source_target_pairs={{0,2},{1,3},{2,0},{3,1},{4,6},{5,7},{6,4},{7,5},{8,10},{9,11},{10,... | collective-permute-start | bytes 221192 | tf_op jit(solution)/shard_map/ppermute | solution.py:520
  40.1 2.0 %collective-permute-done.7 = bf16[32,1152]{1,0:T(8,128)(2,1)S(1)} collective-permute-done((bf16[32,1152]{1,0:T(8,128)(2,1)S(1)}, bf16[32,1152]{1,0:T(8,128)(2,1)S(1)}, u32[]{:S(2)}, u32[]{:S(2)}) %collective-permute-start.7) | collective-permute-done | bytes 73760 | tf_op jit(solution)/shard_map/ppermute | solution.py:520
  42.2 1.6 %collective-permute-start.8 = (bf16[32,1152]{1,0:T(8,128)(2,1)S(1)}, bf16[32,1152]{1,0:T(8,128)(2,1)S(1)}, u32[]{:S(2)}, u32[]{:S(2)}) collective-permute-start(bf16[32,1152]{1,0:T(8,128)(2,1)S(1)} %add_convert_fusion.1.refs_0_), channel_id=1, source_target_pairs={{0,4},{1,5},{2,6},{3,7},{4,0},{5,1},{6,2},{7,3},{8,12},{9,13},{10,... | collective-permute-start | bytes 221192 | tf_op jit(solution)/shard_map/ppermute | solution.py:520
  43.8 2.6 %collective-permute-start.9 = (bf16[32,1152]{1,0:T(8,128)(2,1)S(1)}, bf16[32,1152]{1,0:T(8,128)(2,1)S(1)}, u32[]{:S(2)}, u32[]{:S(2)}) collective-permute-start(bf16[32,1152]{1,0:T(8,128)(2,1)S(1)} %add_convert_fusion.1.refs_0_), channel_id=1, source_target_pairs={{0,8},{1,9},{2,10},{3,11},{4,12},{5,13},{6,14},{7,15},{8,0},{9,1},... | collective-permute-start | bytes 221192 | tf_op jit(solution)/shard_map/ppermute | solution.py:520
  46.6 1.3 %copy-done.6 = bf16[640,1024]{1,0:T(8,128)(2,1)S(1)} copy-done((bf16[640,1024]{1,0:T(8,128)(2,1)S(1)}, bf16[640,1024]{1,0:T(8,128)(2,1)}, u32[]{:S(2)}) %copy-start.6) | copy-done | bytes 1310744
  47.9 2.5 %output.1 = bf16[64,8,1024]{2,1,0:T(8,128)(2,1)} custom-call(bf16[32,1152]{1,0:T(8,128)(2,1)S(1)} %add_convert_fusion.1.refs_0_, bf16[640,1024]{1,0:T(8,128)(2,1)S(1)} %get-tuple-element.63.refs_2_.refs_1_, bf16[640,1024]{1,0:T(8,128)(2,1)S(1)} %copy-done.6, bf16[8,128,768]{2,1,0:T(8,128)(2,1)S(1)} %weights.1.refs_1_.refs_2_.refs_3_.refs_5_.refs_4_.refs_7_), custom_call_target="tpu_custom_call" | custom-call | flops 2415919104 | bytes 5242880 | tf_op jit(solution)/shard_map/output/pallas_call | solution.py:28
  50.8 2.0 %collective-permute-done.10 = bf16[32,1152]{1,0:T(8,128)(2,1)S(1)} collective-permute-done((bf16[32,1152]{1,0:T(8,128)(2,1)S(1)}, bf16[32,1152]{1,0:T(8,128)(2,1)S(1)}, u32[]{:S(2)}, u32[]{:S(2)}) %collective-permute-start.10) | collective-permute-done | bytes 73760 | tf_op jit(solution)/shard_map/ppermute | solution.py:520
  52.8 1.5 %collective-permute-start.11 = (bf16[32,1152]{1,0:T(8,128)(2,1)S(1)}, bf16[32,1152]{1,0:T(8,128)(2,1)S(1)}, u32[]{:S(2)}, u32[]{:S(2)}) collective-permute-start(bf16[32,1152]{1,0:T(8,128)(2,1)S(1)} %add_convert_fusion.refs_0_), channel_id=1, source_target_pairs={{0,2},{1,3},{2,0},{3,1},{4,6},{5,7},{6,4},{7,5},{8,10},{9,11},{10,... | collective-permute-start | bytes 221192 | tf_op jit(solution)/shard_map/ppermute | solution.py:520
  54.4 2.9 %input_grad.1 = bf16[64,8,1024]{2,1,0:T(8,128)(2,1)} custom-call(bf16[32,1152]{1,0:T(8,128)(2,1)S(1)} %add_convert_fusion.refs_0_, bf16[384,1024]{1,0:T(8,128)(2,1)S(1)} %copy-done.8, bf16[64,1024]{1,0:T(8,128)(2,1)S(1)} %get-tuple-element.87.refs_2_, bf16[64,1024]{1,0:T(8,128)(2,1)S(1)} %get-tuple-element.88.refs_3_, ...), custom_call_target="tpu_custom_call" | custom-call | flops 2415919104 | bytes 4980736 | tf_op jit(solution)/shard_map/input_grad/pallas_call | solution.py:28
  57.4 1.4 %collective-permute-done.14.refs_1_ = bf16[64,1152]{1,0:T(8,128)(2,1)S(1)} collective-permute-done((bf16[64,1152]{1,0:T(8,128)(2,1)S(1)}, bf16[64,1152]{1,0:T(8,128)(2,1)S(1)}, u32[]{:S(2)}, u32[]{:S(2)}) %collective-permute-start.14) | collective-permute-done | bytes 147488 | tf_op jit(solution)/shard_map/ppermute | solution.py:520
  (42 shorter events, 7.5 us)
Async XLA Ops:
  0.6 1.2 %copy-start = (bf16[64,8,1024]{2,1,0:T(8,128)(2,1)S(1)}, bf16[64,8,1024]{2,1,0:T(8,128)(2,1)}, u32[]{:S(2)}) copy-start(bf16[64,8,1024]{2,1,0:T(8,128)(2,1)} %refs_0_.1) | copy-start | bytes 3145732
  2.5 12.0 %collective-permute-start.2 = (bf16[256,1024]{1,0:T(8,128)(2,1)S(1)}, bf16[256,1024]{1,0:T(8,128)(2,1)S(1)}, u32[]{:S(2)}, u32[]{:S(2)}) collective-permute-start(bf16[256,1024]{1,0:T(8,128)(2,1)S(1)} %get-tuple-element.53), channel_id=1, source_target_pairs={{0,1},{1,0},{2,3},{3,2},{4,5},{5,4},{6,7},{7,6},{8,9},{9,8},{10,11... | collective-permute-start | bytes 1572872 | tf_op jit(solution)/shard_map/ppermute | solution.py:520
  3.0 15.8 %collective-permute-start.3 = (bf16[256,1024]{1,0:T(8,128)(2,1)S(1)}, bf16[256,1024]{1,0:T(8,128)(2,1)S(1)}, u32[]{:S(2)}, u32[]{:S(2)}) collective-permute-start(bf16[256,1024]{1,0:T(8,128)(2,1)S(1)} %get-tuple-element.48.refs_0_), channel_id=1, source_target_pairs={{1,2},{3,4},{5,6},{7,8},{9,10},{11,12},{13,14},{2,1},{4,3},{6,5},{... | collective-permute-start | bytes 1572872 | tf_op jit(solution)/shard_map/ppermute | solution.py:542
  3.7 1.0 %copy-start.1 = (bf16[2,2,64,576]{3,2,1,0:T(8,128)(2,1)S(1)}, bf16[2,2,64,576]{3,2,1,0:T(8,128)(2,1)}, u32[]{:S(2)}) copy-start(bf16[2,2,64,576]{3,2,1,0:T(8,128)(2,1)} %refs_1_.2) | copy-start | bytes 884740
  5.4 1.7 %copy-start.2 = (bf16[64,8,1024]{2,1,0:T(8,128)(2,1)S(1)}, bf16[64,8,1024]{2,1,0:T(8,128)(2,1)}, u32[]{:S(2)}) copy-start(bf16[64,8,1024]{2,1,0:T(8,128)(2,1)} %refs_1_.3) | copy-start | bytes 3145732
  8.7 12.3 %collective-permute-start = (bf16[128,1024]{1,0:T(8,128)(2,1)S(1)}, bf16[128,1024]{1,0:T(8,128)(2,1)S(1)}, u32[]{:S(2)}, u32[]{:S(2)}) collective-permute-start(bf16[128,1024]{1,0:T(8,128)(2,1)S(1)} %get-tuple-element.51), channel_id=1, source_target_pairs={{1,2},{3,4},{5,6},{7,8},{9,10},{11,12},{13,14},{2,1},{4,3},{6,5},{... | collective-permute-start | bytes 786440 | tf_op jit(solution)/shard_map/ppermute | solution.py:542
  9.3 7.0 %collective-permute-start.1 = (bf16[128,1024]{1,0:T(8,128)(2,1)S(1)}, bf16[128,1024]{1,0:T(8,128)(2,1)S(1)}, u32[]{:S(2)}, u32[]{:S(2)}) collective-permute-start(bf16[128,1024]{1,0:T(8,128)(2,1)S(1)} %get-tuple-element.52.refs_0_), channel_id=1, source_target_pairs={{0,1},{1,0},{2,3},{3,2},{4,5},{5,4},{6,7},{7,6},{8,9},{9,8},{10,11... | collective-permute-start | bytes 786440 | tf_op jit(solution)/shard_map/ppermute | solution.py:520
  21.0 5.8 %copy-start.5 = (bf16[640,1024]{1,0:T(8,128)(2,1)}, bf16[640,1024]{1,0:T(8,128)(2,1)S(1)}, u32[]{:S(2)}) copy-start(bf16[640,1024]{1,0:T(8,128)(2,1)S(1)} %get-tuple-element.66.refs_4_.refs_2_) | copy-start | bytes 3932164
  22.0 8.9 %collective-permute-start.4 = (bf16[64,1024]{1,0:T(8,128)(2,1)S(1)}, bf16[64,1024]{1,0:T(8,128)(2,1)S(1)}, u32[]{:S(2)}, u32[]{:S(2)}) collective-permute-start(bf16[64,1024]{1,0:T(8,128)(2,1)S(1)} %get-tuple-element.70), channel_id=1, source_target_pairs={{0,1},{1,0},{2,3},{3,2},{4,5},{5,4},{6,7},{7,6},{8,9},{9,8},{10,11... | collective-permute-start | bytes 393224 | tf_op jit(solution)/shard_map/ppermute | solution.py:520
  25.9 5.0 %collective-permute-start.5 = (bf16[64,1024]{1,0:T(8,128)(2,1)S(1)}, bf16[64,1024]{1,0:T(8,128)(2,1)S(1)}, u32[]{:S(2)}, u32[]{:S(2)}) collective-permute-start(bf16[64,1024]{1,0:T(8,128)(2,1)S(1)} %get-tuple-element.71), channel_id=1, source_target_pairs={{1,2},{3,4},{5,6},{7,8},{9,10},{11,12},{13,14},{2,1},{4,3},{6,5},{... | collective-permute-start | bytes 393224 | tf_op jit(solution)/shard_map/ppermute | solution.py:542
  30.9 1.5 %copy-start.3 = (bf16[512,1024]{1,0:T(8,128)(2,1)}, bf16[512,1024]{1,0:T(8,128)(2,1)S(1)}, u32[]{:S(2)}) copy-start(bf16[512,1024]{1,0:T(8,128)(2,1)S(1)} %get-tuple-element.69.refs_0_.refs_6_) | copy-start | bytes 3145732
  30.9 1.5 %copy-start.7 = (bf16[384,1024]{1,0:T(8,128)(2,1)}, bf16[384,1024]{1,0:T(8,128)(2,1)S(1)}, u32[]{:S(2)}) copy-start(bf16[384,1024]{1,0:T(8,128)(2,1)S(1)} %get-tuple-element.84.refs_1_) | copy-start | bytes 2359300
  32.4 4.8 %collective-permute-start.6 = (bf16[64,1152]{1,0:T(8,128)(2,1)S(1)}, bf16[64,1152]{1,0:T(8,128)(2,1)S(1)}, u32[]{:S(2)}, u32[]{:S(2)}) collective-permute-start(bf16[64,1152]{1,0:T(8,128)(2,1)S(1)} %get-tuple-element.77), channel_id=1, source_target_pairs={{0,1},{1,0},{2,3},{3,2},{4,5},{5,4},{6,7},{7,6},{8,9},{9,8},{10,11... | collective-permute-start | bytes 442376 | tf_op jit(solution)/shard_map/ppermute | solution.py:520
  37.3 4.9 %collective-permute-start.7 = (bf16[32,1152]{1,0:T(8,128)(2,1)S(1)}, bf16[32,1152]{1,0:T(8,128)(2,1)S(1)}, u32[]{:S(2)}, u32[]{:S(2)}) collective-permute-start(bf16[32,1152]{1,0:T(8,128)(2,1)S(1)} %get-tuple-element.79), channel_id=1, source_target_pairs={{0,2},{1,3},{2,0},{3,1},{4,6},{5,7},{6,4},{7,5},{8,10},{9,11},{10,... | collective-permute-start | bytes 221192 | tf_op jit(solution)/shard_map/ppermute | solution.py:520
  39.4 15.0 %collective-permute-start.12 = (bf16[64,1024]{1,0:T(8,128)(2,1)S(1)}, bf16[64,1024]{1,0:T(8,128)(2,1)S(1)}, u32[]{:S(2)}, u32[]{:S(2)}) collective-permute-start(bf16[64,1024]{1,0:T(8,128)(2,1)S(1)} %get-tuple-element.87.refs_2_), channel_id=1, source_target_pairs={{0,1},{1,0},{2,3},{3,2},{4,5},{5,4},{6,7},{7,6},{8,9},{9,8},{10,11... | collective-permute-start | bytes 393224 | tf_op jit(solution)/shard_map/ppermute | solution.py:520
  39.4 14.9 %collective-permute-start.13 = (bf16[64,1024]{1,0:T(8,128)(2,1)S(1)}, bf16[64,1024]{1,0:T(8,128)(2,1)S(1)}, u32[]{:S(2)}, u32[]{:S(2)}) collective-permute-start(bf16[64,1024]{1,0:T(8,128)(2,1)S(1)} %get-tuple-element.88.refs_3_), channel_id=1, source_target_pairs={{1,2},{3,4},{5,6},{7,8},{9,10},{11,12},{13,14},{2,1},{4,3},{6,5},{... | collective-permute-start | bytes 393224 | tf_op jit(solution)/shard_map/ppermute | solution.py:542
  42.2 12.2 %copy-start.4 = (bf16[512,1024]{1,0:T(8,128)(2,1)S(1)}, bf16[512,1024]{1,0:T(8,128)(2,1)}, u32[]{:S(2)}) copy-start(bf16[512,1024]{1,0:T(8,128)(2,1)} %copy-done.3) | copy-start | bytes 3145732
  42.2 8.3 %collective-permute-start.8 = (bf16[32,1152]{1,0:T(8,128)(2,1)S(1)}, bf16[32,1152]{1,0:T(8,128)(2,1)S(1)}, u32[]{:S(2)}, u32[]{:S(2)}) collective-permute-start(bf16[32,1152]{1,0:T(8,128)(2,1)S(1)} %add_convert_fusion.1.refs_0_), channel_id=1, source_target_pairs={{0,4},{1,5},{2,6},{3,7},{4,0},{5,1},{6,2},{7,3},{8,12},{9,13},{10,... | collective-permute-start | bytes 221192 | tf_op jit(solution)/shard_map/ppermute | solution.py:520
  43.8 7.0 %collective-permute-start.9 = (bf16[32,1152]{1,0:T(8,128)(2,1)S(1)}, bf16[32,1152]{1,0:T(8,128)(2,1)S(1)}, u32[]{:S(2)}, u32[]{:S(2)}) collective-permute-start(bf16[32,1152]{1,0:T(8,128)(2,1)S(1)} %add_convert_fusion.1.refs_0_), channel_id=1, source_target_pairs={{0,8},{1,9},{2,10},{3,11},{4,12},{5,13},{6,14},{7,15},{8,0},{9,1},... | collective-permute-start | bytes 221192 | tf_op jit(solution)/shard_map/ppermute | solution.py:520
  46.4 6.4 %collective-permute-start.10 = (bf16[32,1152]{1,0:T(8,128)(2,1)S(1)}, bf16[32,1152]{1,0:T(8,128)(2,1)S(1)}, u32[]{:S(2)}, u32[]{:S(2)}) collective-permute-start(bf16[32,1152]{1,0:T(8,128)(2,1)S(1)} %add_convert_fusion.1.refs_0_), channel_id=1, source_target_pairs={{0,12},{1,13},{2,14},{3,15},{4,8},{5,9},{6,10},{7,11},{8,4},{9,5},... | collective-permute-start | bytes 221192 | tf_op jit(solution)/shard_map/ppermute | solution.py:520
  46.6 1.3 %copy-start.6 = (bf16[640,1024]{1,0:T(8,128)(2,1)S(1)}, bf16[640,1024]{1,0:T(8,128)(2,1)}, u32[]{:S(2)}) copy-start(bf16[640,1024]{1,0:T(8,128)(2,1)} %copy-done.5) | copy-start | bytes 3932164
  47.9 6.4 %copy-start.8 = (bf16[384,1024]{1,0:T(8,128)(2,1)S(1)}, bf16[384,1024]{1,0:T(8,128)(2,1)}, u32[]{:S(2)}) copy-start(bf16[384,1024]{1,0:T(8,128)(2,1)} %copy-done.7) | copy-start | bytes 2359300
  52.8 4.4 %collective-permute-start.11 = (bf16[32,1152]{1,0:T(8,128)(2,1)S(1)}, bf16[32,1152]{1,0:T(8,128)(2,1)S(1)}, u32[]{:S(2)}, u32[]{:S(2)}) collective-permute-start(bf16[32,1152]{1,0:T(8,128)(2,1)S(1)} %add_convert_fusion.refs_0_), channel_id=1, source_target_pairs={{0,2},{1,3},{2,0},{3,1},{4,6},{5,7},{6,4},{7,5},{8,10},{9,11},{10,... | collective-permute-start | bytes 221192 | tf_op jit(solution)/shard_map/ppermute | solution.py:520
  57.3 1.4 %collective-permute-start.14 = (bf16[64,1152]{1,0:T(8,128)(2,1)S(1)}, bf16[64,1152]{1,0:T(8,128)(2,1)S(1)}, u32[]{:S(2)}, u32[]{:S(2)}) collective-permute-start(bf16[64,1152]{1,0:T(8,128)(2,1)S(1)} %maximum_select_fusion.refs_0_), channel_id=1, source_target_pairs={{0,1},{1,0},{2,3},{3,2},{4,5},{5,4},{6,7},{7,6},{8,9},{9,8},{10,11... | collective-permute-start | bytes 442376 | tf_op jit(solution)/shard_map/ppermute | solution.py:520

commit v11 on v10

--- a/solution.py
+++ b/solution.py
@@ -64,9 +64,9 @@
 
 
 def g_entry_kernel(
-    edge, tile_ref, w_ref, rows_ref, near_ref, far_ref, inner_ref, held, g3, arrived
-):
-    entry_kernel(edge, tile_ref, rows_ref, near_ref, far_ref, held, arrived)
+    edge, tile_ref, w_ref, rows_ref, near_ref, far_ref, inner_ref, g3
+):
+    entry_kernel(edge, tile_ref, rows_ref, near_ref, far_ref)
     rows = tile_ref.shape[1]
     stack_rows(rows_ref, range(rows), g3, 0)
 
@@ -158,21 +158,10 @@
     far_ref[...] = rows_ref[pl.ds(pl.multiple_of(far_at, CHAN), edge * CHAN), :]
 
 
-def entry_kernel(edge, tile_ref, rows_ref, near_ref, far_ref, held, arrived):
+def entry_kernel(edge, tile_ref, rows_ref, near_ref, far_ref):
     piece = CHAN // PIECES
-    copies = [
-        pltpu.make_async_copy(
-            tile_ref.at[i * piece : (i + 1) * piece],
-            held.at[i * piece : (i + 1) * piece],
-            arrived.at[i],
-        )
-        for i in range(PIECES)
-    ]
-    for copy in copies:
-        copy.start()
-    for i, copy in enumerate(copies):
-        copy.wait()
-        part = held[i * piece : (i + 1) * piece].astype(F32)
+    for i in range(PIECES):
+        part = tile_ref[i * piece : (i + 1) * piece].astype(F32)
         turned = jnp.swapaxes(part, 0, 1).astype(BF16)
         for row in range(turned.shape[0]):
             at = row * CHAN + i * piece
@@ -547,11 +536,10 @@
     tile = jax.ShapeDtypeStruct((CHAN, rows, width), BF16)
     wide = pltpu.VMEM((rows, CHAN, width), F32)
     half = (CHAN, 18 * CHAN)
-    entry = [pltpu.VMEM((CHAN, rows, width), BF16), pltpu.SemaphoreType.DMA((PIECES,))]
 
     x, x_near, x_far = call(
         functools.partial(entry_kernel, 4), (features,), (shape(rows), shape(4), shape(4)),
-        entry, 0, "x_rows", place=HBM,
+        [], 0, "x_rows", place=VMEM,
     )
     xnear, xfar = neighbours(x_near, x_far)
     (weights,) = call(
@@ -566,7 +554,7 @@
     g, g_near, g_far, g_inner = call(
         functools.partial(g_entry_kernel, 2), (cotangent, weights),
         (shape(rows), shape(2), shape(2), shape(rows - 2, F32)),
-        [entry[0], vmem(rows), entry[1]], 6 * row_flops, "g_rows", after=(inner[2],), place=HBM,
+        [vmem(rows)], 6 * row_flops, "g_rows", after=(inner[2],), place=VMEM,
     )
     gnear, gfar = neighbours(g_near, g_far)
     near = call(

time: 60 us -> 59.9 us (level)
  no operation moved by 1% of the time
where the time goes in v11:
time: 59.9 us; the launch traced here: 59.6 us
  starting transfers between devices  24.6 us (41%)
  Pallas kernels  23.8 us (40%)
  waiting for transfers between devices  6.76 us (11%)
  local copies, waits for them, and re-layouts  3.53 us (6%)
  between operations  0.89 us (1%)
    pallas_call x15, Pallas kernels, call(): pl.pallas_call(kernel, out_shape=outs, in_specs=[ANY] * len(after) + [pla...  23.8 us
    ppermute x11, starting transfers between devices, exchange(): return lax.ppermute(value, 'space', [(d, d ^ mask) for d in range(count)])  21.7 us
    ppermute x11, waiting for transfers between devices, exchange(): return lax.ppermute(value, 'space', [(d, d ^ mask) for d in range(count)])  6.75 us
    unnamed x18, local copies, waits for them, and re-layouts  3.53 us
    ppermute x4, starting transfers between devices, neighbours(): from_far = lax.ppermute(far, 'space', beyond)  2.89 us
  transfers between devices with their start and end apart: 15, of which 5 were waited for; matrix products, arithmetic and copies ran while one was open for 0% of the time, Pallas kernels for 33%

profile of v11, /device:TPU:0, one launch (start us, length us, event | category | flops | bytes accessed | tf_op | source)
XLA Modules:
  0.0 59.6 jit_solution(10504186098606325398)
XLA Ops:
  0.6 1.2 %copy-done = bf16[64,8,1024]{2,1,0:T(8,128)(2,1)S(1)} copy-done((bf16[64,8,1024]{2,1,0:T(8,128)(2,1)S(1)}, bf16[64,8,1024]{2,1,0:T(8,128)(2,1)}, u32[]{:S(2)}) %copy-start) | copy-done | bytes 1048600
  5.3 1.7 %inner.1 = (bf16[384,1024]{1,0:T(8,128)(2,1)S(1)}, bf16[256,1024]{1,0:T(8,128)(2,1)S(1)}, bf16[128,1024]{1,0:T(8,128)(2,1)S(1)}) custom-call(bf16[512,1024]{1,0:T(8,128)(2,1)S(1)} %get-tuple-element.47.refs_0_.refs_1_.refs_6_.refs_4_, bf16[8,128,768]{2,1,0:T(8,128)(2,1)S(1)} %weights.1.refs_1_.refs_2_.refs_3_.refs_5_.refs_4_.refs_7_), custom_call_target="tpu_custom_call" | custom-call | flops 3623878656 | bytes 4194304 | tf_op jit(solution)/shard_map/inner/pallas_call | solution.py:28
  7.0 1.5 %g_rows.1 = (bf16[512,1024]{1,0:T(8,128)(2,1)S(1)}, bf16[128,1024]{1,0:T(8,128)(2,1)S(1)}, bf16[128,1024]{1,0:T(8,128)(2,1)S(1)}, f32[384,1024]{1,0:T(8,128)S(1)}) custom-call(bf16[128,1024]{1,0:T(8,128)(2,1)S(1)} %get-tuple-element.49.refs_0_.refs_3_.refs_6_, bf16[64,8,1024]{2,1,0:T(8,128)(2,1)S(1)} %copy-done.2, ...), custom_call_target="tpu_custom_call" | custom-call | flops 1811939328 | bytes 5767168 | tf_op jit(solution)/shard_map/g_rows/pallas_call | solution.py:28
  9.2 5.1 %collective-permute-start.1 = (bf16[128,1024]{1,0:T(8,128)(2,1)S(1)}, bf16[128,1024]{1,0:T(8,128)(2,1)S(1)}, u32[]{:S(2)}, u32[]{:S(2)}) collective-permute-start(bf16[128,1024]{1,0:T(8,128)(2,1)S(1)} %get-tuple-element.52.refs_0_), channel_id=1, source_target_pairs={{0,1},{1,0},{2,3},{3,2},{4,5},{5,4},{6,7},{7,6},{8,9},{9,8},{10,11... | collective-permute-start | bytes 786440 | tf_op jit(solution)/shard_map/ppermute | solution.py:509
  14.3 1.8 %forward_near.1 = (bf16[256,1024]{1,0:T(8,128)(2,1)S(1)}, bf16[256,1024]{1,0:T(8,128)(2,1)S(1)}, bf16[256,1024]{1,0:T(8,128)(2,1)S(1)}) custom-call(bf16[128,1024]{1,0:T(8,128)(2,1)S(1)} %get-tuple-element.52.refs_0_, bf16[512,1024]{1,0:T(8,128)(2,1)S(1)} %get-tuple-element.47.refs_0_.refs_1_.refs_6_.refs_4_, ...), custom_call_target="tpu_custom_call" | custom-call | flops 3623878656 | bytes 6029312 | tf_op jit(solution)/shard_map/forward_near/pallas_call | solution.py:28
  16.2 1.1 %backward1_near.1 = (bf16[384,1024]{1,0:T(8,128)(2,1)S(1)}, bf16[128,1024]{1,0:T(8,128)(2,1)S(1)}) custom-call(bf16[512,1024]{1,0:T(8,128)(2,1)S(1)} %get-tuple-element.50.refs_0_.refs_1_, bf16[128,1024]{1,0:T(8,128)(2,1)S(1)} %collective-permute-done.1.refs_1_, bf16[256,1024]{1,0:T(8,128)(2,1)S(1)} %get-tuple-element.56.refs_2_.refs_9_, ...), custom_call_target="tpu_custom_call" | custom-call | flops 1207959552 | bytes 6291456 | tf_op jit(solution)/shard_map/backward1_near/pallas_call | solution.py:28
  17.3 1.4 %grads_near.1 = (f32[192,192]{1,0:T(8,128)S(1)}, f32[192,192]{1,0:T(8,128)S(1)}) custom-call(bf16[128,1024]{1,0:T(8,128)(2,1)S(1)} %get-tuple-element.58.refs_0_.refs_6_, bf16[512,1024]{1,0:T(8,128)(2,1)S(1)} %get-tuple-element.50.refs_0_.refs_1_, bf16[256,1024]{1,0:T(8,128)(2,1)S(1)} %get-tuple-element.56.refs_2_.refs_9_, ...), custom_call_target="tpu_custom_call" | custom-call | flops 2415919104 | bytes 3964928 | tf_op jit(solution)/shard_map/grads_near/pallas_call | solution.py:28
  18.7 2.1 %forward_far.1 = (bf16[640,1024]{1,0:T(8,128)(2,1)S(1)}, bf16[640,1024]{1,0:T(8,128)(2,1)S(1)}, bf16[640,1024]{1,0:T(8,128)(2,1)S(1)}) custom-call(f32[192,192]{1,0:T(8,128)S(1)} %get-tuple-element.61.refs_0_.refs_9_, bf16[512,1024]{1,0:T(8,128)(2,1)S(1)} %get-tuple-element.47.refs_0_.refs_1_.refs_6_.refs_4_, ...), custom_call_target="tpu_custom_call" | custom-call | flops 3623878656 | bytes 10223616 | tf_op jit(solution)/shard_map/forward_far/pallas_call | solution.py:28
  20.8 1.0 %backward1_far.1 = (bf16[64,1024]{1,0:T(8,128)(2,1)S(1)}, bf16[64,1024]{1,0:T(8,128)(2,1)S(1)}, bf16[256,1024]{1,0:T(8,128)(2,1)S(1)}, bf16[640,1024]{1,0:T(8,128)(2,1)S(1)}) custom-call(bf16[512,1024]{1,0:T(8,128)(2,1)S(1)} %get-tuple-element.50.refs_0_.refs_1_, bf16[128,1024]{1,0:T(8,128)(2,1)S(1)} %collective-permute-done.refs_1_, ...), custom_call_target="tpu_custom_call" | custom-call | flops 1207959552 | bytes 8912896 | tf_op jit(solution)/shard_map/backward1_far/pallas_call | solution.py:28
  21.8 4.0 %collective-permute-start.4 = (bf16[64,1024]{1,0:T(8,128)(2,1)S(1)}, bf16[64,1024]{1,0:T(8,128)(2,1)S(1)}, u32[]{:S(2)}, u32[]{:S(2)}) collective-permute-start(bf16[64,1024]{1,0:T(8,128)(2,1)S(1)} %get-tuple-element.70), channel_id=1, source_target_pairs={{0,1},{1,0},{2,3},{3,2},{4,5},{5,4},{6,7},{7,6},{8,9},{9,8},{10,11... | collective-permute-start | bytes 393224 | tf_op jit(solution)/shard_map/ppermute | solution.py:509
  26.7 4.1 %middle.1 = (bf16[512,1024]{1,0:T(8,128)(2,1)S(1)}, bf16[384,1024]{1,0:T(8,128)(2,1)S(1)}, f32[192,192]{1,0:T(8,128)S(1)}, f32[192,192]{1,0:T(8,128)S(1)}, f32[1...) custom-call(bf16[512,1024]{1,0:T(8,128)(2,1)S(1)} %get-tuple-element.50.refs_0_.refs_1_, ...), custom_call_target="tpu_custom_call" | custom-call | flops 10871635968 | bytes 12156928 | tf_op jit(solution)/shard_map/middle/pallas_call | solution.py:28
  30.9 1.4 %backward0.1 = (bf16[64,1024]{1,0:T(8,128)(2,1)S(1)}, bf16[64,1024]{1,0:T(8,128)(2,1)S(1)}, f32[64,1152]{1,0:T(8,128)S(1)}, bf16[64,1152]{1,0:T(8,128)(2,1)S(1)}) custom-call(bf16[512,1024]{1,0:T(8,128)(2,1)S(1)} %get-tuple-element.69.refs_0_.refs_6_, bf16[64,1024]{1,0:T(8,128)(2,1)S(1)} %collective-permute-done.4.refs_1_, ...), custom_call_target="tpu_custom_call" | custom-call | flops 2415919104 | bytes 7585792 | tf_op jit(solution)/shard_map/backward0/pallas_call | solution.py:28
  32.4 3.8 %collective-permute-start.6 = (bf16[64,1152]{1,0:T(8,128)(2,1)S(1)}, bf16[64,1152]{1,0:T(8,128)(2,1)S(1)}, u32[]{:S(2)}, u32[]{:S(2)}) collective-permute-start(bf16[64,1152]{1,0:T(8,128)(2,1)S(1)} %get-tuple-element.77), channel_id=1, source_target_pairs={{0,1},{1,0},{2,3},{3,2},{4,5},{5,4},{6,7},{7,6},{8,9},{9,8},{10,11... | collective-permute-start | bytes 442376 | tf_op jit(solution)/shard_map/ppermute | solution.py:509
  36.2 1.0 %collective-permute-done.6.refs_1_ = bf16[64,1152]{1,0:T(8,128)(2,1)S(1)} collective-permute-done((bf16[64,1152]{1,0:T(8,128)(2,1)S(1)}, bf16[64,1152]{1,0:T(8,128)(2,1)S(1)}, u32[]{:S(2)}, u32[]{:S(2)}) %collective-permute-start.6) | collective-permute-done | bytes 147488 | tf_op jit(solution)/shard_map/ppermute | solution.py:509
  37.2 2.1 %collective-permute-start.7 = (bf16[32,1152]{1,0:T(8,128)(2,1)S(1)}, bf16[32,1152]{1,0:T(8,128)(2,1)S(1)}, u32[]{:S(2)}, u32[]{:S(2)}) collective-permute-start(bf16[32,1152]{1,0:T(8,128)(2,1)S(1)} %get-tuple-element.79), channel_id=1, source_target_pairs={{0,2},{1,3},{2,0},{3,1},{4,6},{5,7},{6,4},{7,5},{8,10},{9,11},{10,... | collective-permute-start | bytes 221192 | tf_op jit(solution)/shard_map/ppermute | solution.py:509
  40.0 2.0 %collective-permute-done.7 = bf16[32,1152]{1,0:T(8,128)(2,1)S(1)} collective-permute-done((bf16[32,1152]{1,0:T(8,128)(2,1)S(1)}, bf16[32,1152]{1,0:T(8,128)(2,1)S(1)}, u32[]{:S(2)}, u32[]{:S(2)}) %collective-permute-start.7) | collective-permute-done | bytes 73760 | tf_op jit(solution)/shard_map/ppermute | solution.py:509
  42.1 1.6 %collective-permute-start.8 = (bf16[32,1152]{1,0:T(8,128)(2,1)S(1)}, bf16[32,1152]{1,0:T(8,128)(2,1)S(1)}, u32[]{:S(2)}, u32[]{:S(2)}) collective-permute-start(bf16[32,1152]{1,0:T(8,128)(2,1)S(1)} %add_convert_fusion.1.refs_0_), channel_id=1, source_target_pairs={{0,4},{1,5},{2,6},{3,7},{4,0},{5,1},{6,2},{7,3},{8,12},{9,13},{10,... | collective-permute-start | bytes 221192 | tf_op jit(solution)/shard_map/ppermute | solution.py:509
  43.8 2.6 %collective-permute-start.9 = (bf16[32,1152]{1,0:T(8,128)(2,1)S(1)}, bf16[32,1152]{1,0:T(8,128)(2,1)S(1)}, u32[]{:S(2)}, u32[]{:S(2)}) collective-permute-start(bf16[32,1152]{1,0:T(8,128)(2,1)S(1)} %add_convert_fusion.1.refs_0_), channel_id=1, source_target_pairs={{0,8},{1,9},{2,10},{3,11},{4,12},{5,13},{6,14},{7,15},{8,0},{9,1},... | collective-permute-start | bytes 221192 | tf_op jit(solution)/shard_map/ppermute | solution.py:509
  46.6 1.3 %copy-done.6 = bf16[640,1024]{1,0:T(8,128)(2,1)S(1)} copy-done((bf16[640,1024]{1,0:T(8,128)(2,1)S(1)}, bf16[640,1024]{1,0:T(8,128)(2,1)}, u32[]{:S(2)}) %copy-start.6) | copy-done | bytes 1310744
  47.9 2.5 %output.1 = bf16[64,8,1024]{2,1,0:T(8,128)(2,1)} custom-call(bf16[32,1152]{1,0:T(8,128)(2,1)S(1)} %add_convert_fusion.1.refs_0_, bf16[640,1024]{1,0:T(8,128)(2,1)S(1)} %get-tuple-element.63.refs_2_.refs_1_, bf16[640,1024]{1,0:T(8,128)(2,1)S(1)} %copy-done.6, bf16[8,128,768]{2,1,0:T(8,128)(2,1)S(1)} %weights.1.refs_1_.refs_2_.refs_3_.refs_5_.refs_4_.refs_7_), custom_call_target="tpu_custom_call" | custom-call | flops 2415919104 | bytes 5242880 | tf_op jit(solution)/shard_map/output/pallas_call | solution.py:28
  50.7 2.0 %collective-permute-done.10 = bf16[32,1152]{1,0:T(8,128)(2,1)S(1)} collective-permute-done((bf16[32,1152]{1,0:T(8,128)(2,1)S(1)}, bf16[32,1152]{1,0:T(8,128)(2,1)S(1)}, u32[]{:S(2)}, u32[]{:S(2)}) %collective-permute-start.10) | collective-permute-done | bytes 73760 | tf_op jit(solution)/shard_map/ppermute | solution.py:509
  52.8 1.5 %collective-permute-start.11 = (bf16[32,1152]{1,0:T(8,128)(2,1)S(1)}, bf16[32,1152]{1,0:T(8,128)(2,1)S(1)}, u32[]{:S(2)}, u32[]{:S(2)}) collective-permute-start(bf16[32,1152]{1,0:T(8,128)(2,1)S(1)} %add_convert_fusion.refs_0_), channel_id=1, source_target_pairs={{0,2},{1,3},{2,0},{3,1},{4,6},{5,7},{6,4},{7,5},{8,10},{9,11},{10,... | collective-permute-start | bytes 221192 | tf_op jit(solution)/shard_map/ppermute | solution.py:509
  54.3 2.9 %input_grad.1 = bf16[64,8,1024]{2,1,0:T(8,128)(2,1)} custom-call(bf16[32,1152]{1,0:T(8,128)(2,1)S(1)} %add_convert_fusion.refs_0_, bf16[384,1024]{1,0:T(8,128)(2,1)S(1)} %copy-done.8, bf16[64,1024]{1,0:T(8,128)(2,1)S(1)} %get-tuple-element.87.refs_2_, bf16[64,1024]{1,0:T(8,128)(2,1)S(1)} %get-tuple-element.88.refs_3_, ...), custom_call_target="tpu_custom_call" | custom-call | flops 2415919104 | bytes 4980736 | tf_op jit(solution)/shard_map/input_grad/pallas_call | solution.py:28
  57.3 1.4 %collective-permute-done.14.refs_1_ = bf16[64,1152]{1,0:T(8,128)(2,1)S(1)} collective-permute-done((bf16[64,1152]{1,0:T(8,128)(2,1)S(1)}, bf16[64,1152]{1,0:T(8,128)(2,1)S(1)}, u32[]{:S(2)}, u32[]{:S(2)}) %collective-permute-start.14) | collective-permute-done | bytes 147488 | tf_op jit(solution)/shard_map/ppermute | solution.py:509
  (42 shorter events, 7.5 us)
Async XLA Ops:
  0.6 1.2 %copy-start = (bf16[64,8,1024]{2,1,0:T(8,128)(2,1)S(1)}, bf16[64,8,1024]{2,1,0:T(8,128)(2,1)}, u32[]{:S(2)}) copy-start(bf16[64,8,1024]{2,1,0:T(8,128)(2,1)} %refs_0_.1) | copy-start | bytes 3145732
  2.4 11.9 %collective-permute-start.2 = (bf16[256,1024]{1,0:T(8,128)(2,1)S(1)}, bf16[256,1024]{1,0:T(8,128)(2,1)S(1)}, u32[]{:S(2)}, u32[]{:S(2)}) collective-permute-start(bf16[256,1024]{1,0:T(8,128)(2,1)S(1)} %get-tuple-element.53), channel_id=1, source_target_pairs={{0,1},{1,0},{2,3},{3,2},{4,5},{5,4},{6,7},{7,6},{8,9},{9,8},{10,11... | collective-permute-start | bytes 1572872 | tf_op jit(solution)/shard_map/ppermute | solution.py:509
  3.0 15.7 %collective-permute-start.3 = (bf16[256,1024]{1,0:T(8,128)(2,1)S(1)}, bf16[256,1024]{1,0:T(8,128)(2,1)S(1)}, u32[]{:S(2)}, u32[]{:S(2)}) collective-permute-start(bf16[256,1024]{1,0:T(8,128)(2,1)S(1)} %get-tuple-element.48.refs_0_), channel_id=1, source_target_pairs={{1,2},{3,4},{5,6},{7,8},{9,10},{11,12},{13,14},{2,1},{4,3},{6,5},{... | collective-permute-start | bytes 1572872 | tf_op jit(solution)/shard_map/ppermute | solution.py:531
  3.6 1.0 %copy-start.1 = (bf16[2,2,64,576]{3,2,1,0:T(8,128)(2,1)S(1)}, bf16[2,2,64,576]{3,2,1,0:T(8,128)(2,1)}, u32[]{:S(2)}) copy-start(bf16[2,2,64,576]{3,2,1,0:T(8,128)(2,1)} %refs_1_.2) | copy-start | bytes 884740
  5.3 1.7 %copy-start.2 = (bf16[64,8,1024]{2,1,0:T(8,128)(2,1)S(1)}, bf16[64,8,1024]{2,1,0:T(8,128)(2,1)}, u32[]{:S(2)}) copy-start(bf16[64,8,1024]{2,1,0:T(8,128)(2,1)} %refs_1_.3) | copy-start | bytes 3145732
  8.5 12.3 %collective-permute-start = (bf16[128,1024]{1,0:T(8,128)(2,1)S(1)}, bf16[128,1024]{1,0:T(8,128)(2,1)S(1)}, u32[]{:S(2)}, u32[]{:S(2)}) collective-permute-start(bf16[128,1024]{1,0:T(8,128)(2,1)S(1)} %get-tuple-element.51), channel_id=1, source_target_pairs={{1,2},{3,4},{5,6},{7,8},{9,10},{11,12},{13,14},{2,1},{4,3},{6,5},{... | collective-permute-start | bytes 786440 | tf_op jit(solution)/shard_map/ppermute | solution.py:531
  9.2 7.0 %collective-permute-start.1 = (bf16[128,1024]{1,0:T(8,128)(2,1)S(1)}, bf16[128,1024]{1,0:T(8,128)(2,1)S(1)}, u32[]{:S(2)}, u32[]{:S(2)}) collective-permute-start(bf16[128,1024]{1,0:T(8,128)(2,1)S(1)} %get-tuple-element.52.refs_0_), channel_id=1, source_target_pairs={{0,1},{1,0},{2,3},{3,2},{4,5},{5,4},{6,7},{7,6},{8,9},{9,8},{10,11... | collective-permute-start | bytes 786440 | tf_op jit(solution)/shard_map/ppermute | solution.py:509
  20.8 5.9 %copy-start.5 = (bf16[640,1024]{1,0:T(8,128)(2,1)}, bf16[640,1024]{1,0:T(8,128)(2,1)S(1)}, u32[]{:S(2)}) copy-start(bf16[640,1024]{1,0:T(8,128)(2,1)S(1)} %get-tuple-element.66.refs_4_.refs_2_) | copy-start | bytes 3932164
  21.8 9.1 %collective-permute-start.4 = (bf16[64,1024]{1,0:T(8,128)(2,1)S(1)}, bf16[64,1024]{1,0:T(8,128)(2,1)S(1)}, u32[]{:S(2)}, u32[]{:S(2)}) collective-permute-start(bf16[64,1024]{1,0:T(8,128)(2,1)S(1)} %get-tuple-element.70), channel_id=1, source_target_pairs={{0,1},{1,0},{2,3},{3,2},{4,5},{5,4},{6,7},{7,6},{8,9},{9,8},{10,11... | collective-permute-start | bytes 393224 | tf_op jit(solution)/shard_map/ppermute | solution.py:509
  25.9 5.0 %collective-permute-start.5 = (bf16[64,1024]{1,0:T(8,128)(2,1)S(1)}, bf16[64,1024]{1,0:T(8,128)(2,1)S(1)}, u32[]{:S(2)}, u32[]{:S(2)}) collective-permute-start(bf16[64,1024]{1,0:T(8,128)(2,1)S(1)} %get-tuple-element.71), channel_id=1, source_target_pairs={{1,2},{3,4},{5,6},{7,8},{9,10},{11,12},{13,14},{2,1},{4,3},{6,5},{... | collective-permute-start | bytes 393224 | tf_op jit(solution)/shard_map/ppermute | solution.py:531
  30.8 1.5 %copy-start.3 = (bf16[512,1024]{1,0:T(8,128)(2,1)}, bf16[512,1024]{1,0:T(8,128)(2,1)S(1)}, u32[]{:S(2)}) copy-start(bf16[512,1024]{1,0:T(8,128)(2,1)S(1)} %get-tuple-element.69.refs_0_.refs_6_) | copy-start | bytes 3145732
  30.9 1.5 %copy-start.7 = (bf16[384,1024]{1,0:T(8,128)(2,1)}, bf16[384,1024]{1,0:T(8,128)(2,1)S(1)}, u32[]{:S(2)}) copy-start(bf16[384,1024]{1,0:T(8,128)(2,1)S(1)} %get-tuple-element.84.refs_1_) | copy-start | bytes 2359300
  32.4 4.8 %collective-permute-start.6 = (bf16[64,1152]{1,0:T(8,128)(2,1)S(1)}, bf16[64,1152]{1,0:T(8,128)(2,1)S(1)}, u32[]{:S(2)}, u32[]{:S(2)}) collective-permute-start(bf16[64,1152]{1,0:T(8,128)(2,1)S(1)} %get-tuple-element.77), channel_id=1, source_target_pairs={{0,1},{1,0},{2,3},{3,2},{4,5},{5,4},{6,7},{7,6},{8,9},{9,8},{10,11... | collective-permute-start | bytes 442376 | tf_op jit(solution)/shard_map/ppermute | solution.py:509
  37.2 4.9 %collective-permute-start.7 = (bf16[32,1152]{1,0:T(8,128)(2,1)S(1)}, bf16[32,1152]{1,0:T(8,128)(2,1)S(1)}, u32[]{:S(2)}, u32[]{:S(2)}) collective-permute-start(bf16[32,1152]{1,0:T(8,128)(2,1)S(1)} %get-tuple-element.79), channel_id=1, source_target_pairs={{0,2},{1,3},{2,0},{3,1},{4,6},{5,7},{6,4},{7,5},{8,10},{9,11},{10,... | collective-permute-start | bytes 221192 | tf_op jit(solution)/shard_map/ppermute | solution.py:509
  39.3 15.0 %collective-permute-start.12 = (bf16[64,1024]{1,0:T(8,128)(2,1)S(1)}, bf16[64,1024]{1,0:T(8,128)(2,1)S(1)}, u32[]{:S(2)}, u32[]{:S(2)}) collective-permute-start(bf16[64,1024]{1,0:T(8,128)(2,1)S(1)} %get-tuple-element.87.refs_2_), channel_id=1, source_target_pairs={{0,1},{1,0},{2,3},{3,2},{4,5},{5,4},{6,7},{7,6},{8,9},{9,8},{10,11... | collective-permute-start | bytes 393224 | tf_op jit(solution)/shard_map/ppermute | solution.py:509
  39.4 14.9 %collective-permute-start.13 = (bf16[64,1024]{1,0:T(8,128)(2,1)S(1)}, bf16[64,1024]{1,0:T(8,128)(2,1)S(1)}, u32[]{:S(2)}, u32[]{:S(2)}) collective-permute-start(bf16[64,1024]{1,0:T(8,128)(2,1)S(1)} %get-tuple-element.88.refs_3_), channel_id=1, source_target_pairs={{1,2},{3,4},{5,6},{7,8},{9,10},{11,12},{13,14},{2,1},{4,3},{6,5},{... | collective-permute-start | bytes 393224 | tf_op jit(solution)/shard_map/ppermute | solution.py:531
  42.1 12.2 %copy-start.4 = (bf16[512,1024]{1,0:T(8,128)(2,1)S(1)}, bf16[512,1024]{1,0:T(8,128)(2,1)}, u32[]{:S(2)}) copy-start(bf16[512,1024]{1,0:T(8,128)(2,1)} %copy-done.3) | copy-start | bytes 3145732
  42.1 8.3 %collective-permute-start.8 = (bf16[32,1152]{1,0:T(8,128)(2,1)S(1)}, bf16[32,1152]{1,0:T(8,128)(2,1)S(1)}, u32[]{:S(2)}, u32[]{:S(2)}) collective-permute-start(bf16[32,1152]{1,0:T(8,128)(2,1)S(1)} %add_convert_fusion.1.refs_0_), channel_id=1, source_target_pairs={{0,4},{1,5},{2,6},{3,7},{4,0},{5,1},{6,2},{7,3},{8,12},{9,13},{10,... | collective-permute-start | bytes 221192 | tf_op jit(solution)/shard_map/ppermute | solution.py:509
  43.8 7.0 %collective-permute-start.9 = (bf16[32,1152]{1,0:T(8,128)(2,1)S(1)}, bf16[32,1152]{1,0:T(8,128)(2,1)S(1)}, u32[]{:S(2)}, u32[]{:S(2)}) collective-permute-start(bf16[32,1152]{1,0:T(8,128)(2,1)S(1)} %add_convert_fusion.1.refs_0_), channel_id=1, source_target_pairs={{0,8},{1,9},{2,10},{3,11},{4,12},{5,13},{6,14},{7,15},{8,0},{9,1},... | collective-permute-start | bytes 221192 | tf_op jit(solution)/shard_map/ppermute | solution.py:509
  46.3 6.4 %collective-permute-start.10 = (bf16[32,1152]{1,0:T(8,128)(2,1)S(1)}, bf16[32,1152]{1,0:T(8,128)(2,1)S(1)}, u32[]{:S(2)}, u32[]{:S(2)}) collective-permute-start(bf16[32,1152]{1,0:T(8,128)(2,1)S(1)} %add_convert_fusion.1.refs_0_), channel_id=1, source_target_pairs={{0,12},{1,13},{2,14},{3,15},{4,8},{5,9},{6,10},{7,11},{8,4},{9,5},... | collective-permute-start | bytes 221192 | tf_op jit(solution)/shard_map/ppermute | solution.py:509
  46.6 1.3 %copy-start.6 = (bf16[640,1024]{1,0:T(8,128)(2,1)S(1)}, bf16[640,1024]{1,0:T(8,128)(2,1)}, u32[]{:S(2)}) copy-start(bf16[640,1024]{1,0:T(8,128)(2,1)} %copy-done.5) | copy-start | bytes 3932164
  47.9 6.4 %copy-start.8 = (bf16[384,1024]{1,0:T(8,128)(2,1)S(1)}, bf16[384,1024]{1,0:T(8,128)(2,1)}, u32[]{:S(2)}) copy-start(bf16[384,1024]{1,0:T(8,128)(2,1)} %copy-done.7) | copy-start | bytes 2359300
  52.8 4.4 %collective-permute-start.11 = (bf16[32,1152]{1,0:T(8,128)(2,1)S(1)}, bf16[32,1152]{1,0:T(8,128)(2,1)S(1)}, u32[]{:S(2)}, u32[]{:S(2)}) collective-permute-start(bf16[32,1152]{1,0:T(8,128)(2,1)S(1)} %add_convert_fusion.refs_0_), channel_id=1, source_target_pairs={{0,2},{1,3},{2,0},{3,1},{4,6},{5,7},{6,4},{7,5},{8,10},{9,11},{10,... | collective-permute-start | bytes 221192 | tf_op jit(solution)/shard_map/ppermute | solution.py:509
  57.2 1.4 %collective-permute-start.14 = (bf16[64,1152]{1,0:T(8,128)(2,1)S(1)}, bf16[64,1152]{1,0:T(8,128)(2,1)S(1)}, u32[]{:S(2)}, u32[]{:S(2)}) collective-permute-start(bf16[64,1152]{1,0:T(8,128)(2,1)S(1)} %maximum_select_fusion.refs_0_), channel_id=1, source_target_pairs={{0,1},{1,0},{2,3},{3,2},{4,5},{5,4},{6,7},{7,6},{8,9},{9,8},{10,11... | collective-permute-start | bytes 442376 | tf_op jit(solution)/shard_map/ppermute | solution.py:509
